TPU v7x, 32 devices: a whole 2x2x4 slice. The times are simulated.
32 devices in a mesh: grp: 2 (over x), seq: 16 (over z, y, core).
Axes of the slice: x: 2, y: 2, z: 4, core: 2. Of those that a mesh axis runs over, the one named last changes fastest.
Arguments:
- query_rows: bfloat16 [4096, 16, 128], P(('grp', 'seq')), parts along dimension 0, may hold values from -120 to 120
- key_rows: bfloat16 [4096, 16, 128], P(('grp', 'seq')), parts along dimension 0, may hold values from -6 to 6
- value_rows: bfloat16 [4096, 16, 128], P(('grp', 'seq')), parts along dimension 0, may hold values from -6 to 6
- out_grad: bfloat16 [4096, 16, 128], P(('grp', 'seq')), parts along dimension 0, may hold values from -6 to 6
- window_blocks: int32 [16], replicated, may hold values from 1 to 3, as said below
- section_heads: int32 [4, 4], replicated, may hold values from 0 to 15, as said below
Outputs:
- attended: bfloat16 [4096, 16, 128], P(('grp', 'seq')), parts along dimension 0
- query_grad: bfloat16 [4096, 16, 128], P(('grp', 'seq')), parts along dimension 0
- key_grad: bfloat16 [4096, 16, 128], P(('grp', 'seq')), parts along dimension 0
- value_grad: bfloat16 [4096, 16, 128], P(('grp', 'seq')), parts along dimension 0
There are 2 independent parts, one for each index of `grp`. A program takes and returns all parts, laid end to end along the dimension named above; an argument that names none is the same for every part. Nothing has to cross between parts.
Inputs may be any that keep to these rules, and one draw needn't show every extreme that they name: `section_heads`: row s lists 4 different heads; every head appears in some row. `window_blocks`: some head has width 1 and some head has width 3.
All inputs are finite; a program needn't handle non-finite values.
Results may differ from a plain program's by a relative error of at most 0.03.
Values may be sent and summed in bfloat16 or wider, within the bound.
No kernel may reach another device: no remote copies, remote signals or barrier semaphores. Data moves between devices by JAX's collectives and lax.ppermute only.
A program may use at most 128 MiB of HBM per device.

v0:
```python
import math

import jax
import jax.numpy as jnp
from jax import lax
from jax.sharding import PartitionSpec as P

BLK = 128
WB = 3


blocked_score = -1e30


def partner(value, axis, apart):
    return lax.ppermute(value, axis, [(i, i ^ 1 << apart) for i in range(lax.axis_size(axis))])


def passed_along(value, axis, by):
    peers = lax.axis_size(axis)
    pairs = [(i, i + by) for i in range(peers) if 0 <= i + by < peers]
    return lax.ppermute(value, axis, pairs)


def to_slots(values, picker):
    return jnp.sum(jnp.where(picker[None, :, :, None], values[:, None, :, :], 0.0), axis=2)


def to_heads(values, picker, filler):
    covered = jnp.any(picker, axis=0)
    summed = jnp.sum(jnp.where(picker[None, :, :, None], values[:, :, None, :], 0.0), axis=1)
    return jnp.where(covered[None, :, None], summed, filler)


def rows_to_heads(values, picker):
    return jnp.einsum(
        "jqid,ih->jqhd", values, picker.astype(jnp.float32), precision=lax.Precision.HIGHEST
    )


def pick_heads(values, picker):
    chooser = picker.astype(jnp.bfloat16)
    return jnp.einsum("ih,jqhd->jqid", chooser, values, preferred_element_type=jnp.float32).astype(
        jnp.bfloat16
    )


def partner_route(values, section_index, low_bits):
    return partner(values, "seq", section_index - low_bits)


def partner_back(values, section_index, low_bits):
    return partner(values, "seq", section_index - low_bits)


def extend_blocks(values, reach, halo_blocks, blocks_dev, mover):
    pieces = [mover(values, distance) for distance in range(reach, 0, -1)]
    pieces = pieces + [values] + [mover(values, -distance) for distance in range(1, reach + 1)]
    start = reach * blocks_dev - halo_blocks
    whole = jnp.concatenate(pieces, axis=1)
    return whole


def move_keys(values, distance):
    return passed_along(values, "seq", distance)


def window_sets(extended, blocks_dev, spread):
    return jnp.stack(
        [extended[:, offset : offset + blocks_dev] for offset in range(spread)], axis=2
    )


def per_device(query_rows, key_rows, value_rows, out_grad, window_blocks, section_heads):
    tokens_dev, head_count, head_width = query_rows.shape
    blocks_dev = tokens_dev // BLK
    low_bits = blocks_dev.bit_length() - 1
    seq_count = lax.axis_size("seq")
    section_total = low_bits + seq_count.bit_length() - 1
    halo_blocks = WB - 1
    reach = (halo_blocks + blocks_dev - 1) // blocks_dev
    padding = reach * blocks_dev
    spread = 2 * WB - 1
    score_scale = 1.0 / math.sqrt(head_width)
    first_block = lax.axis_index("seq") * blocks_dev + jnp.arange(blocks_dev, dtype=jnp.int32)
    all_blocks = blocks_dev * seq_count
    query_blocks = query_rows.reshape(blocks_dev, BLK, head_count, head_width)
    key_blocks = key_rows.reshape(blocks_dev, BLK, head_count, head_width)
    value_blocks = value_rows.reshape(blocks_dev, BLK, head_count, head_width)
    grad_blocks = out_grad.reshape(blocks_dev, BLK, head_count, head_width)
    offsets = jnp.arange(spread, dtype=jnp.int32) - halo_blocks
    near_block = first_block[:, None] + offsets[None, :]
    in_range = (near_block >= 0) & (near_block < all_blocks)
    near_mask = in_range[:, None, :] & (
        jnp.abs(offsets)[None, None, :] < window_blocks[None, :, None]
    )
    wide_mask = near_mask[:, :, None, :, None]
    head_ids = jnp.arange(head_count, dtype=jnp.int32)
    paired = jnp.stack([key_blocks, value_blocks])
    extended = extend_blocks(paired, reach, halo_blocks, blocks_dev, move_keys)
    near_sets = window_sets(extended, blocks_dev, spread)
    near_keys = near_sets[0]
    near_values = near_sets[1]
    near_scores = (
        jnp.einsum("jqhd,jckhd->jhqck", query_blocks, near_keys, preferred_element_type=jnp.float32)
        * score_scale
    )
    near_scores = jnp.where(wide_mask, near_scores, blocked_score)
    top_score = jnp.max(near_scores, axis=(3, 4))
    records = []
    for section_index in range(section_total):
        picker = section_heads[section_index][:, None] == head_ids[None, :]
        slot_width = jnp.sum(jnp.where(picker, window_blocks[None, :], 0), axis=1)
        slot_valid = 2**section_index >= slot_width
        chosen_query = pick_heads(query_blocks, picker)
        chosen_grad = pick_heads(grad_blocks, picker)
        chosen_pair = jnp.stack([pick_heads(key_blocks, picker), pick_heads(value_blocks, picker)])
        partner_pair = partner_route(chosen_pair, section_index, low_bits)
        far_scores = (
            jnp.einsum(
                "jqid,jkid->jiqk", chosen_query, partner_pair[0], preferred_element_type=jnp.float32
            )
            * score_scale
        )
        far_scores = jnp.where(slot_valid[None, :, None, None], far_scores, blocked_score)
        top_score = jnp.maximum(
            top_score, to_heads(jnp.max(far_scores, axis=3), picker, blocked_score)
        )
        records.append(
            (
                section_index,
                picker,
                slot_valid,
                chosen_query,
                chosen_grad,
                chosen_pair,
                partner_pair,
                far_scores,
            )
        )
    row_total = jnp.sum(
        jnp.where(wide_mask, jnp.exp(near_scores - top_score[:, :, :, None, None]), 0.0),
        axis=(3, 4),
    )
    for record in records:
        picker = record[1]
        slot_top = to_slots(top_score, picker)
        far_sum = jnp.sum(
            jnp.where(
                record[2][None, :, None, None], jnp.exp(record[7] - slot_top[:, :, :, None]), 0.0
            ),
            axis=3,
        )
        row_total = row_total + to_heads(far_sum, picker, 0.0)
    log_total = top_score + jnp.log(row_total)
    near_probs = jnp.where(
        wide_mask, jnp.exp(near_scores - log_total[:, :, :, None, None]), 0.0
    ).astype(jnp.bfloat16)
    attended_sum = jnp.einsum(
        "jhqck,jckhd->jqhd", near_probs, near_values, preferred_element_type=jnp.float32
    )
    far_probs_list = []
    for record in records:
        picker = record[1]
        slot_lse = to_slots(log_total, picker)
        far_probs = jnp.where(
            record[2][None, :, None, None], jnp.exp(record[7] - slot_lse[:, :, :, None]), 0.0
        ).astype(jnp.bfloat16)
        far_probs_list.append((far_probs, slot_lse))
        attended_sum = attended_sum + rows_to_heads(
            jnp.einsum(
                "jiqk,jkid->jqid", far_probs, record[6][1], preferred_element_type=jnp.float32
            ),
            picker,
        )
    attended = attended_sum.astype(jnp.bfloat16)
    row_delta = jnp.transpose(
        jnp.sum(grad_blocks.astype(jnp.float32) * attended.astype(jnp.float32), axis=-1), (0, 2, 1)
    )
    near_dprob = jnp.einsum(
        "jqhd,jckhd->jhqck", grad_blocks, near_values, preferred_element_type=jnp.float32
    )
    near_dscore = (
        near_probs.astype(jnp.float32) * (near_dprob - row_delta[:, :, :, None, None])
    ).astype(jnp.bfloat16)
    query_sum = jnp.einsum(
        "jhqck,jckhd->jqhd", near_dscore, near_keys, preferred_element_type=jnp.float32
    )
    far_dscores = []
    for record, probs_pair in zip(records, far_probs_list):
        picker = record[1]
        slot_delta = to_slots(row_delta, picker)
        far_dprob = jnp.einsum(
            "jqid,jkid->jiqk", record[4], record[6][1], preferred_element_type=jnp.float32
        )
        far_dscore = (
            probs_pair[0].astype(jnp.float32) * (far_dprob - slot_delta[:, :, :, None])
        ).astype(jnp.bfloat16)
        far_dscores.append((far_dscore, slot_delta))
        query_sum = query_sum + rows_to_heads(
            jnp.einsum(
                "jiqk,jkid->jqid", far_dscore, record[6][0], preferred_element_type=jnp.float32
            ),
            picker,
        )
    query_grad = (
        (query_sum * score_scale).astype(jnp.bfloat16).reshape(tokens_dev, head_count, head_width)
    )
    near_key_part = (
        jnp.einsum(
            "jhqck,jqhd->jckhd", near_dscore, query_blocks, preferred_element_type=jnp.float32
        )
        * score_scale
    )
    near_value_part = jnp.einsum(
        "jhqck,jqhd->jckhd", near_probs, grad_blocks, preferred_element_type=jnp.float32
    )
    stacked_parts = jnp.stack([near_key_part, near_value_part])
    extended_count = blocks_dev + 2 * padding
    base = padding - halo_blocks
    extended_ids = jnp.arange(extended_count, dtype=jnp.int32)
    own_ids = jnp.arange(blocks_dev, dtype=jnp.int32)
    spread_ids = jnp.arange(spread, dtype=jnp.int32)
    placer = (
        extended_ids[:, None, None] == base + own_ids[None, :, None] + spread_ids[None, None, :]
    ).astype(jnp.float32)
    gathered = jnp.einsum(
        "ejc,xjckhd->xekhd", placer, stacked_parts, precision=lax.Precision.HIGHEST
    )
    own_grads = gathered[:, padding : padding + blocks_dev]
    for distance in range(1, reach + 1):
        lower_slab = gathered[
            :, padding - distance * blocks_dev : padding - (distance - 1) * blocks_dev
        ]
        own_grads = own_grads + passed_along(
            lower_slab.astype(jnp.bfloat16), "seq", -distance
        ).astype(lower_slab.dtype)
        upper_start = padding + blocks_dev + (distance - 1) * blocks_dev
        upper_slab = gathered[:, upper_start : upper_start + blocks_dev]
        own_grads = own_grads + passed_along(
            upper_slab.astype(jnp.bfloat16), "seq", distance
        ).astype(upper_slab.dtype)
    for record, probs_pair, dscore_pair in zip(records, far_probs_list, far_dscores):
        picker = record[1]
        key_part = (
            jnp.einsum(
                "jiqk,jqid->jkid", dscore_pair[0], record[3], preferred_element_type=jnp.float32
            )
            * score_scale
        )
        value_part = jnp.einsum(
            "jiqk,jqid->jkid", probs_pair[0], record[4], preferred_element_type=jnp.float32
        )
        returned = partner_back(jnp.stack([key_part, value_part]), record[0], low_bits)
        own_grads = own_grads + jnp.stack(
            [rows_to_heads(returned[0], picker), rows_to_heads(returned[1], picker)]
        )
    key_grad = own_grads[0].astype(jnp.bfloat16).reshape(tokens_dev, head_count, head_width)
    value_grad = own_grads[1].astype(jnp.bfloat16).reshape(tokens_dev, head_count, head_width)
    return (attended.reshape(tokens_dev, head_count, head_width), query_grad, key_grad, value_grad)


def solution(mesh):
    in_specs = (
        P(("grp", "seq"), None, None),
        P(("grp", "seq"), None, None),
        P(("grp", "seq"), None, None),
        P(("grp", "seq"), None, None),
        P(),
        P(),
    )
    out_specs = (
        P(("grp", "seq"), None, None),
        P(("grp", "seq"), None, None),
        P(("grp", "seq"), None, None),
        P(("grp", "seq"), None, None),
    )
    return jax.shard_map(
        per_device, mesh=mesh, in_specs=in_specs, out_specs=out_specs, check_vma=False
    )
```

profile of v0, /device:TPU:1, one launch (start us, length us, event | category | flops | bytes accessed | tf_op | source)
XLA Modules:
  0.0 320.9 jit_solution(573172104690355855)
XLA Ops:
  3.4 5.0 %collective-permute-start = (bf16[2,1,128,16,128]{4,2,3,0,1:T(8,128)(2,1)}, bf16[2,1,128,16,128]{4,2,3,0,1:T(8,128)(2,1)}, u32[]{:S(2)}, u32[]{:S(2)}) collective-permute-start(bf16[2,1,128,16,128]{4,2,3,0,1:T(8,128)(2,1)} %pad_maximum_fusion), channel_id=1, source_target_pairs={{0,2},{1,3},{2,4},{3,5},{4,6},{5,7},{6,8},{7,9},{8,10},{9,11},{10,... | collective-permute-start | bytes 3145736 | tf_op jit(solution)/shard_map/ppermute | solution.py:22
  8.3 3.0 collective-permute-start.1
  11.3 2.3 collective-permute-start.2
  18.0 1.9 collective-permute-start.7
  48.5 6.7 %collective-permute-start.5 = (bf16[2,1,128,4,128]{4,3,2,1,0:T(4,128)(2,1)}, bf16[2,1,128,4,128]{4,3,2,1,0:T(4,128)(2,1)S(1)}, u32[]{:S(2)}, u32[]{:S(2)}) collective-permute-start(bf16[2,1,128,4,128]{4,3,2,1,0:T(4,128)(2,1)} %pad_maximum_fusion.6), channel_id=1, source_target_pairs={{0,2},{1,3},{2,0},{3,1},{4,6},{5,7},{6,4},{7,5},{8,10},{9,11},{10,... | collective-permute-start | bytes 786440 | tf_op jit(solution)/shard_map/ppermute | solution.py:16
  57.9 23.8 %collective-permute-done.5 = bf16[2,1,128,4,128]{4,3,2,1,0:T(4,128)(2,1)S(1)} collective-permute-done((bf16[2,1,128,4,128]{4,3,2,1,0:T(4,128)(2,1)}, bf16[2,1,128,4,128]{4,3,2,1,0:T(4,128)(2,1)S(1)}, u32[]{:S(2)}, u32[]{:S(2)}) %collective-permute-start.5) | collective-permute-done | bytes 262176 | tf_op jit(solution)/shard_map/ppermute | solution.py:16
  100.0 2.0 fusion.8
  105.9 2.6 copy.466
  113.9 2.7 fusion.104
  116.6 2.6 copy.462
  120.9 1.8 convolution_bitcast_fusion.19
  124.5 2.7 fusion.114
  127.2 2.6 copy.458
  135.9 2.6 copy.454
  138.6 5.1 %fusion.66 = (f32[128,16]{0,1:T(8,128)S(1)}, bf16[1,128,16,128]{1,3,2,0:T(8,128)(2,1)}) fusion(bf16[128,16,128]{0,2,1:T(8,128)(2,1)} %copy.468, f32[16,128,128]{1,2,0:T(8,128)} %copy.466, f32[16,128,128]{1,2,0:T(8,128)} %copy.462, f32[16,128,128]{1,2,0:T(8,128)} %copy.458, f32[16,128,128]{1,2,0:T(8,128)} %copy.454, ...), kind=kOutput, calls=%fused_computation.128 | convolution fusion | flops 337901568 | bytes 10493952 | tf_op jit(solution)/shard_map/jhqck,jckhd->jqhd/dot_general | solution.py:159
  143.8 4.2 %fusion.2 = bf16[16,128,5,128]{1,3,2,0:T(8,128)(2,1)} fusion(bf16[16,128,5,128]{1,3,2,0:T(8,128)(2,1)S(1)} %fusion.8, f32[16,128]{1,0:T(8,128)S(1)} %bitcast.651, bf16[2,1,5,128,16,128]{5,3,2,4,1,0:T(8,128)(2,1)} %copy-done.7, bf16[128,16,128,1]{2,1,0,3:T(8,128)(2,1)S(1)} %bitcast.647), kind=kOutput, calls=%fused_computation.5 | convolution fusion | flops 340787200 | bytes 8396800 | tf_op jit(solution)/shard_map/jqhd,jckhd->jhqck/dot_general | solution.py:180
  148.1 3.2 convolution_bitcast_fusion
  167.0 14.4 %copy.491 = f32[16,128,128]{1,2,0:T(8,128)} copy(f32[16,128,128]{2,0,1:T(8,128)} %fusion.101) | data formatting | bytes 2097152 | tf_op jit(solution)/shard_map/jqid,ih->jqhd/dot_general | solution.py:36
  184.2 2.6 copy.484
  189.7 2.6 copy.477
  192.3 3.2 multiply_bitcast_fusion
  195.5 3.0 fusion.33
  199.6 4.9 %maximum_bitcast_fusion = f32[2,5,128,16,128]{4,2,1,3,0:T(8,128)S(1)} fusion(f32[1,1,5,128,16,128]{5,3,2,4,1,0:T(8,128)} %convolution_bitcast_fusion, f32[1,1,5,128,16,128]{5,3,2,4,1,0:T(8,128)} %multiply_bitcast_fusion), kind=kLoop, calls=%fused_computation.2 | loop fusion | flops 2621440 | bytes 20971520 | tf_op jit(solution)/shard_map/reshape.187
  204.6 24.6 %fusion = f32[2,128,16,128,5]{3,4,2,1,0:T(8,128)} fusion(f32[2,5,128,16,128]{4,2,1,3,0:T(8,128)S(1)} %maximum_bitcast_fusion), kind=kOutput, calls=%fused_computation | convolution fusion | flops 157286432 | bytes 20971520 | tf_op jit(solution)/shard_map/ejc,xjckhd->xekhd/dot_general | solution.py:227
  229.2 8.1 %fusion.134 = (bf16[2,5,128,16,128]{4,3,2,1,0:T(8,128)(2,1)S(1)}, f32[2,5,128,16,128]{4,3,2,1,0:T(8,128)S(1)}) fusion(f32[2,128,16,128,5]{3,4,2,1,0:T(8,128)} %fusion), kind=kLoop, calls=%fused_computation.278 | loop fusion | flops 2621440 | bytes 26214400 | tf_op jit(solution)/shard_map/convert.6
  240.7 2.1 collective-permute-start.15
  243.5 3.4 %collective-permute-start.11 = (bf16[2,1,128,16,128]{4,3,2,1,0:T(8,128)(2,1)S(1)}, bf16[2,1,128,16,128]{4,3,2,1,0:T(8,128)(2,1)S(1)}, u32[]{:S(2)}, u32[]{:S(2)}) collective-permute-start(bf16[2,1,128,16,128]{4,3,2,1,0:T(8,128)(2,1)S(1)} %get-tuple-element.43), channel_id=1, source_target_pairs={{0,2},{1,3},{2,4},{3,5},{4,6},{5,7},{6,8},{7,9},{8,10},{9,11},{10,... | collective-permute-start | bytes 3145736 | tf_op jit(solution)/shard_map/ppermute | solution.py:22
  251.6 4.2 %collective-permute-start.9 = (bf16[2,1,128,16,128]{4,3,2,1,0:T(8,128)(2,1)S(1)}, bf16[2,1,128,16,128]{4,3,2,1,0:T(8,128)(2,1)S(1)}, u32[]{:S(2)}, u32[]{:S(2)}) collective-permute-start(bf16[2,1,128,16,128]{4,3,2,1,0:T(8,128)(2,1)S(1)} %get-tuple-element.45), channel_id=1, source_target_pairs={{0,1},{1,2},{2,3},{3,4},{4,5},{5,6},{6,7},{7,8},{8,9},{9,10},{10,1... | collective-permute-start | bytes 3145736 | tf_op jit(solution)/shard_map/ppermute | solution.py:22
  256.7 6.5 %collective-permute-done.14 = f32[2,1,128,4,128]{4,2,3,1,0:T(8,128)S(1)} collective-permute-done((f32[2,1,128,4,128]{4,2,3,1,0:T(8,128)S(1)}, f32[2,1,128,4,128]{4,2,3,1,0:T(8,128)S(1)}, u32[]{:S(2)}, u32[]{:S(2)}) %collective-permute-start.14) | collective-permute-done | bytes 524320 | tf_op jit(solution)/shard_map/ppermute | solution.py:16
  263.2 3.8 %collective-permute-start.8 = (bf16[2,1,128,16,128]{4,3,2,1,0:T(8,128)(2,1)S(1)}, bf16[2,1,128,16,128]{4,3,2,1,0:T(8,128)(2,1)S(1)}, u32[]{:S(2)}, u32[]{:S(2)}) collective-permute-start(bf16[2,1,128,16,128]{4,3,2,1,0:T(8,128)(2,1)S(1)} %get-tuple-element.42), channel_id=1, source_target_pairs={{1,0},{2,1},{3,2},{4,3},{5,4},{6,5},{7,6},{8,7},{9,8},{10,9},{11,1... | collective-permute-start | bytes 3145736 | tf_op jit(solution)/shard_map/ppermute | solution.py:22
  271.1 35.7 %collective-permute-done.11 = bf16[2,1,128,16,128]{4,3,2,1,0:T(8,128)(2,1)S(1)} collective-permute-done((bf16[2,1,128,16,128]{4,3,2,1,0:T(8,128)(2,1)S(1)}, bf16[2,1,128,16,128]{4,3,2,1,0:T(8,128)(2,1)S(1)}, u32[]{:S(2)}, u32[]{:S(2)}) %collective-permute-start.11) | collective-permute-done | bytes 1048608 | tf_op jit(solution)/shard_map/ppermute | solution.py:22
  306.8 11.7 %collective-permute-done.9 = bf16[2,1,128,16,128]{4,3,2,1,0:T(8,128)(2,1)S(1)} collective-permute-done((bf16[2,1,128,16,128]{4,3,2,1,0:T(8,128)(2,1)S(1)}, bf16[2,1,128,16,128]{4,3,2,1,0:T(8,128)(2,1)S(1)}, u32[]{:S(2)}, u32[]{:S(2)}) %collective-permute-start.9) | collective-permute-done | bytes 1048608 | tf_op jit(solution)/shard_map/ppermute | solution.py:22
  (302 shorter events, 113.1 us)
Async XLA Ops:
  0.6 22.2 %copy-start = (bf16[128,16,128]{2,1,0:T(8,128)(2,1)S(1)}, bf16[128,16,128]{2,1,0:T(8,128)(2,1)}, u32[]{:S(2)}) copy-start(bf16[128,16,128]{2,1,0:T(8,128)(2,1)} %param.6) | copy-start | bytes 1572868
  0.6 19.3 %copy-start.4 = (bf16[128,16,128]{2,1,0:T(8,128)(2,1)S(1)}, bf16[128,16,128]{2,1,0:T(8,128)(2,1)}, u32[]{:S(2)}) copy-start(bf16[128,16,128]{2,1,0:T(8,128)(2,1)} %param.8) | copy-start | bytes 1572868
  0.7 19.6 %copy-start.5 = (bf16[128,16,128]{2,1,0:T(8,128)(2,1)S(1)}, bf16[128,16,128]{2,1,0:T(8,128)(2,1)}, u32[]{:S(2)}) copy-start(bf16[128,16,128]{2,1,0:T(8,128)(2,1)} %param.7) | copy-start | bytes 1572868
  2.3 26.2 %copy-start.2 = (bf16[128,16,128]{2,1,0:T(8,128)(2,1)S(1)}, bf16[128,16,128]{2,1,0:T(8,128)(2,1)}, u32[]{:S(2)}) copy-start(bf16[128,16,128]{2,1,0:T(8,128)(2,1)} %param.9) | copy-start | bytes 1572868
  3.4 85.7 %collective-permute-start = (bf16[2,1,128,16,128]{4,2,3,0,1:T(8,128)(2,1)}, bf16[2,1,128,16,128]{4,2,3,0,1:T(8,128)(2,1)}, u32[]{:S(2)}, u32[]{:S(2)}) collective-permute-start(bf16[2,1,128,16,128]{4,2,3,0,1:T(8,128)(2,1)} %pad_maximum_fusion), channel_id=1, source_target_pairs={{0,2},{1,3},{2,4},{3,5},{4,6},{5,7},{6,8},{7,9},{8,10},{9,11},{10,... | collective-permute-start | bytes 3145736 | tf_op jit(solution)/shard_map/ppermute | solution.py:22
  8.3 82.1 %collective-permute-start.1 = (bf16[2,1,128,16,128]{4,2,3,0,1:T(8,128)(2,1)}, bf16[2,1,128,16,128]{4,2,3,0,1:T(8,128)(2,1)}, u32[]{:S(2)}, u32[]{:S(2)}) collective-permute-start(bf16[2,1,128,16,128]{4,2,3,0,1:T(8,128)(2,1)} %pad_maximum_fusion), channel_id=1, source_target_pairs={{0,1},{1,2},{2,3},{3,4},{4,5},{5,6},{6,7},{7,8},{8,9},{9,10},{10,1... | collective-permute-start | bytes 3145736 | tf_op jit(solution)/shard_map/ppermute | solution.py:22
  11.3 80.7 %collective-permute-start.2 = (bf16[2,1,128,16,128]{4,2,3,0,1:T(8,128)(2,1)}, bf16[2,1,128,16,128]{4,2,3,0,1:T(8,128)(2,1)}, u32[]{:S(2)}, u32[]{:S(2)}) collective-permute-start(bf16[2,1,128,16,128]{4,2,3,0,1:T(8,128)(2,1)} %pad_maximum_fusion), channel_id=1, source_target_pairs={{1,0},{2,1},{3,2},{4,3},{5,4},{6,5},{7,6},{8,7},{9,8},{10,9},{11,1... | collective-permute-start | bytes 3145736 | tf_op jit(solution)/shard_map/ppermute | solution.py:22
  15.8 14.4 %copy-start.73 = (s32[16]{0:T(128)S(1)}, s32[16]{0:T(128)}, u32[]{:S(2)}) copy-start(s32[16]{0:T(128)} %param.10) | copy-start | bytes 196
  18.0 27.5 %collective-permute-start.7 = (bf16[2,1,128,4,128]{4,3,2,1,0:T(4,128)(2,1)}, bf16[2,1,128,4,128]{4,3,2,1,0:T(4,128)(2,1)}, u32[]{:S(2)}, u32[]{:S(2)}) collective-permute-start(bf16[2,1,128,4,128]{4,3,2,1,0:T(4,128)(2,1)} %pad_maximum_fusion.8), channel_id=1, source_target_pairs={{0,8},{1,9},{2,10},{3,11},{4,12},{5,13},{6,14},{7,15},{8,0},{9,1},... | collective-permute-start | bytes 786440 | tf_op jit(solution)/shard_map/ppermute | solution.py:16
  21.4 27.1 %collective-permute-start.6 = (bf16[2,1,128,4,128]{4,3,2,1,0:T(4,128)(2,1)}, bf16[2,1,128,4,128]{4,3,2,1,0:T(4,128)(2,1)}, u32[]{:S(2)}, u32[]{:S(2)}) collective-permute-start(bf16[2,1,128,4,128]{4,3,2,1,0:T(4,128)(2,1)} %pad_maximum_fusion.7), channel_id=1, source_target_pairs={{0,4},{1,5},{2,6},{3,7},{4,0},{5,1},{6,2},{7,3},{8,12},{9,13},{10,... | collective-permute-start | bytes 786440 | tf_op jit(solution)/shard_map/ppermute | solution.py:16
  39.9 47.0 %copy-start.66 = (pred[4]{0:T(512)(128)(4,1)S(1)}, pred[4]{0:T(512)(128)(4,1)}, u32[]{:S(2)}) copy-start(pred[4]{0:T(512)(128)(4,1)} %get-tuple-element.94) | copy-start | bytes 16
  39.9 48.2 %copy-start.65 = (pred[4]{0:T(512)(128)(4,1)S(1)}, pred[4]{0:T(512)(128)(4,1)}, u32[]{:S(2)}) copy-start(pred[4]{0:T(512)(128)(4,1)} %get-tuple-element.95) | copy-start | bytes 16
  40.1 48.0 %copy-start.23 = (bf16[128,4,128]{0,2,1:T(8,128)(2,1)}, bf16[128,4,128]{0,2,1:T(8,128)(2,1)S(1)}, u32[]{:S(2)}) copy-start(bf16[128,4,128]{0,2,1:T(8,128)(2,1)S(1)} %copy.527) | copy-start | bytes 393220
  40.2 47.8 %copy-start.25 = (bf16[128,4,128]{0,2,1:T(8,128)(2,1)}, bf16[128,4,128]{0,2,1:T(8,128)(2,1)S(1)}, u32[]{:S(2)}) copy-start(bf16[128,4,128]{0,2,1:T(8,128)(2,1)S(1)} %copy.519) | copy-start | bytes 393220
  40.4 51.5 %copy-start.27 = (bf16[128,4,128]{0,2,1:T(8,128)(2,1)}, bf16[128,4,128]{0,2,1:T(8,128)(2,1)S(1)}, u32[]{:S(2)}) copy-start(bf16[128,4,128]{0,2,1:T(8,128)(2,1)S(1)} %copy.511) | copy-start | bytes 393220
  41.5 50.4 %copy-start.29 = (bf16[128,4,128]{0,2,1:T(8,128)(2,1)}, bf16[128,4,128]{0,2,1:T(8,128)(2,1)S(1)}, u32[]{:S(2)}) copy-start(bf16[128,4,128]{0,2,1:T(8,128)(2,1)S(1)} %copy.503) | copy-start | bytes 393220
  45.5 47.9 %collective-permute-start.3 = (bf16[2,1,128,16,128]{4,2,3,0,1:T(8,128)(2,1)}, bf16[2,1,128,16,128]{4,2,3,0,1:T(8,128)(2,1)}, u32[]{:S(2)}, u32[]{:S(2)}) collective-permute-start(bf16[2,1,128,16,128]{4,2,3,0,1:T(8,128)(2,1)} %pad_maximum_fusion), channel_id=1, source_target_pairs={{2,0},{3,1},{4,2},{5,3},{6,4},{7,5},{8,6},{9,7},{10,8},{11,9},{12,... | collective-permute-start | bytes 3145736 | tf_op jit(solution)/shard_map/ppermute | solution.py:22
  48.5 33.2 %collective-permute-start.5 = (bf16[2,1,128,4,128]{4,3,2,1,0:T(4,128)(2,1)}, bf16[2,1,128,4,128]{4,3,2,1,0:T(4,128)(2,1)S(1)}, u32[]{:S(2)}, u32[]{:S(2)}) collective-permute-start(bf16[2,1,128,4,128]{4,3,2,1,0:T(4,128)(2,1)} %pad_maximum_fusion.6), channel_id=1, source_target_pairs={{0,2},{1,3},{2,0},{3,1},{4,6},{5,7},{6,4},{7,5},{8,10},{9,11},{10,... | collective-permute-start | bytes 786440 | tf_op jit(solution)/shard_map/ppermute | solution.py:16
  57.1 29.8 %copy-start.31 = (bf16[128,4,128]{0,2,1:T(8,128)(2,1)}, bf16[128,4,128]{0,2,1:T(8,128)(2,1)S(1)}, u32[]{:S(2)}) copy-start(bf16[128,4,128]{0,2,1:T(8,128)(2,1)S(1)} %copy.495) | copy-start | bytes 393220
  81.8 2.7 collective-permute-start.4
  84.4 12.0 %copy-start.14 = (f32[4,128,128]{1,2,0:T(8,128)}, f32[4,128,128]{1,2,0:T(8,128)S(1)}, u32[]{:S(2)}) copy-start(f32[4,128,128]{1,2,0:T(8,128)S(1)} %get-tuple-element.79) | copy-start | bytes 786436
  108.5 21.3 %copy-start.13 = (f32[4,128,128]{1,2,0:T(8,128)S(1)}, f32[4,128,128]{1,2,0:T(8,128)}, u32[]{:S(2)}) copy-start(f32[4,128,128]{1,2,0:T(8,128)} %copy-done.12) | copy-start | bytes 786436
  167.0 25.2 %copy-start.6 = (bf16[16,128,5,128]{1,3,2,0:T(8,128)(2,1)S(1)}, bf16[16,128,5,128]{1,3,2,0:T(8,128)(2,1)}, u32[]{:S(2)}) copy-start(bf16[16,128,5,128]{1,3,2,0:T(8,128)(2,1)} %fusion.2) | copy-start | bytes 7864324
  229.2 11.5 %copy-start.53 = (f32[1,1,128,4,128]{4,2,3,1,0:T(8,128)S(1)}, f32[1,1,128,4,128]{4,2,3,1,0:T(8,128)}, u32[]{:S(2)}) copy-start(f32[1,1,128,4,128]{4,2,3,1,0:T(8,128)} %convolution_bitcast_fusion.9) | copy-start | bytes 786436
  237.4 9.5 %collective-permute-start.12 = (f32[2,1,128,4,128]{4,2,3,1,0:T(8,128)S(1)}, f32[2,1,128,4,128]{4,2,3,1,0:T(8,128)S(1)}, u32[]{:S(2)}, u32[]{:S(2)}) collective-permute-start(f32[2,1,128,4,128]{4,2,3,1,0:T(8,128)S(1)} %pad_maximum_fusion.1), channel_id=1, source_target_pairs={{0,1},{1,0},{2,3},{3,2},{4,5},{5,4},{6,7},{7,6},{8,9},{9,8},{10,11... | collective-permute-start | bytes 1572872 | tf_op jit(solution)/shard_map/ppermute | solution.py:16
  238.0 13.6 %collective-permute-start.13 = (f32[2,1,128,4,128]{4,2,3,1,0:T(8,128)S(1)}, f32[2,1,128,4,128]{4,2,3,1,0:T(8,128)S(1)}, u32[]{:S(2)}, u32[]{:S(2)}) collective-permute-start(f32[2,1,128,4,128]{4,2,3,1,0:T(8,128)S(1)} %pad_maximum_fusion.2), channel_id=1, source_target_pairs={{0,2},{1,3},{2,0},{3,1},{4,6},{5,7},{6,4},{7,5},{8,10},{9,11},{10,... | collective-permute-start | bytes 1572872 | tf_op jit(solution)/shard_map/ppermute | solution.py:16
  239.3 23.9 %collective-permute-start.14 = (f32[2,1,128,4,128]{4,2,3,1,0:T(8,128)S(1)}, f32[2,1,128,4,128]{4,2,3,1,0:T(8,128)S(1)}, u32[]{:S(2)}, u32[]{:S(2)}) collective-permute-start(f32[2,1,128,4,128]{4,2,3,1,0:T(8,128)S(1)} %pad_maximum_fusion.3), channel_id=1, source_target_pairs={{0,4},{1,5},{2,6},{3,7},{4,0},{5,1},{6,2},{7,3},{8,12},{9,13},{10,... | collective-permute-start | bytes 1572872 | tf_op jit(solution)/shard_map/ppermute | solution.py:16
  240.7 28.7 %collective-permute-start.15 = (f32[2,1,128,4,128]{4,2,3,1,0:T(8,128)S(1)}, f32[2,1,128,4,128]{4,2,3,1,0:T(8,128)S(1)}, u32[]{:S(2)}, u32[]{:S(2)}) collective-permute-start(f32[2,1,128,4,128]{4,2,3,1,0:T(8,128)S(1)} %pad_maximum_fusion.4), channel_id=1, source_target_pairs={{0,8},{1,9},{2,10},{3,11},{4,12},{5,13},{6,14},{7,15},{8,0},{9,1},... | collective-permute-start | bytes 1572872 | tf_op jit(solution)/shard_map/ppermute | solution.py:16
  243.5 63.2 %collective-permute-start.11 = (bf16[2,1,128,16,128]{4,3,2,1,0:T(8,128)(2,1)S(1)}, bf16[2,1,128,16,128]{4,3,2,1,0:T(8,128)(2,1)S(1)}, u32[]{:S(2)}, u32[]{:S(2)}) collective-permute-start(bf16[2,1,128,16,128]{4,3,2,1,0:T(8,128)(2,1)S(1)} %get-tuple-element.43), channel_id=1, source_target_pairs={{0,2},{1,3},{2,4},{3,5},{4,6},{5,7},{6,8},{7,9},{8,10},{9,11},{10,... | collective-permute-start | bytes 3145736 | tf_op jit(solution)/shard_map/ppermute | solution.py:22
  247.0 59.8 %collective-permute-start.10 = (bf16[2,1,128,16,128]{4,3,2,1,0:T(8,128)(2,1)S(1)}, bf16[2,1,128,16,128]{4,3,2,1,0:T(8,128)(2,1)S(1)}, u32[]{:S(2)}, u32[]{:S(2)}) collective-permute-start(bf16[2,1,128,16,128]{4,3,2,1,0:T(8,128)(2,1)S(1)} %get-tuple-element.44), channel_id=1, source_target_pairs={{2,0},{3,1},{4,2},{5,3},{6,4},{7,5},{8,6},{9,7},{10,8},{11,9},{12,... | collective-permute-start | bytes 3145736 | tf_op jit(solution)/shard_map/ppermute | solution.py:22
  251.6 66.8 %collective-permute-start.9 = (bf16[2,1,128,16,128]{4,3,2,1,0:T(8,128)(2,1)S(1)}, bf16[2,1,128,16,128]{4,3,2,1,0:T(8,128)(2,1)S(1)}, u32[]{:S(2)}, u32[]{:S(2)}) collective-permute-start(bf16[2,1,128,16,128]{4,3,2,1,0:T(8,128)(2,1)S(1)} %get-tuple-element.45), channel_id=1, source_target_pairs={{0,1},{1,2},{2,3},{3,4},{4,5},{5,6},{6,7},{7,8},{8,9},{9,10},{10,1... | collective-permute-start | bytes 3145736 | tf_op jit(solution)/shard_map/ppermute | solution.py:22
  263.2 55.2 %collective-permute-start.8 = (bf16[2,1,128,16,128]{4,3,2,1,0:T(8,128)(2,1)S(1)}, bf16[2,1,128,16,128]{4,3,2,1,0:T(8,128)(2,1)S(1)}, u32[]{:S(2)}, u32[]{:S(2)}) collective-permute-start(bf16[2,1,128,16,128]{4,3,2,1,0:T(8,128)(2,1)S(1)} %get-tuple-element.42), channel_id=1, source_target_pairs={{1,0},{2,1},{3,2},{4,3},{5,4},{6,5},{7,6},{8,7},{9,8},{10,9},{11,1... | collective-permute-start | bytes 3145736 | tf_op jit(solution)/shard_map/ppermute | solution.py:22
  (58 other events, 322.5 us)
where the time goes:
time: 326 us; the launch traced here: 321 us
  matrix products  93.3 us (29%)
  waiting for transfers between devices  79.3 us (24%)
  local copies, waits for them, and re-layouts  67.9 us (21%)
  other arithmetic  39.8 us (12%)
  starting transfers between devices  38.4 us (12%)
    ppermute x8, waiting for transfers between devices, passed_along(): return lax.ppermute(value, axis, pairs)  47.4 us
    ppermute x8, waiting for transfers between devices, partner(): lax.ppermute(value, axis, [(i, i ^ 1 << apart) for i in range(lax.axis_si...  31.9 us
    dot_general x8, local copies, waits for them, and re-layouts, rows_to_heads(): jnp.einsum('jqid,ih->jqhd', values, picker.astype(jnp.float32), precision...  31.4 us
    dot_general x1, matrix products, per_device(): jnp.einsum('ejc,xjckhd->xekhd', placer, stacked_parts, precision=lax.Prec...  24.6 us
    ppermute x8, starting transfers between devices, passed_along(): return lax.ppermute(value, axis, pairs)  24.5 us
    dot_general x16, matrix products, rows_to_heads(): jnp.einsum('jqid,ih->jqhd', values, picker.astype(jnp.float32), precision...  21.1 us
    another operation x28, local copies, waits for them, and re-layouts  20.4 us
    another operation x3, other arithmetic  14.1 us
  transfers between devices with their start and end apart: 16, of which 5 were waited for; matrix products, arithmetic and copies ran while one was open for 16% of the time, Pallas kernels for 0%

commit v1 on v0

--- a/solution.py
+++ b/solution.py
@@ -1,15 +1,149 @@
+import functools
 import math
 
 import jax
 import jax.numpy as jnp
 from jax import lax
+from jax.experimental import pallas as pl
+from jax.experimental.pallas import tpu as pltpu
 from jax.sharding import PartitionSpec as P
 
 BLK = 128
 WB = 3
-
-
+HALO = WB - 1
+NT = (((1,), (1,)), ((), ()))
+NN = (((1,), (0,)), ((), ()))
 blocked_score = -1e30
+
+
+def mm(a, b, dims=NN):
+    return lax.dot_general(a, b, dims, preferred_element_type=jnp.float32)
+
+
+def pack_kernel(*refs):
+    out = refs[-1]
+    for i, ref in enumerate(refs[:-1]):
+        out[:, i] = jnp.transpose(ref[...], (1, 0, 2))
+
+
+def pack(arrays):
+    tokens, heads, width = arrays[0].shape
+    chunk = 64
+    count = len(arrays)
+    return pl.pallas_call(
+        pack_kernel,
+        grid=(tokens // chunk,),
+        in_specs=[pl.BlockSpec((chunk, heads, width), lambda i: (i, 0, 0))] * count,
+        out_specs=pl.BlockSpec((heads, count, chunk, width), lambda i: (0, 0, i, 0)),
+        out_shape=jax.ShapeDtypeStruct((heads, count, tokens, width), jnp.bfloat16),
+        cost_estimate=pl.CostEstimate(
+            flops=0, transcendentals=0, bytes_accessed=4 * count * tokens * heads * width
+        ),
+    )(*arrays)
+
+
+def unpack_kernel(src, *outs):
+    for i, out in enumerate(outs):
+        out[...] = jnp.transpose(src[:, i], (1, 0, 2))
+
+
+def unpack(stacked):
+    heads, count, tokens, width = stacked.shape
+    chunk = 64
+    return pl.pallas_call(
+        unpack_kernel,
+        grid=(tokens // chunk,),
+        in_specs=[pl.BlockSpec((heads, count, chunk, width), lambda i: (0, 0, i, 0))],
+        out_specs=[pl.BlockSpec((chunk, heads, width), lambda i: (i, 0, 0))] * count,
+        out_shape=[jax.ShapeDtypeStruct((tokens, heads, width), jnp.bfloat16)] * count,
+        cost_estimate=pl.CostEstimate(
+            flops=0, transcendentals=0, bytes_accessed=4 * count * tokens * heads * width
+        ),
+    )(stacked)
+
+
+def attend_kernel(info, x, out, keys, values, key_acc, value_acc, *, blocks, unroll):
+    width = info[0]
+    far_valid = info[1]
+    far_bit = info[2]
+    scale = 1.0 / math.sqrt(x.shape[-1])
+    scale2 = scale * math.log2(math.e)
+    span = (2 * HALO + 1) * BLK
+    zero = jnp.zeros((HALO * BLK, x.shape[-1]), jnp.bfloat16)
+    for ref, part in ((keys, 1), (values, 2)):
+        ref[: HALO * BLK] = zero
+        ref[(HALO + blocks) * BLK :] = zero
+        for b in range(blocks):
+            ref[(HALO + b) * BLK : (HALO + b + 1) * BLK] = x[b, part]
+    key_acc[...] = jnp.zeros_like(key_acc)
+    value_acc[...] = jnp.zeros_like(value_acc)
+    offset = lax.broadcasted_iota(jnp.int32, (1, span), 1) // BLK - HALO
+    near = jnp.abs(offset) < width
+    far_on = jnp.full((1, BLK), far_valid, jnp.int32) > 0
+
+    def one(b):
+        q, g = x[b, 0], x[b, 3]
+        start = pl.multiple_of(b * BLK, BLK)
+        far_start = pl.multiple_of((HALO + (b ^ far_bit)) * BLK, BLK)
+        kw, vw = keys[pl.ds(start, span)], values[pl.ds(start, span)]
+        kf, vf = keys[pl.ds(far_start, BLK)], values[pl.ds(far_start, BLK)]
+        link = near & (offset + b >= 0) & (offset + b < blocks)
+        sw = jnp.where(link, mm(q, kw, NT) * scale2, blocked_score)
+        sf = jnp.where(far_on, mm(q, kf, NT) * scale2, blocked_score)
+        top = jnp.maximum(jnp.max(sw, axis=1, keepdims=True), jnp.max(sf, axis=1, keepdims=True))
+        ew, ef = jnp.exp2(sw - top), jnp.exp2(sf - top)
+        total = jnp.sum(ew, axis=1, keepdims=True) + jnp.sum(ef, axis=1, keepdims=True)
+        inverse = 1.0 / total
+        pw, pf = (ew * inverse).astype(jnp.bfloat16), (ef * inverse).astype(jnp.bfloat16)
+        attended = (mm(pw, vw) + mm(pf, vf)).astype(jnp.bfloat16)
+        delta = jnp.sum(
+            g.astype(jnp.float32) * attended.astype(jnp.float32), axis=1, keepdims=True
+        )
+        dw = (pw.astype(jnp.float32) * (mm(g, vw, NT) - delta)).astype(jnp.bfloat16)
+        df = (pf.astype(jnp.float32) * (mm(g, vf, NT) - delta)).astype(jnp.bfloat16)
+        out[b, 0] = attended
+        out[b, 1] = ((mm(dw, kw) + mm(df, kf)) * scale).astype(jnp.bfloat16)
+        qt, gt = jnp.transpose(q), jnp.transpose(g)
+        key_acc[:, pl.ds(start, span)] += mm(qt, dw)
+        value_acc[:, pl.ds(start, span)] += mm(gt, pw)
+        key_acc[:, pl.ds(far_start, BLK)] += mm(qt, df)
+        value_acc[:, pl.ds(far_start, BLK)] += mm(gt, pf)
+
+    def step(i, carry):
+        for u in range(unroll):
+            one(i * unroll + u)
+        return carry
+
+    lax.fori_loop(0, blocks // unroll, step, 0)
+    for b in range(blocks):
+        cols = slice((HALO + b) * BLK, (HALO + b + 1) * BLK)
+        out[b, 2] = jnp.transpose(key_acc[:, cols] * scale).astype(jnp.bfloat16)
+        out[b, 3] = jnp.transpose(value_acc[:, cols]).astype(jnp.bfloat16)
+
+
+def attend(info, x, unroll=2):
+    blocks, _, _, width = x.shape
+    padded = (blocks + 2 * HALO) * BLK
+    return pl.pallas_call(
+        functools.partial(attend_kernel, blocks=blocks, unroll=unroll),
+        in_specs=[
+            pl.BlockSpec(memory_space=pltpu.SMEM),
+            pl.BlockSpec(memory_space=pltpu.VMEM),
+        ],
+        out_specs=pl.BlockSpec(memory_space=pltpu.VMEM),
+        out_shape=jax.ShapeDtypeStruct(x.shape, jnp.bfloat16),
+        scratch_shapes=[
+            pltpu.VMEM((padded, width), jnp.bfloat16),
+            pltpu.VMEM((padded, width), jnp.bfloat16),
+            pltpu.VMEM((width, padded), jnp.float32),
+            pltpu.VMEM((width, padded), jnp.float32),
+        ],
+        cost_estimate=pl.CostEstimate(
+            flops=blocks * 6 * 6 * 2 * BLK**3,
+            transcendentals=blocks * 6 * BLK * BLK,
+            bytes_accessed=2 * x.size * 2,
+        ),
+    )(info, x)
 
 
 def partner(value, axis, apart):
@@ -260,21 +394,37 @@
     return (attended.reshape(tokens_dev, head_count, head_width), query_grad, key_grad, value_grad)
 
 
+def sharded_by_head(query_rows, key_rows, value_rows, out_grad, window_blocks, section_heads):
+    head = lax.axis_index("seq")
+    sections = section_heads.shape[0]
+    span = 2 ** jnp.arange(sections, dtype=jnp.int32)
+    used = jnp.any(section_heads == head, axis=1)
+    width = jnp.sum(jnp.where(jnp.arange(window_blocks.shape[0]) == head, window_blocks, 0))
+    bit = jnp.sum(jnp.where(used, span, 0))
+    valid = (bit >= width).astype(jnp.int32)
+    info = jnp.stack([width, valid, bit]).astype(jnp.int32)
+    sent = pack([query_rows, key_rows, value_rows, out_grad])
+    mine = lax.all_to_all(sent, "seq", 0, 0, tiled=True)
+    back = lax.all_to_all(attend(info, mine), "seq", 0, 0, tiled=True)
+    return tuple(unpack(back))
+
+
 def solution(mesh):
-    in_specs = (
-        P(("grp", "seq"), None, None),
-        P(("grp", "seq"), None, None),
-        P(("grp", "seq"), None, None),
-        P(("grp", "seq"), None, None),
-        P(),
-        P(),
-    )
-    out_specs = (
-        P(("grp", "seq"), None, None),
-        P(("grp", "seq"), None, None),
-        P(("grp", "seq"), None, None),
-        P(("grp", "seq"), None, None),
-    )
+    spec = P(("grp", "seq"), None, None)
+    peers = mesh.shape["seq"]
+
+    def per_device_any(*args):
+        tokens, heads, width = args[0].shape
+        sections, listed = args[5].shape
+        once = sections * listed == heads
+        if tokens == BLK and heads == peers and once and 1 << sections == peers:
+            return sharded_by_head(*args)
+        return per_device(*args)
+
     return jax.shard_map(
-        per_device, mesh=mesh, in_specs=in_specs, out_specs=out_specs, check_vma=False
-    )
+        per_device_any,
+        mesh=mesh,
+        in_specs=(spec, spec, spec, spec, P(), P()),
+        out_specs=(spec,) * 4,
+        check_vma=False,
+    )

time: 326 us -> 134 us (0.41); the launches traced: 321 us -> 133 us
  matrix products: 93.3 us -> 0 us
  local copies, waits for them, and re-layouts: 67.9 us -> 1.3 us
  blocking collectives: 0 us -> 58.6 us
  waiting for transfers between devices: 79.3 us -> 36.9 us
  other arithmetic: 39.8 us -> 3.27 us
  starting transfers between devices: 38.4 us -> 7.49 us
  Pallas kernels: 0 us -> 23.6 us
    dot_general x63 -> x0, matrix products: 93.3 us -> none  [the longest x1 24.6 us: per_device(): jnp.einsum('ejc,xjckhd->xekhd', placer, stacked_parts, precision=lax.Prec...]
    ppermute x16 -> x0, waiting for transfers between devices: 79.3 us -> none  [the longest x8 47.4 us: passed_along(): return lax.ppermute(value, axis, pairs)]
    all_to_all x0 -> x1, blocking collectives: none -> 58.6 us  [sharded_by_head(): back = lax.all_to_all(attend(info, mine), 'seq', 0, 0, tiled=True)]
    ppermute x16 -> x0, starting transfers between devices: 38.4 us -> none  [the longest x8 24.5 us: passed_along(): return lax.ppermute(value, axis, pairs)]
    all_to_all x0 -> x1, waiting for transfers between devices: none -> 36.9 us  [sharded_by_head(): mine = lax.all_to_all(sent, 'seq', 0, 0, tiled=True)]
    dot_general x8 -> x0, local copies, waits for them, and re-layouts: 31.4 us -> none  [rows_to_heads(): jnp.einsum('jqid,ih->jqhd', values, picker.astype(jnp.float32), precision...]
    pallas_call x0 -> x3, Pallas kernels: none -> 23.6 us  [the longest x1 18.2 us: attend(): pl.pallas_call(functools.partial(attend_kernel, blocks=blocks, unroll=unr...]
    another operation x30 -> x0, local copies, waits for them, and re-layouts: 23.4 us -> none
  transfers between devices with their start and end apart: 16 -> 1, of which waited for: 5 -> 1; matrix products, arithmetic and copies ran while one was open for 16% -> 2% of each run, Pallas kernels for 0% -> 0%
where the time goes in v1:
time: 134 us; the launch traced here: 133 us
  blocking collectives  58.6 us (44%)
  waiting for transfers between devices  36.9 us (28%)
  Pallas kernels  23.6 us (18%)
  starting transfers between devices  7.49 us (6%)
  other arithmetic  3.27 us (2%)
  between operations  1.94 us (1%)
    all_to_all x1, blocking collectives, sharded_by_head(): back = lax.all_to_all(attend(info, mine), 'seq', 0, 0, tiled=True)  58.6 us
    all_to_all x1, waiting for transfers between devices, sharded_by_head(): mine = lax.all_to_all(sent, 'seq', 0, 0, tiled=True)  36.9 us
    pallas_call x1, Pallas kernels, attend(): pl.pallas_call(functools.partial(attend_kernel, blocks=blocks, unroll=unr...  18.2 us
    all_to_all x1, starting transfers between devices, sharded_by_head(): mine = lax.all_to_all(sent, 'seq', 0, 0, tiled=True)  7.49 us
    pallas_call x1, Pallas kernels, pack(): pl.pallas_call(pack_kernel, grid=(tokens // chunk,), in_specs=[pl.BlockSp...  2.82 us
  transfers between devices with their start and end apart: 1, of which 1 were waited for; matrix products, arithmetic and copies ran while one was open for 2% of the time, Pallas kernels for 0%

profile of v1, /device:TPU:1, one launch (start us, length us, event | category | flops | bytes accessed | tf_op | source)
XLA Modules:
  0.0 133.2 jit_solution(7398132224556914925)
XLA Ops:
  0.6 2.8 %shard_map.93 = bf16[16,4,128,128]{3,2,1,0:T(8,128)(2,1)} custom-call(bf16[128,16,128]{2,1,0:T(8,128)(2,1)} %refs_0_.1, bf16[128,16,128]{2,1,0:T(8,128)(2,1)} %refs_1_.1, bf16[128,16,128]{2,1,0:T(8,128)(2,1)} %refs_2_.1, bf16[128,16,128]{2,1,0:T(8,128)(2,1)} %refs_3_.1), custom_call_target="tpu_custom_call" | custom-call | bytes 4194304 | tf_op jit(solution)/shard_map/pallas_call | solution.py:33
  3.5 0.0 copy-start.1
  3.5 0.0 copy-start.2
  3.5 7.5 %all-to-all-start = ((bf16[16,4,128,128]{3,2,1,0:T(8,128)(2,1)}), bf16[16,4,128,128]{3,2,1,0:T(8,128)(2,1)S(1)}, u32[]{:S(2)}, u32[]{:S(2)}) async-start(bf16[16,4,128,128]{3,2,1,0:T(8,128)(2,1)} %shard_map.93), calls=%async_computation | async-start | bytes 4194304 | tf_op jit(solution)/shard_map/all_to_all | solution.py:407
  10.9 0.0 copy-done.1
  10.9 0.1 compare_reduce_fusion
  11.1 0.0 copy-done.2
  11.1 0.6 fusion.2
  11.7 0.6 fusion.4
  13.6 1.9 %pad_add_fusion.info = s32[3]{0:T(128)} fusion(s32[1]{0:T(128)} %bitcast.2, s32[1]{0:T(128)} %bitcast.1, s32[1]{0:T(128)} %bitcast), kind=kLoop, calls=%fused_computation.14 | loop fusion | flops 6 | bytes 24 | tf_op jit(solution)/shard_map/stack | solution.py:405
  15.5 36.9 %all-to-all-done.x = bf16[16,4,128,128]{3,2,1,0:T(8,128)(2,1)S(1)} async-done(((bf16[16,4,128,128]{3,2,1,0:T(8,128)(2,1)}), bf16[16,4,128,128]{3,2,1,0:T(8,128)(2,1)S(1)}, u32[]{:S(2)}, u32[]{:S(2)}) %all-to-all-start) | async-done | bytes 2097184 | tf_op jit(solution)/shard_map/all_to_all | solution.py:407
  52.4 0.0 copy-start
  52.4 1.3 copy-done
  53.7 18.2 %shard_map.94 = bf16[16,4,128,128]{3,2,1,0:T(8,128)(2,1)} custom-call(s32[3]{0:T(128)} %pad_add_fusion.info, bf16[16,4,128,128]{3,2,1,0:T(8,128)(2,1)} %copy-done), custom_call_target="tpu_custom_call" | custom-call | flops 2415919104 | bytes 4194304 | tf_op jit(solution)/shard_map/pallas_call | solution.py:127
  71.9 58.6 %all_to_all.10.src = bf16[16,4,128,128]{3,2,1,0:T(8,128)(2,1)} all-to-all(bf16[16,4,128,128]{3,2,1,0:T(8,128)(2,1)} %shard_map.94), channel_id=1, replica_groups=mesh['grp'=2,'seq'=16] {'seq'}, dimensions={0} | all-to-all | bytes 4194304 | tf_op jit(solution)/shard_map/all_to_all | solution.py:408
  130.5 2.6 %shard_map.95 = (bf16[128,16,128]{2,1,0:T(8,128)(2,1)}, bf16[128,16,128]{2,1,0:T(8,128)(2,1)}, bf16[128,16,128]{2,1,0:T(8,128)(2,1)}, bf16[128,16,128]{2,1,0:T(8,128)(2,1)}) custom-call(bf16[16,4,128,128]{3,2,1,0:T(8,128)(2,1)} %all_to_all.10.src), custom_call_target="tpu_custom_call" | custom-call | bytes 4194304 | tf_op jit(solution)/shard_map/pallas_call | solution.py:53
Async XLA Ops:
  3.5 7.5 %copy-start.1 = (s32[4,4]{1,0:T(4,128)S(1)}, s32[4,4]{1,0:T(4,128)}, u32[]{:S(2)}) copy-start(s32[4,4]{1,0:T(4,128)} %param.11) | copy-start | bytes 196
  3.5 7.6 %copy-start.2 = (s32[16]{0:T(128)S(1)}, s32[16]{0:T(128)}, u32[]{:S(2)}) copy-start(s32[16]{0:T(128)} %param.10) | copy-start | bytes 196
  3.5 49.0 %all-to-all-start = ((bf16[16,4,128,128]{3,2,1,0:T(8,128)(2,1)}), bf16[16,4,128,128]{3,2,1,0:T(8,128)(2,1)S(1)}, u32[]{:S(2)}, u32[]{:S(2)}) async-start(bf16[16,4,128,128]{3,2,1,0:T(8,128)(2,1)} %shard_map.93), calls=%async_computation | async-start | bytes 4194304 | tf_op jit(solution)/shard_map/all_to_all | solution.py:407
  52.4 1.3 copy-start

commit v2 on v1

--- a/solution.py
+++ b/solution.py
@@ -11,6 +11,8 @@
 BLK = 128
 WB = 3
 HALO = WB - 1
+SPAN = (2 * HALO + 1) * BLK
+LINKED = SPAN + BLK
 NT = (((1,), (1,)), ((), ()))
 NN = (((1,), (0,)), ((), ()))
 blocked_score = -1e30
@@ -18,6 +20,12 @@
 
 def mm(a, b, dims=NN):
     return lax.dot_general(a, b, dims, preferred_element_type=jnp.float32)
+
+
+def moved_cost(arrays):
+    return pl.CostEstimate(
+        flops=0, transcendentals=0, bytes_accessed=4 * sum(a.size for a in arrays)
+    )
 
 
 def pack_kernel(*refs):
@@ -36,9 +44,7 @@
         in_specs=[pl.BlockSpec((chunk, heads, width), lambda i: (i, 0, 0))] * count,
         out_specs=pl.BlockSpec((heads, count, chunk, width), lambda i: (0, 0, i, 0)),
         out_shape=jax.ShapeDtypeStruct((heads, count, tokens, width), jnp.bfloat16),
-        cost_estimate=pl.CostEstimate(
-            flops=0, transcendentals=0, bytes_accessed=4 * count * tokens * heads * width
-        ),
+        cost_estimate=moved_cost(arrays),
     )(*arrays)
 
 
@@ -56,94 +62,144 @@
         in_specs=[pl.BlockSpec((heads, count, chunk, width), lambda i: (0, 0, i, 0))],
         out_specs=[pl.BlockSpec((chunk, heads, width), lambda i: (i, 0, 0))] * count,
         out_shape=[jax.ShapeDtypeStruct((tokens, heads, width), jnp.bfloat16)] * count,
-        cost_estimate=pl.CostEstimate(
-            flops=0, transcendentals=0, bytes_accessed=4 * count * tokens * heads * width
-        ),
+        cost_estimate=moved_cost([stacked]),
     )(stacked)
 
 
-def attend_kernel(info, x, out, keys, values, key_acc, value_acc, *, blocks, unroll):
-    width = info[0]
-    far_valid = info[1]
-    far_bit = info[2]
-    scale = 1.0 / math.sqrt(x.shape[-1])
-    scale2 = scale * math.log2(math.e)
-    span = (2 * HALO + 1) * BLK
+def padded_copy(ref, x, part, blocks):
     zero = jnp.zeros((HALO * BLK, x.shape[-1]), jnp.bfloat16)
-    for ref, part in ((keys, 1), (values, 2)):
-        ref[: HALO * BLK] = zero
-        ref[(HALO + blocks) * BLK :] = zero
-        for b in range(blocks):
-            ref[(HALO + b) * BLK : (HALO + b + 1) * BLK] = x[b, part]
-    key_acc[...] = jnp.zeros_like(key_acc)
-    value_acc[...] = jnp.zeros_like(value_acc)
-    offset = lax.broadcasted_iota(jnp.int32, (1, span), 1) // BLK - HALO
+    ref[: HALO * BLK] = zero
+    ref[(HALO + blocks) * BLK :] = zero
+    for b in range(blocks):
+        ref[(HALO + b) * BLK : (HALO + b + 1) * BLK] = x[b, part]
+
+
+def starts(b, far_bit):
+    near = pl.multiple_of(b * BLK, BLK)
+    far = pl.multiple_of((HALO + (b ^ far_bit)) * BLK, BLK)
+    return near, far
+
+
+def forward_kernel(info, x, out, probs, keys, values, *, blocks, group):
+    width, far_valid, far_bit = info[0], info[1], info[2]
+    scale2 = math.log2(math.e) / math.sqrt(x.shape[-1])
+
+    @pl.when(pl.program_id(0) == 0)
+    def _():
+        padded_copy(keys, x, 1, blocks)
+        padded_copy(values, x, 2, blocks)
+
+    offset = lax.broadcasted_iota(jnp.int32, (1, SPAN), 1) // BLK - HALO
     near = jnp.abs(offset) < width
     far_on = jnp.full((1, BLK), far_valid, jnp.int32) > 0
-
-    def one(b):
-        q, g = x[b, 0], x[b, 3]
-        start = pl.multiple_of(b * BLK, BLK)
-        far_start = pl.multiple_of((HALO + (b ^ far_bit)) * BLK, BLK)
-        kw, vw = keys[pl.ds(start, span)], values[pl.ds(start, span)]
-        kf, vf = keys[pl.ds(far_start, BLK)], values[pl.ds(far_start, BLK)]
+    for u in range(group):
+        b = pl.program_id(0) * group + u
+        q = x[b, 0]
+        at, far_at = starts(b, far_bit)
         link = near & (offset + b >= 0) & (offset + b < blocks)
-        sw = jnp.where(link, mm(q, kw, NT) * scale2, blocked_score)
-        sf = jnp.where(far_on, mm(q, kf, NT) * scale2, blocked_score)
+        sw = jnp.where(link, mm(q, keys[pl.ds(at, SPAN)], NT) * scale2, blocked_score)
+        sf = jnp.where(far_on, mm(q, keys[pl.ds(far_at, BLK)], NT) * scale2, blocked_score)
         top = jnp.maximum(jnp.max(sw, axis=1, keepdims=True), jnp.max(sf, axis=1, keepdims=True))
         ew, ef = jnp.exp2(sw - top), jnp.exp2(sf - top)
         total = jnp.sum(ew, axis=1, keepdims=True) + jnp.sum(ef, axis=1, keepdims=True)
         inverse = 1.0 / total
         pw, pf = (ew * inverse).astype(jnp.bfloat16), (ef * inverse).astype(jnp.bfloat16)
-        attended = (mm(pw, vw) + mm(pf, vf)).astype(jnp.bfloat16)
-        delta = jnp.sum(
-            g.astype(jnp.float32) * attended.astype(jnp.float32), axis=1, keepdims=True
-        )
-        dw = (pw.astype(jnp.float32) * (mm(g, vw, NT) - delta)).astype(jnp.bfloat16)
-        df = (pf.astype(jnp.float32) * (mm(g, vf, NT) - delta)).astype(jnp.bfloat16)
-        out[b, 0] = attended
-        out[b, 1] = ((mm(dw, kw) + mm(df, kf)) * scale).astype(jnp.bfloat16)
-        qt, gt = jnp.transpose(q), jnp.transpose(g)
-        key_acc[:, pl.ds(start, span)] += mm(qt, dw)
-        value_acc[:, pl.ds(start, span)] += mm(gt, pw)
-        key_acc[:, pl.ds(far_start, BLK)] += mm(qt, df)
-        value_acc[:, pl.ds(far_start, BLK)] += mm(gt, pf)
-
-    def step(i, carry):
-        for u in range(unroll):
-            one(i * unroll + u)
-        return carry
-
-    lax.fori_loop(0, blocks // unroll, step, 0)
-    for b in range(blocks):
-        cols = slice((HALO + b) * BLK, (HALO + b + 1) * BLK)
-        out[b, 2] = jnp.transpose(key_acc[:, cols] * scale).astype(jnp.bfloat16)
-        out[b, 3] = jnp.transpose(value_acc[:, cols]).astype(jnp.bfloat16)
-
-
-def attend(info, x, unroll=2):
-    blocks, _, _, width = x.shape
+        out[u, 0] = (mm(pw, values[pl.ds(at, SPAN)]) + mm(pf, values[pl.ds(far_at, BLK)])).astype(
+            jnp.bfloat16
+        )
+        probs[u, :, :SPAN] = pw
+        probs[u, :, SPAN:] = pf
+
+
+def forward(info, x, group=2):
+    blocks, count, _, width = x.shape
     padded = (blocks + 2 * HALO) * BLK
     return pl.pallas_call(
-        functools.partial(attend_kernel, blocks=blocks, unroll=unroll),
+        functools.partial(forward_kernel, blocks=blocks, group=group),
+        grid=(blocks // group,),
         in_specs=[
             pl.BlockSpec(memory_space=pltpu.SMEM),
-            pl.BlockSpec(memory_space=pltpu.VMEM),
+            pl.BlockSpec(x.shape, lambda i: (0, 0, 0, 0)),
         ],
-        out_specs=pl.BlockSpec(memory_space=pltpu.VMEM),
-        out_shape=jax.ShapeDtypeStruct(x.shape, jnp.bfloat16),
-        scratch_shapes=[
-            pltpu.VMEM((padded, width), jnp.bfloat16),
-            pltpu.VMEM((padded, width), jnp.bfloat16),
-            pltpu.VMEM((width, padded), jnp.float32),
-            pltpu.VMEM((width, padded), jnp.float32),
+        out_specs=[
+            pl.BlockSpec((group, 1, BLK, width), lambda i: (i, 0, 0, 0)),
+            pl.BlockSpec((group, BLK, LINKED), lambda i: (i, 0, 0)),
         ],
+        out_shape=[
+            jax.ShapeDtypeStruct((blocks, 1, BLK, width), jnp.bfloat16),
+            jax.ShapeDtypeStruct((blocks, BLK, LINKED), jnp.bfloat16),
+        ],
+        scratch_shapes=[pltpu.VMEM((padded, width), jnp.bfloat16)] * 2,
         cost_estimate=pl.CostEstimate(
-            flops=blocks * 6 * 6 * 2 * BLK**3,
-            transcendentals=blocks * 6 * BLK * BLK,
-            bytes_accessed=2 * x.size * 2,
+            flops=blocks * 4 * BLK * LINKED * width,
+            transcendentals=blocks * BLK * LINKED,
+            bytes_accessed=2 * (x.size + blocks * BLK * (LINKED + width)),
         ),
     )(info, x)
+
+
+def backward_kernel(
+    info, x, g_all, o_all, probs, out, keys, values, key_acc, value_acc, *, blocks, group
+):
+    far_bit = info[2]
+    scale = 1.0 / math.sqrt(x.shape[-1])
+    i = pl.program_id(0)
+
+    @pl.when(i == 0)
+    def _():
+        padded_copy(keys, x, 1, blocks)
+        padded_copy(values, x, 2, blocks)
+        key_acc[...] = jnp.zeros_like(key_acc)
+        value_acc[...] = jnp.zeros_like(value_acc)
+
+    for u in range(group):
+        b = i * group + u
+        q, g, o = x[b, 0], g_all[b, 0], o_all[u, 0]
+        at, far_at = starts(b, far_bit)
+        pw, pf = probs[u, :, :SPAN], probs[u, :, SPAN:]
+        delta = jnp.sum(g.astype(jnp.float32) * o.astype(jnp.float32), axis=1, keepdims=True)
+        dw = pw.astype(jnp.float32) * (mm(g, values[pl.ds(at, SPAN)], NT) - delta)
+        df = pf.astype(jnp.float32) * (mm(g, values[pl.ds(far_at, BLK)], NT) - delta)
+        dw, df = dw.astype(jnp.bfloat16), df.astype(jnp.bfloat16)
+        dq = mm(dw, keys[pl.ds(at, SPAN)]) + mm(df, keys[pl.ds(far_at, BLK)])
+        out[b, 0] = (dq * scale).astype(jnp.bfloat16)
+        qt, gt = jnp.transpose(q), jnp.transpose(g)
+        key_acc[:, pl.ds(at, SPAN)] += mm(qt, dw)
+        value_acc[:, pl.ds(at, SPAN)] += mm(gt, pw)
+        key_acc[:, pl.ds(far_at, BLK)] += mm(qt, df)
+        value_acc[:, pl.ds(far_at, BLK)] += mm(gt, pf)
+
+    @pl.when(i == pl.num_programs(0) - 1)
+    def _():
+        for b in range(blocks):
+            cols = slice((HALO + b) * BLK, (HALO + b + 1) * BLK)
+            out[b, 1] = jnp.transpose(key_acc[:, cols] * scale).astype(jnp.bfloat16)
+            out[b, 2] = jnp.transpose(value_acc[:, cols]).astype(jnp.bfloat16)
+
+
+def backward(info, x, g, o, probs, group=2):
+    blocks, count, _, width = x.shape
+    padded = (blocks + 2 * HALO) * BLK
+    return pl.pallas_call(
+        functools.partial(backward_kernel, blocks=blocks, group=group),
+        grid=(blocks // group,),
+        in_specs=[
+            pl.BlockSpec(memory_space=pltpu.SMEM),
+            pl.BlockSpec(x.shape, lambda i: (0, 0, 0, 0)),
+            pl.BlockSpec(g.shape, lambda i: (0, 0, 0, 0)),
+            pl.BlockSpec((group, 1, BLK, width), lambda i: (i, 0, 0, 0)),
+            pl.BlockSpec((group, BLK, LINKED), lambda i: (i, 0, 0)),
+        ],
+        out_specs=pl.BlockSpec(x.shape, lambda i: (0, 0, 0, 0)),
+        out_shape=jax.ShapeDtypeStruct(x.shape, jnp.bfloat16),
+        scratch_shapes=[pltpu.VMEM((padded, width), jnp.bfloat16)] * 2
+        + [pltpu.VMEM((width, padded), jnp.float32)] * 2,
+        cost_estimate=pl.CostEstimate(
+            flops=blocks * 8 * BLK * LINKED * width,
+            transcendentals=0,
+            bytes_accessed=2 * (2 * x.size + 2 * g.size + probs.size),
+        ),
+    )(info, x, g, o, probs)
 
 
 def partner(value, axis, apart):
@@ -160,13 +216,13 @@
     return jnp.sum(jnp.where(picker[None, :, :, None], values[:, None, :, :], 0.0), axis=2)
 
 
-def to_heads(values, picker, filler):
+def slots_to_heads(values, picker, filler):
     covered = jnp.any(picker, axis=0)
     summed = jnp.sum(jnp.where(picker[None, :, :, None], values[:, :, None, :], 0.0), axis=1)
     return jnp.where(covered[None, :, None], summed, filler)
 
 
-def rows_to_heads(values, picker):
+def rows_slots_to_heads(values, picker):
     return jnp.einsum(
         "jqid,ih->jqhd", values, picker.astype(jnp.float32), precision=lax.Precision.HIGHEST
     )
@@ -258,7 +314,7 @@
         )
         far_scores = jnp.where(slot_valid[None, :, None, None], far_scores, blocked_score)
         top_score = jnp.maximum(
-            top_score, to_heads(jnp.max(far_scores, axis=3), picker, blocked_score)
+            top_score, slots_to_heads(jnp.max(far_scores, axis=3), picker, blocked_score)
         )
         records.append(
             (
@@ -285,7 +341,7 @@
             ),
             axis=3,
         )
-        row_total = row_total + to_heads(far_sum, picker, 0.0)
+        row_total = row_total + slots_to_heads(far_sum, picker, 0.0)
     log_total = top_score + jnp.log(row_total)
     near_probs = jnp.where(
         wide_mask, jnp.exp(near_scores - log_total[:, :, :, None, None]), 0.0
@@ -301,7 +357,7 @@
             record[2][None, :, None, None], jnp.exp(record[7] - slot_lse[:, :, :, None]), 0.0
         ).astype(jnp.bfloat16)
         far_probs_list.append((far_probs, slot_lse))
-        attended_sum = attended_sum + rows_to_heads(
+        attended_sum = attended_sum + rows_slots_to_heads(
             jnp.einsum(
                 "jiqk,jkid->jqid", far_probs, record[6][1], preferred_element_type=jnp.float32
             ),
@@ -331,7 +387,7 @@
             probs_pair[0].astype(jnp.float32) * (far_dprob - slot_delta[:, :, :, None])
         ).astype(jnp.bfloat16)
         far_dscores.append((far_dscore, slot_delta))
-        query_sum = query_sum + rows_to_heads(
+        query_sum = query_sum + rows_slots_to_heads(
             jnp.einsum(
                 "jiqk,jkid->jqid", far_dscore, record[6][0], preferred_element_type=jnp.float32
             ),
@@ -387,11 +443,15 @@
         )
         returned = partner_back(jnp.stack([key_part, value_part]), record[0], low_bits)
         own_grads = own_grads + jnp.stack(
-            [rows_to_heads(returned[0], picker), rows_to_heads(returned[1], picker)]
+            [rows_slots_to_heads(returned[0], picker), rows_slots_to_heads(returned[1], picker)]
         )
     key_grad = own_grads[0].astype(jnp.bfloat16).reshape(tokens_dev, head_count, head_width)
     value_grad = own_grads[1].astype(jnp.bfloat16).reshape(tokens_dev, head_count, head_width)
     return (attended.reshape(tokens_dev, head_count, head_width), query_grad, key_grad, value_grad)
+
+
+def to_heads(packed):
+    return lax.all_to_all(packed, "seq", 0, 0, tiled=True)
 
 
 def sharded_by_head(query_rows, key_rows, value_rows, out_grad, window_blocks, section_heads):
@@ -403,10 +463,15 @@
     bit = jnp.sum(jnp.where(used, span, 0))
     valid = (bit >= width).astype(jnp.int32)
     info = jnp.stack([width, valid, bit]).astype(jnp.int32)
-    sent = pack([query_rows, key_rows, value_rows, out_grad])
-    mine = lax.all_to_all(sent, "seq", 0, 0, tiled=True)
-    back = lax.all_to_all(attend(info, mine), "seq", 0, 0, tiled=True)
-    return tuple(unpack(back))
+    x = to_heads(pack([query_rows, key_rows, value_rows]))
+    x, g_sent = lax.optimization_barrier((x, pack([out_grad])))
+    g = to_heads(g_sent)
+    o, probs = forward(info, x)
+    o_back = to_heads(o)
+    grads = backward(info, x, g, o, probs)
+    grads, o_back = lax.optimization_barrier((grads, o_back))
+    grads_back = to_heads(grads)
+    return (*unpack(o_back), *unpack(grads_back))
 
 
 def solution(mesh):

time: 134 us -> 132 us (0.985)
  the two profiles are of different devices: /device:TPU:1 before, /device:TPU:15 now
where the time goes in v2:
time: 132 us; the launch traced here: 131 us
  waiting for transfers between devices  71.5 us (54%)
  Pallas kernels  30 us (23%)
  starting transfers between devices  22.5 us (17%)
  other arithmetic  3.24 us (2%)
  between operations  1.97 us (1%)
  local copies, waits for them, and re-layouts  1.96 us (1%)
    all_to_all x4, waiting for transfers between devices, to_heads(): return lax.all_to_all(packed, 'seq', 0, 0, tiled=True)  71.5 us
    all_to_all x4, starting transfers between devices, to_heads(): return lax.all_to_all(packed, 'seq', 0, 0, tiled=True)  22.5 us
    pallas_call x1, Pallas kernels, backward(): pl.pallas_call(functools.partial(backward_kernel, blocks=blocks, group=gr...  10.8 us
    pallas_call x1, Pallas kernels, forward(): pl.pallas_call(functools.partial(forward_kernel, blocks=blocks, group=gro...  10.7 us
    pallas_call x2, Pallas kernels, pack(): pl.pallas_call(pack_kernel, grid=(tokens // chunk,), in_specs=[pl.BlockSp...  4.31 us
    pallas_call x2, Pallas kernels, unpack(): pl.pallas_call(unpack_kernel, grid=(tokens // chunk,), in_specs=[pl.Block...  4.16 us
  transfers between devices with their start and end apart: 4, of which 3 were waited for; matrix products, arithmetic and copies ran while one was open for 2% of the time, Pallas kernels for 19%

profile of v2, /device:TPU:15, one launch (start us, length us, event | category | flops | bytes accessed | tf_op | source)
XLA Modules:
  0.0 131.1 jit_solution(14573417121461756168)
XLA Ops:
  0.6 2.5 %shard_map.93 = bf16[16,3,128,128]{3,2,1,0:T(8,128)(2,1)} custom-call(bf16[128,16,128]{2,1,0:T(8,128)(2,1)} %refs_0_.2, bf16[128,16,128]{2,1,0:T(8,128)(2,1)} %refs_1_.1, bf16[128,16,128]{2,1,0:T(8,128)(2,1)} %refs_2_.1), custom_call_target="tpu_custom_call" | custom-call | bytes 3145728 | tf_op jit(solution)/shard_map/pallas_call | solution.py:41
  3.1 6.6 %all-to-all-start = ((bf16[16,3,128,128]{3,2,1,0:T(8,128)(2,1)}), bf16[16,3,128,128]{3,2,1,0:T(8,128)(2,1)S(1)}, u32[]{:S(2)}, u32[]{:S(2)}) async-start(bf16[16,3,128,128]{3,2,1,0:T(8,128)(2,1)} %shard_map.93), calls=%async_computation | async-start | bytes 3145728 | tf_op jit(solution)/shard_map/all_to_all | solution.py:454
  9.7 0.0 copy-start.4
  9.7 0.0 copy-start.5
  9.7 1.8 %shard_map.94 = bf16[16,1,128,128]{3,2,1,0:T(8,128)(2,1)} custom-call(bf16[128,16,128]{2,1,0:T(8,128)(2,1)} %refs_0_.3), custom_call_target="tpu_custom_call" | custom-call | bytes 1048576 | tf_op jit(solution)/shard_map/pallas_call | solution.py:41
  11.5 34.3 %all-to-all-done.x = bf16[16,3,128,128]{3,2,1,0:T(8,128)(2,1)S(1)} async-done(((bf16[16,3,128,128]{3,2,1,0:T(8,128)(2,1)}), bf16[16,3,128,128]{3,2,1,0:T(8,128)(2,1)S(1)}, u32[]{:S(2)}, u32[]{:S(2)}) %all-to-all-start) | async-done | bytes 1572896 | tf_op jit(solution)/shard_map/all_to_all | solution.py:454
  45.9 0.0 copy-start.1
  45.9 4.9 %all-to-all-start.1 = ((bf16[16,1,128,128]{3,2,1,0:T(8,128)(2,1)}), bf16[16,1,128,128]{3,2,1,0:T(8,128)(2,1)S(1)}, u32[]{:S(2)}, u32[]{:S(2)}) async-start(bf16[16,1,128,128]{3,2,1,0:T(8,128)(2,1)} %shard_map.94), calls=%async_computation.1 | async-start | bytes 1048576 | tf_op jit(solution)/shard_map/all_to_all | solution.py:454
  50.8 0.0 copy-done.4
  50.8 0.1 compare_reduce_fusion
  50.9 0.0 copy-done.5
  50.9 0.6 fusion.2
  51.5 0.6 fusion.4
  53.5 1.8 %pad_add_fusion.info = s32[3]{0:T(128)} fusion(s32[1]{0:T(128)} %bitcast.2, s32[1]{0:T(128)} %bitcast.1, s32[1]{0:T(128)} %bitcast), kind=kLoop, calls=%fused_computation.14 | loop fusion | flops 6 | bytes 24 | tf_op jit(solution)/shard_map/stack | solution.py:465
  55.3 0.0 copy-done.1
  55.3 10.7 %shard_map.95 = (bf16[16,1,128,128]{3,2,1,0:T(8,128)(2,1)}, bf16[16,128,768]{2,1,0:T(8,128)(2,1)}) custom-call(s32[3]{0:T(128)} %pad_add_fusion.info, bf16[16,3,128,128]{3,2,1,0:T(8,128)(2,1)} %copy-done.1), custom_call_target="tpu_custom_call" | custom-call | flops 805306368 | bytes 5242880 | tf_op jit(solution)/shard_map/pallas_call | solution.py:117
  66.0 0.0 all-to-all-done.1.g_all
  66.0 0.0 copy-start.3
  66.0 6.0 %all-to-all-start.2 = ((bf16[16,1,128,128]{3,2,1,0:T(8,128)(2,1)}), bf16[16,1,128,128]{3,2,1,0:T(8,128)(2,1)S(1)}, u32[]{:S(2)}, u32[]{:S(2)}) async-start(bf16[16,1,128,128]{3,2,1,0:T(8,128)(2,1)} %get-tuple-element.15.o_all), calls=%async_computation.2 | async-start | bytes 1048576 | tf_op jit(solution)/shard_map/all_to_all | solution.py:454
  72.0 0.0 copy-done.3
  72.0 10.8 %shard_map.96 = bf16[16,3,128,128]{3,2,1,0:T(8,128)(2,1)} custom-call(s32[3]{0:T(128)} %pad_add_fusion.info, bf16[16,3,128,128]{3,2,1,0:T(8,128)(2,1)} %copy-done.1, bf16[16,1,128,128]{3,2,1,0:T(8,128)(2,1)} %copy-done.3, bf16[16,1,128,128]{3,2,1,0:T(8,128)(2,1)} %get-tuple-element.15.o_all, bf16[16,128,768]{2,1,0:T(8,128)(2,1)} %get-tuple-element.16.probs), custom_call_target="tpu_custom_call" | custom-call | flops 1610612736 | bytes 7340032 | tf_op jit(solution)/shard_map/pallas_call | solution.py:183
  82.9 2.7 %all-to-all-done.2.src = bf16[16,1,128,128]{3,2,1,0:T(8,128)(2,1)S(1)} async-done(((bf16[16,1,128,128]{3,2,1,0:T(8,128)(2,1)}), bf16[16,1,128,128]{3,2,1,0:T(8,128)(2,1)S(1)}, u32[]{:S(2)}, u32[]{:S(2)}) %all-to-all-start.2) | async-done | bytes 524320 | tf_op jit(solution)/shard_map/all_to_all | solution.py:454
  85.6 0.0 copy-start.2
  85.6 0.8 copy-done.2
  86.4 5.0 %all-to-all-start.3 = ((bf16[16,3,128,128]{3,2,1,0:T(8,128)(2,1)}), bf16[16,3,128,128]{3,2,1,0:T(8,128)(2,1)S(1)}, u32[]{:S(2)}, u32[]{:S(2)}) async-start(bf16[16,3,128,128]{3,2,1,0:T(8,128)(2,1)} %shard_map.96), calls=%async_computation.3 | async-start | bytes 3145728 | tf_op jit(solution)/shard_map/all_to_all | solution.py:454
  91.4 1.8 %shard_map.97 = bf16[128,16,128]{2,1,0:T(8,128)(2,1)} custom-call(bf16[16,1,128,128]{3,2,1,0:T(8,128)(2,1)} %copy-done.2), custom_call_target="tpu_custom_call" | custom-call | bytes 1048576 | tf_op jit(solution)/shard_map/pallas_call | solution.py:59
  93.2 34.4 %all-to-all-done.3.src = bf16[16,3,128,128]{3,2,1,0:T(8,128)(2,1)S(1)} async-done(((bf16[16,3,128,128]{3,2,1,0:T(8,128)(2,1)}), bf16[16,3,128,128]{3,2,1,0:T(8,128)(2,1)S(1)}, u32[]{:S(2)}, u32[]{:S(2)}) %all-to-all-start.3) | async-done | bytes 1572896 | tf_op jit(solution)/shard_map/all_to_all | solution.py:454
  127.6 0.0 copy-start
  127.6 1.1 copy-done
  128.7 2.3 %shard_map.98 = (bf16[128,16,128]{2,1,0:T(8,128)(2,1)}, bf16[128,16,128]{2,1,0:T(8,128)(2,1)}, bf16[128,16,128]{2,1,0:T(8,128)(2,1)}) custom-call(bf16[16,3,128,128]{3,2,1,0:T(8,128)(2,1)} %copy-done), custom_call_target="tpu_custom_call" | custom-call | bytes 3145728 | tf_op jit(solution)/shard_map/pallas_call | solution.py:59
Async XLA Ops:
  3.1 42.7 %all-to-all-start = ((bf16[16,3,128,128]{3,2,1,0:T(8,128)(2,1)}), bf16[16,3,128,128]{3,2,1,0:T(8,128)(2,1)S(1)}, u32[]{:S(2)}, u32[]{:S(2)}) async-start(bf16[16,3,128,128]{3,2,1,0:T(8,128)(2,1)} %shard_map.93), calls=%async_computation | async-start | bytes 3145728 | tf_op jit(solution)/shard_map/all_to_all | solution.py:454
  9.7 41.1 %copy-start.4 = (s32[4,4]{1,0:T(4,128)S(1)}, s32[4,4]{1,0:T(4,128)}, u32[]{:S(2)}) copy-start(s32[4,4]{1,0:T(4,128)} %param.11) | copy-start | bytes 196
  9.7 41.2 %copy-start.5 = (s32[16]{0:T(128)S(1)}, s32[16]{0:T(128)}, u32[]{:S(2)}) copy-start(s32[16]{0:T(128)} %param.10) | copy-start | bytes 196
  45.9 9.5 %copy-start.1 = (bf16[16,3,128,128]{3,2,1,0:T(8,128)(2,1)}, bf16[16,3,128,128]{3,2,1,0:T(8,128)(2,1)S(1)}, u32[]{:S(2)}) copy-start(bf16[16,3,128,128]{3,2,1,0:T(8,128)(2,1)S(1)} %all-to-all-done.x) | copy-start | bytes 4718596
  45.9 20.1 %all-to-all-start.1 = ((bf16[16,1,128,128]{3,2,1,0:T(8,128)(2,1)}), bf16[16,1,128,128]{3,2,1,0:T(8,128)(2,1)S(1)}, u32[]{:S(2)}, u32[]{:S(2)}) async-start(bf16[16,1,128,128]{3,2,1,0:T(8,128)(2,1)} %shard_map.94), calls=%async_computation.1 | async-start | bytes 1048576 | tf_op jit(solution)/shard_map/all_to_all | solution.py:454
  66.0 6.0 %copy-start.3 = (bf16[16,1,128,128]{3,2,1,0:T(8,128)(2,1)}, bf16[16,1,128,128]{3,2,1,0:T(8,128)(2,1)S(1)}, u32[]{:S(2)}) copy-start(bf16[16,1,128,128]{3,2,1,0:T(8,128)(2,1)S(1)} %all-to-all-done.1.g_all) | copy-start | bytes 1572868
  66.0 19.6 %all-to-all-start.2 = ((bf16[16,1,128,128]{3,2,1,0:T(8,128)(2,1)}), bf16[16,1,128,128]{3,2,1,0:T(8,128)(2,1)S(1)}, u32[]{:S(2)}, u32[]{:S(2)}) async-start(bf16[16,1,128,128]{3,2,1,0:T(8,128)(2,1)} %get-tuple-element.15.o_all), calls=%async_computation.2 | async-start | bytes 1048576 | tf_op jit(solution)/shard_map/all_to_all | solution.py:454
  85.6 0.8 copy-start.2
  86.4 41.2 %all-to-all-start.3 = ((bf16[16,3,128,128]{3,2,1,0:T(8,128)(2,1)}), bf16[16,3,128,128]{3,2,1,0:T(8,128)(2,1)S(1)}, u32[]{:S(2)}, u32[]{:S(2)}) async-start(bf16[16,3,128,128]{3,2,1,0:T(8,128)(2,1)} %shard_map.96), calls=%async_computation.3 | async-start | bytes 3145728 | tf_op jit(solution)/shard_map/all_to_all | solution.py:454
  127.6 1.1 copy-start

commit v3 on v1

--- a/solution.py
+++ b/solution.py
@@ -11,6 +11,8 @@
 BLK = 128
 WB = 3
 HALO = WB - 1
+SPAN = (2 * HALO + 1) * BLK
+LINKED = SPAN + BLK
 NT = (((1,), (1,)), ((), ()))
 NN = (((1,), (0,)), ((), ()))
 blocked_score = -1e30
@@ -18,6 +20,12 @@
 
 def mm(a, b, dims=NN):
     return lax.dot_general(a, b, dims, preferred_element_type=jnp.float32)
+
+
+def moved_cost(arrays):
+    return pl.CostEstimate(
+        flops=0, transcendentals=0, bytes_accessed=4 * sum(a.size for a in arrays)
+    )
 
 
 def pack_kernel(*refs):
@@ -36,9 +44,7 @@
         in_specs=[pl.BlockSpec((chunk, heads, width), lambda i: (i, 0, 0))] * count,
         out_specs=pl.BlockSpec((heads, count, chunk, width), lambda i: (0, 0, i, 0)),
         out_shape=jax.ShapeDtypeStruct((heads, count, tokens, width), jnp.bfloat16),
-        cost_estimate=pl.CostEstimate(
-            flops=0, transcendentals=0, bytes_accessed=4 * count * tokens * heads * width
-        ),
+        cost_estimate=moved_cost(arrays),
     )(*arrays)
 
 
@@ -56,19 +62,73 @@
         in_specs=[pl.BlockSpec((heads, count, chunk, width), lambda i: (0, 0, i, 0))],
         out_specs=[pl.BlockSpec((chunk, heads, width), lambda i: (i, 0, 0))] * count,
         out_shape=[jax.ShapeDtypeStruct((tokens, heads, width), jnp.bfloat16)] * count,
-        cost_estimate=pl.CostEstimate(
-            flops=0, transcendentals=0, bytes_accessed=4 * count * tokens * heads * width
-        ),
+        cost_estimate=moved_cost([stacked]),
     )(stacked)
 
 
-def attend_kernel(info, x, out, keys, values, key_acc, value_acc, *, blocks, unroll):
-    width = info[0]
-    far_valid = info[1]
-    far_bit = info[2]
+def softmax_pair(score, far_score, biases, far_bias, scale2):
+    near_parts, far_parts = [], []
+    gap = jnp.zeros((BLK, BLK), jnp.bfloat16)
+    for r in range(2):
+        rows = slice(r * BLK, (r + 1) * BLK)
+        sw = score[rows, r * BLK : r * BLK + SPAN] * scale2 + biases[r]
+        sf = far_score[r] * scale2 + far_bias
+        top = jnp.maximum(jnp.max(sw, axis=1, keepdims=True), jnp.max(sf, axis=1, keepdims=True))
+        ew, ef = jnp.exp2(sw - top), jnp.exp2(sf - top)
+        total = jnp.sum(ew, axis=1, keepdims=True) + jnp.sum(ef, axis=1, keepdims=True)
+        inverse = 1.0 / total
+        near = (ew * inverse).astype(jnp.bfloat16)
+        near_parts.append(jnp.concatenate([near, gap] if r == 0 else [gap, near], axis=1))
+        far_parts.append((ef * inverse).astype(jnp.bfloat16))
+    return jnp.concatenate(near_parts, axis=0), far_parts
+
+
+def attend_pair(q, g, kw, vw, kf, vf, biases, far_bias):
+    scale = 1.0 / math.sqrt(q.shape[-1])
+    scale2 = scale * math.log2(math.e)
+    half = [slice(0, BLK), slice(BLK, 2 * BLK)]
+    far_score = [mm(q[half[r]], kf[r], NT) for r in range(2)]
+    near, far = softmax_pair(mm(q, kw, NT), far_score, biases, far_bias, scale2)
+    far_out = jnp.concatenate([mm(far[r], vf[r]) for r in range(2)], axis=0)
+    attended = (mm(near, vw) + far_out).astype(jnp.bfloat16)
+    delta = jnp.sum(g.astype(jnp.float32) * attended.astype(jnp.float32), axis=1, keepdims=True)
+    d_near = (near.astype(jnp.float32) * (mm(g, vw, NT) - delta)).astype(jnp.bfloat16)
+    d_far = [
+        (far[r].astype(jnp.float32) * (mm(g[half[r]], vf[r], NT) - delta[half[r]])).astype(
+            jnp.bfloat16
+        )
+        for r in range(2)
+    ]
+    far_dq = jnp.concatenate([mm(d_far[r], kf[r]) for r in range(2)], axis=0)
+    query_grad = ((mm(d_near, kw) + far_dq) * scale).astype(jnp.bfloat16)
+    qt, gt = jnp.transpose(q), jnp.transpose(g)
+    key_near, value_near = mm(qt, d_near), mm(gt, near)
+    key_far = [mm(qt[:, half[r]], d_far[r]) for r in range(2)]
+    value_far = [mm(gt[:, half[r]], far[r]) for r in range(2)]
+    return attended, query_grad, key_near, value_near, key_far, value_far
+
+
+def near_biases(b, width, low, high):
+    offset = lax.broadcasted_iota(jnp.int32, (1, SPAN), 1) // BLK - HALO
+    inside = jnp.abs(offset) < width
+    out = []
+    for r in range(2):
+        there = offset + b + r
+        out.append(jnp.where(inside & (there >= low) & (there < high), 0.0, blocked_score))
+    return out
+
+
+def attend_kernel(
+    head_ref, widths, sections, x, out, keys, values, key_acc, value_acc, *, blocks, unroll
+):
+    head = head_ref[0]
+    width = widths[head]
+    far_bit = jnp.int32(0)
+    for s in range(sections.shape[0]):
+        for i in range(sections.shape[1]):
+            far_bit = jnp.where(sections[s, i] == head, 1 << s, far_bit)
+    far_bias = jnp.where(far_bit >= width, 0.0, blocked_score).astype(jnp.float32)
     scale = 1.0 / math.sqrt(x.shape[-1])
-    scale2 = scale * math.log2(math.e)
-    span = (2 * HALO + 1) * BLK
     zero = jnp.zeros((HALO * BLK, x.shape[-1]), jnp.bfloat16)
     for ref, part in ((keys, 1), (values, 2)):
         ref[: HALO * BLK] = zero
@@ -77,73 +137,63 @@
             ref[(HALO + b) * BLK : (HALO + b + 1) * BLK] = x[b, part]
     key_acc[...] = jnp.zeros_like(key_acc)
     value_acc[...] = jnp.zeros_like(value_acc)
-    offset = lax.broadcasted_iota(jnp.int32, (1, span), 1) // BLK - HALO
-    near = jnp.abs(offset) < width
-    far_on = jnp.full((1, BLK), far_valid, jnp.int32) > 0
+    pair_span = SPAN + BLK
 
     def one(b):
-        q, g = x[b, 0], x[b, 3]
-        start = pl.multiple_of(b * BLK, BLK)
-        far_start = pl.multiple_of((HALO + (b ^ far_bit)) * BLK, BLK)
-        kw, vw = keys[pl.ds(start, span)], values[pl.ds(start, span)]
-        kf, vf = keys[pl.ds(far_start, BLK)], values[pl.ds(far_start, BLK)]
-        link = near & (offset + b >= 0) & (offset + b < blocks)
-        sw = jnp.where(link, mm(q, kw, NT) * scale2, blocked_score)
-        sf = jnp.where(far_on, mm(q, kf, NT) * scale2, blocked_score)
-        top = jnp.maximum(jnp.max(sw, axis=1, keepdims=True), jnp.max(sf, axis=1, keepdims=True))
-        ew, ef = jnp.exp2(sw - top), jnp.exp2(sf - top)
-        total = jnp.sum(ew, axis=1, keepdims=True) + jnp.sum(ef, axis=1, keepdims=True)
-        inverse = 1.0 / total
-        pw, pf = (ew * inverse).astype(jnp.bfloat16), (ef * inverse).astype(jnp.bfloat16)
-        attended = (mm(pw, vw) + mm(pf, vf)).astype(jnp.bfloat16)
-        delta = jnp.sum(
-            g.astype(jnp.float32) * attended.astype(jnp.float32), axis=1, keepdims=True
-        )
-        dw = (pw.astype(jnp.float32) * (mm(g, vw, NT) - delta)).astype(jnp.bfloat16)
-        df = (pf.astype(jnp.float32) * (mm(g, vf, NT) - delta)).astype(jnp.bfloat16)
-        out[b, 0] = attended
-        out[b, 1] = ((mm(dw, kw) + mm(df, kf)) * scale).astype(jnp.bfloat16)
-        qt, gt = jnp.transpose(q), jnp.transpose(g)
-        key_acc[:, pl.ds(start, span)] += mm(qt, dw)
-        value_acc[:, pl.ds(start, span)] += mm(gt, pw)
-        key_acc[:, pl.ds(far_start, BLK)] += mm(qt, df)
-        value_acc[:, pl.ds(far_start, BLK)] += mm(gt, pf)
+        q = jnp.concatenate([x[b, 0], x[b + 1, 0]], axis=0)
+        g = jnp.concatenate([x[b, 3], x[b + 1, 3]], axis=0)
+        at = pl.multiple_of(b * BLK, BLK)
+        far_at = [pl.multiple_of((HALO + ((b + r) ^ far_bit)) * BLK, BLK) for r in range(2)]
+        attended, dq, key_near, value_near, key_far, value_far = attend_pair(
+            q,
+            g,
+            keys[pl.ds(at, pair_span)],
+            values[pl.ds(at, pair_span)],
+            [keys[pl.ds(far_at[r], BLK)] for r in range(2)],
+            [values[pl.ds(far_at[r], BLK)] for r in range(2)],
+            near_biases(b, width, 0, blocks),
+            far_bias,
+        )
+        for r in range(2):
+            rows = slice(r * BLK, (r + 1) * BLK)
+            out[b + r, 0] = attended[rows]
+            out[b + r, 1] = dq[rows]
+        key_acc[:, pl.ds(at, pair_span)] += key_near
+        value_acc[:, pl.ds(at, pair_span)] += value_near
+        for r in range(2):
+            key_acc[:, pl.ds(far_at[r], BLK)] += key_far[r]
+            value_acc[:, pl.ds(far_at[r], BLK)] += value_far[r]
 
     def step(i, carry):
         for u in range(unroll):
-            one(i * unroll + u)
+            one((i * unroll + u) * 2)
         return carry
 
-    lax.fori_loop(0, blocks // unroll, step, 0)
+    lax.fori_loop(0, blocks // (2 * unroll), step, 0)
     for b in range(blocks):
         cols = slice((HALO + b) * BLK, (HALO + b + 1) * BLK)
-        out[b, 2] = jnp.transpose(key_acc[:, cols] * scale).astype(jnp.bfloat16)
-        out[b, 3] = jnp.transpose(value_acc[:, cols]).astype(jnp.bfloat16)
-
-
-def attend(info, x, unroll=2):
+        out[b, 2] = jnp.transpose((key_acc[:, cols] * scale).astype(jnp.bfloat16))
+        out[b, 3] = jnp.transpose(value_acc[:, cols].astype(jnp.bfloat16))
+
+
+def attend(head, window_blocks, section_heads, x, unroll=2):
     blocks, _, _, width = x.shape
     padded = (blocks + 2 * HALO) * BLK
     return pl.pallas_call(
         functools.partial(attend_kernel, blocks=blocks, unroll=unroll),
-        in_specs=[
-            pl.BlockSpec(memory_space=pltpu.SMEM),
-            pl.BlockSpec(memory_space=pltpu.VMEM),
-        ],
+        in_specs=[pl.BlockSpec(memory_space=pltpu.SMEM)] * 3
+        + [pl.BlockSpec(memory_space=pltpu.VMEM)],
         out_specs=pl.BlockSpec(memory_space=pltpu.VMEM),
         out_shape=jax.ShapeDtypeStruct(x.shape, jnp.bfloat16),
-        scratch_shapes=[
-            pltpu.VMEM((padded, width), jnp.bfloat16),
-            pltpu.VMEM((padded, width), jnp.bfloat16),
-            pltpu.VMEM((width, padded), jnp.float32),
-            pltpu.VMEM((width, padded), jnp.float32),
-        ],
+        scratch_shapes=[pltpu.VMEM((padded, width), jnp.bfloat16)] * 2
+        + [pltpu.VMEM((width, padded), jnp.float32)] * 2,
+        compiler_params=pltpu.CompilerParams(vmem_limit_bytes=24 << 20),
         cost_estimate=pl.CostEstimate(
-            flops=blocks * 6 * 6 * 2 * BLK**3,
-            transcendentals=blocks * 6 * BLK * BLK,
-            bytes_accessed=2 * x.size * 2,
+            flops=blocks * 12 * BLK * LINKED * width,
+            transcendentals=blocks * BLK * LINKED,
+            bytes_accessed=4 * x.size,
         ),
-    )(info, x)
+    )(head, window_blocks, section_heads, x)
 
 
 def partner(value, axis, apart):
@@ -160,13 +210,13 @@
     return jnp.sum(jnp.where(picker[None, :, :, None], values[:, None, :, :], 0.0), axis=2)
 
 
-def to_heads(values, picker, filler):
+def slots_to_heads(values, picker, filler):
     covered = jnp.any(picker, axis=0)
     summed = jnp.sum(jnp.where(picker[None, :, :, None], values[:, :, None, :], 0.0), axis=1)
     return jnp.where(covered[None, :, None], summed, filler)
 
 
-def rows_to_heads(values, picker):
+def rows_slots_to_heads(values, picker):
     return jnp.einsum(
         "jqid,ih->jqhd", values, picker.astype(jnp.float32), precision=lax.Precision.HIGHEST
     )
@@ -258,7 +308,7 @@
         )
         far_scores = jnp.where(slot_valid[None, :, None, None], far_scores, blocked_score)
         top_score = jnp.maximum(
-            top_score, to_heads(jnp.max(far_scores, axis=3), picker, blocked_score)
+            top_score, slots_to_heads(jnp.max(far_scores, axis=3), picker, blocked_score)
         )
         records.append(
             (
@@ -285,7 +335,7 @@
             ),
             axis=3,
         )
-        row_total = row_total + to_heads(far_sum, picker, 0.0)
+        row_total = row_total + slots_to_heads(far_sum, picker, 0.0)
     log_total = top_score + jnp.log(row_total)
     near_probs = jnp.where(
         wide_mask, jnp.exp(near_scores - log_total[:, :, :, None, None]), 0.0
@@ -301,7 +351,7 @@
             record[2][None, :, None, None], jnp.exp(record[7] - slot_lse[:, :, :, None]), 0.0
         ).astype(jnp.bfloat16)
         far_probs_list.append((far_probs, slot_lse))
-        attended_sum = attended_sum + rows_to_heads(
+        attended_sum = attended_sum + rows_slots_to_heads(
             jnp.einsum(
                 "jiqk,jkid->jqid", far_probs, record[6][1], preferred_element_type=jnp.float32
             ),
@@ -331,7 +381,7 @@
             probs_pair[0].astype(jnp.float32) * (far_dprob - slot_delta[:, :, :, None])
         ).astype(jnp.bfloat16)
         far_dscores.append((far_dscore, slot_delta))
-        query_sum = query_sum + rows_to_heads(
+        query_sum = query_sum + rows_slots_to_heads(
             jnp.einsum(
                 "jiqk,jkid->jqid", far_dscore, record[6][0], preferred_element_type=jnp.float32
             ),
@@ -387,7 +437,7 @@
         )
         returned = partner_back(jnp.stack([key_part, value_part]), record[0], low_bits)
         own_grads = own_grads + jnp.stack(
-            [rows_to_heads(returned[0], picker), rows_to_heads(returned[1], picker)]
+            [rows_slots_to_heads(returned[0], picker), rows_slots_to_heads(returned[1], picker)]
         )
     key_grad = own_grads[0].astype(jnp.bfloat16).reshape(tokens_dev, head_count, head_width)
     value_grad = own_grads[1].astype(jnp.bfloat16).reshape(tokens_dev, head_count, head_width)
@@ -395,18 +445,11 @@
 
 
 def sharded_by_head(query_rows, key_rows, value_rows, out_grad, window_blocks, section_heads):
-    head = lax.axis_index("seq")
-    sections = section_heads.shape[0]
-    span = 2 ** jnp.arange(sections, dtype=jnp.int32)
-    used = jnp.any(section_heads == head, axis=1)
-    width = jnp.sum(jnp.where(jnp.arange(window_blocks.shape[0]) == head, window_blocks, 0))
-    bit = jnp.sum(jnp.where(used, span, 0))
-    valid = (bit >= width).astype(jnp.int32)
-    info = jnp.stack([width, valid, bit]).astype(jnp.int32)
+    head = lax.axis_index("seq").astype(jnp.int32).reshape(1)
     sent = pack([query_rows, key_rows, value_rows, out_grad])
-    mine = lax.all_to_all(sent, "seq", 0, 0, tiled=True)
-    back = lax.all_to_all(attend(info, mine), "seq", 0, 0, tiled=True)
-    return tuple(unpack(back))
+    x = lax.all_to_all(sent, "seq", 0, 0, tiled=True)
+    grads = attend(head, window_blocks, section_heads, x)
+    return tuple(unpack(lax.all_to_all(grads, "seq", 0, 0, tiled=True)))
 
 
 def solution(mesh):

time: 134 us -> 125 us (0.933)
  Pallas kernels: 23.6 us -> 16.3 us
  waiting for transfers between devices: 36.9 us -> 41.5 us
  other arithmetic: 3.27 us -> 0 us
    pallas_call x1, Pallas kernels: 18.2 us -> 10.9 us  [attend(): pl.pallas_call(functools.partial(attend_kernel, blocks=blocks, unroll=unr...]
    all_to_all x1, waiting for transfers between devices: 36.9 us -> 41.5 us  [sharded_by_head(): x = lax.all_to_all(sent, 'seq', 0, 0, tiled=True)]
    another operation x1 -> x0, other arithmetic: 1.88 us -> none  [sharded_by_head(): info = jnp.stack([width, valid, bit]).astype(jnp.int32)]
  transfers between devices with their start and end apart: 1 -> 1, of which waited for: 1 -> 1; matrix products, arithmetic and copies ran while one was open for 2% -> 0% of each run, Pallas kernels for 0% -> 0%
where the time goes in v3:
time: 125 us; the launch traced here: 124 us
  blocking collectives  58.4 us (47%)
  waiting for transfers between devices  41.5 us (33%)
  Pallas kernels  16.3 us (13%)
  starting transfers between devices  7.49 us (6%)
    all_to_all x1, blocking collectives, sharded_by_head(): return tuple(unpack(lax.all_to_all(grads, 'seq', 0, 0, tiled=True)))  58.4 us
    all_to_all x1, waiting for transfers between devices, sharded_by_head(): x = lax.all_to_all(sent, 'seq', 0, 0, tiled=True)  41.5 us
    pallas_call x1, Pallas kernels, attend(): pl.pallas_call(functools.partial(attend_kernel, blocks=blocks, unroll=unr...  10.9 us
    all_to_all x1, starting transfers between devices, sharded_by_head(): x = lax.all_to_all(sent, 'seq', 0, 0, tiled=True)  7.49 us
    pallas_call x1, Pallas kernels, pack(): pl.pallas_call(pack_kernel, grid=(tokens // chunk,), in_specs=[pl.BlockSp...  2.79 us
    pallas_call x1, Pallas kernels, unpack(): pl.pallas_call(unpack_kernel, grid=(tokens // chunk,), in_specs=[pl.Block...  2.64 us
  transfers between devices with their start and end apart: 1, of which 1 were waited for; matrix products, arithmetic and copies ran while one was open for 0% of the time, Pallas kernels for 0%

profile of v3, /device:TPU:1, one launch (start us, length us, event | category | flops | bytes accessed | tf_op | source)
XLA Modules:
  0.0 124.3 jit_solution(17676104175132206789)
XLA Ops:
  0.6 2.8 %shard_map.93 = bf16[16,4,128,128]{3,2,1,0:T(8,128)(2,1)} custom-call(bf16[128,16,128]{2,1,0:T(8,128)(2,1)} %refs_0_.1, bf16[128,16,128]{2,1,0:T(8,128)(2,1)} %refs_1_.1, bf16[128,16,128]{2,1,0:T(8,128)(2,1)} %refs_2_.1, bf16[128,16,128]{2,1,0:T(8,128)(2,1)} %refs_3_.1), custom_call_target="tpu_custom_call" | custom-call | bytes 4194304 | tf_op jit(solution)/shard_map/pallas_call | solution.py:41
  3.4 0.0 copy-start
  3.4 0.0 copy-start.1
  3.4 7.5 %all-to-all-start = ((bf16[16,4,128,128]{3,2,1,0:T(8,128)(2,1)}), bf16[16,4,128,128]{3,2,1,0:T(8,128)(2,1)S(1)}, u32[]{:S(2)}, u32[]{:S(2)}) async-start(bf16[16,4,128,128]{3,2,1,0:T(8,128)(2,1)} %shard_map.93), calls=%async_computation | async-start | bytes 4194304 | tf_op jit(solution)/shard_map/all_to_all | solution.py:450
  10.9 41.5 %all-to-all-done.x = bf16[16,4,128,128]{3,2,1,0:T(8,128)(2,1)S(1)} async-done(((bf16[16,4,128,128]{3,2,1,0:T(8,128)(2,1)}), bf16[16,4,128,128]{3,2,1,0:T(8,128)(2,1)S(1)}, u32[]{:S(2)}, u32[]{:S(2)}) %all-to-all-start) | async-done | bytes 2097184 | tf_op jit(solution)/shard_map/all_to_all | solution.py:450
  52.4 0.0 copy-done
  52.4 0.0 copy-done.1
  52.4 10.9 %shard_map.94 = bf16[16,4,128,128]{3,2,1,0:T(8,128)(2,1)S(1)} custom-call(s32[1]{0:T(128)} %bitcast.head_ref, s32[16]{0:T(128)S(1)} %copy-done.1, s32[4,4]{1,0:T(4,128)S(1)} %copy-done, bf16[16,4,128,128]{3,2,1,0:T(8,128)(2,1)S(1)} %all-to-all-done.x), custom_call_target="tpu_custom_call" | custom-call | flops 2415919104 | bytes 4194304 | tf_op jit(solution)/shard_map/pallas_call | solution.py:182
  63.3 58.4 %all_to_all.10.src = bf16[16,4,128,128]{3,2,1,0:T(8,128)(2,1)} all-to-all(bf16[16,4,128,128]{3,2,1,0:T(8,128)(2,1)S(1)} %shard_map.94), channel_id=1, replica_groups=mesh['grp'=2,'seq'=16] {'seq'}, dimensions={0} | all-to-all | bytes 4194304 | tf_op jit(solution)/shard_map/all_to_all | solution.py:452
  121.7 2.6 %shard_map.95 = (bf16[128,16,128]{2,1,0:T(8,128)(2,1)}, bf16[128,16,128]{2,1,0:T(8,128)(2,1)}, bf16[128,16,128]{2,1,0:T(8,128)(2,1)}, bf16[128,16,128]{2,1,0:T(8,128)(2,1)}) custom-call(bf16[16,4,128,128]{3,2,1,0:T(8,128)(2,1)} %all_to_all.10.src), custom_call_target="tpu_custom_call" | custom-call | bytes 4194304 | tf_op jit(solution)/shard_map/pallas_call | solution.py:59
Async XLA Ops:
  3.4 49.0 %copy-start = (s32[4,4]{1,0:T(4,128)S(1)}, s32[4,4]{1,0:T(4,128)}, u32[]{:S(2)}) copy-start(s32[4,4]{1,0:T(4,128)} %sections.1) | copy-start | bytes 196
  3.4 49.0 %copy-start.1 = (s32[16]{0:T(128)S(1)}, s32[16]{0:T(128)}, u32[]{:S(2)}) copy-start(s32[16]{0:T(128)} %widths.1) | copy-start | bytes 196
  3.4 49.0 %all-to-all-start = ((bf16[16,4,128,128]{3,2,1,0:T(8,128)(2,1)}), bf16[16,4,128,128]{3,2,1,0:T(8,128)(2,1)S(1)}, u32[]{:S(2)}, u32[]{:S(2)}) async-start(bf16[16,4,128,128]{3,2,1,0:T(8,128)(2,1)} %shard_map.93), calls=%async_computation | async-start | bytes 4194304 | tf_op jit(solution)/shard_map/all_to_all | solution.py:450

commit v4 on v3

--- a/solution.py
+++ b/solution.py
@@ -13,6 +13,8 @@
 HALO = WB - 1
 SPAN = (2 * HALO + 1) * BLK
 LINKED = SPAN + BLK
+PLANE = 2 * HALO
+PADDED = PLANE + 2 * HALO
 NT = (((1,), (1,)), ((), ()))
 NN = (((1,), (0,)), ((), ()))
 blocked_score = -1e30
@@ -26,44 +28,6 @@
     return pl.CostEstimate(
         flops=0, transcendentals=0, bytes_accessed=4 * sum(a.size for a in arrays)
     )
-
-
-def pack_kernel(*refs):
-    out = refs[-1]
-    for i, ref in enumerate(refs[:-1]):
-        out[:, i] = jnp.transpose(ref[...], (1, 0, 2))
-
-
-def pack(arrays):
-    tokens, heads, width = arrays[0].shape
-    chunk = 64
-    count = len(arrays)
-    return pl.pallas_call(
-        pack_kernel,
-        grid=(tokens // chunk,),
-        in_specs=[pl.BlockSpec((chunk, heads, width), lambda i: (i, 0, 0))] * count,
-        out_specs=pl.BlockSpec((heads, count, chunk, width), lambda i: (0, 0, i, 0)),
-        out_shape=jax.ShapeDtypeStruct((heads, count, tokens, width), jnp.bfloat16),
-        cost_estimate=moved_cost(arrays),
-    )(*arrays)
-
-
-def unpack_kernel(src, *outs):
-    for i, out in enumerate(outs):
-        out[...] = jnp.transpose(src[:, i], (1, 0, 2))
-
-
-def unpack(stacked):
-    heads, count, tokens, width = stacked.shape
-    chunk = 64
-    return pl.pallas_call(
-        unpack_kernel,
-        grid=(tokens // chunk,),
-        in_specs=[pl.BlockSpec((heads, count, chunk, width), lambda i: (0, 0, i, 0))],
-        out_specs=[pl.BlockSpec((chunk, heads, width), lambda i: (i, 0, 0))] * count,
-        out_shape=[jax.ShapeDtypeStruct((tokens, heads, width), jnp.bfloat16)] * count,
-        cost_estimate=moved_cost([stacked]),
-    )(stacked)
 
 
 def softmax_pair(score, far_score, biases, far_bias, scale2):
@@ -118,82 +82,293 @@
     return out
 
 
-def attend_kernel(
-    head_ref, widths, sections, x, out, keys, values, key_acc, value_acc, *, blocks, unroll
-):
-    head = head_ref[0]
-    width = widths[head]
-    far_bit = jnp.int32(0)
-    for s in range(sections.shape[0]):
-        for i in range(sections.shape[1]):
-            far_bit = jnp.where(sections[s, i] == head, 1 << s, far_bit)
-    far_bias = jnp.where(far_bit >= width, 0.0, blocked_score).astype(jnp.float32)
-    scale = 1.0 / math.sqrt(x.shape[-1])
-    zero = jnp.zeros((HALO * BLK, x.shape[-1]), jnp.bfloat16)
-    for ref, part in ((keys, 1), (values, 2)):
-        ref[: HALO * BLK] = zero
-        ref[(HALO + blocks) * BLK :] = zero
-        for b in range(blocks):
-            ref[(HALO + b) * BLK : (HALO + b + 1) * BLK] = x[b, part]
-    key_acc[...] = jnp.zeros_like(key_acc)
-    value_acc[...] = jnp.zeros_like(value_acc)
-    pair_span = SPAN + BLK
-
-    def one(b):
-        q = jnp.concatenate([x[b, 0], x[b + 1, 0]], axis=0)
-        g = jnp.concatenate([x[b, 3], x[b + 1, 3]], axis=0)
-        at = pl.multiple_of(b * BLK, BLK)
-        far_at = [pl.multiple_of((HALO + ((b + r) ^ far_bit)) * BLK, BLK) for r in range(2)]
-        attended, dq, key_near, value_near, key_far, value_far = attend_pair(
-            q,
-            g,
-            keys[pl.ds(at, pair_span)],
-            values[pl.ds(at, pair_span)],
-            [keys[pl.ds(far_at[r], BLK)] for r in range(2)],
-            [values[pl.ds(far_at[r], BLK)] for r in range(2)],
-            near_biases(b, width, 0, blocks),
+def rows_of(block):
+    return pl.ds(pl.multiple_of(block * BLK, BLK), BLK)
+
+
+def whole(shape):
+    return pl.BlockSpec(shape, lambda *_: (0,) * len(shape))
+
+
+SMEM = pl.BlockSpec(memory_space=pltpu.SMEM)
+VMEM = pl.BlockSpec(memory_space=pltpu.VMEM)
+LIMIT = pltpu.CompilerParams(vmem_limit_bytes=20 << 20)
+
+
+def pack_kernel(place, sections, *refs, groups, count):
+    ins, outs, held = refs[:count], refs[count:-1], refs[-1]
+    for i in range(count):
+        held[i] = jnp.transpose(ins[i][...], (1, 0, 2))
+    for number, group in enumerate(groups):
+        for m in range(PLANE):
+            for k, s in enumerate(group):
+                head = sections[s, place[0] ^ m]
+                for i in range(count):
+                    outs[number * PLANE + m][k, i] = held[i, head]
+
+
+def pack(place, sections, arrays, groups):
+    tokens, heads, width = arrays[0].shape
+    chunk = tokens // 2
+    count = len(arrays)
+    shapes = [(len(group), count, tokens, width) for group in groups for _ in range(PLANE)]
+    outs = pl.pallas_call(
+        functools.partial(pack_kernel, groups=groups, count=count),
+        grid=(tokens // chunk,),
+        in_specs=[SMEM, SMEM]
+        + [pl.BlockSpec((chunk, heads, width), lambda i: (i, 0, 0))] * count,
+        out_specs=[
+            pl.BlockSpec((*shape[:2], chunk, width), lambda i: (0, 0, i, 0)) for shape in shapes
+        ],
+        out_shape=[jax.ShapeDtypeStruct(shape, jnp.bfloat16) for shape in shapes],
+        scratch_shapes=[pltpu.VMEM((count, heads, chunk, width), jnp.bfloat16)],
+        compiler_params=LIMIT,
+        cost_estimate=moved_cost(arrays),
+    )(place, sections, *arrays)
+    return [outs[i * PLANE : (i + 1) * PLANE] for i in range(len(groups))]
+
+
+def unpack_kernel(place, sections, *refs, groups, count):
+    pieces, outs, held = refs[: len(groups) * PLANE], refs[len(groups) * PLANE : -1], refs[-1]
+    for number, group in enumerate(groups):
+        for m in range(PLANE):
+            for k, s in enumerate(group):
+                head = sections[s, place[0] ^ m]
+                for i in range(count):
+                    held[i, head] = pieces[number * PLANE + m][k, i]
+    for i in range(count):
+        outs[i][...] = jnp.transpose(held[i], (1, 0, 2))
+
+
+def unpack(place, sections, pieces, groups):
+    flat = [piece for group in pieces for piece in group]
+    _, count, tokens, width = flat[0].shape
+    heads = sections.size
+    chunk = tokens // 2
+    return pl.pallas_call(
+        functools.partial(unpack_kernel, groups=groups, count=count),
+        grid=(tokens // chunk,),
+        in_specs=[SMEM, SMEM]
+        + [
+            pl.BlockSpec((*piece.shape[:2], chunk, width), lambda i: (0, 0, i, 0))
+            for piece in flat
+        ],
+        out_specs=[pl.BlockSpec((chunk, heads, width), lambda i: (i, 0, 0))] * count,
+        out_shape=[jax.ShapeDtypeStruct((tokens, heads, width), jnp.bfloat16)] * count,
+        scratch_shapes=[pltpu.VMEM((count, heads, chunk, width), jnp.bfloat16)],
+        compiler_params=LIMIT,
+        cost_estimate=moved_cost(flat),
+    )(place, sections, *flat)
+
+
+def far_kernel(*refs):
+    pieces, outs = refs[:PLANE], refs[PLANE:]
+    for k, out in enumerate(outs):
+        for m, piece in enumerate(pieces):
+            out[m] = piece[k]
+
+
+def far_parts(pieces):
+    group, *rest = pieces[0].shape
+    return pl.pallas_call(
+        far_kernel,
+        in_specs=[VMEM] * PLANE,
+        out_specs=[VMEM] * group,
+        out_shape=[jax.ShapeDtypeStruct((PLANE, *rest), jnp.bfloat16)] * group,
+        compiler_params=LIMIT,
+        cost_estimate=moved_cost(pieces),
+    )(*pieces)
+
+
+def halo_kernel(place, *refs, groups):
+    pieces, (up, down) = refs[:-2], refs[-2:]
+    upper_chip = place[0] // HALO
+
+    def fill(high, low):
+        for m in range(HALO):
+            slot = 0
+            for number in range(groups):
+                for k in range(pieces[number * PLANE].shape[0]):
+                    up[m, slot] = pieces[number * PLANE + high + m][k]
+                    down[m, slot] = pieces[number * PLANE + low + m][k]
+                    slot += 1
+
+    @pl.when(upper_chip == 1)
+    def _():
+        fill(0, HALO)
+
+    @pl.when(upper_chip == 0)
+    def _():
+        fill(HALO, 0)
+
+
+def halo_parts(place, pieces):
+    flat = [piece for group in pieces for piece in group]
+    slots = sum(group[0].shape[0] for group in pieces)
+    shape = jax.ShapeDtypeStruct((HALO, slots, *flat[0].shape[1:]), jnp.bfloat16)
+    return pl.pallas_call(
+        functools.partial(halo_kernel, groups=len(pieces)),
+        in_specs=[SMEM] + [VMEM] * len(flat),
+        out_specs=[VMEM] * 2,
+        out_shape=[shape] * 2,
+        compiler_params=LIMIT,
+        cost_estimate=moved_cost(flat),
+    )(place, *flat)
+
+
+def attend_kernel(place, widths, sections, *refs, first, remote, blocks):
+    pairs, graded = refs[:PLANE], refs[PLANE : 2 * PLANE]
+    below, above = refs[2 * PLANE : 2 * PLANE + 2]
+    rest = refs[2 * PLANE + 2 :]
+    far_in, rest = rest[:remote], rest[remote:]
+    outs, rest = rest[:PLANE], rest[PLANE:]
+    (part, to_below, to_above), rest = rest[:3], rest[3:]
+    far_out, rest = rest[:remote], rest[remote:]
+    keys, values, far_keys, far_values, queries, grads, attended, dq = rest[:8]
+    accs, far_accs = rest[8:10], rest[10:12]
+    k = pl.program_id(0)
+    section = first + k
+    me = place[0]
+    width = widths[sections[section, me]]
+    bit = jnp.left_shift(jnp.int32(1), section)
+    far_bias = jnp.where(bit >= width, 0.0, blocked_score).astype(jnp.float32)
+    scales = (1.0 / math.sqrt(keys.shape[-1]), 1.0)
+    for m in range(PLANE):
+        b = me ^ m
+        keys[rows_of(HALO + b)] = pairs[m][0, 0]
+        values[rows_of(HALO + b)] = pairs[m][0, 1]
+        queries[rows_of(b)] = graded[m][0, 0]
+        grads[rows_of(b)] = graded[m][0, 1]
+    for m in range(HALO):
+        b = (me % HALO) ^ m
+        keys[rows_of(b)] = below[m, 0, 0]
+        values[rows_of(b)] = below[m, 0, 1]
+        keys[rows_of(HALO + PLANE + b)] = above[m, 0, 0]
+        values[rows_of(HALO + PLANE + b)] = above[m, 0, 1]
+    if remote:
+        for n in range(remote):
+
+            @pl.when(k == n)
+            def _(n=n):
+                for m in range(PLANE):
+                    far_keys[rows_of(me ^ m)] = far_in[n][m, 0]
+                    far_values[rows_of(me ^ m)] = far_in[n][m, 1]
+    else:
+        for b in range(PLANE):
+            far_keys[rows_of(b)] = keys[rows_of(HALO + (b ^ bit))]
+            far_values[rows_of(b)] = values[rows_of(HALO + (b ^ bit))]
+    for acc in accs:
+        acc[...] = jnp.zeros_like(acc)
+    for b in range(0, PLANE, 2):
+        own = slice(b * BLK, (b + 2) * BLK)
+        seen = slice(b * BLK, (b + 2 * HALO + 2) * BLK)
+        one = [slice((b + r) * BLK, (b + r + 1) * BLK) for r in range(2)]
+        o, d, key_near, value_near, key_far, value_far = attend_pair(
+            queries[own],
+            grads[own],
+            keys[seen],
+            values[seen],
+            [far_keys[one[r]] for r in range(2)],
+            [far_values[one[r]] for r in range(2)],
+            near_biases(place[1] * PLANE + b, width, 0, blocks),
             far_bias,
         )
-        for r in range(2):
-            rows = slice(r * BLK, (r + 1) * BLK)
-            out[b + r, 0] = attended[rows]
-            out[b + r, 1] = dq[rows]
-        key_acc[:, pl.ds(at, pair_span)] += key_near
-        value_acc[:, pl.ds(at, pair_span)] += value_near
-        for r in range(2):
-            key_acc[:, pl.ds(far_at[r], BLK)] += key_far[r]
-            value_acc[:, pl.ds(far_at[r], BLK)] += value_far[r]
-
-    def step(i, carry):
-        for u in range(unroll):
-            one((i * unroll + u) * 2)
-        return carry
-
-    lax.fori_loop(0, blocks // (2 * unroll), step, 0)
-    for b in range(blocks):
-        cols = slice((HALO + b) * BLK, (HALO + b + 1) * BLK)
-        out[b, 2] = jnp.transpose((key_acc[:, cols] * scale).astype(jnp.bfloat16))
-        out[b, 3] = jnp.transpose(value_acc[:, cols].astype(jnp.bfloat16))
-
-
-def attend(head, window_blocks, section_heads, x, unroll=2):
-    blocks, _, _, width = x.shape
-    padded = (blocks + 2 * HALO) * BLK
+        attended[own] = o
+        dq[own] = d
+        for acc, near in zip(accs, (key_near, value_near)):
+            acc[:, seen] += near
+        for acc, far in zip(far_accs, (key_far, value_far)):
+            for r in range(2):
+                acc[:, one[r]] = far[r]
+    for i, (acc, far_acc) in enumerate(zip(accs, far_accs)):
+        if not remote:
+            for b in range(PLANE):
+                acc[:, rows_of(HALO + (b ^ bit))] += far_acc[:, b * BLK : (b + 1) * BLK]
+        for n in range(remote):
+
+            @pl.when(k == n)
+            def _(n=n, i=i, far_acc=far_acc):
+                for m in range(PLANE):
+                    far_out[n][m, i] = (far_acc[:, rows_of(me ^ m)] * scales[i]).astype(
+                        jnp.bfloat16
+                    )
+
+        for m in range(PLANE):
+            part[0, m, i] = acc[:, rows_of(HALO + (me ^ m))] * scales[i]
+        for m in range(HALO):
+            b = (me % HALO) ^ m
+            to_below[m, 0, i] = (acc[:, rows_of(b)] * scales[i]).astype(jnp.bfloat16)
+            to_above[m, 0, i] = (acc[:, rows_of(HALO + PLANE + b)] * scales[i]).astype(
+                jnp.bfloat16
+            )
+    for m in range(PLANE):
+        outs[m][0, 0] = attended[rows_of(me ^ m)]
+        outs[m][0, 1] = dq[rows_of(me ^ m)]
+
+
+def attend(place, widths, sections, pairs, graded, below, above, far, first, slot, blocks):
+    group, count, _, width = pairs[0].shape
+    tile = (BLK, width)
+    remote = len(far)
+    piece = pl.BlockSpec((1, count, *tile), lambda k: (k, 0, 0, 0))
+    graded_piece = pl.BlockSpec((1, count, *tile), lambda k: (slot + k, 0, 0, 0))
+    halo_in = pl.BlockSpec((HALO, 1, count, *tile), lambda k: (0, slot + k, 0, 0, 0))
+    halo_out = pl.BlockSpec((HALO, 1, count, *tile), lambda k: (0, k, 0, 0, 0))
+    far_spec = whole((PLANE, count, *tile))
+    bf16 = jnp.bfloat16
+    outs = pl.pallas_call(
+        functools.partial(attend_kernel, first=first, remote=remote, blocks=blocks),
+        grid=(group,),
+        in_specs=[SMEM] * 3
+        + [piece] * PLANE
+        + [graded_piece] * PLANE
+        + [halo_in] * 2
+        + [far_spec] * remote,
+        out_specs=[piece] * PLANE
+        + [pl.BlockSpec((1, PLANE, count, *tile), lambda k: (k, 0, 0, 0, 0))]
+        + [halo_out] * 2
+        + [far_spec] * remote,
+        out_shape=[jax.ShapeDtypeStruct((group, count, *tile), bf16)] * PLANE
+        + [jax.ShapeDtypeStruct((group, PLANE, count, *tile), jnp.float32)]
+        + [jax.ShapeDtypeStruct((HALO, group, count, *tile), bf16)] * 2
+        + [jax.ShapeDtypeStruct((PLANE, count, *tile), bf16)] * remote,
+        scratch_shapes=[pltpu.VMEM((PADDED * BLK, width), bf16)] * 2
+        + [pltpu.VMEM((PLANE * BLK, width), bf16)] * 6
+        + [pltpu.VMEM((width, PADDED * BLK), jnp.float32)] * 2
+        + [pltpu.VMEM((width, PLANE * BLK), jnp.float32)] * 2,
+        compiler_params=LIMIT,
+        cost_estimate=pl.CostEstimate(
+            flops=group * PLANE * 12 * BLK * LINKED * width,
+            transcendentals=group * PLANE * BLK * LINKED,
+            bytes_accessed=40 * group * PLANE * BLK * width,
+        ),
+    )(place, widths, sections, *pairs, *graded, below, above, *far)
+    return outs[:PLANE], outs[PLANE], outs[PLANE + 1], outs[PLANE + 2], outs[PLANE + 3 :]
+
+
+def combine_kernel(place, part, above, below, *refs, remote):
+    far, outs = refs[:remote], refs[remote:]
+    for m in range(PLANE):
+        upper = (m // HALO) ^ (place[0] // HALO)
+        for k in range(part.shape[0]):
+            for i in range(part.shape[2]):
+                owed = jnp.where(upper == 1, above[m % HALO, k, i], below[m % HALO, k, i])
+                total = part[k, m, i] + owed.astype(jnp.float32)
+                if remote:
+                    total += far[k][m, i].astype(jnp.float32)
+                outs[m][k, i] = jnp.transpose(total.astype(jnp.bfloat16))
+
+
+def combine(place, part, above, below, far):
+    group, _, *rest = part.shape
     return pl.pallas_call(
-        functools.partial(attend_kernel, blocks=blocks, unroll=unroll),
-        in_specs=[pl.BlockSpec(memory_space=pltpu.SMEM)] * 3
-        + [pl.BlockSpec(memory_space=pltpu.VMEM)],
-        out_specs=pl.BlockSpec(memory_space=pltpu.VMEM),
-        out_shape=jax.ShapeDtypeStruct(x.shape, jnp.bfloat16),
-        scratch_shapes=[pltpu.VMEM((padded, width), jnp.bfloat16)] * 2
-        + [pltpu.VMEM((width, padded), jnp.float32)] * 2,
-        compiler_params=pltpu.CompilerParams(vmem_limit_bytes=24 << 20),
-        cost_estimate=pl.CostEstimate(
-            flops=blocks * 12 * BLK * LINKED * width,
-            transcendentals=blocks * BLK * LINKED,
-            bytes_accessed=4 * x.size,
-        ),
-    )(head, window_blocks, section_heads, x)
+        functools.partial(combine_kernel, remote=len(far)),
+        in_specs=[SMEM] + [VMEM] * (3 + len(far)),
+        out_specs=[VMEM] * PLANE,
+        out_shape=[jax.ShapeDtypeStruct((group, *rest), jnp.bfloat16)] * PLANE,
+        compiler_params=LIMIT,
+        cost_estimate=moved_cost([part, above, below, *far]),
+    )(place, part, above, below, *far)
 
 
 def partner(value, axis, apart):
@@ -444,12 +619,53 @@
     return (attended.reshape(tokens_dev, head_count, head_width), query_grad, key_grad, value_grad)
 
 
-def sharded_by_head(query_rows, key_rows, value_rows, out_grad, window_blocks, section_heads):
-    head = lax.axis_index("seq").astype(jnp.int32).reshape(1)
-    sent = pack([query_rows, key_rows, value_rows, out_grad])
-    x = lax.all_to_all(sent, "seq", 0, 0, tiled=True)
-    grads = attend(head, window_blocks, section_heads, x)
-    return tuple(unpack(lax.all_to_all(grads, "seq", 0, 0, tiled=True)))
+def in_plane(pieces):
+    peers = lax.axis_size("seq")
+    return [pieces[0]] + [
+        lax.ppermute(pieces[m], "seq", [(i, i ^ m) for i in range(peers)])
+        for m in range(1, PLANE)
+    ]
+
+
+def between_planes(value, by):
+    return passed_along(value, "seq", by * PLANE)
+
+
+def sharded_by_plane(query_rows, key_rows, value_rows, out_grad, widths, sections):
+    position = lax.axis_index("seq").astype(jnp.int32)
+    place = jnp.stack([position % PLANE, position // PLANE])
+    blocks = lax.axis_size("seq")
+    local = PLANE.bit_length() - 1
+    total = sections.shape[0]
+    groups = [tuple(range(local, total)), tuple(range(local))]
+    order = tuple(s for group in groups for s in group)
+    sent_far, sent_near = pack(place, sections, [key_rows, value_rows], groups)
+    pairs_far, pairs_near = in_plane(sent_far), in_plane(sent_near)
+    far_sent = far_parts(pairs_far)
+    (sent,) = pack(place, sections, [query_rows, out_grad], [order])
+    far_sent, sent = lax.optimization_barrier((far_sent, sent))
+    far = [partner(value, "seq", local + n) for n, value in enumerate(far_sent)]
+    up, down = halo_parts(place, [pairs_far, pairs_near])
+    below, above = between_planes(up, 1), between_planes(down, -1)
+    graded = in_plane(sent)
+    shared = (place, widths, sections)
+    outs_far, part_far, low_far, high_far, far_owed = attend(
+        *shared, pairs_far, graded, below, above, far, local, 0, blocks
+    )
+    far_back = [partner(value, "seq", local + n) for n, value in enumerate(far_owed)]
+    above_far, below_far = between_planes(low_far, -1), between_planes(high_far, 1)
+    outs_near, part_near, low_near, high_near, _ = attend(
+        *shared, pairs_near, graded, below, above, [], 0, total - local, blocks
+    )
+    above_near, below_near = between_planes(low_near, -1), between_planes(high_near, 1)
+    rows = [in_plane(outs_far), in_plane(outs_near)]
+    columns = [
+        in_plane(combine(place, part_far, above_far, below_far, far_back)),
+        in_plane(combine(place, part_near, above_near, below_near, [])),
+    ]
+    attended, query_grad = unpack(place, sections, rows, groups)
+    key_grad, value_grad = unpack(place, sections, columns, groups)
+    return attended, query_grad, key_grad, value_grad
 
 
 def solution(mesh):
@@ -460,8 +676,8 @@
         tokens, heads, width = args[0].shape
         sections, listed = args[5].shape
         once = sections * listed == heads
-        if tokens == BLK and heads == peers and once and 1 << sections == peers:
-            return sharded_by_head(*args)
+        if tokens == BLK and once and listed == PLANE and 1 << sections == peers == PLANE**2:
+            return sharded_by_plane(*args)
         return per_device(*args)
 
     return jax.shard_map(

time: 125 us -> 104 us (0.83)
  the two profiles are of different devices: /device:TPU:1 before, /device:TPU:27 now
where the time goes in v4:
time: 104 us
  starting transfers between devices  42.9 us (41%)
  waiting for transfers between devices  36.8 us (35%)
  Pallas kernels  20.2 us (19%)
  local copies, waits for them, and re-layouts  2.69 us (3%)
    ppermute x21, waiting for transfers between devices, in_plane(): lax.ppermute(pieces[m], 'seq', [(i, i ^ m) for i in range(peers)])  27.9 us
    ppermute x21, starting transfers between devices, in_plane(): lax.ppermute(pieces[m], 'seq', [(i, i ^ m) for i in range(peers)])  21.6 us
    ppermute x6, starting transfers between devices, passed_along(): return lax.ppermute(value, axis, pairs)  14.6 us
    pallas_call x2, Pallas kernels, attend(): pl.pallas_call(functools.partial(attend_kernel, first=first, remote=remot...  12.2 us
    ppermute x4, waiting for transfers between devices, partner(): lax.ppermute(value, axis, [(i, i ^ 1 << apart) for i in range(lax.axis_si...  8.95 us
    ppermute x4, starting transfers between devices, partner(): lax.ppermute(value, axis, [(i, i ^ 1 << apart) for i in range(lax.axis_si...  6.73 us
    pallas_call x2, Pallas kernels, unpack(): pl.pallas_call(functools.partial(unpack_kernel, groups=groups, count=coun...  3.64 us
    unnamed x12, local copies, waits for them, and re-layouts  2.69 us
  transfers between devices with their start and end apart: 31, of which 12 were waited for; matrix products, arithmetic and copies ran while one was open for 0% of the time, Pallas kernels for 16%

profile of v4, /device:TPU:27, one launch (start us, length us, event | category | flops | bytes accessed | tf_op | source)
XLA Modules:
  0.0 103.6 jit_solution(3265052604566880846)
XLA Ops:
  5.3 1.3 %collective-permute-start.1 = (bf16[2,2,128,128]{3,2,1,0:T(8,128)(2,1)S(1)}, bf16[2,2,128,128]{3,2,1,0:T(8,128)(2,1)S(1)}, u32[]{:S(2)}, u32[]{:S(2)}) collective-permute-start(bf16[2,2,128,128]{3,2,1,0:T(8,128)(2,1)S(1)} %get-tuple-element.56), channel_id=1, source_target_pairs={{0,2},{1,3},{2,0},{3,1},{4,6},{5,7},{6,4},{7,5},{8,10},{9,11},{10,... | collective-permute-start | bytes 393224 | tf_op jit(solution)/shard_map/ppermute | solution.py:625
  7.1 1.2 %collective-permute-start.7 = (bf16[2,2,128,128]{3,2,1,0:T(8,128)(2,1)S(1)}, bf16[2,2,128,128]{3,2,1,0:T(8,128)(2,1)S(1)}, u32[]{:S(2)}, u32[]{:S(2)}) collective-permute-start(bf16[2,2,128,128]{3,2,1,0:T(8,128)(2,1)S(1)} %get-tuple-element.70), channel_id=1, source_target_pairs={{0,2},{1,3},{2,0},{3,1},{4,6},{5,7},{6,4},{7,5},{8,10},{9,11},{10,... | collective-permute-start | bytes 393224 | tf_op jit(solution)/shard_map/ppermute | solution.py:625
  10.3 3.4 %collective-permute-done.2.refs_3_ = bf16[2,2,128,128]{3,2,1,0:T(8,128)(2,1)S(1)} collective-permute-done((bf16[2,2,128,128]{3,2,1,0:T(8,128)(2,1)S(1)}, bf16[2,2,128,128]{3,2,1,0:T(8,128)(2,1)S(1)}, u32[]{:S(2)}, u32[]{:S(2)}) %collective-permute-start.2) | collective-permute-done | bytes 131104 | tf_op jit(solution)/shard_map/ppermute | solution.py:625
  13.8 2.2 %collective-permute-done.7.refs_6_.refs_2_ = bf16[2,2,128,128]{3,2,1,0:T(8,128)(2,1)S(1)} collective-permute-done((bf16[2,2,128,128]{3,2,1,0:T(8,128)(2,1)S(1)}, bf16[2,2,128,128]{3,2,1,0:T(8,128)(2,1)S(1)}, u32[]{:S(2)}, u32[]{:S(2)}) %collective-permute-start.7) | collective-permute-done | bytes 131104 | tf_op jit(solution)/shard_map/ppermute | solution.py:625
  16.0 3.0 %collective-permute-done.8.refs_7_.refs_3_ = bf16[2,2,128,128]{3,2,1,0:T(8,128)(2,1)S(1)} collective-permute-done((bf16[2,2,128,128]{3,2,1,0:T(8,128)(2,1)S(1)}, bf16[2,2,128,128]{3,2,1,0:T(8,128)(2,1)S(1)}, u32[]{:S(2)}, u32[]{:S(2)}) %collective-permute-start.8) | collective-permute-done | bytes 131104 | tf_op jit(solution)/shard_map/ppermute | solution.py:625
  19.6 2.1 %collective-permute-start.10 = (bf16[2,4,2,128,128]{4,3,2,1,0:T(8,128)(2,1)S(1)}, bf16[2,4,2,128,128]{4,3,2,1,0:T(8,128)(2,1)S(1)}, u32[]{:S(2)}, u32[]{:S(2)}) collective-permute-start(bf16[2,4,2,128,128]{4,3,2,1,0:T(8,128)(2,1)S(1)} %get-tuple-element.73), channel_id=1, source_target_pairs={{4,0},{5,1},{6,2},{7,3},{8,4},{9,5},{10,6},{11,7},{12,8},{13,9},{1... | collective-permute-start | bytes 1572872 | tf_op jit(solution)/shard_map/ppermute | solution.py:381
  21.7 1.3 %collective-permute-start.9 = (bf16[2,4,2,128,128]{4,3,2,1,0:T(8,128)(2,1)S(1)}, bf16[2,4,2,128,128]{4,3,2,1,0:T(8,128)(2,1)S(1)}, u32[]{:S(2)}, u32[]{:S(2)}) collective-permute-start(bf16[2,4,2,128,128]{4,3,2,1,0:T(8,128)(2,1)S(1)} %get-tuple-element.72), channel_id=1, source_target_pairs={{0,4},{1,5},{2,6},{3,7},{4,8},{5,9},{6,10},{7,11},{8,12},{9,13},{1... | collective-permute-start | bytes 1572872 | tf_op jit(solution)/shard_map/ppermute | solution.py:381
  24.7 1.3 %collective-permute-start.4 = (bf16[4,2,128,128]{3,2,1,0:T(8,128)(2,1)S(1)}, bf16[4,2,128,128]{3,2,1,0:T(8,128)(2,1)S(1)}, u32[]{:S(2)}, u32[]{:S(2)}) collective-permute-start(bf16[4,2,128,128]{3,2,1,0:T(8,128)(2,1)S(1)} %get-tuple-element.66), channel_id=1, source_target_pairs={{0,2},{1,3},{2,0},{3,1},{4,6},{5,7},{6,4},{7,5},{8,10},{9,11},{10,... | collective-permute-start | bytes 786440 | tf_op jit(solution)/shard_map/ppermute | solution.py:625
  26.4 2.4 %collective-permute-start.11 = (bf16[4,2,128,128]{3,2,1,0:T(8,128)(2,1)S(1)}, bf16[4,2,128,128]{3,2,1,0:T(8,128)(2,1)S(1)}, u32[]{:S(2)}, u32[]{:S(2)}) collective-permute-start(bf16[4,2,128,128]{3,2,1,0:T(8,128)(2,1)S(1)} %get-tuple-element.74), channel_id=1, source_target_pairs={{0,4},{1,5},{2,6},{3,7},{4,0},{5,1},{6,2},{7,3},{8,12},{9,13},{10,... | collective-permute-start | bytes 786440 | tf_op jit(solution)/shard_map/ppermute | solution.py:375
  28.8 3.8 %collective-permute-done.4.refs_6_ = bf16[4,2,128,128]{3,2,1,0:T(8,128)(2,1)S(1)} collective-permute-done((bf16[4,2,128,128]{3,2,1,0:T(8,128)(2,1)S(1)}, bf16[4,2,128,128]{3,2,1,0:T(8,128)(2,1)S(1)}, u32[]{:S(2)}, u32[]{:S(2)}) %collective-permute-start.4) | collective-permute-done | bytes 262176 | tf_op jit(solution)/shard_map/ppermute | solution.py:625
  32.6 2.2 %collective-permute-start.12 = (bf16[4,2,128,128]{3,2,1,0:T(8,128)(2,1)S(1)}, bf16[4,2,128,128]{3,2,1,0:T(8,128)(2,1)S(1)}, u32[]{:S(2)}, u32[]{:S(2)}) collective-permute-start(bf16[4,2,128,128]{3,2,1,0:T(8,128)(2,1)S(1)} %get-tuple-element.75), channel_id=1, source_target_pairs={{0,8},{1,9},{2,10},{3,11},{4,12},{5,13},{6,14},{7,15},{8,0},{9,1},... | collective-permute-start | bytes 786440 | tf_op jit(solution)/shard_map/ppermute | solution.py:375
  34.8 3.9 %collective-permute-done.5.refs_7_ = bf16[4,2,128,128]{3,2,1,0:T(8,128)(2,1)S(1)} collective-permute-done((bf16[4,2,128,128]{3,2,1,0:T(8,128)(2,1)S(1)}, bf16[4,2,128,128]{3,2,1,0:T(8,128)(2,1)S(1)}, u32[]{:S(2)}, u32[]{:S(2)}) %collective-permute-start.5) | collective-permute-done | bytes 262176 | tf_op jit(solution)/shard_map/ppermute | solution.py:625
  38.7 6.0 %shard_map.98 = (bf16[2,2,128,128]{3,2,1,0:T(8,128)(2,1)S(1)}, bf16[2,2,128,128]{3,2,1,0:T(8,128)(2,1)S(1)}, bf16[2,2,128,128]{3,2,1,0:T(8,128)(2,1)S(1)}, bf16[...) custom-call(s32[2]{0:T(128)S(1)} %pad_add_fusion.place, ...), custom_call_target="tpu_custom_call" | custom-call | flops 1207959552 | bytes 5242880 | tf_op jit(solution)/shard_map/pallas_call | solution.py:319
  44.7 4.3 %collective-permute-start.26 = (bf16[2,2,2,128,128]{4,3,2,1,0:T(8,128)(2,1)S(1)}, bf16[2,2,2,128,128]{4,3,2,1,0:T(8,128)(2,1)S(1)}, u32[]{:S(2)}, u32[]{:S(2)}) collective-permute-start(bf16[2,2,2,128,128]{4,3,2,1,0:T(8,128)(2,1)S(1)} %get-tuple-element.96), channel_id=1, source_target_pairs={{4,0},{5,1},{6,2},{7,3},{8,4},{9,5},{10,6},{11,7},{12,8},{13,9},{1... | collective-permute-start | bytes 786440 | tf_op jit(solution)/shard_map/ppermute | solution.py:381
  49.0 1.3 %collective-permute-start.27 = (bf16[2,2,2,128,128]{4,3,2,1,0:T(8,128)(2,1)S(1)}, bf16[2,2,2,128,128]{4,3,2,1,0:T(8,128)(2,1)S(1)}, u32[]{:S(2)}, u32[]{:S(2)}) collective-permute-start(bf16[2,2,2,128,128]{4,3,2,1,0:T(8,128)(2,1)S(1)} %get-tuple-element.97), channel_id=1, source_target_pairs={{0,4},{1,5},{2,6},{3,7},{4,8},{5,9},{6,10},{7,11},{8,12},{9,13},{1... | collective-permute-start | bytes 786440 | tf_op jit(solution)/shard_map/ppermute | solution.py:381
  50.3 2.8 %collective-permute-start.16 = (bf16[2,2,128,128]{3,2,1,0:T(8,128)(2,1)S(1)}, bf16[2,2,128,128]{3,2,1,0:T(8,128)(2,1)S(1)}, u32[]{:S(2)}, u32[]{:S(2)}) collective-permute-start(bf16[2,2,128,128]{3,2,1,0:T(8,128)(2,1)S(1)} %get-tuple-element.81), channel_id=1, source_target_pairs={{0,1},{1,0},{2,3},{3,2},{4,5},{5,4},{6,7},{7,6},{8,9},{9,8},{10,11... | collective-permute-start | bytes 393224 | tf_op jit(solution)/shard_map/ppermute | solution.py:625
  53.1 6.2 %shard_map.97 = (bf16[2,2,128,128]{3,2,1,0:T(8,128)(2,1)S(1)}, bf16[2,2,128,128]{3,2,1,0:T(8,128)(2,1)S(1)}, bf16[2,2,128,128]{3,2,1,0:T(8,128)(2,1)S(1)}, bf16[...) custom-call(s32[2]{0:T(128)S(1)} %pad_add_fusion.place, ...), custom_call_target="tpu_custom_call" | custom-call | flops 1207959552 | bytes 5242880 | tf_op jit(solution)/shard_map/pallas_call | solution.py:319
  59.3 4.3 %collective-permute-start.19 = (bf16[2,2,2,128,128]{4,3,2,1,0:T(8,128)(2,1)S(1)}, bf16[2,2,2,128,128]{4,3,2,1,0:T(8,128)(2,1)S(1)}, u32[]{:S(2)}, u32[]{:S(2)}) collective-permute-start(bf16[2,2,2,128,128]{4,3,2,1,0:T(8,128)(2,1)S(1)} %get-tuple-element.87), channel_id=1, source_target_pairs={{4,0},{5,1},{6,2},{7,3},{8,4},{9,5},{10,6},{11,7},{12,8},{13,9},{1... | collective-permute-start | bytes 786440 | tf_op jit(solution)/shard_map/ppermute | solution.py:381
  63.6 1.3 %collective-permute-start.20 = (bf16[2,2,2,128,128]{4,3,2,1,0:T(8,128)(2,1)S(1)}, bf16[2,2,2,128,128]{4,3,2,1,0:T(8,128)(2,1)S(1)}, u32[]{:S(2)}, u32[]{:S(2)}) collective-permute-start(bf16[2,2,2,128,128]{4,3,2,1,0:T(8,128)(2,1)S(1)} %get-tuple-element.88), channel_id=1, source_target_pairs={{0,4},{1,5},{2,6},{3,7},{4,8},{5,9},{6,10},{7,11},{8,12},{9,13},{1... | collective-permute-start | bytes 786440 | tf_op jit(solution)/shard_map/ppermute | solution.py:381
  64.9 2.1 %collective-permute-start.21 = (bf16[4,2,128,128]{3,2,1,0:T(8,128)(2,1)S(1)}, bf16[4,2,128,128]{3,2,1,0:T(8,128)(2,1)S(1)}, u32[]{:S(2)}, u32[]{:S(2)}) collective-permute-start(bf16[4,2,128,128]{3,2,1,0:T(8,128)(2,1)S(1)} %get-tuple-element.89), channel_id=1, source_target_pairs={{0,4},{1,5},{2,6},{3,7},{4,0},{5,1},{6,2},{7,3},{8,12},{9,13},{10,... | collective-permute-start | bytes 786440 | tf_op jit(solution)/shard_map/ppermute | solution.py:375
  67.1 1.3 %collective-permute-start.17 = (bf16[2,2,128,128]{3,2,1,0:T(8,128)(2,1)S(1)}, bf16[2,2,128,128]{3,2,1,0:T(8,128)(2,1)S(1)}, u32[]{:S(2)}, u32[]{:S(2)}) collective-permute-start(bf16[2,2,128,128]{3,2,1,0:T(8,128)(2,1)S(1)} %get-tuple-element.82), channel_id=1, source_target_pairs={{0,2},{1,3},{2,0},{3,1},{4,6},{5,7},{6,4},{7,5},{8,10},{9,11},{10,... | collective-permute-start | bytes 393224 | tf_op jit(solution)/shard_map/ppermute | solution.py:625
  69.1 2.1 %collective-permute-done.17.refs_6_ = bf16[2,2,128,128]{3,2,1,0:T(8,128)(2,1)S(1)} collective-permute-done((bf16[2,2,128,128]{3,2,1,0:T(8,128)(2,1)S(1)}, bf16[2,2,128,128]{3,2,1,0:T(8,128)(2,1)S(1)}, u32[]{:S(2)}, u32[]{:S(2)}) %collective-permute-start.17) | collective-permute-done | bytes 131104 | tf_op jit(solution)/shard_map/ppermute | solution.py:625
  71.2 2.9 %collective-permute-start.18 = (bf16[2,2,128,128]{3,2,1,0:T(8,128)(2,1)S(1)}, bf16[2,2,128,128]{3,2,1,0:T(8,128)(2,1)S(1)}, u32[]{:S(2)}, u32[]{:S(2)}) collective-permute-start(bf16[2,2,128,128]{3,2,1,0:T(8,128)(2,1)S(1)} %get-tuple-element.83), channel_id=1, source_target_pairs={{0,3},{1,2},{2,1},{3,0},{4,7},{5,6},{6,5},{7,4},{8,11},{9,10},{10,... | collective-permute-start | bytes 393224 | tf_op jit(solution)/shard_map/ppermute | solution.py:625
  74.5 8.9 %collective-permute-done.21.refs_0_ = bf16[4,2,128,128]{3,2,1,0:T(8,128)(2,1)S(1)} collective-permute-done((bf16[4,2,128,128]{3,2,1,0:T(8,128)(2,1)S(1)}, bf16[4,2,128,128]{3,2,1,0:T(8,128)(2,1)S(1)}, u32[]{:S(2)}, u32[]{:S(2)}) %collective-permute-start.21) | collective-permute-done | bytes 262176 | tf_op jit(solution)/shard_map/ppermute | solution.py:375
  83.4 3.2 %collective-permute-start.15 = (bf16[2,2,128,128]{3,2,1,0:T(8,128)(2,1)S(1)}, bf16[2,2,128,128]{3,2,1,0:T(8,128)(2,1)S(1)}, u32[]{:S(2)}, u32[]{:S(2)}) collective-permute-start(bf16[2,2,128,128]{3,2,1,0:T(8,128)(2,1)S(1)} %get-tuple-element.79), channel_id=1, source_target_pairs={{0,3},{1,2},{2,1},{3,0},{4,7},{5,6},{6,5},{7,4},{8,11},{9,10},{10,... | collective-permute-start | bytes 393224 | tf_op jit(solution)/shard_map/ppermute | solution.py:625
  87.7 1.9 %collective-permute-start.30 = (bf16[2,2,128,128]{3,2,1,0:T(8,128)(2,1)S(1)}, bf16[2,2,128,128]{3,2,1,0:T(8,128)(2,1)S(1)}, u32[]{:S(2)}, u32[]{:S(2)}) collective-permute-start(bf16[2,2,128,128]{3,2,1,0:T(8,128)(2,1)S(1)} %get-tuple-element.101), channel_id=1, source_target_pairs={{0,3},{1,2},{2,1},{3,0},{4,7},{5,6},{6,5},{7,4},{8,11},{9,10},{10,... | collective-permute-start | bytes 393224 | tf_op jit(solution)/shard_map/ppermute | solution.py:625
  90.8 2.0 %collective-permute-start.25 = (bf16[2,2,128,128]{3,2,1,0:T(8,128)(2,1)S(1)}, bf16[2,2,128,128]{3,2,1,0:T(8,128)(2,1)S(1)}, u32[]{:S(2)}, u32[]{:S(2)}) collective-permute-start(bf16[2,2,128,128]{3,2,1,0:T(8,128)(2,1)S(1)} %get-tuple-element.94), channel_id=1, source_target_pairs={{0,3},{1,2},{2,1},{3,0},{4,7},{5,6},{6,5},{7,4},{8,11},{9,10},{10,... | collective-permute-start | bytes 393224 | tf_op jit(solution)/shard_map/ppermute | solution.py:625
  92.8 1.8 %shard_map.99 = (bf16[128,16,128]{2,1,0:T(8,128)(2,1)}, bf16[128,16,128]{2,1,0:T(8,128)(2,1)}) custom-call(s32[2]{0:T(128)S(1)} %pad_add_fusion.place, s32[4,4]{1,0:T(4,128)S(1)} %copy-done.4, bf16[2,2,128,128]{3,2,1,0:T(8,128)(2,1)S(1)} %get-tuple-element.76.refs_0_, bf16[2,2,128,128]{3,2,1,0:T(8,128)(2,1)S(1)} %collective-permute-done.13.refs_1_, ...), custom_call_target="tpu_custom_call" | custom-call | bytes 2097152 | tf_op jit(solution)/shard_map/pallas_call | solution.py:148
  94.6 1.9 %collective-permute-done.30.refs_7_ = bf16[2,2,128,128]{3,2,1,0:T(8,128)(2,1)S(1)} collective-permute-done((bf16[2,2,128,128]{3,2,1,0:T(8,128)(2,1)S(1)}, bf16[2,2,128,128]{3,2,1,0:T(8,128)(2,1)S(1)}, u32[]{:S(2)}, u32[]{:S(2)}) %collective-permute-start.30) | collective-permute-done | bytes 131104 | tf_op jit(solution)/shard_map/ppermute | solution.py:625
  96.6 2.3 %collective-permute-done.24.refs_2_ = bf16[2,2,128,128]{3,2,1,0:T(8,128)(2,1)S(1)} collective-permute-done((bf16[2,2,128,128]{3,2,1,0:T(8,128)(2,1)S(1)}, bf16[2,2,128,128]{3,2,1,0:T(8,128)(2,1)S(1)}, u32[]{:S(2)}, u32[]{:S(2)}) %collective-permute-start.24) | collective-permute-done | bytes 131104 | tf_op jit(solution)/shard_map/ppermute | solution.py:625
  98.9 2.9 %collective-permute-done.25.refs_3_ = bf16[2,2,128,128]{3,2,1,0:T(8,128)(2,1)S(1)} collective-permute-done((bf16[2,2,128,128]{3,2,1,0:T(8,128)(2,1)S(1)}, bf16[2,2,128,128]{3,2,1,0:T(8,128)(2,1)S(1)}, u32[]{:S(2)}, u32[]{:S(2)}) %collective-permute-start.25) | collective-permute-done | bytes 131104 | tf_op jit(solution)/shard_map/ppermute | solution.py:625
  101.8 1.8 %shard_map.102 = (bf16[128,16,128]{2,1,0:T(8,128)(2,1)}, bf16[128,16,128]{2,1,0:T(8,128)(2,1)}) custom-call(s32[2]{0:T(128)S(1)} %pad_add_fusion.place, s32[4,4]{1,0:T(4,128)S(1)} %copy-done.4, bf16[2,2,128,128]{3,2,1,0:T(8,128)(2,1)S(1)} %get-tuple-element.91.refs_0_, bf16[2,2,128,128]{3,2,1,0:T(8,128)(2,1)S(1)} %collective-permute-done.23.refs_1_, ...), custom_call_target="tpu_custom_call" | custom-call | bytes 2097152 | tf_op jit(solution)/shard_map/pallas_call | solution.py:148
  (53 shorter events, 13.3 us)
Async XLA Ops:
  4.5 3.9 %collective-permute-start = (bf16[2,2,128,128]{3,2,1,0:T(8,128)(2,1)S(1)}, bf16[2,2,128,128]{3,2,1,0:T(8,128)(2,1)S(1)}, u32[]{:S(2)}, u32[]{:S(2)}) collective-permute-start(bf16[2,2,128,128]{3,2,1,0:T(8,128)(2,1)S(1)} %get-tuple-element.55), channel_id=1, source_target_pairs={{0,1},{1,0},{2,3},{3,2},{4,5},{5,4},{6,7},{7,6},{8,9},{9,8},{10,11... | collective-permute-start | bytes 393224 | tf_op jit(solution)/shard_map/ppermute | solution.py:625
  5.3 5.1 %collective-permute-start.1 = (bf16[2,2,128,128]{3,2,1,0:T(8,128)(2,1)S(1)}, bf16[2,2,128,128]{3,2,1,0:T(8,128)(2,1)S(1)}, u32[]{:S(2)}, u32[]{:S(2)}) collective-permute-start(bf16[2,2,128,128]{3,2,1,0:T(8,128)(2,1)S(1)} %get-tuple-element.56), channel_id=1, source_target_pairs={{0,2},{1,3},{2,0},{3,1},{4,6},{5,7},{6,4},{7,5},{8,10},{9,11},{10,... | collective-permute-start | bytes 393224 | tf_op jit(solution)/shard_map/ppermute | solution.py:625
  6.5 7.2 %collective-permute-start.2 = (bf16[2,2,128,128]{3,2,1,0:T(8,128)(2,1)S(1)}, bf16[2,2,128,128]{3,2,1,0:T(8,128)(2,1)S(1)}, u32[]{:S(2)}, u32[]{:S(2)}) collective-permute-start(bf16[2,2,128,128]{3,2,1,0:T(8,128)(2,1)S(1)} %get-tuple-element.57), channel_id=1, source_target_pairs={{0,3},{1,2},{2,1},{3,0},{4,7},{5,6},{6,5},{7,4},{8,11},{9,10},{10,... | collective-permute-start | bytes 393224 | tf_op jit(solution)/shard_map/ppermute | solution.py:625
  7.0 6.8 %collective-permute-start.6 = (bf16[2,2,128,128]{3,2,1,0:T(8,128)(2,1)S(1)}, bf16[2,2,128,128]{3,2,1,0:T(8,128)(2,1)S(1)}, u32[]{:S(2)}, u32[]{:S(2)}) collective-permute-start(bf16[2,2,128,128]{3,2,1,0:T(8,128)(2,1)S(1)} %get-tuple-element.69), channel_id=1, source_target_pairs={{0,1},{1,0},{2,3},{3,2},{4,5},{5,4},{6,7},{7,6},{8,9},{9,8},{10,11... | collective-permute-start | bytes 393224 | tf_op jit(solution)/shard_map/ppermute | solution.py:625
  7.1 8.8 %collective-permute-start.7 = (bf16[2,2,128,128]{3,2,1,0:T(8,128)(2,1)S(1)}, bf16[2,2,128,128]{3,2,1,0:T(8,128)(2,1)S(1)}, u32[]{:S(2)}, u32[]{:S(2)}) collective-permute-start(bf16[2,2,128,128]{3,2,1,0:T(8,128)(2,1)S(1)} %get-tuple-element.70), channel_id=1, source_target_pairs={{0,2},{1,3},{2,0},{3,1},{4,6},{5,7},{6,4},{7,5},{8,10},{9,11},{10,... | collective-permute-start | bytes 393224 | tf_op jit(solution)/shard_map/ppermute | solution.py:625
  8.4 10.5 %collective-permute-start.8 = (bf16[2,2,128,128]{3,2,1,0:T(8,128)(2,1)S(1)}, bf16[2,2,128,128]{3,2,1,0:T(8,128)(2,1)S(1)}, u32[]{:S(2)}, u32[]{:S(2)}) collective-permute-start(bf16[2,2,128,128]{3,2,1,0:T(8,128)(2,1)S(1)} %get-tuple-element.71), channel_id=1, source_target_pairs={{0,3},{1,2},{2,1},{3,0},{4,7},{5,6},{6,5},{7,4},{8,11},{9,10},{10,... | collective-permute-start | bytes 393224 | tf_op jit(solution)/shard_map/ppermute | solution.py:625
  19.6 19.1 %collective-permute-start.10 = (bf16[2,4,2,128,128]{4,3,2,1,0:T(8,128)(2,1)S(1)}, bf16[2,4,2,128,128]{4,3,2,1,0:T(8,128)(2,1)S(1)}, u32[]{:S(2)}, u32[]{:S(2)}) collective-permute-start(bf16[2,4,2,128,128]{4,3,2,1,0:T(8,128)(2,1)S(1)} %get-tuple-element.73), channel_id=1, source_target_pairs={{4,0},{5,1},{6,2},{7,3},{8,4},{9,5},{10,6},{11,7},{12,8},{13,9},{1... | collective-permute-start | bytes 1572872 | tf_op jit(solution)/shard_map/ppermute | solution.py:381
  21.7 17.0 %collective-permute-start.9 = (bf16[2,4,2,128,128]{4,3,2,1,0:T(8,128)(2,1)S(1)}, bf16[2,4,2,128,128]{4,3,2,1,0:T(8,128)(2,1)S(1)}, u32[]{:S(2)}, u32[]{:S(2)}) collective-permute-start(bf16[2,4,2,128,128]{4,3,2,1,0:T(8,128)(2,1)S(1)} %get-tuple-element.72), channel_id=1, source_target_pairs={{0,4},{1,5},{2,6},{3,7},{4,8},{5,9},{6,10},{7,11},{8,12},{9,13},{1... | collective-permute-start | bytes 1572872 | tf_op jit(solution)/shard_map/ppermute | solution.py:381
  24.1 14.6 %copy-start.5 = (s32[16]{0:T(128)S(1)}, s32[16]{0:T(128)}, u32[]{:S(2)}) copy-start(s32[16]{0:T(128)} %widths.3) | copy-start | bytes 196
  24.1 2.3 %collective-permute-start.3 = (bf16[4,2,128,128]{3,2,1,0:T(8,128)(2,1)S(1)}, bf16[4,2,128,128]{3,2,1,0:T(8,128)(2,1)S(1)}, u32[]{:S(2)}, u32[]{:S(2)}) collective-permute-start(bf16[4,2,128,128]{3,2,1,0:T(8,128)(2,1)S(1)} %get-tuple-element.65), channel_id=1, source_target_pairs={{0,1},{1,0},{2,3},{3,2},{4,5},{5,4},{6,7},{7,6},{8,9},{9,8},{10,11... | collective-permute-start | bytes 786440 | tf_op jit(solution)/shard_map/ppermute | solution.py:625
  24.7 7.9 %collective-permute-start.4 = (bf16[4,2,128,128]{3,2,1,0:T(8,128)(2,1)S(1)}, bf16[4,2,128,128]{3,2,1,0:T(8,128)(2,1)S(1)}, u32[]{:S(2)}, u32[]{:S(2)}) collective-permute-start(bf16[4,2,128,128]{3,2,1,0:T(8,128)(2,1)S(1)} %get-tuple-element.66), channel_id=1, source_target_pairs={{0,2},{1,3},{2,0},{3,1},{4,6},{5,7},{6,4},{7,5},{8,10},{9,11},{10,... | collective-permute-start | bytes 786440 | tf_op jit(solution)/shard_map/ppermute | solution.py:625
  25.9 12.7 %collective-permute-start.5 = (bf16[4,2,128,128]{3,2,1,0:T(8,128)(2,1)S(1)}, bf16[4,2,128,128]{3,2,1,0:T(8,128)(2,1)S(1)}, u32[]{:S(2)}, u32[]{:S(2)}) collective-permute-start(bf16[4,2,128,128]{3,2,1,0:T(8,128)(2,1)S(1)} %get-tuple-element.67), channel_id=1, source_target_pairs={{0,3},{1,2},{2,1},{3,0},{4,7},{5,6},{6,5},{7,4},{8,11},{9,10},{10,... | collective-permute-start | bytes 786440 | tf_op jit(solution)/shard_map/ppermute | solution.py:625
  26.4 26.7 %collective-permute-start.11 = (bf16[4,2,128,128]{3,2,1,0:T(8,128)(2,1)S(1)}, bf16[4,2,128,128]{3,2,1,0:T(8,128)(2,1)S(1)}, u32[]{:S(2)}, u32[]{:S(2)}) collective-permute-start(bf16[4,2,128,128]{3,2,1,0:T(8,128)(2,1)S(1)} %get-tuple-element.74), channel_id=1, source_target_pairs={{0,4},{1,5},{2,6},{3,7},{4,0},{5,1},{6,2},{7,3},{8,12},{9,13},{10,... | collective-permute-start | bytes 786440 | tf_op jit(solution)/shard_map/ppermute | solution.py:375
  32.6 20.5 %collective-permute-start.12 = (bf16[4,2,128,128]{3,2,1,0:T(8,128)(2,1)S(1)}, bf16[4,2,128,128]{3,2,1,0:T(8,128)(2,1)S(1)}, u32[]{:S(2)}, u32[]{:S(2)}) collective-permute-start(bf16[4,2,128,128]{3,2,1,0:T(8,128)(2,1)S(1)} %get-tuple-element.75), channel_id=1, source_target_pairs={{0,8},{1,9},{2,10},{3,11},{4,12},{5,13},{6,14},{7,15},{8,0},{9,1},... | collective-permute-start | bytes 786440 | tf_op jit(solution)/shard_map/ppermute | solution.py:375
  44.7 22.4 %collective-permute-start.26 = (bf16[2,2,2,128,128]{4,3,2,1,0:T(8,128)(2,1)S(1)}, bf16[2,2,2,128,128]{4,3,2,1,0:T(8,128)(2,1)S(1)}, u32[]{:S(2)}, u32[]{:S(2)}) collective-permute-start(bf16[2,2,2,128,128]{4,3,2,1,0:T(8,128)(2,1)S(1)} %get-tuple-element.96), channel_id=1, source_target_pairs={{4,0},{5,1},{6,2},{7,3},{8,4},{9,5},{10,6},{11,7},{12,8},{13,9},{1... | collective-permute-start | bytes 786440 | tf_op jit(solution)/shard_map/ppermute | solution.py:381
  49.0 18.1 %collective-permute-start.27 = (bf16[2,2,2,128,128]{4,3,2,1,0:T(8,128)(2,1)S(1)}, bf16[2,2,2,128,128]{4,3,2,1,0:T(8,128)(2,1)S(1)}, u32[]{:S(2)}, u32[]{:S(2)}) collective-permute-start(bf16[2,2,2,128,128]{4,3,2,1,0:T(8,128)(2,1)S(1)} %get-tuple-element.97), channel_id=1, source_target_pairs={{0,4},{1,5},{2,6},{3,7},{4,8},{5,9},{6,10},{7,11},{8,12},{9,13},{1... | collective-permute-start | bytes 786440 | tf_op jit(solution)/shard_map/ppermute | solution.py:381
  50.3 14.6 %collective-permute-start.16 = (bf16[2,2,128,128]{3,2,1,0:T(8,128)(2,1)S(1)}, bf16[2,2,128,128]{3,2,1,0:T(8,128)(2,1)S(1)}, u32[]{:S(2)}, u32[]{:S(2)}) collective-permute-start(bf16[2,2,128,128]{3,2,1,0:T(8,128)(2,1)S(1)} %get-tuple-element.81), channel_id=1, source_target_pairs={{0,1},{1,0},{2,3},{3,2},{4,5},{5,4},{6,7},{7,6},{8,9},{9,8},{10,11... | collective-permute-start | bytes 393224 | tf_op jit(solution)/shard_map/ppermute | solution.py:625
  59.3 14.9 %collective-permute-start.19 = (bf16[2,2,2,128,128]{4,3,2,1,0:T(8,128)(2,1)S(1)}, bf16[2,2,2,128,128]{4,3,2,1,0:T(8,128)(2,1)S(1)}, u32[]{:S(2)}, u32[]{:S(2)}) collective-permute-start(bf16[2,2,2,128,128]{4,3,2,1,0:T(8,128)(2,1)S(1)} %get-tuple-element.87), channel_id=1, source_target_pairs={{4,0},{5,1},{6,2},{7,3},{8,4},{9,5},{10,6},{11,7},{12,8},{13,9},{1... | collective-permute-start | bytes 786440 | tf_op jit(solution)/shard_map/ppermute | solution.py:381
  63.6 10.6 %collective-permute-start.20 = (bf16[2,2,2,128,128]{4,3,2,1,0:T(8,128)(2,1)S(1)}, bf16[2,2,2,128,128]{4,3,2,1,0:T(8,128)(2,1)S(1)}, u32[]{:S(2)}, u32[]{:S(2)}) collective-permute-start(bf16[2,2,2,128,128]{4,3,2,1,0:T(8,128)(2,1)S(1)} %get-tuple-element.88), channel_id=1, source_target_pairs={{0,4},{1,5},{2,6},{3,7},{4,8},{5,9},{6,10},{7,11},{8,12},{9,13},{1... | collective-permute-start | bytes 786440 | tf_op jit(solution)/shard_map/ppermute | solution.py:381
  64.9 18.5 %collective-permute-start.21 = (bf16[4,2,128,128]{3,2,1,0:T(8,128)(2,1)S(1)}, bf16[4,2,128,128]{3,2,1,0:T(8,128)(2,1)S(1)}, u32[]{:S(2)}, u32[]{:S(2)}) collective-permute-start(bf16[4,2,128,128]{3,2,1,0:T(8,128)(2,1)S(1)} %get-tuple-element.89), channel_id=1, source_target_pairs={{0,4},{1,5},{2,6},{3,7},{4,0},{5,1},{6,2},{7,3},{8,12},{9,13},{10,... | collective-permute-start | bytes 786440 | tf_op jit(solution)/shard_map/ppermute | solution.py:375
  67.1 19.5 %collective-permute-start.22 = (bf16[4,2,128,128]{3,2,1,0:T(8,128)(2,1)S(1)}, bf16[4,2,128,128]{3,2,1,0:T(8,128)(2,1)S(1)}, u32[]{:S(2)}, u32[]{:S(2)}) collective-permute-start(bf16[4,2,128,128]{3,2,1,0:T(8,128)(2,1)S(1)} %get-tuple-element.90), channel_id=1, source_target_pairs={{0,8},{1,9},{2,10},{3,11},{4,12},{5,13},{6,14},{7,15},{8,0},{9,1},... | collective-permute-start | bytes 786440 | tf_op jit(solution)/shard_map/ppermute | solution.py:375
  67.1 4.2 %collective-permute-start.17 = (bf16[2,2,128,128]{3,2,1,0:T(8,128)(2,1)S(1)}, bf16[2,2,128,128]{3,2,1,0:T(8,128)(2,1)S(1)}, u32[]{:S(2)}, u32[]{:S(2)}) collective-permute-start(bf16[2,2,128,128]{3,2,1,0:T(8,128)(2,1)S(1)} %get-tuple-element.82), channel_id=1, source_target_pairs={{0,2},{1,3},{2,0},{3,1},{4,6},{5,7},{6,4},{7,5},{8,10},{9,11},{10,... | collective-permute-start | bytes 393224 | tf_op jit(solution)/shard_map/ppermute | solution.py:625
  71.2 16.2 %collective-permute-start.18 = (bf16[2,2,128,128]{3,2,1,0:T(8,128)(2,1)S(1)}, bf16[2,2,128,128]{3,2,1,0:T(8,128)(2,1)S(1)}, u32[]{:S(2)}, u32[]{:S(2)}) collective-permute-start(bf16[2,2,128,128]{3,2,1,0:T(8,128)(2,1)S(1)} %get-tuple-element.83), channel_id=1, source_target_pairs={{0,3},{1,2},{2,1},{3,0},{4,7},{5,6},{6,5},{7,4},{8,11},{9,10},{10,... | collective-permute-start | bytes 393224 | tf_op jit(solution)/shard_map/ppermute | solution.py:625
  74.2 13.6 %collective-permute-start.13 = (bf16[2,2,128,128]{3,2,1,0:T(8,128)(2,1)S(1)}, bf16[2,2,128,128]{3,2,1,0:T(8,128)(2,1)S(1)}, u32[]{:S(2)}, u32[]{:S(2)}) collective-permute-start(bf16[2,2,128,128]{3,2,1,0:T(8,128)(2,1)S(1)} %get-tuple-element.77), channel_id=1, source_target_pairs={{0,1},{1,0},{2,3},{3,2},{4,5},{5,4},{6,7},{7,6},{8,9},{9,8},{10,11... | collective-permute-start | bytes 393224 | tf_op jit(solution)/shard_map/ppermute | solution.py:625
  74.2 15.5 %collective-permute-start.14 = (bf16[2,2,128,128]{3,2,1,0:T(8,128)(2,1)S(1)}, bf16[2,2,128,128]{3,2,1,0:T(8,128)(2,1)S(1)}, u32[]{:S(2)}, u32[]{:S(2)}) collective-permute-start(bf16[2,2,128,128]{3,2,1,0:T(8,128)(2,1)S(1)} %get-tuple-element.78), channel_id=1, source_target_pairs={{0,2},{1,3},{2,0},{3,1},{4,6},{5,7},{6,4},{7,5},{8,10},{9,11},{10,... | collective-permute-start | bytes 393224 | tf_op jit(solution)/shard_map/ppermute | solution.py:625
  83.4 7.4 %collective-permute-start.15 = (bf16[2,2,128,128]{3,2,1,0:T(8,128)(2,1)S(1)}, bf16[2,2,128,128]{3,2,1,0:T(8,128)(2,1)S(1)}, u32[]{:S(2)}, u32[]{:S(2)}) collective-permute-start(bf16[2,2,128,128]{3,2,1,0:T(8,128)(2,1)S(1)} %get-tuple-element.79), channel_id=1, source_target_pairs={{0,3},{1,2},{2,1},{3,0},{4,7},{5,6},{6,5},{7,4},{8,11},{9,10},{10,... | collective-permute-start | bytes 393224 | tf_op jit(solution)/shard_map/ppermute | solution.py:625
  86.6 4.2 %collective-permute-start.28 = (bf16[2,2,128,128]{3,2,1,0:T(8,128)(2,1)S(1)}, bf16[2,2,128,128]{3,2,1,0:T(8,128)(2,1)S(1)}, u32[]{:S(2)}, u32[]{:S(2)}) collective-permute-start(bf16[2,2,128,128]{3,2,1,0:T(8,128)(2,1)S(1)} %get-tuple-element.99), channel_id=1, source_target_pairs={{0,1},{1,0},{2,3},{3,2},{4,5},{5,4},{6,7},{7,6},{8,9},{9,8},{10,11... | collective-permute-start | bytes 393224 | tf_op jit(solution)/shard_map/ppermute | solution.py:625
  87.4 7.2 %collective-permute-start.29 = (bf16[2,2,128,128]{3,2,1,0:T(8,128)(2,1)S(1)}, bf16[2,2,128,128]{3,2,1,0:T(8,128)(2,1)S(1)}, u32[]{:S(2)}, u32[]{:S(2)}) collective-permute-start(bf16[2,2,128,128]{3,2,1,0:T(8,128)(2,1)S(1)} %get-tuple-element.100), channel_id=1, source_target_pairs={{0,2},{1,3},{2,0},{3,1},{4,6},{5,7},{6,4},{7,5},{8,10},{9,11},{10,... | collective-permute-start | bytes 393224 | tf_op jit(solution)/shard_map/ppermute | solution.py:625
  87.7 8.8 %collective-permute-start.30 = (bf16[2,2,128,128]{3,2,1,0:T(8,128)(2,1)S(1)}, bf16[2,2,128,128]{3,2,1,0:T(8,128)(2,1)S(1)}, u32[]{:S(2)}, u32[]{:S(2)}) collective-permute-start(bf16[2,2,128,128]{3,2,1,0:T(8,128)(2,1)S(1)} %get-tuple-element.101), channel_id=1, source_target_pairs={{0,3},{1,2},{2,1},{3,0},{4,7},{5,6},{6,5},{7,4},{8,11},{9,10},{10,... | collective-permute-start | bytes 393224 | tf_op jit(solution)/shard_map/ppermute | solution.py:625
  89.6 6.9 %collective-permute-start.23 = (bf16[2,2,128,128]{3,2,1,0:T(8,128)(2,1)S(1)}, bf16[2,2,128,128]{3,2,1,0:T(8,128)(2,1)S(1)}, u32[]{:S(2)}, u32[]{:S(2)}) collective-permute-start(bf16[2,2,128,128]{3,2,1,0:T(8,128)(2,1)S(1)} %get-tuple-element.92), channel_id=1, source_target_pairs={{0,1},{1,0},{2,3},{3,2},{4,5},{5,4},{6,7},{7,6},{8,9},{9,8},{10,11... | collective-permute-start | bytes 393224 | tf_op jit(solution)/shard_map/ppermute | solution.py:625
  90.8 8.1 %collective-permute-start.24 = (bf16[2,2,128,128]{3,2,1,0:T(8,128)(2,1)S(1)}, bf16[2,2,128,128]{3,2,1,0:T(8,128)(2,1)S(1)}, u32[]{:S(2)}, u32[]{:S(2)}) collective-permute-start(bf16[2,2,128,128]{3,2,1,0:T(8,128)(2,1)S(1)} %get-tuple-element.93), channel_id=1, source_target_pairs={{0,2},{1,3},{2,0},{3,1},{4,6},{5,7},{6,4},{7,5},{8,10},{9,11},{10,... | collective-permute-start | bytes 393224 | tf_op jit(solution)/shard_map/ppermute | solution.py:625
  90.8 11.0 %collective-permute-start.25 = (bf16[2,2,128,128]{3,2,1,0:T(8,128)(2,1)S(1)}, bf16[2,2,128,128]{3,2,1,0:T(8,128)(2,1)S(1)}, u32[]{:S(2)}, u32[]{:S(2)}) collective-permute-start(bf16[2,2,128,128]{3,2,1,0:T(8,128)(2,1)S(1)} %get-tuple-element.94), channel_id=1, source_target_pairs={{0,3},{1,2},{2,1},{3,0},{4,7},{5,6},{6,5},{7,4},{8,11},{9,10},{10,... | collective-permute-start | bytes 393224 | tf_op jit(solution)/shard_map/ppermute | solution.py:625
  (5 other events, 10.9 us)

commit v5 on v4

--- a/solution.py
+++ b/solution.py
@@ -122,7 +122,6 @@
         ],
         out_shape=[jax.ShapeDtypeStruct(shape, jnp.bfloat16) for shape in shapes],
         scratch_shapes=[pltpu.VMEM((count, heads, chunk, width), jnp.bfloat16)],
-        compiler_params=LIMIT,
         cost_estimate=moved_cost(arrays),
     )(place, sections, *arrays)
     return [outs[i * PLANE : (i + 1) * PLANE] for i in range(len(groups))]
@@ -161,78 +160,104 @@
     )(place, sections, *flat)
 
 
-def far_kernel(*refs):
-    pieces, outs = refs[:PLANE], refs[PLANE:]
-    for k, out in enumerate(outs):
-        for m, piece in enumerate(pieces):
-            out[m] = piece[k]
-
-
-def far_parts(pieces):
+def facing(place):
+    return place[0] // HALO == 1 - place[1] % 2
+
+
+def collect_far_kernel(place, *refs):
+    pieces, (with_next, with_other) = refs[:PLANE], refs[PLANE:]
+    group = pieces[0].shape[0]
+    for m in range(PLANE):
+        with_next[m] = pieces[m][0]
+        with_other[m] = pieces[m][1]
+
+    def fill(base):
+        for m in range(HALO):
+            for k in range(group):
+                with_next[PLANE + m * group + k] = pieces[base + m][k]
+
+    @pl.when(facing(place))
+    def _():
+        fill(0)
+
+    @pl.when(jnp.logical_not(facing(place)))
+    def _():
+        fill(HALO)
+
+
+def collect_far(place, pieces):
     group, *rest = pieces[0].shape
     return pl.pallas_call(
-        far_kernel,
-        in_specs=[VMEM] * PLANE,
-        out_specs=[VMEM] * group,
-        out_shape=[jax.ShapeDtypeStruct((PLANE, *rest), jnp.bfloat16)] * group,
+        collect_far_kernel,
+        in_specs=[SMEM] + [VMEM] * PLANE,
+        out_specs=[VMEM] * 2,
+        out_shape=[
+            jax.ShapeDtypeStruct((PLANE + HALO * group, *rest), jnp.bfloat16),
+            jax.ShapeDtypeStruct((PLANE, *rest), jnp.bfloat16),
+        ],
         compiler_params=LIMIT,
         cost_estimate=moved_cost(pieces),
-    )(*pieces)
-
-
-def halo_kernel(place, *refs, groups):
-    pieces, (up, down) = refs[:-2], refs[-2:]
-    upper_chip = place[0] // HALO
-
-    def fill(high, low):
+    )(place, *pieces)
+
+
+def collect_near_kernel(place, *refs):
+    far, near, (with_next, with_last) = refs[:PLANE], refs[PLANE:-2], refs[-2:]
+    group = near[0].shape[0]
+
+    def fill(base, other):
         for m in range(HALO):
-            slot = 0
-            for number in range(groups):
-                for k in range(pieces[number * PLANE].shape[0]):
-                    up[m, slot] = pieces[number * PLANE + high + m][k]
-                    down[m, slot] = pieces[number * PLANE + low + m][k]
-                    slot += 1
-
-    @pl.when(upper_chip == 1)
+            for k in range(group):
+                with_next[m * group + k] = near[base + m][k]
+                with_last[m * group + k] = far[other + m][k]
+                with_last[(HALO + m) * group + k] = near[other + m][k]
+
+    @pl.when(facing(place))
     def _():
         fill(0, HALO)
 
-    @pl.when(upper_chip == 0)
+    @pl.when(jnp.logical_not(facing(place)))
     def _():
         fill(HALO, 0)
 
 
-def halo_parts(place, pieces):
-    flat = [piece for group in pieces for piece in group]
-    slots = sum(group[0].shape[0] for group in pieces)
-    shape = jax.ShapeDtypeStruct((HALO, slots, *flat[0].shape[1:]), jnp.bfloat16)
+def collect_near(place, far, near):
+    group, *rest = near[0].shape
     return pl.pallas_call(
-        functools.partial(halo_kernel, groups=len(pieces)),
-        in_specs=[SMEM] + [VMEM] * len(flat),
+        collect_near_kernel,
+        in_specs=[SMEM] + [VMEM] * (2 * PLANE),
         out_specs=[VMEM] * 2,
-        out_shape=[shape] * 2,
+        out_shape=[
+            jax.ShapeDtypeStruct((HALO * group, *rest), jnp.bfloat16),
+            jax.ShapeDtypeStruct((2 * HALO * group, *rest), jnp.bfloat16),
+        ],
         compiler_params=LIMIT,
-        cost_estimate=moved_cost(flat),
-    )(place, *flat)
-
-
-def attend_kernel(place, widths, sections, *refs, first, remote, blocks):
+        cost_estimate=moved_cost([*far, *near]),
+    )(place, *far, *near)
+
+
+def attend_kernel(place, widths, sections, *refs, first, remote, base, blocks, aliased):
     pairs, graded = refs[:PLANE], refs[PLANE : 2 * PLANE]
-    below, above = refs[2 * PLANE : 2 * PLANE + 2]
-    rest = refs[2 * PLANE + 2 :]
-    far_in, rest = rest[:remote], rest[remote:]
+    (with_next, with_last), rest = refs[2 * PLANE : 2 * PLANE + 2], refs[2 * PLANE + 2 :]
+    if remote:
+        with_other, rest = rest[0], rest[1:]
+    rest = rest[aliased:]
     outs, rest = rest[:PLANE], rest[PLANE:]
-    (part, to_below, to_above), rest = rest[:3], rest[3:]
-    far_out, rest = rest[:remote], rest[remote:]
+    (part, to_next, to_last), rest = rest[:3], rest[3:]
+    if remote:
+        to_other, rest = rest[0], rest[1:]
     keys, values, far_keys, far_values, queries, grads, attended, dq = rest[:8]
     accs, far_accs = rest[8:10], rest[10:12]
     k = pl.program_id(0)
+    group = pl.num_programs(0)
     section = first + k
     me = place[0]
     width = widths[sections[section, me]]
     bit = jnp.left_shift(jnp.int32(1), section)
     far_bias = jnp.where(bit >= width, 0.0, blocked_score).astype(jnp.float32)
     scales = (1.0 / math.sqrt(keys.shape[-1]), 1.0)
+    lead = PLANE if remote else 0
+    next_at = jnp.where(place[1] % 2 == 0, HALO + PLANE, 0)
+    last_at = HALO + PLANE - next_at
     for m in range(PLANE):
         b = me ^ m
         keys[rows_of(HALO + b)] = pairs[m][0, 0]
@@ -241,18 +266,19 @@
         grads[rows_of(b)] = graded[m][0, 1]
     for m in range(HALO):
         b = (me % HALO) ^ m
-        keys[rows_of(b)] = below[m, 0, 0]
-        values[rows_of(b)] = below[m, 0, 1]
-        keys[rows_of(HALO + PLANE + b)] = above[m, 0, 0]
-        values[rows_of(HALO + PLANE + b)] = above[m, 0, 1]
+        slot = m * group + k
+        keys[rows_of(next_at + b)] = with_next[lead + slot, 0]
+        values[rows_of(next_at + b)] = with_next[lead + slot, 1]
+        keys[rows_of(last_at + b)] = with_last[base + slot, 0]
+        values[rows_of(last_at + b)] = with_last[base + slot, 1]
     if remote:
-        for n in range(remote):
+        for n, source in enumerate((with_next, with_other)):
 
             @pl.when(k == n)
-            def _(n=n):
+            def _(source=source):
                 for m in range(PLANE):
-                    far_keys[rows_of(me ^ m)] = far_in[n][m, 0]
-                    far_values[rows_of(me ^ m)] = far_in[n][m, 1]
+                    far_keys[rows_of(me ^ m)] = source[m, 0]
+                    far_values[rows_of(me ^ m)] = source[m, 1]
     else:
         for b in range(PLANE):
             far_keys[rows_of(b)] = keys[rows_of(HALO + (b ^ bit))]
@@ -281,94 +307,106 @@
             for r in range(2):
                 acc[:, one[r]] = far[r]
     for i, (acc, far_acc) in enumerate(zip(accs, far_accs)):
-        if not remote:
+        if remote:
+            for n, target in enumerate((to_next, to_other)):
+
+                @pl.when(k == n)
+                def _(target=target, i=i, far_acc=far_acc):
+                    for m in range(PLANE):
+                        target[m, i] = (far_acc[:, rows_of(me ^ m)] * scales[i]).astype(
+                            jnp.bfloat16
+                        )
+        else:
             for b in range(PLANE):
                 acc[:, rows_of(HALO + (b ^ bit))] += far_acc[:, b * BLK : (b + 1) * BLK]
-        for n in range(remote):
-
-            @pl.when(k == n)
-            def _(n=n, i=i, far_acc=far_acc):
-                for m in range(PLANE):
-                    far_out[n][m, i] = (far_acc[:, rows_of(me ^ m)] * scales[i]).astype(
-                        jnp.bfloat16
-                    )
-
         for m in range(PLANE):
             part[0, m, i] = acc[:, rows_of(HALO + (me ^ m))] * scales[i]
         for m in range(HALO):
             b = (me % HALO) ^ m
-            to_below[m, 0, i] = (acc[:, rows_of(b)] * scales[i]).astype(jnp.bfloat16)
-            to_above[m, 0, i] = (acc[:, rows_of(HALO + PLANE + b)] * scales[i]).astype(
+            slot = m * group + k
+            to_next[lead + slot, i] = (acc[:, rows_of(next_at + b)] * scales[i]).astype(
                 jnp.bfloat16
             )
+            to_last[slot, i] = (acc[:, rows_of(last_at + b)] * scales[i]).astype(jnp.bfloat16)
     for m in range(PLANE):
         outs[m][0, 0] = attended[rows_of(me ^ m)]
         outs[m][0, 1] = dq[rows_of(me ^ m)]
 
 
-def attend(place, widths, sections, pairs, graded, below, above, far, first, slot, blocks):
+def attend(place, widths, sections, pairs, graded, halos, first, slot, blocks, rows=()):
     group, count, _, width = pairs[0].shape
     tile = (BLK, width)
-    remote = len(far)
+    remote = len(halos) > 2
     piece = pl.BlockSpec((1, count, *tile), lambda k: (k, 0, 0, 0))
     graded_piece = pl.BlockSpec((1, count, *tile), lambda k: (slot + k, 0, 0, 0))
-    halo_in = pl.BlockSpec((HALO, 1, count, *tile), lambda k: (0, slot + k, 0, 0, 0))
-    halo_out = pl.BlockSpec((HALO, 1, count, *tile), lambda k: (0, k, 0, 0, 0))
-    far_spec = whole((PLANE, count, *tile))
     bf16 = jnp.bfloat16
+    owed = [(HALO * group + (PLANE if remote else 0), count, *tile), (HALO * group, count, *tile)]
+    if remote:
+        owed.append((PLANE, count, *tile))
     outs = pl.pallas_call(
-        functools.partial(attend_kernel, first=first, remote=remote, blocks=blocks),
+        functools.partial(
+            attend_kernel,
+            first=first,
+            remote=remote,
+            base=HALO * slot,
+            blocks=blocks,
+            aliased=len(rows),
+        ),
         grid=(group,),
         in_specs=[SMEM] * 3
         + [piece] * PLANE
         + [graded_piece] * PLANE
-        + [halo_in] * 2
-        + [far_spec] * remote,
-        out_specs=[piece] * PLANE
+        + [whole(halo.shape) for halo in halos]
+        + [pl.BlockSpec(memory_space=pl.ANY)] * len(rows),
+        out_specs=[graded_piece] * PLANE
         + [pl.BlockSpec((1, PLANE, count, *tile), lambda k: (k, 0, 0, 0, 0))]
-        + [halo_out] * 2
-        + [far_spec] * remote,
-        out_shape=[jax.ShapeDtypeStruct((group, count, *tile), bf16)] * PLANE
+        + [whole(shape) for shape in owed],
+        out_shape=[jax.ShapeDtypeStruct(graded[0].shape, bf16)] * PLANE
         + [jax.ShapeDtypeStruct((group, PLANE, count, *tile), jnp.float32)]
-        + [jax.ShapeDtypeStruct((HALO, group, count, *tile), bf16)] * 2
-        + [jax.ShapeDtypeStruct((PLANE, count, *tile), bf16)] * remote,
+        + [jax.ShapeDtypeStruct(shape, bf16) for shape in owed],
         scratch_shapes=[pltpu.VMEM((PADDED * BLK, width), bf16)] * 2
         + [pltpu.VMEM((PLANE * BLK, width), bf16)] * 6
         + [pltpu.VMEM((width, PADDED * BLK), jnp.float32)] * 2
         + [pltpu.VMEM((width, PLANE * BLK), jnp.float32)] * 2,
+        input_output_aliases={3 + 2 * PLANE + len(halos) + m: m for m in range(len(rows))},
         compiler_params=LIMIT,
         cost_estimate=pl.CostEstimate(
             flops=group * PLANE * 12 * BLK * LINKED * width,
             transcendentals=group * PLANE * BLK * LINKED,
             bytes_accessed=40 * group * PLANE * BLK * width,
         ),
-    )(place, widths, sections, *pairs, *graded, below, above, *far)
-    return outs[:PLANE], outs[PLANE], outs[PLANE + 1], outs[PLANE + 2], outs[PLANE + 3 :]
-
-
-def combine_kernel(place, part, above, below, *refs, remote):
-    far, outs = refs[:remote], refs[remote:]
+    )(place, widths, sections, *pairs, *graded, *halos, *rows)
+    return outs[:PLANE], outs[PLANE], outs[PLANE + 1 :]
+
+
+def combine_kernel(place, part, with_next, with_last, *refs, remote):
+    outs = refs[remote:]
+    group = part.shape[0]
+    lead = PLANE if remote else 0
     for m in range(PLANE):
-        upper = (m // HALO) ^ (place[0] // HALO)
-        for k in range(part.shape[0]):
+        own_chip = m < HALO
+        next_side = facing(place) if own_chip else jnp.logical_not(facing(place))
+        for k in range(group):
+            slot = (m % HALO) * group + k
             for i in range(part.shape[2]):
-                owed = jnp.where(upper == 1, above[m % HALO, k, i], below[m % HALO, k, i])
+                owed = jnp.where(next_side, with_next[lead + slot, i], with_last[slot, i])
                 total = part[k, m, i] + owed.astype(jnp.float32)
                 if remote:
-                    total += far[k][m, i].astype(jnp.float32)
+                    far = (with_next, refs[0])[k]
+                    total += far[m, i].astype(jnp.float32)
                 outs[m][k, i] = jnp.transpose(total.astype(jnp.bfloat16))
 
 
-def combine(place, part, above, below, far):
+def combine(place, part, owed):
     group, _, *rest = part.shape
     return pl.pallas_call(
-        functools.partial(combine_kernel, remote=len(far)),
-        in_specs=[SMEM] + [VMEM] * (3 + len(far)),
+        functools.partial(combine_kernel, remote=len(owed) - 2),
+        in_specs=[SMEM] + [VMEM] * (1 + len(owed)),
         out_specs=[VMEM] * PLANE,
         out_shape=[jax.ShapeDtypeStruct((group, *rest), jnp.bfloat16)] * PLANE,
         compiler_params=LIMIT,
-        cost_estimate=moved_cost([part, above, below, *far]),
-    )(place, part, above, below, *far)
+        cost_estimate=moved_cost([part, *owed]),
+    )(place, part, *owed)
 
 
 def partner(value, axis, apart):
@@ -627,8 +665,22 @@
     ]
 
 
-def between_planes(value, by):
-    return passed_along(value, "seq", by * PLANE)
+def with_next_plane(value):
+    return partner(value, "seq", PLANE.bit_length() - 1)
+
+
+def with_other_plane(value):
+    return partner(value, "seq", PLANE.bit_length())
+
+
+def with_last_plane(value):
+    peers = lax.axis_size("seq")
+    pairs = []
+    for i in range(peers):
+        other = i + PLANE if i // PLANE % 2 else i - PLANE
+        if 0 <= other < peers:
+            pairs.append((i, other))
+    return lax.ppermute(value, "seq", pairs)
 
 
 def sharded_by_plane(query_rows, key_rows, value_rows, out_grad, widths, sections):
@@ -640,30 +692,35 @@
     groups = [tuple(range(local, total)), tuple(range(local))]
     order = tuple(s for group in groups for s in group)
     sent_far, sent_near = pack(place, sections, [key_rows, value_rows], groups)
-    pairs_far, pairs_near = in_plane(sent_far), in_plane(sent_near)
-    far_sent = far_parts(pairs_far)
+    pairs_far = in_plane(sent_far)
+    next_sent, other_sent = collect_far(place, pairs_far)
+    (next_sent, other_sent), sent_near = lax.optimization_barrier(
+        ((next_sent, other_sent), sent_near)
+    )
+    other_far = with_other_plane(other_sent)
+    next_far = with_next_plane(next_sent)
+    pairs_near = in_plane(sent_near)
+    next_sent, last_sent = collect_near(place, pairs_far, pairs_near)
     (sent,) = pack(place, sections, [query_rows, out_grad], [order])
-    far_sent, sent = lax.optimization_barrier((far_sent, sent))
-    far = [partner(value, "seq", local + n) for n, value in enumerate(far_sent)]
-    up, down = halo_parts(place, [pairs_far, pairs_near])
-    below, above = between_planes(up, 1), between_planes(down, -1)
+    (next_sent, last_sent), sent = lax.optimization_barrier(((next_sent, last_sent), sent))
+    last = with_last_plane(last_sent)
+    next_near = with_next_plane(next_sent)
     graded = in_plane(sent)
-    shared = (place, widths, sections)
-    outs_far, part_far, low_far, high_far, far_owed = attend(
-        *shared, pairs_far, graded, below, above, far, local, 0, blocks
-    )
-    far_back = [partner(value, "seq", local + n) for n, value in enumerate(far_owed)]
-    above_far, below_far = between_planes(low_far, -1), between_planes(high_far, 1)
-    outs_near, part_near, low_near, high_near, _ = attend(
-        *shared, pairs_near, graded, below, above, [], 0, total - local, blocks
-    )
-    above_near, below_near = between_planes(low_near, -1), between_planes(high_near, 1)
-    rows = [in_plane(outs_far), in_plane(outs_near)]
+    rows, part_far, owed = attend(
+        place, widths, sections, pairs_far, graded, [next_far, last, other_far], local, 0, blocks
+    )
+    other_back = with_other_plane(owed[2])
+    owed_far = [with_next_plane(owed[0]), with_last_plane(owed[1]), other_back]
+    rows, part_near, owed = attend(
+        place, widths, sections, pairs_near, graded, [next_near, last], 0, total - local, blocks, rows
+    )
+    owed_near = [with_next_plane(owed[0]), with_last_plane(owed[1])]
+    rows = in_plane(rows)
     columns = [
-        in_plane(combine(place, part_far, above_far, below_far, far_back)),
-        in_plane(combine(place, part_near, above_near, below_near, [])),
+        in_plane(combine(place, part_far, owed_far)),
+        in_plane(combine(place, part_near, owed_near)),
     ]
-    attended, query_grad = unpack(place, sections, rows, groups)
+    attended, query_grad = unpack(place, sections, [rows], [order])
     key_grad, value_grad = unpack(place, sections, columns, groups)
     return attended, query_grad, key_grad, value_grad
 

time: 104 us -> 104 us (level)
  the two profiles are of different devices: /device:TPU:27 before, /device:TPU:1 now
where the time goes in v5:
time: 104 us; the launch traced here: 103 us
  waiting for transfers between devices  44.4 us (43%)
  starting transfers between devices  33.1 us (32%)
  Pallas kernels  22.9 us (22%)
  local copies, waits for them, and re-layouts  1.25 us (1%)
    ppermute x6, waiting for transfers between devices, partner(): lax.ppermute(value, axis, [(i, i ^ 1 << apart) for i in range(lax.axis_si...  23.1 us
    ppermute x18, waiting for transfers between devices, in_plane(): lax.ppermute(pieces[m], 'seq', [(i, i ^ m) for i in range(peers)])  21.3 us
    ppermute x18, starting transfers between devices, in_plane(): lax.ppermute(pieces[m], 'seq', [(i, i ^ m) for i in range(peers)])  17 us
    ppermute x6, starting transfers between devices, partner(): lax.ppermute(value, axis, [(i, i ^ 1 << apart) for i in range(lax.axis_si...  14.1 us
    pallas_call x2, Pallas kernels, attend(): pl.pallas_call(functools.partial(attend_kernel, first=first, remote=remot...  12 us
    pallas_call x2, Pallas kernels, pack(): pl.pallas_call(functools.partial(pack_kernel, groups=groups, count=count)...  4.52 us
    pallas_call x2, Pallas kernels, unpack(): pl.pallas_call(functools.partial(unpack_kernel, groups=groups, count=coun...  3.62 us
  transfers between devices with their start and end apart: 27, of which 10 were waited for; matrix products, arithmetic and copies ran while one was open for 0% of the time, Pallas kernels for 18%

profile of v5, /device:TPU:1, one launch (start us, length us, event | category | flops | bytes accessed | tf_op | source)
XLA Modules:
  0.0 103.1 jit_solution(9762601118588083360)
XLA Ops:
  1.2 2.3 %shard_map.93 = (bf16[2,2,128,128]{3,2,1,0:T(8,128)(2,1)}, bf16[2,2,128,128]{3,2,1,0:T(8,128)(2,1)}, bf16[2,2,128,128]{3,2,1,0:T(8,128)(2,1)}, bf16[2,2,128,128]...) custom-call(s32[2]{0:T(128)} %pad_add_fusion.place, ...), custom_call_target="tpu_custom_call" | custom-call | bytes 2097152 | tf_op jit(solution)/shard_map/pallas_call | solution.py:115
  3.6 2.7 %collective-permute-start.1 = (bf16[2,2,128,128]{3,2,1,0:T(8,128)(2,1)}, bf16[2,2,128,128]{3,2,1,0:T(8,128)(2,1)S(1)}, u32[]{:S(2)}, u32[]{:S(2)}) collective-permute-start(bf16[2,2,128,128]{3,2,1,0:T(8,128)(2,1)} %get-tuple-element.61), channel_id=1, source_target_pairs={{0,2},{1,3},{2,0},{3,1},{4,6},{5,7},{6,4},{7,5},{8,10},{9,11},{10,... | collective-permute-start | bytes 393224 | tf_op jit(solution)/shard_map/ppermute | solution.py:663
  6.4 3.9 %collective-permute-done.1.refs_2_ = bf16[2,2,128,128]{3,2,1,0:T(8,128)(2,1)S(1)} collective-permute-done((bf16[2,2,128,128]{3,2,1,0:T(8,128)(2,1)}, bf16[2,2,128,128]{3,2,1,0:T(8,128)(2,1)S(1)}, u32[]{:S(2)}, u32[]{:S(2)}) %collective-permute-start.1) | collective-permute-done | bytes 131104 | tf_op jit(solution)/shard_map/ppermute | solution.py:663
  10.3 2.8 %collective-permute-done.2.refs_3_ = bf16[2,2,128,128]{3,2,1,0:T(8,128)(2,1)S(1)} collective-permute-done((bf16[2,2,128,128]{3,2,1,0:T(8,128)(2,1)}, bf16[2,2,128,128]{3,2,1,0:T(8,128)(2,1)S(1)}, u32[]{:S(2)}, u32[]{:S(2)}) %collective-permute-start.2) | collective-permute-done | bytes 131104 | tf_op jit(solution)/shard_map/ppermute | solution.py:663
  13.1 0.9 copy-done
  15.4 1.3 %collective-permute-start.4 = (bf16[2,2,128,128]{3,2,1,0:T(8,128)(2,1)S(1)}, bf16[2,2,128,128]{3,2,1,0:T(8,128)(2,1)S(1)}, u32[]{:S(2)}, u32[]{:S(2)}) collective-permute-start(bf16[2,2,128,128]{3,2,1,0:T(8,128)(2,1)S(1)} %copy-done.12), channel_id=1, source_target_pairs={{0,2},{1,3},{2,0},{3,1},{4,6},{5,7},{6,4},{7,5},{8,10},{9,11},{10,... | collective-permute-start | bytes 393224 | tf_op jit(solution)/shard_map/ppermute | solution.py:663
  17.1 2.2 %shard_map.96 = (bf16[4,2,128,128]{3,2,1,0:T(8,128)(2,1)}, bf16[4,2,128,128]{3,2,1,0:T(8,128)(2,1)}, bf16[4,2,128,128]{3,2,1,0:T(8,128)(2,1)}, bf16[4,2,128,128]{3,2,1,0:T(8,128)(2,1)}) custom-call(s32[2]{0:T(128)} %pad_add_fusion.place, s32[4,4]{1,0:T(4,128)} %sections.11, bf16[128,16,128]{2,1,0:T(8,128)(2,1)} %refs_0_.3, bf16[128,16,128]{2,1,0:T(8,128)(2,1)} %refs_1_.3), custom_call_target="tpu_custom_call" | custom-call | bytes 2097152 | tf_op jit(solution)/shard_map/pallas_call | solution.py:115
  19.4 2.5 %collective-permute-start.12 = (bf16[4,2,128,128]{3,2,1,0:T(8,128)(2,1)S(1)}, bf16[4,2,128,128]{3,2,1,0:T(8,128)(2,1)S(1)}, u32[]{:S(2)}, u32[]{:S(2)}) collective-permute-start(bf16[4,2,128,128]{3,2,1,0:T(8,128)(2,1)S(1)} %get-tuple-element.86), channel_id=1, source_target_pairs={{0,8},{1,9},{2,10},{3,11},{4,12},{5,13},{6,14},{7,15},{8,0},{9,1},... | collective-permute-start | bytes 786440 | tf_op jit(solution)/shard_map/ppermute | solution.py:413
  22.0 1.3 %collective-permute-start.11 = (bf16[8,2,128,128]{3,2,1,0:T(8,128)(2,1)S(1)}, bf16[8,2,128,128]{3,2,1,0:T(8,128)(2,1)S(1)}, u32[]{:S(2)}, u32[]{:S(2)}) collective-permute-start(bf16[8,2,128,128]{3,2,1,0:T(8,128)(2,1)S(1)} %get-tuple-element.85), channel_id=1, source_target_pairs={{0,4},{1,5},{2,6},{3,7},{4,0},{5,1},{6,2},{7,3},{8,12},{9,13},{10,... | collective-permute-start | bytes 1572872 | tf_op jit(solution)/shard_map/ppermute | solution.py:413
  24.4 0.7 collective-permute-start.10
  25.3 1.3 %collective-permute-start.7 = (bf16[4,2,128,128]{3,2,1,0:T(8,128)(2,1)S(1)}, bf16[4,2,128,128]{3,2,1,0:T(8,128)(2,1)S(1)}, u32[]{:S(2)}, u32[]{:S(2)}) collective-permute-start(bf16[4,2,128,128]{3,2,1,0:T(8,128)(2,1)S(1)} %copy-done.9), channel_id=1, source_target_pairs={{0,2},{1,3},{2,0},{3,1},{4,6},{5,7},{6,4},{7,5},{8,10},{9,11},{10,... | collective-permute-start | bytes 786440 | tf_op jit(solution)/shard_map/ppermute | solution.py:663
  26.5 7.6 %collective-permute-done.12.refs_10_ = bf16[4,2,128,128]{3,2,1,0:T(8,128)(2,1)S(1)} collective-permute-done((bf16[4,2,128,128]{3,2,1,0:T(8,128)(2,1)S(1)}, bf16[4,2,128,128]{3,2,1,0:T(8,128)(2,1)S(1)}, u32[]{:S(2)}, u32[]{:S(2)}) %collective-permute-start.12) | collective-permute-done | bytes 262176 | tf_op jit(solution)/shard_map/ppermute | solution.py:413
  34.1 2.3 %collective-permute-start.8 = (bf16[4,2,128,128]{3,2,1,0:T(8,128)(2,1)S(1)}, bf16[4,2,128,128]{3,2,1,0:T(8,128)(2,1)S(1)}, u32[]{:S(2)}, u32[]{:S(2)}) collective-permute-start(bf16[4,2,128,128]{3,2,1,0:T(8,128)(2,1)S(1)} %copy-done.8), channel_id=1, source_target_pairs={{0,3},{1,2},{2,1},{3,0},{4,7},{5,6},{6,5},{7,4},{8,11},{9,10},{10,... | collective-permute-start | bytes 786440 | tf_op jit(solution)/shard_map/ppermute | solution.py:663
  36.5 7.0 %collective-permute-done.8.refs_7_ = bf16[4,2,128,128]{3,2,1,0:T(8,128)(2,1)S(1)} collective-permute-done((bf16[4,2,128,128]{3,2,1,0:T(8,128)(2,1)S(1)}, bf16[4,2,128,128]{3,2,1,0:T(8,128)(2,1)S(1)}, u32[]{:S(2)}, u32[]{:S(2)}) %collective-permute-start.8) | collective-permute-done | bytes 262176 | tf_op jit(solution)/shard_map/ppermute | solution.py:663
  43.5 6.1 %shard_map.97 = (bf16[4,2,128,128]{3,2,1,0:T(8,128)(2,1)S(1)}, bf16[4,2,128,128]{3,2,1,0:T(8,128)(2,1)S(1)}, bf16[4,2,128,128]{3,2,1,0:T(8,128)(2,1)S(1)}, bf16[...) custom-call(s32[2]{0:T(128)S(1)} %copy-done.5, ...), custom_call_target="tpu_custom_call" | custom-call | flops 1207959552 | bytes 5242880 | tf_op jit(solution)/shard_map/pallas_call | solution.py:346
  49.6 2.7 %collective-permute-start.16 = (bf16[8,2,128,128]{3,2,1,0:T(8,128)(2,1)S(1)}, bf16[8,2,128,128]{3,2,1,0:T(8,128)(2,1)S(1)}, u32[]{:S(2)}, u32[]{:S(2)}) collective-permute-start(bf16[8,2,128,128]{3,2,1,0:T(8,128)(2,1)S(1)} %get-tuple-element.98), channel_id=1, source_target_pairs={{0,4},{1,5},{2,6},{3,7},{4,0},{5,1},{6,2},{7,3},{8,12},{9,13},{10,... | collective-permute-start | bytes 1572872 | tf_op jit(solution)/shard_map/ppermute | solution.py:413
  52.3 5.9 %shard_map.98 = (bf16[4,2,128,128]{3,2,1,0:T(8,128)(2,1)S(1)}, bf16[4,2,128,128]{3,2,1,0:T(8,128)(2,1)S(1)}, bf16[4,2,128,128]{3,2,1,0:T(8,128)(2,1)S(1)}, bf16[...) custom-call(s32[2]{0:T(128)S(1)} %copy-done.5, ...), custom_call_target="tpu_custom_call", output_to_operand_aliasing={{0}: (13, {}), {1}: (14, {}), {2}: (15, {}), {3}: (16, {})} | custom-call | flops 1207959552 | bytes 5242880 | tf_op jit(solution)/shard_map/pallas_call | solution.py:346
  59.7 7.3 %collective-permute-start.18 = (bf16[4,2,128,128]{3,2,1,0:T(8,128)(2,1)S(1)}, bf16[4,2,128,128]{3,2,1,0:T(8,128)(2,1)S(1)}, u32[]{:S(2)}, u32[]{:S(2)}) collective-permute-start(bf16[4,2,128,128]{3,2,1,0:T(8,128)(2,1)S(1)} %get-tuple-element.100), channel_id=1, source_target_pairs={{0,8},{1,9},{2,10},{3,11},{4,12},{5,13},{6,14},{7,15},{8,0},{9,1},... | collective-permute-start | bytes 786440 | tf_op jit(solution)/shard_map/ppermute | solution.py:413
  67.0 2.8 %collective-permute-done.22.with_next = bf16[4,2,128,128]{3,2,1,0:T(8,128)(2,1)S(1)} collective-permute-done((bf16[4,2,128,128]{3,2,1,0:T(8,128)(2,1)S(1)}, bf16[4,2,128,128]{3,2,1,0:T(8,128)(2,1)S(1)}, u32[]{:S(2)}, u32[]{:S(2)}) %collective-permute-start.22) | collective-permute-done | bytes 262176 | tf_op jit(solution)/shard_map/ppermute | solution.py:413
  69.8 1.2 %collective-permute-start.13 = (bf16[4,2,128,128]{3,2,1,0:T(8,128)(2,1)S(1)}, bf16[4,2,128,128]{3,2,1,0:T(8,128)(2,1)S(1)}, u32[]{:S(2)}, u32[]{:S(2)}) collective-permute-start(bf16[4,2,128,128]{3,2,1,0:T(8,128)(2,1)S(1)} %get-tuple-element.92), channel_id=1, source_target_pairs={{0,1},{1,0},{2,3},{3,2},{4,5},{5,4},{6,7},{7,6},{8,9},{9,8},{10,11... | collective-permute-start | bytes 786440 | tf_op jit(solution)/shard_map/ppermute | solution.py:663
  71.0 1.2 %collective-permute-start.14 = (bf16[4,2,128,128]{3,2,1,0:T(8,128)(2,1)S(1)}, bf16[4,2,128,128]{3,2,1,0:T(8,128)(2,1)S(1)}, u32[]{:S(2)}, u32[]{:S(2)}) collective-permute-start(bf16[4,2,128,128]{3,2,1,0:T(8,128)(2,1)S(1)} %get-tuple-element.93), channel_id=1, source_target_pairs={{0,2},{1,3},{2,0},{3,1},{4,6},{5,7},{6,4},{7,5},{8,10},{9,11},{10,... | collective-permute-start | bytes 786440 | tf_op jit(solution)/shard_map/ppermute | solution.py:663
  72.6 0.8 shard_map.101
  73.4 12.7 %collective-permute-done.18.refs_0_ = bf16[4,2,128,128]{3,2,1,0:T(8,128)(2,1)S(1)} collective-permute-done((bf16[4,2,128,128]{3,2,1,0:T(8,128)(2,1)S(1)}, bf16[4,2,128,128]{3,2,1,0:T(8,128)(2,1)S(1)}, u32[]{:S(2)}, u32[]{:S(2)}) %collective-permute-start.18) | collective-permute-done | bytes 262176 | tf_op jit(solution)/shard_map/ppermute | solution.py:413
  86.1 1.6 %collective-permute-start.24 = (bf16[2,2,128,128]{3,2,1,0:T(8,128)(2,1)S(1)}, bf16[2,2,128,128]{3,2,1,0:T(8,128)(2,1)S(1)}, u32[]{:S(2)}, u32[]{:S(2)}) collective-permute-start(bf16[2,2,128,128]{3,2,1,0:T(8,128)(2,1)S(1)} %get-tuple-element.109), channel_id=1, source_target_pairs={{0,1},{1,0},{2,3},{3,2},{4,5},{5,4},{6,7},{7,6},{8,9},{9,8},{10,11... | collective-permute-start | bytes 393224 | tf_op jit(solution)/shard_map/ppermute | solution.py:663
  87.7 1.2 %collective-permute-start.25 = (bf16[2,2,128,128]{3,2,1,0:T(8,128)(2,1)S(1)}, bf16[2,2,128,128]{3,2,1,0:T(8,128)(2,1)S(1)}, u32[]{:S(2)}, u32[]{:S(2)}) collective-permute-start(bf16[2,2,128,128]{3,2,1,0:T(8,128)(2,1)S(1)} %get-tuple-element.110), channel_id=1, source_target_pairs={{0,2},{1,3},{2,0},{3,1},{4,6},{5,7},{6,4},{7,5},{8,10},{9,11},{10,... | collective-permute-start | bytes 393224 | tf_op jit(solution)/shard_map/ppermute | solution.py:663
  88.9 0.8 shard_map.100
  90.4 1.2 %collective-permute-start.20 = (bf16[2,2,128,128]{3,2,1,0:T(8,128)(2,1)S(1)}, bf16[2,2,128,128]{3,2,1,0:T(8,128)(2,1)S(1)}, u32[]{:S(2)}, u32[]{:S(2)}) collective-permute-start(bf16[2,2,128,128]{3,2,1,0:T(8,128)(2,1)S(1)} %get-tuple-element.103), channel_id=1, source_target_pairs={{0,2},{1,3},{2,0},{3,1},{4,6},{5,7},{6,4},{7,5},{8,10},{9,11},{10,... | collective-permute-start | bytes 393224 | tf_op jit(solution)/shard_map/ppermute | solution.py:663
  92.3 1.8 %shard_map.99 = (bf16[128,16,128]{2,1,0:T(8,128)(2,1)}, bf16[128,16,128]{2,1,0:T(8,128)(2,1)}) custom-call(s32[2]{0:T(128)S(1)} %copy-done.5, s32[4,4]{1,0:T(4,128)S(1)} %copy-done.3, bf16[4,2,128,128]{3,2,1,0:T(8,128)(2,1)S(1)} %get-tuple-element.91.refs_0_, bf16[4,2,128,128]{3,2,1,0:T(8,128)(2,1)S(1)} %collective-permute-done.13.refs_1_, ...), custom_call_target="tpu_custom_call" | custom-call | bytes 2097152 | tf_op jit(solution)/shard_map/pallas_call | solution.py:147
  94.1 1.9 %collective-permute-done.26.refs_7_ = bf16[2,2,128,128]{3,2,1,0:T(8,128)(2,1)S(1)} collective-permute-done((bf16[2,2,128,128]{3,2,1,0:T(8,128)(2,1)S(1)}, bf16[2,2,128,128]{3,2,1,0:T(8,128)(2,1)S(1)}, u32[]{:S(2)}, u32[]{:S(2)}) %collective-permute-start.26) | collective-permute-done | bytes 131104 | tf_op jit(solution)/shard_map/ppermute | solution.py:663
  96.1 2.3 %collective-permute-done.20.refs_2_ = bf16[2,2,128,128]{3,2,1,0:T(8,128)(2,1)S(1)} collective-permute-done((bf16[2,2,128,128]{3,2,1,0:T(8,128)(2,1)S(1)}, bf16[2,2,128,128]{3,2,1,0:T(8,128)(2,1)S(1)}, u32[]{:S(2)}, u32[]{:S(2)}) %collective-permute-start.20) | collective-permute-done | bytes 131104 | tf_op jit(solution)/shard_map/ppermute | solution.py:663
  98.4 2.9 %collective-permute-done.21.refs_3_ = bf16[2,2,128,128]{3,2,1,0:T(8,128)(2,1)S(1)} collective-permute-done((bf16[2,2,128,128]{3,2,1,0:T(8,128)(2,1)S(1)}, bf16[2,2,128,128]{3,2,1,0:T(8,128)(2,1)S(1)}, u32[]{:S(2)}, u32[]{:S(2)}) %collective-permute-start.21) | collective-permute-done | bytes 131104 | tf_op jit(solution)/shard_map/ppermute | solution.py:663
  101.3 1.8 %shard_map.102 = (bf16[128,16,128]{2,1,0:T(8,128)(2,1)}, bf16[128,16,128]{2,1,0:T(8,128)(2,1)}) custom-call(s32[2]{0:T(128)S(1)} %copy-done.5, s32[4,4]{1,0:T(4,128)S(1)} %copy-done.3, bf16[2,2,128,128]{3,2,1,0:T(8,128)(2,1)S(1)} %get-tuple-element.101.refs_0_, bf16[2,2,128,128]{3,2,1,0:T(8,128)(2,1)S(1)} %collective-permute-done.19.refs_1_, ...), custom_call_target="tpu_custom_call" | custom-call | bytes 2097152 | tf_op jit(solution)/shard_map/pallas_call | solution.py:147
  (61 shorter events, 7.2 us)
Async XLA Ops:
  3.5 2.9 %collective-permute-start = (bf16[2,2,128,128]{3,2,1,0:T(8,128)(2,1)}, bf16[2,2,128,128]{3,2,1,0:T(8,128)(2,1)S(1)}, u32[]{:S(2)}, u32[]{:S(2)}) collective-permute-start(bf16[2,2,128,128]{3,2,1,0:T(8,128)(2,1)} %get-tuple-element.60), channel_id=1, source_target_pairs={{0,1},{1,0},{2,3},{3,2},{4,5},{5,4},{6,7},{7,6},{8,9},{9,8},{10,11... | collective-permute-start | bytes 393224 | tf_op jit(solution)/shard_map/ppermute | solution.py:663
  3.6 6.7 %collective-permute-start.1 = (bf16[2,2,128,128]{3,2,1,0:T(8,128)(2,1)}, bf16[2,2,128,128]{3,2,1,0:T(8,128)(2,1)S(1)}, u32[]{:S(2)}, u32[]{:S(2)}) collective-permute-start(bf16[2,2,128,128]{3,2,1,0:T(8,128)(2,1)} %get-tuple-element.61), channel_id=1, source_target_pairs={{0,2},{1,3},{2,0},{3,1},{4,6},{5,7},{6,4},{7,5},{8,10},{9,11},{10,... | collective-permute-start | bytes 393224 | tf_op jit(solution)/shard_map/ppermute | solution.py:663
  6.3 6.8 %collective-permute-start.2 = (bf16[2,2,128,128]{3,2,1,0:T(8,128)(2,1)}, bf16[2,2,128,128]{3,2,1,0:T(8,128)(2,1)S(1)}, u32[]{:S(2)}, u32[]{:S(2)}) collective-permute-start(bf16[2,2,128,128]{3,2,1,0:T(8,128)(2,1)} %get-tuple-element.62), channel_id=1, source_target_pairs={{0,3},{1,2},{2,1},{3,0},{4,7},{5,6},{6,5},{7,4},{8,11},{9,10},{10,... | collective-permute-start | bytes 393224 | tf_op jit(solution)/shard_map/ppermute | solution.py:663
  15.0 8.7 %copy-start.5 = (s32[2]{0:T(128)S(1)}, s32[2]{0:T(128)}, u32[]{:S(2)}) copy-start(s32[2]{0:T(128)} %pad_add_fusion.place) | copy-start | bytes 28
  15.0 8.3 %collective-permute-start.3 = (bf16[2,2,128,128]{3,2,1,0:T(8,128)(2,1)S(1)}, bf16[2,2,128,128]{3,2,1,0:T(8,128)(2,1)S(1)}, u32[]{:S(2)}, u32[]{:S(2)}) collective-permute-start(bf16[2,2,128,128]{3,2,1,0:T(8,128)(2,1)S(1)} %copy-done.13), channel_id=1, source_target_pairs={{0,1},{1,0},{2,3},{3,2},{4,5},{5,4},{6,7},{7,6},{8,9},{9,8},{10,11... | collective-permute-start | bytes 393224 | tf_op jit(solution)/shard_map/ppermute | solution.py:663
  15.4 7.9 %collective-permute-start.4 = (bf16[2,2,128,128]{3,2,1,0:T(8,128)(2,1)S(1)}, bf16[2,2,128,128]{3,2,1,0:T(8,128)(2,1)S(1)}, u32[]{:S(2)}, u32[]{:S(2)}) collective-permute-start(bf16[2,2,128,128]{3,2,1,0:T(8,128)(2,1)S(1)} %copy-done.12), channel_id=1, source_target_pairs={{0,2},{1,3},{2,0},{3,1},{4,6},{5,7},{6,4},{7,5},{8,10},{9,11},{10,... | collective-permute-start | bytes 393224 | tf_op jit(solution)/shard_map/ppermute | solution.py:663
  16.6 7.0 %collective-permute-start.5 = (bf16[2,2,128,128]{3,2,1,0:T(8,128)(2,1)S(1)}, bf16[2,2,128,128]{3,2,1,0:T(8,128)(2,1)S(1)}, u32[]{:S(2)}, u32[]{:S(2)}) collective-permute-start(bf16[2,2,128,128]{3,2,1,0:T(8,128)(2,1)S(1)} %copy-done.11), channel_id=1, source_target_pairs={{0,3},{1,2},{2,1},{3,0},{4,7},{5,6},{6,5},{7,4},{8,11},{9,10},{10,... | collective-permute-start | bytes 393224 | tf_op jit(solution)/shard_map/ppermute | solution.py:663
  19.4 14.8 %copy-start.8 = (bf16[4,2,128,128]{3,2,1,0:T(8,128)(2,1)S(1)}, bf16[4,2,128,128]{3,2,1,0:T(8,128)(2,1)}, u32[]{:S(2)}) copy-start(bf16[4,2,128,128]{3,2,1,0:T(8,128)(2,1)} %get-tuple-element.82) | copy-start | bytes 786436
  19.4 24.1 %copy-start.6 = (bf16[4,2,128,128]{3,2,1,0:T(8,128)(2,1)S(1)}, bf16[4,2,128,128]{3,2,1,0:T(8,128)(2,1)}, u32[]{:S(2)}) copy-start(bf16[4,2,128,128]{3,2,1,0:T(8,128)(2,1)} %get-tuple-element.79.refs_4_) | copy-start | bytes 786436
  19.4 14.7 %collective-permute-start.12 = (bf16[4,2,128,128]{3,2,1,0:T(8,128)(2,1)S(1)}, bf16[4,2,128,128]{3,2,1,0:T(8,128)(2,1)S(1)}, u32[]{:S(2)}, u32[]{:S(2)}) collective-permute-start(bf16[4,2,128,128]{3,2,1,0:T(8,128)(2,1)S(1)} %get-tuple-element.86), channel_id=1, source_target_pairs={{0,8},{1,9},{2,10},{3,11},{4,12},{5,13},{6,14},{7,15},{8,0},{9,1},... | collective-permute-start | bytes 786440 | tf_op jit(solution)/shard_map/ppermute | solution.py:413
  22.0 21.5 %collective-permute-start.11 = (bf16[8,2,128,128]{3,2,1,0:T(8,128)(2,1)S(1)}, bf16[8,2,128,128]{3,2,1,0:T(8,128)(2,1)S(1)}, u32[]{:S(2)}, u32[]{:S(2)}) collective-permute-start(bf16[8,2,128,128]{3,2,1,0:T(8,128)(2,1)S(1)} %get-tuple-element.85), channel_id=1, source_target_pairs={{0,4},{1,5},{2,6},{3,7},{4,0},{5,1},{6,2},{7,3},{8,12},{9,13},{10,... | collective-permute-start | bytes 1572872 | tf_op jit(solution)/shard_map/ppermute | solution.py:413
  24.3 19.1 %copy-start.3 = (s32[4,4]{1,0:T(4,128)S(1)}, s32[4,4]{1,0:T(4,128)}, u32[]{:S(2)}) copy-start(s32[4,4]{1,0:T(4,128)} %sections.11) | copy-start | bytes 196
  24.3 19.1 %copy-start.7 = (s32[16]{0:T(128)S(1)}, s32[16]{0:T(128)}, u32[]{:S(2)}) copy-start(s32[16]{0:T(128)} %widths.3) | copy-start | bytes 196
  24.4 19.1 %collective-permute-start.10 = (bf16[8,2,128,128]{3,2,1,0:T(8,128)(2,1)S(1)}, bf16[8,2,128,128]{3,2,1,0:T(8,128)(2,1)S(1)}, u32[]{:S(2)}, u32[]{:S(2)}) collective-permute-start(bf16[8,2,128,128]{3,2,1,0:T(8,128)(2,1)S(1)} %get-tuple-element.84), channel_id=1, source_target_pairs={{4,8},{5,9},{6,10},{7,11},{8,4},{9,5},{10,6},{11,7},{20,24},{21,25... | collective-permute-start | bytes 1572872 | tf_op jit(solution)/shard_map/ppermute | solution.py:683
  25.1 11.3 %collective-permute-start.6 = (bf16[4,2,128,128]{3,2,1,0:T(8,128)(2,1)S(1)}, bf16[4,2,128,128]{3,2,1,0:T(8,128)(2,1)S(1)}, u32[]{:S(2)}, u32[]{:S(2)}) collective-permute-start(bf16[4,2,128,128]{3,2,1,0:T(8,128)(2,1)S(1)} %copy-done.10), channel_id=1, source_target_pairs={{0,1},{1,0},{2,3},{3,2},{4,5},{5,4},{6,7},{7,6},{8,9},{9,8},{10,11... | collective-permute-start | bytes 786440 | tf_op jit(solution)/shard_map/ppermute | solution.py:663
  25.3 11.2 %collective-permute-start.7 = (bf16[4,2,128,128]{3,2,1,0:T(8,128)(2,1)S(1)}, bf16[4,2,128,128]{3,2,1,0:T(8,128)(2,1)S(1)}, u32[]{:S(2)}, u32[]{:S(2)}) collective-permute-start(bf16[4,2,128,128]{3,2,1,0:T(8,128)(2,1)S(1)} %copy-done.9), channel_id=1, source_target_pairs={{0,2},{1,3},{2,0},{3,1},{4,6},{5,7},{6,4},{7,5},{8,10},{9,11},{10,... | collective-permute-start | bytes 786440 | tf_op jit(solution)/shard_map/ppermute | solution.py:663
  34.1 9.3 %collective-permute-start.8 = (bf16[4,2,128,128]{3,2,1,0:T(8,128)(2,1)S(1)}, bf16[4,2,128,128]{3,2,1,0:T(8,128)(2,1)S(1)}, u32[]{:S(2)}, u32[]{:S(2)}) collective-permute-start(bf16[4,2,128,128]{3,2,1,0:T(8,128)(2,1)S(1)} %copy-done.8), channel_id=1, source_target_pairs={{0,3},{1,2},{2,1},{3,0},{4,7},{5,6},{6,5},{7,4},{8,11},{9,10},{10,... | collective-permute-start | bytes 786440 | tf_op jit(solution)/shard_map/ppermute | solution.py:663
  36.4 15.9 %collective-permute-start.9 = (bf16[4,2,128,128]{3,2,1,0:T(8,128)(2,1)S(1)}, bf16[4,2,128,128]{3,2,1,0:T(8,128)(2,1)S(1)}, u32[]{:S(2)}, u32[]{:S(2)}) collective-permute-start(bf16[4,2,128,128]{3,2,1,0:T(8,128)(2,1)S(1)} %get-tuple-element.83), channel_id=1, source_target_pairs={{0,4},{1,5},{2,6},{3,7},{4,0},{5,1},{6,2},{7,3},{8,12},{9,13},{10,... | collective-permute-start | bytes 786440 | tf_op jit(solution)/shard_map/ppermute | solution.py:413
  49.6 38.1 %collective-permute-start.16 = (bf16[8,2,128,128]{3,2,1,0:T(8,128)(2,1)S(1)}, bf16[8,2,128,128]{3,2,1,0:T(8,128)(2,1)S(1)}, u32[]{:S(2)}, u32[]{:S(2)}) collective-permute-start(bf16[8,2,128,128]{3,2,1,0:T(8,128)(2,1)S(1)} %get-tuple-element.98), channel_id=1, source_target_pairs={{0,4},{1,5},{2,6},{3,7},{4,0},{5,1},{6,2},{7,3},{8,12},{9,13},{10,... | collective-permute-start | bytes 1572872 | tf_op jit(solution)/shard_map/ppermute | solution.py:413
  58.2 11.6 %collective-permute-start.22 = (bf16[4,2,128,128]{3,2,1,0:T(8,128)(2,1)S(1)}, bf16[4,2,128,128]{3,2,1,0:T(8,128)(2,1)S(1)}, u32[]{:S(2)}, u32[]{:S(2)}) collective-permute-start(bf16[4,2,128,128]{3,2,1,0:T(8,128)(2,1)S(1)} %get-tuple-element.106), channel_id=1, source_target_pairs={{0,4},{1,5},{2,6},{3,7},{4,0},{5,1},{6,2},{7,3},{8,12},{9,13},{10,... | collective-permute-start | bytes 786440 | tf_op jit(solution)/shard_map/ppermute | solution.py:413
  58.3 12.6 %collective-permute-start.23 = (bf16[4,2,128,128]{3,2,1,0:T(8,128)(2,1)S(1)}, bf16[4,2,128,128]{3,2,1,0:T(8,128)(2,1)S(1)}, u32[]{:S(2)}, u32[]{:S(2)}) collective-permute-start(bf16[4,2,128,128]{3,2,1,0:T(8,128)(2,1)S(1)} %get-tuple-element.107), channel_id=1, source_target_pairs={{4,8},{5,9},{6,10},{7,11},{8,4},{9,5},{10,6},{11,7},{20,24},{21,25... | collective-permute-start | bytes 786440 | tf_op jit(solution)/shard_map/ppermute | solution.py:683
  59.0 13.2 %collective-permute-start.17 = (bf16[4,2,128,128]{3,2,1,0:T(8,128)(2,1)S(1)}, bf16[4,2,128,128]{3,2,1,0:T(8,128)(2,1)S(1)}, u32[]{:S(2)}, u32[]{:S(2)}) collective-permute-start(bf16[4,2,128,128]{3,2,1,0:T(8,128)(2,1)S(1)} %get-tuple-element.99), channel_id=1, source_target_pairs={{4,8},{5,9},{6,10},{7,11},{8,4},{9,5},{10,6},{11,7},{20,24},{21,25... | collective-permute-start | bytes 786440 | tf_op jit(solution)/shard_map/ppermute | solution.py:683
  59.7 26.4 %collective-permute-start.18 = (bf16[4,2,128,128]{3,2,1,0:T(8,128)(2,1)S(1)}, bf16[4,2,128,128]{3,2,1,0:T(8,128)(2,1)S(1)}, u32[]{:S(2)}, u32[]{:S(2)}) collective-permute-start(bf16[4,2,128,128]{3,2,1,0:T(8,128)(2,1)S(1)} %get-tuple-element.100), channel_id=1, source_target_pairs={{0,8},{1,9},{2,10},{3,11},{4,12},{5,13},{6,14},{7,15},{8,0},{9,1},... | collective-permute-start | bytes 786440 | tf_op jit(solution)/shard_map/ppermute | solution.py:413
  69.8 19.9 %collective-permute-start.13 = (bf16[4,2,128,128]{3,2,1,0:T(8,128)(2,1)S(1)}, bf16[4,2,128,128]{3,2,1,0:T(8,128)(2,1)S(1)}, u32[]{:S(2)}, u32[]{:S(2)}) collective-permute-start(bf16[4,2,128,128]{3,2,1,0:T(8,128)(2,1)S(1)} %get-tuple-element.92), channel_id=1, source_target_pairs={{0,1},{1,0},{2,3},{3,2},{4,5},{5,4},{6,7},{7,6},{8,9},{9,8},{10,11... | collective-permute-start | bytes 786440 | tf_op jit(solution)/shard_map/ppermute | solution.py:663
  71.0 19.2 %collective-permute-start.14 = (bf16[4,2,128,128]{3,2,1,0:T(8,128)(2,1)S(1)}, bf16[4,2,128,128]{3,2,1,0:T(8,128)(2,1)S(1)}, u32[]{:S(2)}, u32[]{:S(2)}) collective-permute-start(bf16[4,2,128,128]{3,2,1,0:T(8,128)(2,1)S(1)} %get-tuple-element.93), channel_id=1, source_target_pairs={{0,2},{1,3},{2,0},{3,1},{4,6},{5,7},{6,4},{7,5},{8,10},{9,11},{10,... | collective-permute-start | bytes 786440 | tf_op jit(solution)/shard_map/ppermute | solution.py:663
  72.2 18.2 %collective-permute-start.15 = (bf16[4,2,128,128]{3,2,1,0:T(8,128)(2,1)S(1)}, bf16[4,2,128,128]{3,2,1,0:T(8,128)(2,1)S(1)}, u32[]{:S(2)}, u32[]{:S(2)}) collective-permute-start(bf16[4,2,128,128]{3,2,1,0:T(8,128)(2,1)S(1)} %get-tuple-element.94), channel_id=1, source_target_pairs={{0,3},{1,2},{2,1},{3,0},{4,7},{5,6},{6,5},{7,4},{8,11},{9,10},{10,... | collective-permute-start | bytes 786440 | tf_op jit(solution)/shard_map/ppermute | solution.py:663
  86.1 5.6 %collective-permute-start.24 = (bf16[2,2,128,128]{3,2,1,0:T(8,128)(2,1)S(1)}, bf16[2,2,128,128]{3,2,1,0:T(8,128)(2,1)S(1)}, u32[]{:S(2)}, u32[]{:S(2)}) collective-permute-start(bf16[2,2,128,128]{3,2,1,0:T(8,128)(2,1)S(1)} %get-tuple-element.109), channel_id=1, source_target_pairs={{0,1},{1,0},{2,3},{3,2},{4,5},{5,4},{6,7},{7,6},{8,9},{9,8},{10,11... | collective-permute-start | bytes 393224 | tf_op jit(solution)/shard_map/ppermute | solution.py:663
  87.7 6.5 %collective-permute-start.25 = (bf16[2,2,128,128]{3,2,1,0:T(8,128)(2,1)S(1)}, bf16[2,2,128,128]{3,2,1,0:T(8,128)(2,1)S(1)}, u32[]{:S(2)}, u32[]{:S(2)}) collective-permute-start(bf16[2,2,128,128]{3,2,1,0:T(8,128)(2,1)S(1)} %get-tuple-element.110), channel_id=1, source_target_pairs={{0,2},{1,3},{2,0},{3,1},{4,6},{5,7},{6,4},{7,5},{8,10},{9,11},{10,... | collective-permute-start | bytes 393224 | tf_op jit(solution)/shard_map/ppermute | solution.py:663
  89.7 6.3 %collective-permute-start.26 = (bf16[2,2,128,128]{3,2,1,0:T(8,128)(2,1)S(1)}, bf16[2,2,128,128]{3,2,1,0:T(8,128)(2,1)S(1)}, u32[]{:S(2)}, u32[]{:S(2)}) collective-permute-start(bf16[2,2,128,128]{3,2,1,0:T(8,128)(2,1)S(1)} %get-tuple-element.111), channel_id=1, source_target_pairs={{0,3},{1,2},{2,1},{3,0},{4,7},{5,6},{6,5},{7,4},{8,11},{9,10},{10,... | collective-permute-start | bytes 393224 | tf_op jit(solution)/shard_map/ppermute | solution.py:663
  90.2 5.9 %collective-permute-start.19 = (bf16[2,2,128,128]{3,2,1,0:T(8,128)(2,1)S(1)}, bf16[2,2,128,128]{3,2,1,0:T(8,128)(2,1)S(1)}, u32[]{:S(2)}, u32[]{:S(2)}) collective-permute-start(bf16[2,2,128,128]{3,2,1,0:T(8,128)(2,1)S(1)} %get-tuple-element.102), channel_id=1, source_target_pairs={{0,1},{1,0},{2,3},{3,2},{4,5},{5,4},{6,7},{7,6},{8,9},{9,8},{10,11... | collective-permute-start | bytes 393224 | tf_op jit(solution)/shard_map/ppermute | solution.py:663
  90.4 8.0 %collective-permute-start.20 = (bf16[2,2,128,128]{3,2,1,0:T(8,128)(2,1)S(1)}, bf16[2,2,128,128]{3,2,1,0:T(8,128)(2,1)S(1)}, u32[]{:S(2)}, u32[]{:S(2)}) collective-permute-start(bf16[2,2,128,128]{3,2,1,0:T(8,128)(2,1)S(1)} %get-tuple-element.103), channel_id=1, source_target_pairs={{0,2},{1,3},{2,0},{3,1},{4,6},{5,7},{6,4},{7,5},{8,10},{9,11},{10,... | collective-permute-start | bytes 393224 | tf_op jit(solution)/shard_map/ppermute | solution.py:663
  91.7 9.6 %collective-permute-start.21 = (bf16[2,2,128,128]{3,2,1,0:T(8,128)(2,1)S(1)}, bf16[2,2,128,128]{3,2,1,0:T(8,128)(2,1)S(1)}, u32[]{:S(2)}, u32[]{:S(2)}) collective-permute-start(bf16[2,2,128,128]{3,2,1,0:T(8,128)(2,1)S(1)} %get-tuple-element.104), channel_id=1, source_target_pairs={{0,3},{1,2},{2,1},{3,0},{4,7},{5,6},{6,5},{7,4},{8,11},{9,10},{10,... | collective-permute-start | bytes 393224 | tf_op jit(solution)/shard_map/ppermute | solution.py:663
  (9 other events, 41.5 us)

commit v6 on v5

--- a/solution.py
+++ b/solution.py
@@ -95,39 +95,45 @@
 LIMIT = pltpu.CompilerParams(vmem_limit_bytes=20 << 20)
 
 
-def pack_kernel(place, sections, *refs, groups, count):
+def pack_kernel(place, sections, *refs, order, count, crossed):
     ins, outs, held = refs[:count], refs[count:-1], refs[-1]
     for i in range(count):
         held[i] = jnp.transpose(ins[i][...], (1, 0, 2))
-    for number, group in enumerate(groups):
-        for m in range(PLANE):
-            for k, s in enumerate(group):
-                head = sections[s, place[0] ^ m]
-                for i in range(count):
-                    outs[number * PLANE + m][k, i] = held[i, head]
-
-
-def pack(place, sections, arrays, groups):
+    for m in range(PLANE):
+        owner = place[0] ^ m if crossed else m
+        for k, s in enumerate(order):
+            head = sections[s, owner]
+            for i in range(count):
+                if crossed:
+                    outs[m][k, i] = held[i, head]
+                else:
+                    outs[0][m, k, i] = held[i, head]
+
+
+def pack(place, sections, arrays, order, crossed):
     tokens, heads, width = arrays[0].shape
     chunk = tokens // 2
     count = len(arrays)
-    shapes = [(len(group), count, tokens, width) for group in groups for _ in range(PLANE)]
-    outs = pl.pallas_call(
-        functools.partial(pack_kernel, groups=groups, count=count),
+    shape = (len(order), count, tokens, width)
+    if crossed:
+        shapes = [shape] * PLANE
+        specs = [pl.BlockSpec((*shape[:2], chunk, width), lambda i: (0, 0, i, 0))] * PLANE
+    else:
+        shapes = [(PLANE, *shape)]
+        specs = [pl.BlockSpec((PLANE, *shape[:2], chunk, width), lambda i: (0, 0, 0, i, 0))]
+    return pl.pallas_call(
+        functools.partial(pack_kernel, order=order, count=count, crossed=crossed),
         grid=(tokens // chunk,),
         in_specs=[SMEM, SMEM]
         + [pl.BlockSpec((chunk, heads, width), lambda i: (i, 0, 0))] * count,
-        out_specs=[
-            pl.BlockSpec((*shape[:2], chunk, width), lambda i: (0, 0, i, 0)) for shape in shapes
-        ],
+        out_specs=specs,
         out_shape=[jax.ShapeDtypeStruct(shape, jnp.bfloat16) for shape in shapes],
         scratch_shapes=[pltpu.VMEM((count, heads, chunk, width), jnp.bfloat16)],
         cost_estimate=moved_cost(arrays),
     )(place, sections, *arrays)
-    return [outs[i * PLANE : (i + 1) * PLANE] for i in range(len(groups))]
-
-
-def unpack_kernel(place, sections, *refs, groups, count):
+
+
+def unpack_crossed_kernel(place, sections, *refs, groups, count):
     pieces, outs, held = refs[: len(groups) * PLANE], refs[len(groups) * PLANE : -1], refs[-1]
     for number, group in enumerate(groups):
         for m in range(PLANE):
@@ -139,110 +145,100 @@
         outs[i][...] = jnp.transpose(held[i], (1, 0, 2))
 
 
-def unpack(place, sections, pieces, groups):
-    flat = [piece for group in pieces for piece in group]
-    _, count, tokens, width = flat[0].shape
+def unpack_kernel(place, sections, src, *refs, order, count):
+    outs, held = refs[:-1], refs[-1]
+    for m in range(PLANE):
+        for k, s in enumerate(order):
+            head = sections[s, m]
+            for i in range(count):
+                held[i, head] = src[m, k, i]
+    for i in range(count):
+        outs[i][...] = jnp.transpose(held[i], (1, 0, 2))
+
+
+def unpack(place, sections, kernel, pieces):
+    *lead, count, tokens, width = pieces[0].shape
     heads = sections.size
     chunk = tokens // 2
     return pl.pallas_call(
-        functools.partial(unpack_kernel, groups=groups, count=count),
+        functools.partial(kernel, count=count),
         grid=(tokens // chunk,),
         in_specs=[SMEM, SMEM]
         + [
-            pl.BlockSpec((*piece.shape[:2], chunk, width), lambda i: (0, 0, i, 0))
-            for piece in flat
+            pl.BlockSpec(
+                (*piece.shape[:-2], chunk, width),
+                lambda i, zeros=(0,) * (piece.ndim - 2): (*zeros, i, 0),
+            )
+            for piece in pieces
         ],
         out_specs=[pl.BlockSpec((chunk, heads, width), lambda i: (i, 0, 0))] * count,
         out_shape=[jax.ShapeDtypeStruct((tokens, heads, width), jnp.bfloat16)] * count,
         scratch_shapes=[pltpu.VMEM((count, heads, chunk, width), jnp.bfloat16)],
         compiler_params=LIMIT,
-        cost_estimate=moved_cost(flat),
-    )(place, sections, *flat)
+        cost_estimate=moved_cost(pieces),
+    )(place, sections, *pieces)
 
 
 def facing(place):
     return place[0] // HALO == 1 - place[1] % 2
 
 
-def collect_far_kernel(place, *refs):
-    pieces, (with_next, with_other) = refs[:PLANE], refs[PLANE:]
-    group = pieces[0].shape[0]
-    for m in range(PLANE):
-        with_next[m] = pieces[m][0]
-        with_other[m] = pieces[m][1]
-
-    def fill(base):
+def far_kernel(*refs):
+    pieces, outs = refs[:PLANE], refs[PLANE:]
+    for k, out in enumerate(outs):
+        for m, piece in enumerate(pieces):
+            out[m] = piece[k]
+
+
+def far_parts(pieces, count):
+    rest = pieces[0].shape[1:]
+    return pl.pallas_call(
+        far_kernel,
+        in_specs=[VMEM] * PLANE,
+        out_specs=[VMEM] * count,
+        out_shape=[jax.ShapeDtypeStruct((PLANE, *rest), jnp.bfloat16)] * count,
+        compiler_params=LIMIT,
+        cost_estimate=moved_cost(pieces),
+    )(*pieces)
+
+
+def halo_kernel(place, *refs):
+    pieces, (with_next, with_last) = refs[:PLANE], refs[PLANE:]
+    slots = pieces[0].shape[0]
+
+    def fill(base, other):
         for m in range(HALO):
-            for k in range(group):
-                with_next[PLANE + m * group + k] = pieces[base + m][k]
+            with_next[m * slots : (m + 1) * slots] = pieces[base + m][...]
+            with_last[m * slots : (m + 1) * slots] = pieces[other + m][...]
 
     @pl.when(facing(place))
     def _():
-        fill(0)
+        fill(0, HALO)
 
     @pl.when(jnp.logical_not(facing(place)))
     def _():
-        fill(HALO)
-
-
-def collect_far(place, pieces):
-    group, *rest = pieces[0].shape
+        fill(HALO, 0)
+
+
+def halo_parts(place, pieces):
+    slots, *rest = pieces[0].shape
     return pl.pallas_call(
-        collect_far_kernel,
+        halo_kernel,
         in_specs=[SMEM] + [VMEM] * PLANE,
         out_specs=[VMEM] * 2,
-        out_shape=[
-            jax.ShapeDtypeStruct((PLANE + HALO * group, *rest), jnp.bfloat16),
-            jax.ShapeDtypeStruct((PLANE, *rest), jnp.bfloat16),
-        ],
+        out_shape=[jax.ShapeDtypeStruct((HALO * slots, *rest), jnp.bfloat16)] * 2,
         compiler_params=LIMIT,
         cost_estimate=moved_cost(pieces),
     )(place, *pieces)
 
 
-def collect_near_kernel(place, *refs):
-    far, near, (with_next, with_last) = refs[:PLANE], refs[PLANE:-2], refs[-2:]
-    group = near[0].shape[0]
-
-    def fill(base, other):
-        for m in range(HALO):
-            for k in range(group):
-                with_next[m * group + k] = near[base + m][k]
-                with_last[m * group + k] = far[other + m][k]
-                with_last[(HALO + m) * group + k] = near[other + m][k]
-
-    @pl.when(facing(place))
-    def _():
-        fill(0, HALO)
-
-    @pl.when(jnp.logical_not(facing(place)))
-    def _():
-        fill(HALO, 0)
-
-
-def collect_near(place, far, near):
-    group, *rest = near[0].shape
-    return pl.pallas_call(
-        collect_near_kernel,
-        in_specs=[SMEM] + [VMEM] * (2 * PLANE),
-        out_specs=[VMEM] * 2,
-        out_shape=[
-            jax.ShapeDtypeStruct((HALO * group, *rest), jnp.bfloat16),
-            jax.ShapeDtypeStruct((2 * HALO * group, *rest), jnp.bfloat16),
-        ],
-        compiler_params=LIMIT,
-        cost_estimate=moved_cost([*far, *near]),
-    )(place, *far, *near)
-
-
-def attend_kernel(place, widths, sections, *refs, first, remote, base, blocks, aliased):
-    pairs, graded = refs[:PLANE], refs[PLANE : 2 * PLANE]
-    (with_next, with_last), rest = refs[2 * PLANE : 2 * PLANE + 2], refs[2 * PLANE + 2 :]
+def attend_kernel(place, widths, sections, *refs, first, slot, remote, blocks, aliased):
+    pairs, (graded, with_next, with_last) = refs[:PLANE], refs[PLANE : PLANE + 3]
+    rest = refs[PLANE + 3 :]
     if remote:
-        with_other, rest = rest[0], rest[1:]
+        far_in, rest = rest[:2], rest[2:]
     rest = rest[aliased:]
-    outs, rest = rest[:PLANE], rest[PLANE:]
-    (part, to_next, to_last), rest = rest[:3], rest[3:]
+    (rows, part, to_next, to_last), rest = rest[:4], rest[4:]
     if remote:
         to_other, rest = rest[0], rest[1:]
     keys, values, far_keys, far_values, queries, grads, attended, dq = rest[:8]
@@ -256,23 +252,24 @@
     far_bias = jnp.where(bit >= width, 0.0, blocked_score).astype(jnp.float32)
     scales = (1.0 / math.sqrt(keys.shape[-1]), 1.0)
     lead = PLANE if remote else 0
+    pairs_slots = with_next.shape[0] // HALO
     next_at = jnp.where(place[1] % 2 == 0, HALO + PLANE, 0)
     last_at = HALO + PLANE - next_at
     for m in range(PLANE):
         b = me ^ m
         keys[rows_of(HALO + b)] = pairs[m][0, 0]
         values[rows_of(HALO + b)] = pairs[m][0, 1]
-        queries[rows_of(b)] = graded[m][0, 0]
-        grads[rows_of(b)] = graded[m][0, 1]
+        queries[m * BLK : (m + 1) * BLK] = graded[m, 0, 0]
+        grads[m * BLK : (m + 1) * BLK] = graded[m, 0, 1]
     for m in range(HALO):
         b = (me % HALO) ^ m
-        slot = m * group + k
-        keys[rows_of(next_at + b)] = with_next[lead + slot, 0]
-        values[rows_of(next_at + b)] = with_next[lead + slot, 1]
-        keys[rows_of(last_at + b)] = with_last[base + slot, 0]
-        values[rows_of(last_at + b)] = with_last[base + slot, 1]
+        at = m * pairs_slots + slot + k
+        keys[rows_of(next_at + b)] = with_next[at, 0]
+        values[rows_of(next_at + b)] = with_next[at, 1]
+        keys[rows_of(last_at + b)] = with_last[at, 0]
+        values[rows_of(last_at + b)] = with_last[at, 1]
     if remote:
-        for n, source in enumerate((with_next, with_other)):
+        for n, source in enumerate(far_in):
 
             @pl.when(k == n)
             def _(source=source):
@@ -323,22 +320,20 @@
             part[0, m, i] = acc[:, rows_of(HALO + (me ^ m))] * scales[i]
         for m in range(HALO):
             b = (me % HALO) ^ m
-            slot = m * group + k
-            to_next[lead + slot, i] = (acc[:, rows_of(next_at + b)] * scales[i]).astype(
-                jnp.bfloat16
-            )
-            to_last[slot, i] = (acc[:, rows_of(last_at + b)] * scales[i]).astype(jnp.bfloat16)
-    for m in range(PLANE):
-        outs[m][0, 0] = attended[rows_of(me ^ m)]
-        outs[m][0, 1] = dq[rows_of(me ^ m)]
-
-
-def attend(place, widths, sections, pairs, graded, halos, first, slot, blocks, rows=()):
-    group, count, _, width = pairs[0].shape
+            at = m * group + k
+            to_next[lead + at, i] = (acc[:, rows_of(next_at + b)] * scales[i]).astype(jnp.bfloat16)
+            to_last[at, i] = (acc[:, rows_of(last_at + b)] * scales[i]).astype(jnp.bfloat16)
+    for b in range(PLANE):
+        rows[b, 0, 0] = attended[b * BLK : (b + 1) * BLK]
+        rows[b, 0, 1] = dq[b * BLK : (b + 1) * BLK]
+
+
+def attend(place, widths, sections, pairs, graded, halos, far, group, first, slot, blocks, rows=()):
+    count, _, width = pairs[0].shape[1:]
     tile = (BLK, width)
-    remote = len(halos) > 2
-    piece = pl.BlockSpec((1, count, *tile), lambda k: (k, 0, 0, 0))
-    graded_piece = pl.BlockSpec((1, count, *tile), lambda k: (slot + k, 0, 0, 0))
+    remote = len(far)
+    piece = pl.BlockSpec((1, count, *tile), lambda k: (slot + k, 0, 0, 0))
+    row_piece = pl.BlockSpec((PLANE, 1, count, *tile), lambda k: (0, slot + k, 0, 0, 0))
     bf16 = jnp.bfloat16
     owed = [(HALO * group + (PLANE if remote else 0), count, *tile), (HALO * group, count, *tile)]
     if remote:
@@ -347,36 +342,36 @@
         functools.partial(
             attend_kernel,
             first=first,
+            slot=slot,
             remote=remote,
-            base=HALO * slot,
             blocks=blocks,
             aliased=len(rows),
         ),
         grid=(group,),
         in_specs=[SMEM] * 3
         + [piece] * PLANE
-        + [graded_piece] * PLANE
-        + [whole(halo.shape) for halo in halos]
+        + [row_piece]
+        + [whole(halo.shape) for halo in (*halos, *far)]
         + [pl.BlockSpec(memory_space=pl.ANY)] * len(rows),
-        out_specs=[graded_piece] * PLANE
-        + [pl.BlockSpec((1, PLANE, count, *tile), lambda k: (k, 0, 0, 0, 0))]
+        out_specs=[row_piece, pl.BlockSpec((1, PLANE, count, *tile), lambda k: (k, 0, 0, 0, 0))]
         + [whole(shape) for shape in owed],
-        out_shape=[jax.ShapeDtypeStruct(graded[0].shape, bf16)] * PLANE
-        + [jax.ShapeDtypeStruct((group, PLANE, count, *tile), jnp.float32)]
+        out_shape=[
+            jax.ShapeDtypeStruct(graded.shape, bf16),
+            jax.ShapeDtypeStruct((group, PLANE, count, *tile), jnp.float32),
+        ]
         + [jax.ShapeDtypeStruct(shape, bf16) for shape in owed],
         scratch_shapes=[pltpu.VMEM((PADDED * BLK, width), bf16)] * 2
         + [pltpu.VMEM((PLANE * BLK, width), bf16)] * 6
         + [pltpu.VMEM((width, PADDED * BLK), jnp.float32)] * 2
         + [pltpu.VMEM((width, PLANE * BLK), jnp.float32)] * 2,
-        input_output_aliases={3 + 2 * PLANE + len(halos) + m: m for m in range(len(rows))},
-        compiler_params=LIMIT,
+        input_output_aliases={4 + PLANE + len(halos) + len(far): 0} if rows else {},
         cost_estimate=pl.CostEstimate(
             flops=group * PLANE * 12 * BLK * LINKED * width,
             transcendentals=group * PLANE * BLK * LINKED,
             bytes_accessed=40 * group * PLANE * BLK * width,
         ),
-    )(place, widths, sections, *pairs, *graded, *halos, *rows)
-    return outs[:PLANE], outs[PLANE], outs[PLANE + 1 :]
+    )(place, widths, sections, *pairs, graded, *halos, *far, *rows)
+    return outs[0], outs[1], outs[2:]
 
 
 def combine_kernel(place, part, with_next, with_last, *refs, remote):
@@ -683,6 +678,12 @@
     return lax.ppermute(value, "seq", pairs)
 
 
+def plane_all_to_all(value):
+    peers = lax.axis_size("seq")
+    planes = [list(range(i, i + PLANE)) for i in range(0, peers, PLANE)]
+    return lax.all_to_all(value, "seq", 0, 0, axis_index_groups=planes, tiled=True)
+
+
 def sharded_by_plane(query_rows, key_rows, value_rows, out_grad, widths, sections):
     position = lax.axis_index("seq").astype(jnp.int32)
     place = jnp.stack([position % PLANE, position // PLANE])
@@ -691,37 +692,35 @@
     total = sections.shape[0]
     groups = [tuple(range(local, total)), tuple(range(local))]
     order = tuple(s for group in groups for s in group)
-    sent_far, sent_near = pack(place, sections, [key_rows, value_rows], groups)
-    pairs_far = in_plane(sent_far)
-    next_sent, other_sent = collect_far(place, pairs_far)
-    (next_sent, other_sent), sent_near = lax.optimization_barrier(
-        ((next_sent, other_sent), sent_near)
-    )
-    other_far = with_other_plane(other_sent)
-    next_far = with_next_plane(next_sent)
-    pairs_near = in_plane(sent_near)
-    next_sent, last_sent = collect_near(place, pairs_far, pairs_near)
-    (sent,) = pack(place, sections, [query_rows, out_grad], [order])
-    (next_sent, last_sent), sent = lax.optimization_barrier(((next_sent, last_sent), sent))
-    last = with_last_plane(last_sent)
-    next_near = with_next_plane(next_sent)
-    graded = in_plane(sent)
+    tables = (place, widths, sections)
+    sent = pack(place, sections, [key_rows, value_rows], order, True)
+    (graded_sent,) = pack(place, sections, [query_rows, out_grad], order, False)
+    graded = plane_all_to_all(graded_sent)
+    pairs = in_plane(sent)
+    next_sent, last_sent = halo_parts(place, pairs)
+    far_sent = far_parts(pairs, total - local)
+    halos = (with_next_plane(next_sent), with_last_plane(last_sent))
+    far = (with_next_plane(far_sent[0]), with_other_plane(far_sent[1]))
+    rows, part_near, owed = attend(
+        *tables, pairs, graded, halos, (), local, 0, total - local, blocks
+    )
+    owed_near = [with_next_plane(owed[0]), with_last_plane(owed[1])]
     rows, part_far, owed = attend(
-        place, widths, sections, pairs_far, graded, [next_far, last, other_far], local, 0, blocks
-    )
+        *tables, pairs, graded, halos, far, total - local, local, 0, blocks, (rows,)
+    )
+    near = combine(place, part_near, owed_near)
+    owed, near, rows = lax.optimization_barrier((owed, near, rows))
     other_back = with_other_plane(owed[2])
     owed_far = [with_next_plane(owed[0]), with_last_plane(owed[1]), other_back]
-    rows, part_near, owed = attend(
-        place, widths, sections, pairs_near, graded, [next_near, last], 0, total - local, blocks, rows
-    )
-    owed_near = [with_next_plane(owed[0]), with_last_plane(owed[1])]
-    rows = in_plane(rows)
-    columns = [
-        in_plane(combine(place, part_far, owed_far)),
-        in_plane(combine(place, part_near, owed_near)),
-    ]
-    attended, query_grad = unpack(place, sections, [rows], [order])
-    key_grad, value_grad = unpack(place, sections, columns, groups)
+    near = in_plane(near)
+    rows = plane_all_to_all(rows)
+    columns = in_plane(combine(place, part_far, owed_far)) + near
+    attended, query_grad = unpack(
+        place, sections, functools.partial(unpack_kernel, order=order), [rows]
+    )
+    key_grad, value_grad = unpack(
+        place, sections, functools.partial(unpack_crossed_kernel, groups=groups), columns
+    )
     return attended, query_grad, key_grad, value_grad
 
 

time: 104 us -> 102 us (0.981)
  waiting for transfers between devices: 44.4 us -> 37 us
  Pallas kernels: 22.9 us -> 26.8 us
  local copies, waits for them, and re-layouts: 1.25 us -> 3.15 us
    ppermute x18 -> x9, starting transfers between devices: 17 us -> 7.89 us  [in_plane(): lax.ppermute(pieces[m], 'seq', [(i, i ^ m) for i in range(peers)])]
    ppermute x18 -> x9, waiting for transfers between devices: 21.3 us -> 13 us  [in_plane(): lax.ppermute(pieces[m], 'seq', [(i, i ^ m) for i in range(peers)])]
    all_to_all x0 -> x2, starting transfers between devices: none -> 8.04 us  [plane_all_to_all(): lax.all_to_all(value, 'seq', 0, 0, axis_index_groups=planes, tiled=True)]
    pallas_call x8, Pallas kernels: 21.4 us -> 25.2 us  [the longest x2 16.5 us: attend(): pl.pallas_call(functools.partial(attend_kernel, first=first, slot=slot, r...]
    unnamed x28 -> x30, local copies, waits for them, and re-layouts: 1.25 us -> 3.15 us
  transfers between devices with their start and end apart: 27 -> 20, of which waited for: 10 -> 7; matrix products, arithmetic and copies ran while one was open for 0% -> 0% of each run, Pallas kernels for 18% -> 22%
where the time goes in v6:
time: 102 us; the launch traced here: 101 us
  waiting for transfers between devices  37 us (36%)
  starting transfers between devices  32.4 us (32%)
  Pallas kernels  26.8 us (26%)
  local copies, waits for them, and re-layouts  3.15 us (3%)
    ppermute x6, waiting for transfers between devices, partner(): lax.ppermute(value, axis, [(i, i ^ 1 << apart) for i in range(lax.axis_si...  24.1 us
    pallas_call x2, Pallas kernels, attend(): pl.pallas_call(functools.partial(attend_kernel, first=first, slot=slot, r...  16.5 us
    ppermute x6, starting transfers between devices, partner(): lax.ppermute(value, axis, [(i, i ^ 1 << apart) for i in range(lax.axis_si...  13.7 us
    ppermute x9, waiting for transfers between devices, in_plane(): lax.ppermute(pieces[m], 'seq', [(i, i ^ m) for i in range(peers)])  13 us
    all_to_all x2, starting transfers between devices, plane_all_to_all(): lax.all_to_all(value, 'seq', 0, 0, axis_index_groups=planes, tiled=True)  8.04 us
    ppermute x9, starting transfers between devices, in_plane(): lax.ppermute(pieces[m], 'seq', [(i, i ^ m) for i in range(peers)])  7.89 us
    pallas_call x2, Pallas kernels, pack(): pl.pallas_call(functools.partial(pack_kernel, order=order, count=count, c...  4.48 us
    pallas_call x2, Pallas kernels, unpack(): pl.pallas_call(functools.partial(kernel, count=count), grid=(tokens // ch...  3.59 us
  transfers between devices with their start and end apart: 20, of which 7 were waited for; matrix products, arithmetic and copies ran while one was open for 0% of the time, Pallas kernels for 22%

profile of v6, /device:TPU:1, one launch (start us, length us, event | category | flops | bytes accessed | tf_op | source)
XLA Modules:
  0.0 100.9 jit_solution(5366312540542383431)
XLA Ops:
  1.3 2.2 %shard_map.93 = (bf16[4,2,128,128]{3,2,1,0:T(8,128)(2,1)}, bf16[4,2,128,128]{3,2,1,0:T(8,128)(2,1)}, bf16[4,2,128,128]{3,2,1,0:T(8,128)(2,1)}, bf16[4,2,128,128]{3,2,1,0:T(8,128)(2,1)}) custom-call(s32[2]{0:T(128)} %pad_add_fusion.place, s32[4,4]{1,0:T(4,128)} %sections.11, bf16[128,16,128]{2,1,0:T(8,128)(2,1)} %refs_0_.2, bf16[128,16,128]{2,1,0:T(8,128)(2,1)} %refs_1_.2), custom_call_target="tpu_custom_call" | custom-call | bytes 2097152 | tf_op jit(solution)/shard_map/pallas_call | solution.py:124
  3.6 2.7 %collective-permute-start.1 = (bf16[4,2,128,128]{3,2,1,0:T(8,128)(2,1)}, bf16[4,2,128,128]{3,2,1,0:T(8,128)(2,1)S(1)}, u32[]{:S(2)}, u32[]{:S(2)}) collective-permute-start(bf16[4,2,128,128]{3,2,1,0:T(8,128)(2,1)} %get-tuple-element.43), channel_id=1, source_target_pairs={{0,2},{1,3},{2,0},{3,1},{4,6},{5,7},{6,4},{7,5},{8,10},{9,11},{10,... | collective-permute-start | bytes 786440 | tf_op jit(solution)/shard_map/ppermute | solution.py:658
  6.4 2.2 %shard_map.94 = bf16[4,4,2,128,128]{4,3,2,1,0:T(8,128)(2,1)} custom-call(s32[2]{0:T(128)} %pad_add_fusion.place, s32[4,4]{1,0:T(4,128)} %sections.11, bf16[128,16,128]{2,1,0:T(8,128)(2,1)} %refs_0_.3, bf16[128,16,128]{2,1,0:T(8,128)(2,1)} %refs_1_.3), custom_call_target="tpu_custom_call" | custom-call | bytes 2097152 | tf_op jit(solution)/shard_map/pallas_call | solution.py:124
  8.6 4.0 %all-to-all-start = ((bf16[4,4,2,128,128]{4,3,2,1,0:T(8,128)(2,1)}), bf16[4,4,2,128,128]{4,3,2,1,0:T(8,128)(2,1)S(1)}, u32[]{:S(2)}, u32[]{:S(2)}) async-start(bf16[4,4,2,128,128]{4,3,2,1,0:T(8,128)(2,1)} %shard_map.94), calls=%async_computation | async-start | bytes 2097152 | tf_op jit(solution)/shard_map/all_to_all | solution.py:684
  13.1 6.1 %collective-permute-done.2.refs_3_ = bf16[4,2,128,128]{3,2,1,0:T(8,128)(2,1)S(1)} collective-permute-done((bf16[4,2,128,128]{3,2,1,0:T(8,128)(2,1)}, bf16[4,2,128,128]{3,2,1,0:T(8,128)(2,1)S(1)}, u32[]{:S(2)}, u32[]{:S(2)}) %collective-permute-start.2) | collective-permute-done | bytes 262176 | tf_op jit(solution)/shard_map/ppermute | solution.py:658
  19.9 1.8 %collective-permute-start.3 = (bf16[8,2,128,128]{3,2,1,0:T(8,128)(2,1)S(1)}, bf16[8,2,128,128]{3,2,1,0:T(8,128)(2,1)S(1)}, u32[]{:S(2)}, u32[]{:S(2)}) collective-permute-start(bf16[8,2,128,128]{3,2,1,0:T(8,128)(2,1)S(1)} %get-tuple-element.45), channel_id=1, source_target_pairs={{0,4},{1,5},{2,6},{3,7},{4,0},{5,1},{6,2},{7,3},{8,12},{9,13},{10,... | collective-permute-start | bytes 1572872 | tf_op jit(solution)/shard_map/ppermute | solution.py:408
  21.7 1.5 %collective-permute-start.4 = (bf16[8,2,128,128]{3,2,1,0:T(8,128)(2,1)S(1)}, bf16[8,2,128,128]{3,2,1,0:T(8,128)(2,1)}, u32[]{:S(2)}, u32[]{:S(2)}) collective-permute-start(bf16[8,2,128,128]{3,2,1,0:T(8,128)(2,1)S(1)} %get-tuple-element.46), channel_id=1, source_target_pairs={{4,8},{5,9},{6,10},{7,11},{8,4},{9,5},{10,6},{11,7},{20,24},{21,25... | collective-permute-start | bytes 1572872 | tf_op jit(solution)/shard_map/ppermute | solution.py:678
  23.2 3.2 %collective-permute-start.5 = (bf16[4,2,128,128]{3,2,1,0:T(8,128)(2,1)S(1)}, bf16[4,2,128,128]{3,2,1,0:T(8,128)(2,1)S(1)}, u32[]{:S(2)}, u32[]{:S(2)}) collective-permute-start(bf16[4,2,128,128]{3,2,1,0:T(8,128)(2,1)S(1)} %get-tuple-element.47), channel_id=1, source_target_pairs={{0,4},{1,5},{2,6},{3,7},{4,0},{5,1},{6,2},{7,3},{8,12},{9,13},{10,... | collective-permute-start | bytes 786440 | tf_op jit(solution)/shard_map/ppermute | solution.py:408
  26.4 7.7 %collective-permute-done.3.refs_5_ = bf16[8,2,128,128]{3,2,1,0:T(8,128)(2,1)S(1)} collective-permute-done((bf16[8,2,128,128]{3,2,1,0:T(8,128)(2,1)S(1)}, bf16[8,2,128,128]{3,2,1,0:T(8,128)(2,1)S(1)}, u32[]{:S(2)}, u32[]{:S(2)}) %collective-permute-start.3) | collective-permute-done | bytes 524320 | tf_op jit(solution)/shard_map/ppermute | solution.py:408
  34.0 0.8 copy-done.10
  34.8 1.0 copy-done.9
  35.8 8.1 %shard_map.97 = (bf16[4,4,2,128,128]{4,3,2,1,0:T(8,128)(2,1)}, f32[2,4,2,128,128]{4,3,2,1,0:T(8,128)}, bf16[4,2,128,128]{3,2,1,0:T(8,128)(2,1)}, bf16[4,2,128,128]{3,2,1,0:T(8,128)(2,1)}) custom-call(s32[2]{0:T(128)} %pad_add_fusion.place, s32[16]{0:T(128)} %widths.3, s32[4,4]{1,0:T(4,128)} %sections.11, bf16[4,2,128,128]{3,2,1,0:T(8,128)(2,1)} %get-tuple-element.41.refs_0_, ...), custom_call_target="tpu_custom_call" | custom-call | flops 1207959552 | bytes 5242880 | tf_op jit(solution)/shard_map/pallas_call | solution.py:341
  43.9 4.0 %collective-permute-start.7 = (bf16[4,2,128,128]{3,2,1,0:T(8,128)(2,1)}, bf16[4,2,128,128]{3,2,1,0:T(8,128)(2,1)S(1)}, u32[]{:S(2)}, u32[]{:S(2)}) collective-permute-start(bf16[4,2,128,128]{3,2,1,0:T(8,128)(2,1)} %get-tuple-element.54), channel_id=1, source_target_pairs={{0,4},{1,5},{2,6},{3,7},{4,0},{5,1},{6,2},{7,3},{8,12},{9,13},{10,... | collective-permute-start | bytes 786440 | tf_op jit(solution)/shard_map/ppermute | solution.py:408
  47.9 0.7 collective-permute-start.8
  48.6 1.1 %collective-permute-done.6.refs_8_ = bf16[4,2,128,128]{3,2,1,0:T(8,128)(2,1)S(1)} collective-permute-done((bf16[4,2,128,128]{3,2,1,0:T(8,128)(2,1)S(1)}, bf16[4,2,128,128]{3,2,1,0:T(8,128)(2,1)S(1)}, u32[]{:S(2)}, u32[]{:S(2)}) %collective-permute-start.6) | collective-permute-done | bytes 262176 | tf_op jit(solution)/shard_map/ppermute | solution.py:408
  49.7 0.7 copy-done.12
  50.4 8.4 %shard_map.98 = (bf16[4,4,2,128,128]{4,3,2,1,0:T(8,128)(2,1)}, f32[2,4,2,128,128]{4,3,2,1,0:T(8,128)}, bf16[8,2,128,128]{3,2,1,0:T(8,128)(2,1)}, bf16[4,2,128,12...) custom-call(s32[2]{0:T(128)} %pad_add_fusion.place, s32[16]{0:T(128)} %widths.3, ...), custom_call_target="tpu_custom_call", output_to_operand_aliasing={{0}: (12, {})} | custom-call | flops 1207959552 | bytes 5242880 | tf_op jit(solution)/shard_map/pallas_call | solution.py:341
  59.4 0.8 shard_map.99
  60.2 4.0 %all-to-all-start.1 = ((bf16[4,4,2,128,128]{4,3,2,1,0:T(8,128)(2,1)}), bf16[4,4,2,128,128]{4,3,2,1,0:T(8,128)(2,1)S(1)}, u32[]{:S(2)}, u32[]{:S(2)}) async-start(bf16[4,4,2,128,128]{4,3,2,1,0:T(8,128)(2,1)} %get-tuple-element.61), calls=%async_computation.1 | async-start | bytes 2097152 | tf_op jit(solution)/shard_map/all_to_all | solution.py:684
  64.3 2.3 %collective-permute-start.9 = (bf16[8,2,128,128]{3,2,1,0:T(8,128)(2,1)S(1)}, bf16[8,2,128,128]{3,2,1,0:T(8,128)(2,1)S(1)}, u32[]{:S(2)}, u32[]{:S(2)}) collective-permute-start(bf16[8,2,128,128]{3,2,1,0:T(8,128)(2,1)S(1)} %copy-done.13), channel_id=1, source_target_pairs={{0,4},{1,5},{2,6},{3,7},{4,0},{5,1},{6,2},{7,3},{8,12},{9,13},{10,... | collective-permute-start | bytes 1572872 | tf_op jit(solution)/shard_map/ppermute | solution.py:408
  66.6 0.7 collective-permute-start.10
  67.3 2.4 %collective-permute-start.11 = (bf16[4,2,128,128]{3,2,1,0:T(8,128)(2,1)S(1)}, bf16[4,2,128,128]{3,2,1,0:T(8,128)(2,1)S(1)}, u32[]{:S(2)}, u32[]{:S(2)}) collective-permute-start(bf16[4,2,128,128]{3,2,1,0:T(8,128)(2,1)S(1)} %copy-done.14), channel_id=1, source_target_pairs={{0,8},{1,9},{2,10},{3,11},{4,12},{5,13},{6,14},{7,15},{8,0},{9,1},... | collective-permute-start | bytes 786440 | tf_op jit(solution)/shard_map/ppermute | solution.py:408
  69.7 0.7 collective-permute-start.15
  70.4 1.6 %collective-permute-start.16 = (bf16[2,2,128,128]{3,2,1,0:T(8,128)(2,1)S(1)}, bf16[2,2,128,128]{3,2,1,0:T(8,128)(2,1)S(1)}, u32[]{:S(2)}, u32[]{:S(2)}) collective-permute-start(bf16[2,2,128,128]{3,2,1,0:T(8,128)(2,1)S(1)} %get-tuple-element.74), channel_id=1, source_target_pairs={{0,2},{1,3},{2,0},{3,1},{4,6},{5,7},{6,4},{7,5},{8,10},{9,11},{10,... | collective-permute-start | bytes 393224 | tf_op jit(solution)/shard_map/ppermute | solution.py:658
  72.1 15.3 %collective-permute-done.11.refs_0_ = bf16[4,2,128,128]{3,2,1,0:T(8,128)(2,1)S(1)} collective-permute-done((bf16[4,2,128,128]{3,2,1,0:T(8,128)(2,1)S(1)}, bf16[4,2,128,128]{3,2,1,0:T(8,128)(2,1)S(1)}, u32[]{:S(2)}, u32[]{:S(2)}) %collective-permute-start.11) | collective-permute-done | bytes 262176 | tf_op jit(solution)/shard_map/ppermute | solution.py:408
  87.4 0.9 shard_map.101
  88.3 1.0 %collective-permute-start.12 = (bf16[2,2,128,128]{3,2,1,0:T(8,128)(2,1)S(1)}, bf16[2,2,128,128]{3,2,1,0:T(8,128)(2,1)S(1)}, u32[]{:S(2)}, u32[]{:S(2)}) collective-permute-start(bf16[2,2,128,128]{3,2,1,0:T(8,128)(2,1)S(1)} %get-tuple-element.69), channel_id=1, source_target_pairs={{0,1},{1,0},{2,3},{3,2},{4,5},{5,4},{6,7},{7,6},{8,9},{9,8},{10,11... | collective-permute-start | bytes 393224 | tf_op jit(solution)/shard_map/ppermute | solution.py:658
  89.3 1.4 %collective-permute-start.13 = (bf16[2,2,128,128]{3,2,1,0:T(8,128)(2,1)S(1)}, bf16[2,2,128,128]{3,2,1,0:T(8,128)(2,1)S(1)}, u32[]{:S(2)}, u32[]{:S(2)}) collective-permute-start(bf16[2,2,128,128]{3,2,1,0:T(8,128)(2,1)S(1)} %get-tuple-element.70), channel_id=1, source_target_pairs={{0,2},{1,3},{2,0},{3,1},{4,6},{5,7},{6,4},{7,5},{8,10},{9,11},{10,... | collective-permute-start | bytes 393224 | tf_op jit(solution)/shard_map/ppermute | solution.py:658
  91.0 3.3 %collective-permute-done.13.refs_2_ = bf16[2,2,128,128]{3,2,1,0:T(8,128)(2,1)S(1)} collective-permute-done((bf16[2,2,128,128]{3,2,1,0:T(8,128)(2,1)S(1)}, bf16[2,2,128,128]{3,2,1,0:T(8,128)(2,1)S(1)}, u32[]{:S(2)}, u32[]{:S(2)}) %collective-permute-start.13) | collective-permute-done | bytes 131104 | tf_op jit(solution)/shard_map/ppermute | solution.py:658
  94.4 3.0 %collective-permute-done.14.refs_3_ = bf16[2,2,128,128]{3,2,1,0:T(8,128)(2,1)S(1)} collective-permute-done((bf16[2,2,128,128]{3,2,1,0:T(8,128)(2,1)S(1)}, bf16[2,2,128,128]{3,2,1,0:T(8,128)(2,1)S(1)}, u32[]{:S(2)}, u32[]{:S(2)}) %collective-permute-start.14) | collective-permute-done | bytes 131104 | tf_op jit(solution)/shard_map/ppermute | solution.py:658
  97.4 1.8 %shard_map.102 = (bf16[128,16,128]{2,1,0:T(8,128)(2,1)}, bf16[128,16,128]{2,1,0:T(8,128)(2,1)}) custom-call(s32[2]{0:T(128)S(1)} %copy-done.8, s32[4,4]{1,0:T(4,128)S(1)} %copy-done.6, bf16[2,2,128,128]{3,2,1,0:T(8,128)(2,1)S(1)} %get-tuple-element.68.refs_0_, bf16[2,2,128,128]{3,2,1,0:T(8,128)(2,1)S(1)} %collective-permute-done.12.refs_1_, ...), custom_call_target="tpu_custom_call" | custom-call | bytes 2097152 | tf_op jit(solution)/shard_map/pallas_call | solution.py:163
  99.2 1.8 %shard_map.100 = (bf16[128,16,128]{2,1,0:T(8,128)(2,1)}, bf16[128,16,128]{2,1,0:T(8,128)(2,1)}) custom-call(s32[2]{0:T(128)S(1)} %copy-done.8, s32[4,4]{1,0:T(4,128)S(1)} %copy-done.6, bf16[4,4,2,128,128]{4,3,2,1,0:T(8,128)(2,1)S(1)} %all-to-all-done.1.src), custom_call_target="tpu_custom_call" | custom-call | bytes 2097152 | tf_op jit(solution)/shard_map/pallas_call | solution.py:163
  (49 shorter events, 3.1 us)
Async XLA Ops:
  3.6 9.0 %collective-permute-start = (bf16[4,2,128,128]{3,2,1,0:T(8,128)(2,1)}, bf16[4,2,128,128]{3,2,1,0:T(8,128)(2,1)S(1)}, u32[]{:S(2)}, u32[]{:S(2)}) collective-permute-start(bf16[4,2,128,128]{3,2,1,0:T(8,128)(2,1)} %get-tuple-element.42), channel_id=1, source_target_pairs={{0,1},{1,0},{2,3},{3,2},{4,5},{5,4},{6,7},{7,6},{8,9},{9,8},{10,11... | collective-permute-start | bytes 786440 | tf_op jit(solution)/shard_map/ppermute | solution.py:658
  3.6 9.5 %collective-permute-start.1 = (bf16[4,2,128,128]{3,2,1,0:T(8,128)(2,1)}, bf16[4,2,128,128]{3,2,1,0:T(8,128)(2,1)S(1)}, u32[]{:S(2)}, u32[]{:S(2)}) collective-permute-start(bf16[4,2,128,128]{3,2,1,0:T(8,128)(2,1)} %get-tuple-element.43), channel_id=1, source_target_pairs={{0,2},{1,3},{2,0},{3,1},{4,6},{5,7},{6,4},{7,5},{8,10},{9,11},{10,... | collective-permute-start | bytes 786440 | tf_op jit(solution)/shard_map/ppermute | solution.py:658
  6.3 12.9 %collective-permute-start.2 = (bf16[4,2,128,128]{3,2,1,0:T(8,128)(2,1)}, bf16[4,2,128,128]{3,2,1,0:T(8,128)(2,1)S(1)}, u32[]{:S(2)}, u32[]{:S(2)}) collective-permute-start(bf16[4,2,128,128]{3,2,1,0:T(8,128)(2,1)} %get-tuple-element.44), channel_id=1, source_target_pairs={{0,3},{1,2},{2,1},{3,0},{4,7},{5,6},{6,5},{7,4},{8,11},{9,10},{10,... | collective-permute-start | bytes 786440 | tf_op jit(solution)/shard_map/ppermute | solution.py:658
  8.6 10.7 %copy-start = (bf16[4,2,128,128]{3,2,1,0:T(8,128)(2,1)S(1)}, bf16[4,2,128,128]{3,2,1,0:T(8,128)(2,1)}, u32[]{:S(2)}) copy-start(bf16[4,2,128,128]{3,2,1,0:T(8,128)(2,1)} %get-tuple-element.41.refs_0_) | copy-start | bytes 786436
  8.6 25.4 %all-to-all-start = ((bf16[4,4,2,128,128]{4,3,2,1,0:T(8,128)(2,1)}), bf16[4,4,2,128,128]{4,3,2,1,0:T(8,128)(2,1)S(1)}, u32[]{:S(2)}, u32[]{:S(2)}) async-start(bf16[4,4,2,128,128]{4,3,2,1,0:T(8,128)(2,1)} %shard_map.94), calls=%async_computation | async-start | bytes 2097152 | tf_op jit(solution)/shard_map/all_to_all | solution.py:684
  12.6 6.7 %copy-start.7 = (s32[2]{0:T(128)S(1)}, s32[2]{0:T(128)}, u32[]{:S(2)}) copy-start(s32[2]{0:T(128)} %pad_add_fusion.place) | copy-start | bytes 28
  12.6 10.6 %copy-start.1 = (bf16[4,2,128,128]{3,2,1,0:T(8,128)(2,1)}, bf16[4,2,128,128]{3,2,1,0:T(8,128)(2,1)S(1)}, u32[]{:S(2)}) copy-start(bf16[4,2,128,128]{3,2,1,0:T(8,128)(2,1)S(1)} %collective-permute-done.refs_1_) | copy-start | bytes 786436
  13.1 10.0 %copy-start.2 = (bf16[4,2,128,128]{3,2,1,0:T(8,128)(2,1)}, bf16[4,2,128,128]{3,2,1,0:T(8,128)(2,1)S(1)}, u32[]{:S(2)}) copy-start(bf16[4,2,128,128]{3,2,1,0:T(8,128)(2,1)S(1)} %collective-permute-done.1.refs_2_) | copy-start | bytes 786436
  19.2 3.9 %copy-start.3 = (bf16[4,2,128,128]{3,2,1,0:T(8,128)(2,1)}, bf16[4,2,128,128]{3,2,1,0:T(8,128)(2,1)S(1)}, u32[]{:S(2)}) copy-start(bf16[4,2,128,128]{3,2,1,0:T(8,128)(2,1)S(1)} %collective-permute-done.2.refs_3_) | copy-start | bytes 786436
  19.9 14.1 %collective-permute-start.3 = (bf16[8,2,128,128]{3,2,1,0:T(8,128)(2,1)S(1)}, bf16[8,2,128,128]{3,2,1,0:T(8,128)(2,1)S(1)}, u32[]{:S(2)}, u32[]{:S(2)}) collective-permute-start(bf16[8,2,128,128]{3,2,1,0:T(8,128)(2,1)S(1)} %get-tuple-element.45), channel_id=1, source_target_pairs={{0,4},{1,5},{2,6},{3,7},{4,0},{5,1},{6,2},{7,3},{8,12},{9,13},{10,... | collective-permute-start | bytes 1572872 | tf_op jit(solution)/shard_map/ppermute | solution.py:408
  21.7 12.3 %collective-permute-start.4 = (bf16[8,2,128,128]{3,2,1,0:T(8,128)(2,1)S(1)}, bf16[8,2,128,128]{3,2,1,0:T(8,128)(2,1)}, u32[]{:S(2)}, u32[]{:S(2)}) collective-permute-start(bf16[8,2,128,128]{3,2,1,0:T(8,128)(2,1)S(1)} %get-tuple-element.46), channel_id=1, source_target_pairs={{4,8},{5,9},{6,10},{7,11},{8,4},{9,5},{10,6},{11,7},{20,24},{21,25... | collective-permute-start | bytes 1572872 | tf_op jit(solution)/shard_map/ppermute | solution.py:678
  23.2 25.4 %collective-permute-start.5 = (bf16[4,2,128,128]{3,2,1,0:T(8,128)(2,1)S(1)}, bf16[4,2,128,128]{3,2,1,0:T(8,128)(2,1)S(1)}, u32[]{:S(2)}, u32[]{:S(2)}) collective-permute-start(bf16[4,2,128,128]{3,2,1,0:T(8,128)(2,1)S(1)} %get-tuple-element.47), channel_id=1, source_target_pairs={{0,4},{1,5},{2,6},{3,7},{4,0},{5,1},{6,2},{7,3},{8,12},{9,13},{10,... | collective-permute-start | bytes 786440 | tf_op jit(solution)/shard_map/ppermute | solution.py:408
  26.4 23.3 %collective-permute-start.6 = (bf16[4,2,128,128]{3,2,1,0:T(8,128)(2,1)S(1)}, bf16[4,2,128,128]{3,2,1,0:T(8,128)(2,1)S(1)}, u32[]{:S(2)}, u32[]{:S(2)}) collective-permute-start(bf16[4,2,128,128]{3,2,1,0:T(8,128)(2,1)S(1)} %get-tuple-element.48), channel_id=1, source_target_pairs={{0,8},{1,9},{2,10},{3,11},{4,12},{5,13},{6,14},{7,15},{8,0},{9,1},... | collective-permute-start | bytes 786440 | tf_op jit(solution)/shard_map/ppermute | solution.py:408
  34.8 1.0 copy-start.9
  43.9 14.9 %collective-permute-start.7 = (bf16[4,2,128,128]{3,2,1,0:T(8,128)(2,1)}, bf16[4,2,128,128]{3,2,1,0:T(8,128)(2,1)S(1)}, u32[]{:S(2)}, u32[]{:S(2)}) collective-permute-start(bf16[4,2,128,128]{3,2,1,0:T(8,128)(2,1)} %get-tuple-element.54), channel_id=1, source_target_pairs={{0,4},{1,5},{2,6},{3,7},{4,0},{5,1},{6,2},{7,3},{8,12},{9,13},{10,... | collective-permute-start | bytes 786440 | tf_op jit(solution)/shard_map/ppermute | solution.py:408
  47.9 10.9 %collective-permute-start.8 = (bf16[4,2,128,128]{3,2,1,0:T(8,128)(2,1)}, bf16[4,2,128,128]{3,2,1,0:T(8,128)(2,1)S(1)}, u32[]{:S(2)}, u32[]{:S(2)}) collective-permute-start(bf16[4,2,128,128]{3,2,1,0:T(8,128)(2,1)} %get-tuple-element.55), channel_id=1, source_target_pairs={{4,8},{5,9},{6,10},{7,11},{8,4},{9,5},{10,6},{11,7},{20,24},{21,25... | collective-permute-start | bytes 786440 | tf_op jit(solution)/shard_map/ppermute | solution.py:678
  48.6 1.1 %copy-start.11 = (bf16[4,2,128,128]{3,2,1,0:T(8,128)(2,1)}, bf16[4,2,128,128]{3,2,1,0:T(8,128)(2,1)S(1)}, u32[]{:S(2)}) copy-start(bf16[4,2,128,128]{3,2,1,0:T(8,128)(2,1)S(1)} %collective-permute-done.5.refs_7_) | copy-start | bytes 786436
  50.4 8.4 %copy-start.5 = (f32[2,4,2,128,128]{4,3,2,1,0:T(8,128)S(1)}, f32[2,4,2,128,128]{4,3,2,1,0:T(8,128)}, u32[]{:S(2)}) copy-start(f32[2,4,2,128,128]{4,3,2,1,0:T(8,128)} %get-tuple-element.53.part) | copy-start | bytes 3145732
  60.2 4.1 %copy-start.13 = (bf16[8,2,128,128]{3,2,1,0:T(8,128)(2,1)S(1)}, bf16[8,2,128,128]{3,2,1,0:T(8,128)(2,1)}, u32[]{:S(2)}) copy-start(bf16[8,2,128,128]{3,2,1,0:T(8,128)(2,1)} %get-tuple-element.65) | copy-start | bytes 1572868
  60.2 7.0 %copy-start.14 = (bf16[4,2,128,128]{3,2,1,0:T(8,128)(2,1)S(1)}, bf16[4,2,128,128]{3,2,1,0:T(8,128)(2,1)}, u32[]{:S(2)}) copy-start(bf16[4,2,128,128]{3,2,1,0:T(8,128)(2,1)} %get-tuple-element.67) | copy-start | bytes 786436
  60.2 27.2 %copy-start.4 = (f32[2,4,2,128,128]{4,3,2,1,0:T(8,128)S(1)}, f32[2,4,2,128,128]{4,3,2,1,0:T(8,128)}, u32[]{:S(2)}) copy-start(f32[2,4,2,128,128]{4,3,2,1,0:T(8,128)} %get-tuple-element.64.part) | copy-start | bytes 3145732
  60.2 38.9 %all-to-all-start.1 = ((bf16[4,4,2,128,128]{4,3,2,1,0:T(8,128)(2,1)}), bf16[4,4,2,128,128]{4,3,2,1,0:T(8,128)(2,1)S(1)}, u32[]{:S(2)}, u32[]{:S(2)}) async-start(bf16[4,4,2,128,128]{4,3,2,1,0:T(8,128)(2,1)} %get-tuple-element.61), calls=%async_computation.1 | async-start | bytes 2097152 | tf_op jit(solution)/shard_map/all_to_all | solution.py:684
  64.3 23.1 %collective-permute-start.9 = (bf16[8,2,128,128]{3,2,1,0:T(8,128)(2,1)S(1)}, bf16[8,2,128,128]{3,2,1,0:T(8,128)(2,1)S(1)}, u32[]{:S(2)}, u32[]{:S(2)}) collective-permute-start(bf16[8,2,128,128]{3,2,1,0:T(8,128)(2,1)S(1)} %copy-done.13), channel_id=1, source_target_pairs={{0,4},{1,5},{2,6},{3,7},{4,0},{5,1},{6,2},{7,3},{8,12},{9,13},{10,... | collective-permute-start | bytes 1572872 | tf_op jit(solution)/shard_map/ppermute | solution.py:408
  66.6 5.4 %collective-permute-start.10 = (bf16[4,2,128,128]{3,2,1,0:T(8,128)(2,1)}, bf16[4,2,128,128]{3,2,1,0:T(8,128)(2,1)S(1)}, u32[]{:S(2)}, u32[]{:S(2)}) collective-permute-start(bf16[4,2,128,128]{3,2,1,0:T(8,128)(2,1)} %get-tuple-element.66), channel_id=1, source_target_pairs={{4,8},{5,9},{6,10},{7,11},{8,4},{9,5},{10,6},{11,7},{20,24},{21,25... | collective-permute-start | bytes 786440 | tf_op jit(solution)/shard_map/ppermute | solution.py:678
  67.3 20.1 %collective-permute-start.11 = (bf16[4,2,128,128]{3,2,1,0:T(8,128)(2,1)S(1)}, bf16[4,2,128,128]{3,2,1,0:T(8,128)(2,1)S(1)}, u32[]{:S(2)}, u32[]{:S(2)}) collective-permute-start(bf16[4,2,128,128]{3,2,1,0:T(8,128)(2,1)S(1)} %copy-done.14), channel_id=1, source_target_pairs={{0,8},{1,9},{2,10},{3,11},{4,12},{5,13},{6,14},{7,15},{8,0},{9,1},... | collective-permute-start | bytes 786440 | tf_op jit(solution)/shard_map/ppermute | solution.py:408
  69.7 21.0 %collective-permute-start.15 = (bf16[2,2,128,128]{3,2,1,0:T(8,128)(2,1)S(1)}, bf16[2,2,128,128]{3,2,1,0:T(8,128)(2,1)S(1)}, u32[]{:S(2)}, u32[]{:S(2)}) collective-permute-start(bf16[2,2,128,128]{3,2,1,0:T(8,128)(2,1)S(1)} %get-tuple-element.73), channel_id=1, source_target_pairs={{0,1},{1,0},{2,3},{3,2},{4,5},{5,4},{6,7},{7,6},{8,9},{9,8},{10,11... | collective-permute-start | bytes 393224 | tf_op jit(solution)/shard_map/ppermute | solution.py:658
  70.4 20.6 %collective-permute-start.16 = (bf16[2,2,128,128]{3,2,1,0:T(8,128)(2,1)S(1)}, bf16[2,2,128,128]{3,2,1,0:T(8,128)(2,1)S(1)}, u32[]{:S(2)}, u32[]{:S(2)}) collective-permute-start(bf16[2,2,128,128]{3,2,1,0:T(8,128)(2,1)S(1)} %get-tuple-element.74), channel_id=1, source_target_pairs={{0,2},{1,3},{2,0},{3,1},{4,6},{5,7},{6,4},{7,5},{8,10},{9,11},{10,... | collective-permute-start | bytes 393224 | tf_op jit(solution)/shard_map/ppermute | solution.py:658
  72.0 19.0 %collective-permute-start.17 = (bf16[2,2,128,128]{3,2,1,0:T(8,128)(2,1)S(1)}, bf16[2,2,128,128]{3,2,1,0:T(8,128)(2,1)S(1)}, u32[]{:S(2)}, u32[]{:S(2)}) collective-permute-start(bf16[2,2,128,128]{3,2,1,0:T(8,128)(2,1)S(1)} %get-tuple-element.75), channel_id=1, source_target_pairs={{0,3},{1,2},{2,1},{3,0},{4,7},{5,6},{6,5},{7,4},{8,11},{9,10},{10,... | collective-permute-start | bytes 393224 | tf_op jit(solution)/shard_map/ppermute | solution.py:658
  88.3 2.8 %collective-permute-start.12 = (bf16[2,2,128,128]{3,2,1,0:T(8,128)(2,1)S(1)}, bf16[2,2,128,128]{3,2,1,0:T(8,128)(2,1)S(1)}, u32[]{:S(2)}, u32[]{:S(2)}) collective-permute-start(bf16[2,2,128,128]{3,2,1,0:T(8,128)(2,1)S(1)} %get-tuple-element.69), channel_id=1, source_target_pairs={{0,1},{1,0},{2,3},{3,2},{4,5},{5,4},{6,7},{7,6},{8,9},{9,8},{10,11... | collective-permute-start | bytes 393224 | tf_op jit(solution)/shard_map/ppermute | solution.py:658
  89.3 8.1 %copy-start.6 = (s32[4,4]{1,0:T(4,128)S(1)}, s32[4,4]{1,0:T(4,128)}, u32[]{:S(2)}) copy-start(s32[4,4]{1,0:T(4,128)} %sections.11) | copy-start | bytes 196
  89.3 5.1 %collective-permute-start.13 = (bf16[2,2,128,128]{3,2,1,0:T(8,128)(2,1)S(1)}, bf16[2,2,128,128]{3,2,1,0:T(8,128)(2,1)S(1)}, u32[]{:S(2)}, u32[]{:S(2)}) collective-permute-start(bf16[2,2,128,128]{3,2,1,0:T(8,128)(2,1)S(1)} %get-tuple-element.70), channel_id=1, source_target_pairs={{0,2},{1,3},{2,0},{3,1},{4,6},{5,7},{6,4},{7,5},{8,10},{9,11},{10,... | collective-permute-start | bytes 393224 | tf_op jit(solution)/shard_map/ppermute | solution.py:658
  90.7 6.6 %collective-permute-start.14 = (bf16[2,2,128,128]{3,2,1,0:T(8,128)(2,1)S(1)}, bf16[2,2,128,128]{3,2,1,0:T(8,128)(2,1)S(1)}, u32[]{:S(2)}, u32[]{:S(2)}) collective-permute-start(bf16[2,2,128,128]{3,2,1,0:T(8,128)(2,1)S(1)} %get-tuple-element.71), channel_id=1, source_target_pairs={{0,3},{1,2},{2,1},{3,0},{4,7},{5,6},{6,5},{7,4},{8,11},{9,10},{10,... | collective-permute-start | bytes 393224 | tf_op jit(solution)/shard_map/ppermute | solution.py:658
  (3 other events, 2.2 us)

commit v7 on v6

--- a/solution.py
+++ b/solution.py
@@ -232,146 +232,132 @@
     )(place, *pieces)
 
 
-def attend_kernel(place, widths, sections, *refs, first, slot, remote, blocks, aliased):
+def attend_kernel(place, widths, sections, *refs, first, slot, group, remote, blocks, aliased):
     pairs, (graded, with_next, with_last) = refs[:PLANE], refs[PLANE : PLANE + 3]
     rest = refs[PLANE + 3 :]
     if remote:
         far_in, rest = rest[:2], rest[2:]
     rest = rest[aliased:]
-    (rows, part, to_next, to_last), rest = rest[:4], rest[4:]
+    rows, rest = rest[:PLANE], rest[PLANE:]
+    (part, to_next, to_last), rest = rest[:3], rest[3:]
     if remote:
         to_other, rest = rest[0], rest[1:]
-    keys, values, far_keys, far_values, queries, grads, attended, dq = rest[:8]
-    accs, far_accs = rest[8:10], rest[10:12]
-    k = pl.program_id(0)
-    group = pl.num_programs(0)
-    section = first + k
+    keys, values, far_keys, far_values, attended, dq = rest[:6]
+    accs, far_accs = rest[6:8], rest[8:10]
     me = place[0]
-    width = widths[sections[section, me]]
-    bit = jnp.left_shift(jnp.int32(1), section)
-    far_bias = jnp.where(bit >= width, 0.0, blocked_score).astype(jnp.float32)
     scales = (1.0 / math.sqrt(keys.shape[-1]), 1.0)
     lead = PLANE if remote else 0
-    pairs_slots = with_next.shape[0] // HALO
+    slots = with_next.shape[0] // HALO
     next_at = jnp.where(place[1] % 2 == 0, HALO + PLANE, 0)
     last_at = HALO + PLANE - next_at
-    for m in range(PLANE):
-        b = me ^ m
-        keys[rows_of(HALO + b)] = pairs[m][0, 0]
-        values[rows_of(HALO + b)] = pairs[m][0, 1]
-        queries[m * BLK : (m + 1) * BLK] = graded[m, 0, 0]
-        grads[m * BLK : (m + 1) * BLK] = graded[m, 0, 1]
-    for m in range(HALO):
-        b = (me % HALO) ^ m
-        at = m * pairs_slots + slot + k
-        keys[rows_of(next_at + b)] = with_next[at, 0]
-        values[rows_of(next_at + b)] = with_next[at, 1]
-        keys[rows_of(last_at + b)] = with_last[at, 0]
-        values[rows_of(last_at + b)] = with_last[at, 1]
-    if remote:
-        for n, source in enumerate(far_in):
-
-            @pl.when(k == n)
-            def _(source=source):
-                for m in range(PLANE):
-                    far_keys[rows_of(me ^ m)] = source[m, 0]
-                    far_values[rows_of(me ^ m)] = source[m, 1]
-    else:
-        for b in range(PLANE):
-            far_keys[rows_of(b)] = keys[rows_of(HALO + (b ^ bit))]
-            far_values[rows_of(b)] = values[rows_of(HALO + (b ^ bit))]
-    for acc in accs:
-        acc[...] = jnp.zeros_like(acc)
-    for b in range(0, PLANE, 2):
-        own = slice(b * BLK, (b + 2) * BLK)
-        seen = slice(b * BLK, (b + 2 * HALO + 2) * BLK)
-        one = [slice((b + r) * BLK, (b + r + 1) * BLK) for r in range(2)]
-        o, d, key_near, value_near, key_far, value_far = attend_pair(
-            queries[own],
-            grads[own],
-            keys[seen],
-            values[seen],
-            [far_keys[one[r]] for r in range(2)],
-            [far_values[one[r]] for r in range(2)],
-            near_biases(place[1] * PLANE + b, width, 0, blocks),
-            far_bias,
-        )
-        attended[own] = o
-        dq[own] = d
-        for acc, near in zip(accs, (key_near, value_near)):
-            acc[:, seen] += near
-        for acc, far in zip(far_accs, (key_far, value_far)):
-            for r in range(2):
-                acc[:, one[r]] = far[r]
-    for i, (acc, far_acc) in enumerate(zip(accs, far_accs)):
-        if remote:
-            for n, target in enumerate((to_next, to_other)):
-
-                @pl.when(k == n)
-                def _(target=target, i=i, far_acc=far_acc):
-                    for m in range(PLANE):
-                        target[m, i] = (far_acc[:, rows_of(me ^ m)] * scales[i]).astype(
-                            jnp.bfloat16
-                        )
-        else:
-            for b in range(PLANE):
-                acc[:, rows_of(HALO + (b ^ bit))] += far_acc[:, b * BLK : (b + 1) * BLK]
+    for k in range(group):
+        width = widths[sections[first + k, me]]
+        bit = 1 << first + k
+        far_bias = jnp.where(bit >= width, 0.0, blocked_score).astype(jnp.float32)
         for m in range(PLANE):
-            part[0, m, i] = acc[:, rows_of(HALO + (me ^ m))] * scales[i]
+            keys[rows_of(HALO + (me ^ m))] = pairs[m][slot + k, 0]
+            values[rows_of(HALO + (me ^ m))] = pairs[m][slot + k, 1]
         for m in range(HALO):
             b = (me % HALO) ^ m
-            at = m * group + k
-            to_next[lead + at, i] = (acc[:, rows_of(next_at + b)] * scales[i]).astype(jnp.bfloat16)
-            to_last[at, i] = (acc[:, rows_of(last_at + b)] * scales[i]).astype(jnp.bfloat16)
-    for b in range(PLANE):
-        rows[b, 0, 0] = attended[b * BLK : (b + 1) * BLK]
-        rows[b, 0, 1] = dq[b * BLK : (b + 1) * BLK]
+            at = m * slots + slot + k
+            keys[rows_of(next_at + b)] = with_next[at, 0]
+            values[rows_of(next_at + b)] = with_next[at, 1]
+            keys[rows_of(last_at + b)] = with_last[at, 0]
+            values[rows_of(last_at + b)] = with_last[at, 1]
+        if remote:
+            for m in range(PLANE):
+                far_keys[rows_of(me ^ m)] = far_in[k][m, 0]
+                far_values[rows_of(me ^ m)] = far_in[k][m, 1]
+        for acc in accs:
+            acc[...] = jnp.zeros_like(acc)
+        for b in range(0, PLANE, 2):
+            own = slice(b * BLK, (b + 2) * BLK)
+            seen = slice(b * BLK, (b + 2 * HALO + 2) * BLK)
+            one = [slice((b + r) * BLK, (b + r + 1) * BLK) for r in range(2)]
+            if remote:
+                kf, vf = [[ref[at] for at in one] for ref in (far_keys, far_values)]
+            else:
+                there = [HALO + ((b + r) ^ bit) for r in range(2)]
+                kf, vf = [
+                    [ref[at * BLK : (at + 1) * BLK] for at in there] for ref in (keys, values)
+                ]
+            o, d, key_near, value_near, key_far, value_far = attend_pair(
+                jnp.concatenate([graded[b, slot + k, 0], graded[b + 1, slot + k, 0]], axis=0),
+                jnp.concatenate([graded[b, slot + k, 1], graded[b + 1, slot + k, 1]], axis=0),
+                keys[seen],
+                values[seen],
+                kf,
+                vf,
+                near_biases(place[1] * PLANE + b, width, 0, blocks),
+                far_bias,
+            )
+            attended[own] = o
+            dq[own] = d
+            for acc, near in zip(accs, (key_near, value_near)):
+                acc[:, seen] += near
+            for acc, far_acc, far in zip(accs, far_accs, (key_far, value_far)):
+                for r in range(2):
+                    if remote:
+                        far_acc[:, one[r]] = far[r]
+                    else:
+                        acc[:, there[r] * BLK : (there[r] + 1) * BLK] += far[r]
+        for i, (acc, far_acc) in enumerate(zip(accs, far_accs)):
+            if remote:
+                target = (to_next, to_other)[k]
+                for m in range(PLANE):
+                    owed = far_acc[:, rows_of(me ^ m)] * scales[i]
+                    target[m, i] = owed.astype(jnp.bfloat16)
+            for m in range(PLANE):
+                part[k, m, i] = acc[:, rows_of(HALO + (me ^ m))] * scales[i]
+            for m in range(HALO):
+                b = (me % HALO) ^ m
+                at = m * group + k
+                to_next[lead + at, i] = (acc[:, rows_of(next_at + b)] * scales[i]).astype(
+                    jnp.bfloat16
+                )
+                to_last[at, i] = (acc[:, rows_of(last_at + b)] * scales[i]).astype(jnp.bfloat16)
+        for m in range(PLANE):
+            rows[m][slot + k, 0] = attended[rows_of(me ^ m)]
+            rows[m][slot + k, 1] = dq[rows_of(me ^ m)]
 
 
 def attend(place, widths, sections, pairs, graded, halos, far, group, first, slot, blocks, rows=()):
     count, _, width = pairs[0].shape[1:]
     tile = (BLK, width)
     remote = len(far)
-    piece = pl.BlockSpec((1, count, *tile), lambda k: (slot + k, 0, 0, 0))
-    row_piece = pl.BlockSpec((PLANE, 1, count, *tile), lambda k: (0, slot + k, 0, 0, 0))
     bf16 = jnp.bfloat16
     owed = [(HALO * group + (PLANE if remote else 0), count, *tile), (HALO * group, count, *tile)]
     if remote:
         owed.append((PLANE, count, *tile))
+    inputs = (*pairs, graded, *halos, *far, *rows)
     outs = pl.pallas_call(
         functools.partial(
             attend_kernel,
             first=first,
             slot=slot,
+            group=group,
             remote=remote,
             blocks=blocks,
             aliased=len(rows),
         ),
-        grid=(group,),
-        in_specs=[SMEM] * 3
-        + [piece] * PLANE
-        + [row_piece]
-        + [whole(halo.shape) for halo in (*halos, *far)]
-        + [pl.BlockSpec(memory_space=pl.ANY)] * len(rows),
-        out_specs=[row_piece, pl.BlockSpec((1, PLANE, count, *tile), lambda k: (k, 0, 0, 0, 0))]
-        + [whole(shape) for shape in owed],
-        out_shape=[
-            jax.ShapeDtypeStruct(graded.shape, bf16),
-            jax.ShapeDtypeStruct((group, PLANE, count, *tile), jnp.float32),
-        ]
+        in_specs=[SMEM] * 3 + [VMEM] * len(inputs),
+        out_specs=[VMEM] * (PLANE + 1 + len(owed)),
+        out_shape=[jax.ShapeDtypeStruct(pairs[0].shape, bf16)] * PLANE
+        + [jax.ShapeDtypeStruct((group, PLANE, count, *tile), jnp.float32)]
         + [jax.ShapeDtypeStruct(shape, bf16) for shape in owed],
         scratch_shapes=[pltpu.VMEM((PADDED * BLK, width), bf16)] * 2
-        + [pltpu.VMEM((PLANE * BLK, width), bf16)] * 6
+        + [pltpu.VMEM((PLANE * BLK, width), bf16)] * 4
         + [pltpu.VMEM((width, PADDED * BLK), jnp.float32)] * 2
         + [pltpu.VMEM((width, PLANE * BLK), jnp.float32)] * 2,
-        input_output_aliases={4 + PLANE + len(halos) + len(far): 0} if rows else {},
+        input_output_aliases={3 + len(inputs) - len(rows) + m: m for m in range(len(rows))},
+        compiler_params=LIMIT,
         cost_estimate=pl.CostEstimate(
             flops=group * PLANE * 12 * BLK * LINKED * width,
             transcendentals=group * PLANE * BLK * LINKED,
             bytes_accessed=40 * group * PLANE * BLK * width,
         ),
-    )(place, widths, sections, *pairs, graded, *halos, *far, *rows)
-    return outs[0], outs[1], outs[2:]
+    )(place, widths, sections, *inputs)
+    return outs[:PLANE], outs[PLANE], outs[PLANE + 1 :]
 
 
 def combine_kernel(place, part, with_next, with_last, *refs, remote):
@@ -706,18 +692,21 @@
     )
     owed_near = [with_next_plane(owed[0]), with_last_plane(owed[1])]
     rows, part_far, owed = attend(
-        *tables, pairs, graded, halos, far, total - local, local, 0, blocks, (rows,)
+        *tables, pairs, graded, halos, far, total - local, local, 0, blocks, rows
     )
     near = combine(place, part_near, owed_near)
     owed, near, rows = lax.optimization_barrier((owed, near, rows))
     other_back = with_other_plane(owed[2])
     owed_far = [with_next_plane(owed[0]), with_last_plane(owed[1]), other_back]
     near = in_plane(near)
-    rows = plane_all_to_all(rows)
+    attended, query_grad = unpack(
+        place,
+        sections,
+        functools.partial(unpack_crossed_kernel, groups=[order]),
+        in_plane(rows),
+    )
+    owed_far, attended, query_grad = lax.optimization_barrier((owed_far, attended, query_grad))
     columns = in_plane(combine(place, part_far, owed_far)) + near
-    attended, query_grad = unpack(
-        place, sections, functools.partial(unpack_kernel, order=order), [rows]
-    )
     key_grad, value_grad = unpack(
         place, sections, functools.partial(unpack_crossed_kernel, groups=groups), columns
     )

time: 102 us -> 93.4 us (0.916)
  Pallas kernels: 26.8 us -> 22.6 us
  local copies, waits for them, and re-layouts: 3.15 us -> 0.01 us
  starting transfers between devices: 32.4 us -> 31.2 us
    ppermute x9 -> x12, waiting for transfers between devices: 13 us -> 18.4 us  [in_plane(): lax.ppermute(pieces[m], 'seq', [(i, i ^ m) for i in range(peers)])]
    pallas_call x2, Pallas kernels: 16.5 us -> 11.4 us  [attend(): pl.pallas_call(functools.partial(attend_kernel, first=first, slot=slot, g...]
    ppermute x6, waiting for transfers between devices: 24.1 us -> 19.5 us  [partner(): lax.ppermute(value, axis, [(i, i ^ 1 << apart) for i in range(lax.axis_si...]
    all_to_all x2 -> x1, starting transfers between devices: 8.04 us -> 3.99 us  [plane_all_to_all(): lax.all_to_all(value, 'seq', 0, 0, axis_index_groups=planes, tiled=True)]
    unnamed x30 -> x8, local copies, waits for them, and re-layouts: 3.15 us -> 0.01 us
    ppermute x9 -> x12, starting transfers between devices: 7.89 us -> 10.5 us  [in_plane(): lax.ppermute(pieces[m], 'seq', [(i, i ^ m) for i in range(peers)])]
  transfers between devices with their start and end apart: 20 -> 22, of which waited for: 7 -> 9; matrix products, arithmetic and copies ran while one was open for 0% -> 0% of each run, Pallas kernels for 22% -> 19%
where the time goes in v7:
time: 93.4 us; the launch traced here: 93 us
  waiting for transfers between devices  37.9 us (41%)
  starting transfers between devices  31.2 us (33%)
  Pallas kernels  22.6 us (24%)
    ppermute x6, waiting for transfers between devices, partner(): lax.ppermute(value, axis, [(i, i ^ 1 << apart) for i in range(lax.axis_si...  19.5 us
    ppermute x12, waiting for transfers between devices, in_plane(): lax.ppermute(pieces[m], 'seq', [(i, i ^ m) for i in range(peers)])  18.4 us
    ppermute x6, starting transfers between devices, partner(): lax.ppermute(value, axis, [(i, i ^ 1 << apart) for i in range(lax.axis_si...  14.6 us
    pallas_call x2, Pallas kernels, attend(): pl.pallas_call(functools.partial(attend_kernel, first=first, slot=slot, g...  11.4 us
    ppermute x12, starting transfers between devices, in_plane(): lax.ppermute(pieces[m], 'seq', [(i, i ^ m) for i in range(peers)])  10.5 us
    pallas_call x2, Pallas kernels, pack(): pl.pallas_call(functools.partial(pack_kernel, order=order, count=count, c...  4.49 us
    all_to_all x1, starting transfers between devices, plane_all_to_all(): lax.all_to_all(value, 'seq', 0, 0, axis_index_groups=planes, tiled=True)  3.99 us
    pallas_call x2, Pallas kernels, unpack(): pl.pallas_call(functools.partial(kernel, count=count), grid=(tokens // ch...  3.6 us
  transfers between devices with their start and end apart: 22, of which 9 were waited for; matrix products, arithmetic and copies ran while one was open for 0% of the time, Pallas kernels for 19%

profile of v7, /device:TPU:1, one launch (start us, length us, event | category | flops | bytes accessed | tf_op | source)
XLA Modules:
  0.0 93.0 jit_solution(17410044821262431442)
XLA Ops:
  1.2 2.2 %shard_map.93 = (bf16[4,2,128,128]{3,2,1,0:T(8,128)(2,1)}, bf16[4,2,128,128]{3,2,1,0:T(8,128)(2,1)}, bf16[4,2,128,128]{3,2,1,0:T(8,128)(2,1)}, bf16[4,2,128,128]{3,2,1,0:T(8,128)(2,1)}) custom-call(s32[2]{0:T(128)} %pad_add_fusion.place, s32[4,4]{1,0:T(4,128)} %sections.11, bf16[128,16,128]{2,1,0:T(8,128)(2,1)} %refs_0_.2, bf16[128,16,128]{2,1,0:T(8,128)(2,1)} %refs_1_.2), custom_call_target="tpu_custom_call" | custom-call | bytes 2097152 | tf_op jit(solution)/shard_map/pallas_call | solution.py:124
  3.5 2.7 %collective-permute-start.1 = (bf16[4,2,128,128]{3,2,1,0:T(8,128)(2,1)}, bf16[4,2,128,128]{3,2,1,0:T(8,128)(2,1)S(1)}, u32[]{:S(2)}, u32[]{:S(2)}) collective-permute-start(bf16[4,2,128,128]{3,2,1,0:T(8,128)(2,1)} %get-tuple-element.57), channel_id=1, source_target_pairs={{0,2},{1,3},{2,0},{3,1},{4,6},{5,7},{6,4},{7,5},{8,10},{9,11},{10,... | collective-permute-start | bytes 786440 | tf_op jit(solution)/shard_map/ppermute | solution.py:644
  6.2 2.2 %shard_map.94 = bf16[4,4,2,128,128]{4,3,2,1,0:T(8,128)(2,1)} custom-call(s32[2]{0:T(128)} %pad_add_fusion.place, s32[4,4]{1,0:T(4,128)} %sections.11, bf16[128,16,128]{2,1,0:T(8,128)(2,1)} %refs_0_.3, bf16[128,16,128]{2,1,0:T(8,128)(2,1)} %refs_1_.3), custom_call_target="tpu_custom_call" | custom-call | bytes 2097152 | tf_op jit(solution)/shard_map/pallas_call | solution.py:124
  8.5 4.0 %all-to-all-start = ((bf16[4,4,2,128,128]{4,3,2,1,0:T(8,128)(2,1)}), bf16[4,4,2,128,128]{4,3,2,1,0:T(8,128)(2,1)S(1)}, u32[]{:S(2)}, u32[]{:S(2)}) async-start(bf16[4,4,2,128,128]{4,3,2,1,0:T(8,128)(2,1)} %shard_map.94), calls=%async_computation | async-start | bytes 2097152 | tf_op jit(solution)/shard_map/all_to_all | solution.py:670
  13.0 6.1 %collective-permute-done.2.refs_3_ = bf16[4,2,128,128]{3,2,1,0:T(8,128)(2,1)S(1)} collective-permute-done((bf16[4,2,128,128]{3,2,1,0:T(8,128)(2,1)}, bf16[4,2,128,128]{3,2,1,0:T(8,128)(2,1)S(1)}, u32[]{:S(2)}, u32[]{:S(2)}) %collective-permute-start.2) | collective-permute-done | bytes 262176 | tf_op jit(solution)/shard_map/ppermute | solution.py:644
  19.1 0.6 shard_map.95
  19.8 1.8 %collective-permute-start.3 = (bf16[8,2,128,128]{3,2,1,0:T(8,128)(2,1)S(1)}, bf16[8,2,128,128]{3,2,1,0:T(8,128)(2,1)S(1)}, u32[]{:S(2)}, u32[]{:S(2)}) collective-permute-start(bf16[8,2,128,128]{3,2,1,0:T(8,128)(2,1)S(1)} %get-tuple-element.59), channel_id=1, source_target_pairs={{0,4},{1,5},{2,6},{3,7},{4,0},{5,1},{6,2},{7,3},{8,12},{9,13},{10,... | collective-permute-start | bytes 1572872 | tf_op jit(solution)/shard_map/ppermute | solution.py:394
  21.6 0.7 collective-permute-start.4
  22.3 0.8 shard_map.96
  23.1 3.8 %collective-permute-start.5 = (bf16[4,2,128,128]{3,2,1,0:T(8,128)(2,1)}, bf16[4,2,128,128]{3,2,1,0:T(8,128)(2,1)S(1)}, u32[]{:S(2)}, u32[]{:S(2)}) collective-permute-start(bf16[4,2,128,128]{3,2,1,0:T(8,128)(2,1)} %get-tuple-element.61), channel_id=1, source_target_pairs={{0,4},{1,5},{2,6},{3,7},{4,0},{5,1},{6,2},{7,3},{8,12},{9,13},{10,... | collective-permute-start | bytes 786440 | tf_op jit(solution)/shard_map/ppermute | solution.py:394
  26.9 7.0 %collective-permute-done.3.refs_5_ = bf16[8,2,128,128]{3,2,1,0:T(8,128)(2,1)S(1)} collective-permute-done((bf16[8,2,128,128]{3,2,1,0:T(8,128)(2,1)S(1)}, bf16[8,2,128,128]{3,2,1,0:T(8,128)(2,1)S(1)}, u32[]{:S(2)}, u32[]{:S(2)}) %collective-permute-start.3) | collective-permute-done | bytes 524320 | tf_op jit(solution)/shard_map/ppermute | solution.py:394
  33.9 5.5 %shard_map.97 = (bf16[4,2,128,128]{3,2,1,0:T(8,128)(2,1)S(1)}, bf16[4,2,128,128]{3,2,1,0:T(8,128)(2,1)S(1)}, bf16[4,2,128,128]{3,2,1,0:T(8,128)(2,1)S(1)}, bf16[...) custom-call(s32[2]{0:T(128)S(1)} %copy-done.2, ...), custom_call_target="tpu_custom_call" | custom-call | flops 1207959552 | bytes 5242880 | tf_op jit(solution)/shard_map/pallas_call | solution.py:333
  39.5 4.7 %collective-permute-start.7 = (bf16[4,2,128,128]{3,2,1,0:T(8,128)(2,1)S(1)}, bf16[4,2,128,128]{3,2,1,0:T(8,128)(2,1)S(1)}, u32[]{:S(2)}, u32[]{:S(2)}) collective-permute-start(bf16[4,2,128,128]{3,2,1,0:T(8,128)(2,1)S(1)} %get-tuple-element.71), channel_id=1, source_target_pairs={{0,4},{1,5},{2,6},{3,7},{4,0},{5,1},{6,2},{7,3},{8,12},{9,13},{10,... | collective-permute-start | bytes 786440 | tf_op jit(solution)/shard_map/ppermute | solution.py:394
  44.2 0.7 collective-permute-start.8
  44.8 4.8 %collective-permute-done.6.refs_8_ = bf16[4,2,128,128]{3,2,1,0:T(8,128)(2,1)} collective-permute-done((bf16[4,2,128,128]{3,2,1,0:T(8,128)(2,1)}, bf16[4,2,128,128]{3,2,1,0:T(8,128)(2,1)}, u32[]{:S(2)}, u32[]{:S(2)}) %collective-permute-start.6) | collective-permute-done | bytes 262176 | tf_op jit(solution)/shard_map/ppermute | solution.py:394
  49.7 5.9 %shard_map.98 = (bf16[4,2,128,128]{3,2,1,0:T(8,128)(2,1)S(1)}, bf16[4,2,128,128]{3,2,1,0:T(8,128)(2,1)S(1)}, bf16[4,2,128,128]{3,2,1,0:T(8,128)(2,1)S(1)}, bf16[...) custom-call(s32[2]{0:T(128)S(1)} %copy-done.2, ...), custom_call_target="tpu_custom_call", output_to_operand_aliasing={{0}: (12, {}), {1}: (13, {}), {2}: (14, {}), {3}: (15, {})} | custom-call | flops 1207959552 | bytes 5242880 | tf_op jit(solution)/shard_map/pallas_call | solution.py:333
  55.6 0.8 shard_map.99
  56.9 1.1 %collective-permute-start.13 = (bf16[4,2,128,128]{3,2,1,0:T(8,128)(2,1)S(1)}, bf16[4,2,128,128]{3,2,1,0:T(8,128)(2,1)S(1)}, u32[]{:S(2)}, u32[]{:S(2)}) collective-permute-start(bf16[4,2,128,128]{3,2,1,0:T(8,128)(2,1)S(1)} %get-tuple-element.86), channel_id=1, source_target_pairs={{0,2},{1,3},{2,0},{3,1},{4,6},{5,7},{6,4},{7,5},{8,10},{9,11},{10,... | collective-permute-start | bytes 786440 | tf_op jit(solution)/shard_map/ppermute | solution.py:644
  58.0 0.8 collective-permute-start.14
  58.8 0.7 collective-permute-start.10
  59.5 4.3 %collective-permute-start.11 = (bf16[4,2,128,128]{3,2,1,0:T(8,128)(2,1)S(1)}, bf16[4,2,128,128]{3,2,1,0:T(8,128)(2,1)S(1)}, u32[]{:S(2)}, u32[]{:S(2)}) collective-permute-start(bf16[4,2,128,128]{3,2,1,0:T(8,128)(2,1)S(1)} %get-tuple-element.83), channel_id=1, source_target_pairs={{0,8},{1,9},{2,10},{3,11},{4,12},{5,13},{6,14},{7,15},{8,0},{9,1},... | collective-permute-start | bytes 786440 | tf_op jit(solution)/shard_map/ppermute | solution.py:394
  63.8 0.8 collective-permute-done.13.refs_2_
  64.6 1.7 %collective-permute-start.18 = (bf16[2,2,128,128]{3,2,1,0:T(8,128)(2,1)S(1)}, bf16[2,2,128,128]{3,2,1,0:T(8,128)(2,1)S(1)}, u32[]{:S(2)}, u32[]{:S(2)}) collective-permute-start(bf16[2,2,128,128]{3,2,1,0:T(8,128)(2,1)S(1)} %get-tuple-element.101), channel_id=1, source_target_pairs={{0,1},{1,0},{2,3},{3,2},{4,5},{5,4},{6,7},{7,6},{8,9},{9,8},{10,11... | collective-permute-start | bytes 393224 | tf_op jit(solution)/shard_map/ppermute | solution.py:644
  66.3 4.6 %collective-permute-done.14.refs_3_ = bf16[4,2,128,128]{3,2,1,0:T(8,128)(2,1)S(1)} collective-permute-done((bf16[4,2,128,128]{3,2,1,0:T(8,128)(2,1)S(1)}, bf16[4,2,128,128]{3,2,1,0:T(8,128)(2,1)S(1)}, u32[]{:S(2)}, u32[]{:S(2)}) %collective-permute-start.14) | collective-permute-done | bytes 262176 | tf_op jit(solution)/shard_map/ppermute | solution.py:644
  70.9 1.1 %collective-permute-start.19 = (bf16[2,2,128,128]{3,2,1,0:T(8,128)(2,1)S(1)}, bf16[2,2,128,128]{3,2,1,0:T(8,128)(2,1)S(1)}, u32[]{:S(2)}, u32[]{:S(2)}) collective-permute-start(bf16[2,2,128,128]{3,2,1,0:T(8,128)(2,1)S(1)} %get-tuple-element.102), channel_id=1, source_target_pairs={{0,2},{1,3},{2,0},{3,1},{4,6},{5,7},{6,4},{7,5},{8,10},{9,11},{10,... | collective-permute-start | bytes 393224 | tf_op jit(solution)/shard_map/ppermute | solution.py:644
  71.9 1.8 %shard_map.100 = (bf16[128,16,128]{2,1,0:T(8,128)(2,1)}, bf16[128,16,128]{2,1,0:T(8,128)(2,1)}) custom-call(s32[2]{0:T(128)S(1)} %copy-done.2, s32[4,4]{1,0:T(4,128)S(1)} %copy-done.1, bf16[4,2,128,128]{3,2,1,0:T(8,128)(2,1)S(1)} %get-tuple-element.84.refs_0_, bf16[4,2,128,128]{3,2,1,0:T(8,128)(2,1)S(1)} %collective-permute-done.12.refs_1_, ...), custom_call_target="tpu_custom_call" | custom-call | bytes 2097152 | tf_op jit(solution)/shard_map/pallas_call | solution.py:163
  74.0 7.7 %collective-permute-done.11.refs_0_ = bf16[4,2,128,128]{3,2,1,0:T(8,128)(2,1)S(1)} collective-permute-done((bf16[4,2,128,128]{3,2,1,0:T(8,128)(2,1)S(1)}, bf16[4,2,128,128]{3,2,1,0:T(8,128)(2,1)S(1)}, u32[]{:S(2)}, u32[]{:S(2)}) %collective-permute-start.11) | collective-permute-done | bytes 262176 | tf_op jit(solution)/shard_map/ppermute | solution.py:394
  81.7 0.8 shard_map.101
  83.1 1.2 %collective-permute-start.16 = (bf16[2,2,128,128]{3,2,1,0:T(8,128)(2,1)S(1)}, bf16[2,2,128,128]{3,2,1,0:T(8,128)(2,1)S(1)}, u32[]{:S(2)}, u32[]{:S(2)}) collective-permute-start(bf16[2,2,128,128]{3,2,1,0:T(8,128)(2,1)S(1)} %get-tuple-element.98), channel_id=1, source_target_pairs={{0,2},{1,3},{2,0},{3,1},{4,6},{5,7},{6,4},{7,5},{8,10},{9,11},{10,... | collective-permute-start | bytes 393224 | tf_op jit(solution)/shard_map/ppermute | solution.py:644
  84.8 3.4 %collective-permute-done.16.refs_2_ = bf16[2,2,128,128]{3,2,1,0:T(8,128)(2,1)S(1)} collective-permute-done((bf16[2,2,128,128]{3,2,1,0:T(8,128)(2,1)S(1)}, bf16[2,2,128,128]{3,2,1,0:T(8,128)(2,1)S(1)}, u32[]{:S(2)}, u32[]{:S(2)}) %collective-permute-start.16) | collective-permute-done | bytes 131104 | tf_op jit(solution)/shard_map/ppermute | solution.py:644
  88.2 3.0 %collective-permute-done.17.refs_3_ = bf16[2,2,128,128]{3,2,1,0:T(8,128)(2,1)S(1)} collective-permute-done((bf16[2,2,128,128]{3,2,1,0:T(8,128)(2,1)S(1)}, bf16[2,2,128,128]{3,2,1,0:T(8,128)(2,1)S(1)}, u32[]{:S(2)}, u32[]{:S(2)}) %collective-permute-start.17) | collective-permute-done | bytes 131104 | tf_op jit(solution)/shard_map/ppermute | solution.py:644
  91.1 1.8 %shard_map.102 = (bf16[128,16,128]{2,1,0:T(8,128)(2,1)}, bf16[128,16,128]{2,1,0:T(8,128)(2,1)}) custom-call(s32[2]{0:T(128)S(1)} %copy-done.2, s32[4,4]{1,0:T(4,128)S(1)} %copy-done.1, bf16[2,2,128,128]{3,2,1,0:T(8,128)(2,1)S(1)} %get-tuple-element.96.refs_0_, bf16[2,2,128,128]{3,2,1,0:T(8,128)(2,1)S(1)} %collective-permute-done.15.refs_1_, ...), custom_call_target="tpu_custom_call" | custom-call | bytes 2097152 | tf_op jit(solution)/shard_map/pallas_call | solution.py:163
  (31 shorter events, 3.2 us)
Async XLA Ops:
  3.5 9.0 %collective-permute-start = (bf16[4,2,128,128]{3,2,1,0:T(8,128)(2,1)}, bf16[4,2,128,128]{3,2,1,0:T(8,128)(2,1)S(1)}, u32[]{:S(2)}, u32[]{:S(2)}) collective-permute-start(bf16[4,2,128,128]{3,2,1,0:T(8,128)(2,1)} %get-tuple-element.56), channel_id=1, source_target_pairs={{0,1},{1,0},{2,3},{3,2},{4,5},{5,4},{6,7},{7,6},{8,9},{9,8},{10,11... | collective-permute-start | bytes 786440 | tf_op jit(solution)/shard_map/ppermute | solution.py:644
  3.5 9.5 %collective-permute-start.1 = (bf16[4,2,128,128]{3,2,1,0:T(8,128)(2,1)}, bf16[4,2,128,128]{3,2,1,0:T(8,128)(2,1)S(1)}, u32[]{:S(2)}, u32[]{:S(2)}) collective-permute-start(bf16[4,2,128,128]{3,2,1,0:T(8,128)(2,1)} %get-tuple-element.57), channel_id=1, source_target_pairs={{0,2},{1,3},{2,0},{3,1},{4,6},{5,7},{6,4},{7,5},{8,10},{9,11},{10,... | collective-permute-start | bytes 786440 | tf_op jit(solution)/shard_map/ppermute | solution.py:644
  6.2 12.9 %collective-permute-start.2 = (bf16[4,2,128,128]{3,2,1,0:T(8,128)(2,1)}, bf16[4,2,128,128]{3,2,1,0:T(8,128)(2,1)S(1)}, u32[]{:S(2)}, u32[]{:S(2)}) collective-permute-start(bf16[4,2,128,128]{3,2,1,0:T(8,128)(2,1)} %get-tuple-element.58), channel_id=1, source_target_pairs={{0,3},{1,2},{2,1},{3,0},{4,7},{5,6},{6,5},{7,4},{8,11},{9,10},{10,... | collective-permute-start | bytes 786440 | tf_op jit(solution)/shard_map/ppermute | solution.py:644
  8.5 10.7 %copy-start = (bf16[4,2,128,128]{3,2,1,0:T(8,128)(2,1)S(1)}, bf16[4,2,128,128]{3,2,1,0:T(8,128)(2,1)}, u32[]{:S(2)}) copy-start(bf16[4,2,128,128]{3,2,1,0:T(8,128)(2,1)} %get-tuple-element.55.refs_0_) | copy-start | bytes 786436
  8.5 25.4 %all-to-all-start = ((bf16[4,4,2,128,128]{4,3,2,1,0:T(8,128)(2,1)}), bf16[4,4,2,128,128]{4,3,2,1,0:T(8,128)(2,1)S(1)}, u32[]{:S(2)}, u32[]{:S(2)}) async-start(bf16[4,4,2,128,128]{4,3,2,1,0:T(8,128)(2,1)} %shard_map.94), calls=%async_computation | async-start | bytes 2097152 | tf_op jit(solution)/shard_map/all_to_all | solution.py:670
  12.5 6.7 %copy-start.2 = (s32[2]{0:T(128)S(1)}, s32[2]{0:T(128)}, u32[]{:S(2)}) copy-start(s32[2]{0:T(128)} %pad_add_fusion.place) | copy-start | bytes 28
  19.8 14.1 %collective-permute-start.3 = (bf16[8,2,128,128]{3,2,1,0:T(8,128)(2,1)S(1)}, bf16[8,2,128,128]{3,2,1,0:T(8,128)(2,1)S(1)}, u32[]{:S(2)}, u32[]{:S(2)}) collective-permute-start(bf16[8,2,128,128]{3,2,1,0:T(8,128)(2,1)S(1)} %get-tuple-element.59), channel_id=1, source_target_pairs={{0,4},{1,5},{2,6},{3,7},{4,0},{5,1},{6,2},{7,3},{8,12},{9,13},{10,... | collective-permute-start | bytes 1572872 | tf_op jit(solution)/shard_map/ppermute | solution.py:394
  21.6 12.3 %collective-permute-start.4 = (bf16[8,2,128,128]{3,2,1,0:T(8,128)(2,1)S(1)}, bf16[8,2,128,128]{3,2,1,0:T(8,128)(2,1)S(1)}, u32[]{:S(2)}, u32[]{:S(2)}) collective-permute-start(bf16[8,2,128,128]{3,2,1,0:T(8,128)(2,1)S(1)} %get-tuple-element.60), channel_id=1, source_target_pairs={{4,8},{5,9},{6,10},{7,11},{8,4},{9,5},{10,6},{11,7},{20,24},{21,25... | collective-permute-start | bytes 1572872 | tf_op jit(solution)/shard_map/ppermute | solution.py:664
  23.1 10.8 %copy-start.1 = (s32[4,4]{1,0:T(4,128)S(1)}, s32[4,4]{1,0:T(4,128)}, u32[]{:S(2)}) copy-start(s32[4,4]{1,0:T(4,128)} %sections.11) | copy-start | bytes 196
  23.1 10.8 %copy-start.3 = (s32[16]{0:T(128)S(1)}, s32[16]{0:T(128)}, u32[]{:S(2)}) copy-start(s32[16]{0:T(128)} %widths.3) | copy-start | bytes 196
  23.1 21.7 %collective-permute-start.5 = (bf16[4,2,128,128]{3,2,1,0:T(8,128)(2,1)}, bf16[4,2,128,128]{3,2,1,0:T(8,128)(2,1)S(1)}, u32[]{:S(2)}, u32[]{:S(2)}) collective-permute-start(bf16[4,2,128,128]{3,2,1,0:T(8,128)(2,1)} %get-tuple-element.61), channel_id=1, source_target_pairs={{0,4},{1,5},{2,6},{3,7},{4,0},{5,1},{6,2},{7,3},{8,12},{9,13},{10,... | collective-permute-start | bytes 786440 | tf_op jit(solution)/shard_map/ppermute | solution.py:394
  26.9 22.8 %collective-permute-start.6 = (bf16[4,2,128,128]{3,2,1,0:T(8,128)(2,1)}, bf16[4,2,128,128]{3,2,1,0:T(8,128)(2,1)}, u32[]{:S(2)}, u32[]{:S(2)}) collective-permute-start(bf16[4,2,128,128]{3,2,1,0:T(8,128)(2,1)} %get-tuple-element.62), channel_id=1, source_target_pairs={{0,8},{1,9},{2,10},{3,11},{4,12},{5,13},{6,14},{7,15},{8,0},{9,1},... | collective-permute-start | bytes 786440 | tf_op jit(solution)/shard_map/ppermute | solution.py:394
  39.5 16.1 %collective-permute-start.7 = (bf16[4,2,128,128]{3,2,1,0:T(8,128)(2,1)S(1)}, bf16[4,2,128,128]{3,2,1,0:T(8,128)(2,1)S(1)}, u32[]{:S(2)}, u32[]{:S(2)}) collective-permute-start(bf16[4,2,128,128]{3,2,1,0:T(8,128)(2,1)S(1)} %get-tuple-element.71), channel_id=1, source_target_pairs={{0,4},{1,5},{2,6},{3,7},{4,0},{5,1},{6,2},{7,3},{8,12},{9,13},{10,... | collective-permute-start | bytes 786440 | tf_op jit(solution)/shard_map/ppermute | solution.py:394
  44.2 11.5 %collective-permute-start.8 = (bf16[4,2,128,128]{3,2,1,0:T(8,128)(2,1)S(1)}, bf16[4,2,128,128]{3,2,1,0:T(8,128)(2,1)S(1)}, u32[]{:S(2)}, u32[]{:S(2)}) collective-permute-start(bf16[4,2,128,128]{3,2,1,0:T(8,128)(2,1)S(1)} %get-tuple-element.72), channel_id=1, source_target_pairs={{4,8},{5,9},{6,10},{7,11},{8,4},{9,5},{10,6},{11,7},{20,24},{21,25... | collective-permute-start | bytes 786440 | tf_op jit(solution)/shard_map/ppermute | solution.py:664
  56.4 3.1 %collective-permute-start.12 = (bf16[4,2,128,128]{3,2,1,0:T(8,128)(2,1)S(1)}, bf16[4,2,128,128]{3,2,1,0:T(8,128)(2,1)S(1)}, u32[]{:S(2)}, u32[]{:S(2)}) collective-permute-start(bf16[4,2,128,128]{3,2,1,0:T(8,128)(2,1)S(1)} %get-tuple-element.85), channel_id=1, source_target_pairs={{0,1},{1,0},{2,3},{3,2},{4,5},{5,4},{6,7},{7,6},{8,9},{9,8},{10,11... | collective-permute-start | bytes 786440 | tf_op jit(solution)/shard_map/ppermute | solution.py:644
  56.9 24.8 %collective-permute-start.9 = (bf16[8,2,128,128]{3,2,1,0:T(8,128)(2,1)S(1)}, bf16[8,2,128,128]{3,2,1,0:T(8,128)(2,1)S(1)}, u32[]{:S(2)}, u32[]{:S(2)}) collective-permute-start(bf16[8,2,128,128]{3,2,1,0:T(8,128)(2,1)S(1)} %get-tuple-element.81), channel_id=1, source_target_pairs={{0,4},{1,5},{2,6},{3,7},{4,0},{5,1},{6,2},{7,3},{8,12},{9,13},{10,... | collective-permute-start | bytes 1572872 | tf_op jit(solution)/shard_map/ppermute | solution.py:394
  56.9 7.7 %collective-permute-start.13 = (bf16[4,2,128,128]{3,2,1,0:T(8,128)(2,1)S(1)}, bf16[4,2,128,128]{3,2,1,0:T(8,128)(2,1)S(1)}, u32[]{:S(2)}, u32[]{:S(2)}) collective-permute-start(bf16[4,2,128,128]{3,2,1,0:T(8,128)(2,1)S(1)} %get-tuple-element.86), channel_id=1, source_target_pairs={{0,2},{1,3},{2,0},{3,1},{4,6},{5,7},{6,4},{7,5},{8,10},{9,11},{10,... | collective-permute-start | bytes 786440 | tf_op jit(solution)/shard_map/ppermute | solution.py:644
  58.0 12.9 %collective-permute-start.14 = (bf16[4,2,128,128]{3,2,1,0:T(8,128)(2,1)S(1)}, bf16[4,2,128,128]{3,2,1,0:T(8,128)(2,1)S(1)}, u32[]{:S(2)}, u32[]{:S(2)}) collective-permute-start(bf16[4,2,128,128]{3,2,1,0:T(8,128)(2,1)S(1)} %get-tuple-element.87), channel_id=1, source_target_pairs={{0,3},{1,2},{2,1},{3,0},{4,7},{5,6},{6,5},{7,4},{8,11},{9,10},{10,... | collective-permute-start | bytes 786440 | tf_op jit(solution)/shard_map/ppermute | solution.py:644
  58.8 14.9 %collective-permute-start.10 = (bf16[4,2,128,128]{3,2,1,0:T(8,128)(2,1)S(1)}, bf16[4,2,128,128]{3,2,1,0:T(8,128)(2,1)S(1)}, u32[]{:S(2)}, u32[]{:S(2)}) collective-permute-start(bf16[4,2,128,128]{3,2,1,0:T(8,128)(2,1)S(1)} %get-tuple-element.82), channel_id=1, source_target_pairs={{4,8},{5,9},{6,10},{7,11},{8,4},{9,5},{10,6},{11,7},{20,24},{21,25... | collective-permute-start | bytes 786440 | tf_op jit(solution)/shard_map/ppermute | solution.py:664
  59.5 22.2 %collective-permute-start.11 = (bf16[4,2,128,128]{3,2,1,0:T(8,128)(2,1)S(1)}, bf16[4,2,128,128]{3,2,1,0:T(8,128)(2,1)S(1)}, u32[]{:S(2)}, u32[]{:S(2)}) collective-permute-start(bf16[4,2,128,128]{3,2,1,0:T(8,128)(2,1)S(1)} %get-tuple-element.83), channel_id=1, source_target_pairs={{0,8},{1,9},{2,10},{3,11},{4,12},{5,13},{6,14},{7,15},{8,0},{9,1},... | collective-permute-start | bytes 786440 | tf_op jit(solution)/shard_map/ppermute | solution.py:394
  64.6 19.7 %collective-permute-start.18 = (bf16[2,2,128,128]{3,2,1,0:T(8,128)(2,1)S(1)}, bf16[2,2,128,128]{3,2,1,0:T(8,128)(2,1)S(1)}, u32[]{:S(2)}, u32[]{:S(2)}) collective-permute-start(bf16[2,2,128,128]{3,2,1,0:T(8,128)(2,1)S(1)} %get-tuple-element.101), channel_id=1, source_target_pairs={{0,1},{1,0},{2,3},{3,2},{4,5},{5,4},{6,7},{7,6},{8,9},{9,8},{10,11... | collective-permute-start | bytes 393224 | tf_op jit(solution)/shard_map/ppermute | solution.py:644
  70.9 13.9 %collective-permute-start.19 = (bf16[2,2,128,128]{3,2,1,0:T(8,128)(2,1)S(1)}, bf16[2,2,128,128]{3,2,1,0:T(8,128)(2,1)S(1)}, u32[]{:S(2)}, u32[]{:S(2)}) collective-permute-start(bf16[2,2,128,128]{3,2,1,0:T(8,128)(2,1)S(1)} %get-tuple-element.102), channel_id=1, source_target_pairs={{0,2},{1,3},{2,0},{3,1},{4,6},{5,7},{6,4},{7,5},{8,10},{9,11},{10,... | collective-permute-start | bytes 393224 | tf_op jit(solution)/shard_map/ppermute | solution.py:644
  73.7 11.1 %collective-permute-start.20 = (bf16[2,2,128,128]{3,2,1,0:T(8,128)(2,1)S(1)}, bf16[2,2,128,128]{3,2,1,0:T(8,128)(2,1)S(1)}, u32[]{:S(2)}, u32[]{:S(2)}) collective-permute-start(bf16[2,2,128,128]{3,2,1,0:T(8,128)(2,1)S(1)} %get-tuple-element.103), channel_id=1, source_target_pairs={{0,3},{1,2},{2,1},{3,0},{4,7},{5,6},{6,5},{7,4},{8,11},{9,10},{10,... | collective-permute-start | bytes 393224 | tf_op jit(solution)/shard_map/ppermute | solution.py:644
  82.5 2.3 %collective-permute-start.15 = (bf16[2,2,128,128]{3,2,1,0:T(8,128)(2,1)S(1)}, bf16[2,2,128,128]{3,2,1,0:T(8,128)(2,1)S(1)}, u32[]{:S(2)}, u32[]{:S(2)}) collective-permute-start(bf16[2,2,128,128]{3,2,1,0:T(8,128)(2,1)S(1)} %get-tuple-element.97), channel_id=1, source_target_pairs={{0,1},{1,0},{2,3},{3,2},{4,5},{5,4},{6,7},{7,6},{8,9},{9,8},{10,11... | collective-permute-start | bytes 393224 | tf_op jit(solution)/shard_map/ppermute | solution.py:644
  83.1 5.1 %collective-permute-start.16 = (bf16[2,2,128,128]{3,2,1,0:T(8,128)(2,1)S(1)}, bf16[2,2,128,128]{3,2,1,0:T(8,128)(2,1)S(1)}, u32[]{:S(2)}, u32[]{:S(2)}) collective-permute-start(bf16[2,2,128,128]{3,2,1,0:T(8,128)(2,1)S(1)} %get-tuple-element.98), channel_id=1, source_target_pairs={{0,2},{1,3},{2,0},{3,1},{4,6},{5,7},{6,4},{7,5},{8,10},{9,11},{10,... | collective-permute-start | bytes 393224 | tf_op jit(solution)/shard_map/ppermute | solution.py:644
  84.3 6.9 %collective-permute-start.17 = (bf16[2,2,128,128]{3,2,1,0:T(8,128)(2,1)S(1)}, bf16[2,2,128,128]{3,2,1,0:T(8,128)(2,1)S(1)}, u32[]{:S(2)}, u32[]{:S(2)}) collective-permute-start(bf16[2,2,128,128]{3,2,1,0:T(8,128)(2,1)S(1)} %get-tuple-element.99), channel_id=1, source_target_pairs={{0,3},{1,2},{2,1},{3,0},{4,7},{5,6},{6,5},{7,4},{8,11},{9,10},{10,... | collective-permute-start | bytes 393224 | tf_op jit(solution)/shard_map/ppermute | solution.py:644

commit v8 on v7

--- a/solution.py
+++ b/solution.py
@@ -100,7 +100,7 @@
     for i in range(count):
         held[i] = jnp.transpose(ins[i][...], (1, 0, 2))
     for m in range(PLANE):
-        owner = place[0] ^ m if crossed else m
+        owner = seat(place) ^ m if crossed else m
         for k, s in enumerate(order):
             head = sections[s, owner]
             for i in range(count):
@@ -133,54 +133,50 @@
     )(place, sections, *arrays)
 
 
-def unpack_crossed_kernel(place, sections, *refs, groups, count):
+def unpack_kernel(place, sections, *refs, groups, count):
     pieces, outs, held = refs[: len(groups) * PLANE], refs[len(groups) * PLANE : -1], refs[-1]
     for number, group in enumerate(groups):
         for m in range(PLANE):
             for k, s in enumerate(group):
-                head = sections[s, place[0] ^ m]
+                head = sections[s, seat(place) ^ m]
                 for i in range(count):
                     held[i, head] = pieces[number * PLANE + m][k, i]
     for i in range(count):
         outs[i][...] = jnp.transpose(held[i], (1, 0, 2))
 
 
-def unpack_kernel(place, sections, src, *refs, order, count):
-    outs, held = refs[:-1], refs[-1]
-    for m in range(PLANE):
-        for k, s in enumerate(order):
-            head = sections[s, m]
-            for i in range(count):
-                held[i, head] = src[m, k, i]
-    for i in range(count):
-        outs[i][...] = jnp.transpose(held[i], (1, 0, 2))
-
-
-def unpack(place, sections, kernel, pieces):
-    *lead, count, tokens, width = pieces[0].shape
+def unpack(place, sections, parts):
+    flat = [piece for _, pieces, _ in parts for piece in pieces]
+    count, tokens, width = flat[0].shape[1:]
     heads = sections.size
     chunk = tokens // 2
+    specs = [
+        pl.BlockSpec((len(group), count, chunk, width), lambda i, run=run: (run, 0, i, 0))
+        for group, _, run in parts
+        for _ in range(PLANE)
+    ]
     return pl.pallas_call(
-        functools.partial(kernel, count=count),
+        functools.partial(unpack_kernel, groups=[group for group, _, _ in parts], count=count),
         grid=(tokens // chunk,),
-        in_specs=[SMEM, SMEM]
-        + [
-            pl.BlockSpec(
-                (*piece.shape[:-2], chunk, width),
-                lambda i, zeros=(0,) * (piece.ndim - 2): (*zeros, i, 0),
-            )
-            for piece in pieces
-        ],
+        in_specs=[SMEM, SMEM] + specs,
         out_specs=[pl.BlockSpec((chunk, heads, width), lambda i: (i, 0, 0))] * count,
         out_shape=[jax.ShapeDtypeStruct((tokens, heads, width), jnp.bfloat16)] * count,
         scratch_shapes=[pltpu.VMEM((count, heads, chunk, width), jnp.bfloat16)],
         compiler_params=LIMIT,
-        cost_estimate=moved_cost(pieces),
-    )(place, sections, *pieces)
+        cost_estimate=moved_cost(flat),
+    )(place, sections, *flat)
+
+
+def seat(place):
+    return place[0] % PLANE
+
+
+def plane(place):
+    return place[0] // PLANE
 
 
 def facing(place):
-    return place[0] // HALO == 1 - place[1] % 2
+    return seat(place) // HALO == 1 - plane(place) % 2
 
 
 def far_kernel(*refs):
@@ -244,11 +240,11 @@
         to_other, rest = rest[0], rest[1:]
     keys, values, far_keys, far_values, attended, dq = rest[:6]
     accs, far_accs = rest[6:8], rest[8:10]
-    me = place[0]
+    me = seat(place)
     scales = (1.0 / math.sqrt(keys.shape[-1]), 1.0)
     lead = PLANE if remote else 0
     slots = with_next.shape[0] // HALO
-    next_at = jnp.where(place[1] % 2 == 0, HALO + PLANE, 0)
+    next_at = jnp.where(plane(place) % 2 == 0, HALO + PLANE, 0)
     last_at = HALO + PLANE - next_at
     for k in range(group):
         width = widths[sections[first + k, me]]
@@ -266,8 +262,8 @@
             values[rows_of(last_at + b)] = with_last[at, 1]
         if remote:
             for m in range(PLANE):
-                far_keys[rows_of(me ^ m)] = far_in[k][m, 0]
-                far_values[rows_of(me ^ m)] = far_in[k][m, 1]
+                far_keys[rows_of(me ^ m)] = far_in[1 - k][m, 0]
+                far_values[rows_of(me ^ m)] = far_in[1 - k][m, 1]
         for acc in accs:
             acc[...] = jnp.zeros_like(acc)
         for b in range(0, PLANE, 2):
@@ -288,7 +284,7 @@
                 values[seen],
                 kf,
                 vf,
-                near_biases(place[1] * PLANE + b, width, 0, blocks),
+                near_biases(plane(place) * PLANE + b, width, 0, blocks),
                 far_bias,
             )
             attended[own] = o
@@ -325,6 +321,7 @@
     count, _, width = pairs[0].shape[1:]
     tile = (BLK, width)
     remote = len(far)
+    room = pairs[0].shape[0] + group
     bf16 = jnp.bfloat16
     owed = [(HALO * group + (PLANE if remote else 0), count, *tile), (HALO * group, count, *tile)]
     if remote:
@@ -342,7 +339,7 @@
         ),
         in_specs=[SMEM] * 3 + [VMEM] * len(inputs),
         out_specs=[VMEM] * (PLANE + 1 + len(owed)),
-        out_shape=[jax.ShapeDtypeStruct(pairs[0].shape, bf16)] * PLANE
+        out_shape=[jax.ShapeDtypeStruct((room, count, *tile), bf16)] * PLANE
         + [jax.ShapeDtypeStruct((group, PLANE, count, *tile), jnp.float32)]
         + [jax.ShapeDtypeStruct(shape, bf16) for shape in owed],
         scratch_shapes=[pltpu.VMEM((PADDED * BLK, width), bf16)] * 2
@@ -360,8 +357,9 @@
     return outs[:PLANE], outs[PLANE], outs[PLANE + 1 :]
 
 
-def combine_kernel(place, part, with_next, with_last, *refs, remote):
-    outs = refs[remote:]
+def combine_kernel(place, part, *refs, remote, base, aliased):
+    with_other, (with_next, with_last) = refs[0], refs[remote : remote + 2]
+    outs = refs[remote + 2 + aliased :]
     group = part.shape[0]
     lead = PLANE if remote else 0
     for m in range(PLANE):
@@ -373,21 +371,26 @@
                 owed = jnp.where(next_side, with_next[lead + slot, i], with_last[slot, i])
                 total = part[k, m, i] + owed.astype(jnp.float32)
                 if remote:
-                    far = (with_next, refs[0])[k]
+                    far = (with_next, with_other)[k]
                     total += far[m, i].astype(jnp.float32)
-                outs[m][k, i] = jnp.transpose(total.astype(jnp.bfloat16))
-
-
-def combine(place, part, owed):
+                outs[m][base + k, i] = jnp.transpose(total.astype(jnp.bfloat16))
+
+
+def combine(place, part, owed, rows=(), base=0):
     group, _, *rest = part.shape
+    inputs = (part, *owed, *rows)
+    shape = rows[0].shape if rows else (group, *rest)
     return pl.pallas_call(
-        functools.partial(combine_kernel, remote=len(owed) - 2),
-        in_specs=[SMEM] + [VMEM] * (1 + len(owed)),
+        functools.partial(
+            combine_kernel, remote=len(owed) - 2, base=base, aliased=len(rows)
+        ),
+        in_specs=[SMEM] + [VMEM] * len(inputs),
         out_specs=[VMEM] * PLANE,
-        out_shape=[jax.ShapeDtypeStruct((group, *rest), jnp.bfloat16)] * PLANE,
+        out_shape=[jax.ShapeDtypeStruct(shape, jnp.bfloat16)] * PLANE,
+        input_output_aliases={1 + len(inputs) - len(rows) + m: m for m in range(len(rows))},
         compiler_params=LIMIT,
         cost_estimate=moved_cost([part, *owed]),
-    )(place, part, *owed)
+    )(place, *inputs)
 
 
 def partner(value, axis, apart):
@@ -638,12 +641,14 @@
     return (attended.reshape(tokens_dev, head_count, head_width), query_grad, key_grad, value_grad)
 
 
-def in_plane(pieces):
+def in_plane(pieces, chip_first=False):
     peers = lax.axis_size("seq")
-    return [pieces[0]] + [
-        lax.ppermute(pieces[m], "seq", [(i, i ^ m) for i in range(peers)])
-        for m in range(1, PLANE)
-    ]
+    pieces = list(pieces)
+    for m in range(1, PLANE):
+        pieces[m] = lax.ppermute(pieces[m], "seq", [(i, i ^ m) for i in range(peers)])
+        if chip_first and m == 1:
+            pieces = lax.optimization_barrier(pieces)
+    return pieces
 
 
 def with_next_plane(value):
@@ -671,8 +676,7 @@
 
 
 def sharded_by_plane(query_rows, key_rows, value_rows, out_grad, widths, sections):
-    position = lax.axis_index("seq").astype(jnp.int32)
-    place = jnp.stack([position % PLANE, position // PLANE])
+    place = lax.axis_index("seq").astype(jnp.int32).reshape(1)
     blocks = lax.axis_size("seq")
     local = PLANE.bit_length() - 1
     total = sections.shape[0]
@@ -686,7 +690,7 @@
     next_sent, last_sent = halo_parts(place, pairs)
     far_sent = far_parts(pairs, total - local)
     halos = (with_next_plane(next_sent), with_last_plane(last_sent))
-    far = (with_next_plane(far_sent[0]), with_other_plane(far_sent[1]))
+    far = (with_other_plane(far_sent[1]), with_next_plane(far_sent[0]))
     rows, part_near, owed = attend(
         *tables, pairs, graded, halos, (), local, 0, total - local, blocks
     )
@@ -694,22 +698,13 @@
     rows, part_far, owed = attend(
         *tables, pairs, graded, halos, far, total - local, local, 0, blocks, rows
     )
-    near = combine(place, part_near, owed_near)
-    owed, near, rows = lax.optimization_barrier((owed, near, rows))
     other_back = with_other_plane(owed[2])
-    owed_far = [with_next_plane(owed[0]), with_last_plane(owed[1]), other_back]
-    near = in_plane(near)
-    attended, query_grad = unpack(
-        place,
-        sections,
-        functools.partial(unpack_crossed_kernel, groups=[order]),
-        in_plane(rows),
-    )
-    owed_far, attended, query_grad = lax.optimization_barrier((owed_far, attended, query_grad))
-    columns = in_plane(combine(place, part_far, owed_far)) + near
-    key_grad, value_grad = unpack(
-        place, sections, functools.partial(unpack_crossed_kernel, groups=groups), columns
-    )
+    owed_far = [other_back, with_next_plane(owed[0]), with_last_plane(owed[1])]
+    rows = in_plane(combine(place, part_near, owed_near, rows, total), True)
+    attended, query_grad = unpack(place, sections, [(groups[0], rows, 0), (groups[1], rows, 1)])
+    columns = in_plane(combine(place, part_far, owed_far))
+    columns, attended, query_grad = lax.optimization_barrier((columns, attended, query_grad))
+    key_grad, value_grad = unpack(place, sections, [(groups[0], columns, 0), (groups[1], rows, 2)])
     return attended, query_grad, key_grad, value_grad
 
 

time: 93.4 us -> 89.3 us (0.956)
  waiting for transfers between devices: 37.9 us -> 32.3 us
  starting transfers between devices: 31.2 us -> 34.4 us
  Pallas kernels: 22.6 us -> 21 us
    ppermute x12 -> x9, waiting for transfers between devices: 18.4 us -> 11.2 us  [in_plane(): lax.ppermute(pieces[m], 'seq', [(i, i ^ m) for i in range(peers)])]
    ppermute x6, starting transfers between devices: 14.6 us -> 20.4 us  [partner(): lax.ppermute(value, axis, [(i, i ^ 1 << apart) for i in range(lax.axis_si...]
    ppermute x12 -> x9, starting transfers between devices: 10.5 us -> 8.03 us  [in_plane(): lax.ppermute(pieces[m], 'seq', [(i, i ^ m) for i in range(peers)])]
    ppermute x6, waiting for transfers between devices: 19.5 us -> 21.1 us  [partner(): lax.ppermute(value, axis, [(i, i ^ 1 << apart) for i in range(lax.axis_si...]
    pallas_call x4, Pallas kernels: 5.18 us -> 4.15 us  [the longest x2 3.65 us: unpack(): pl.pallas_call(functools.partial(unpack_kernel, groups=[group for group,...]
  transfers between devices with their start and end apart: 22 -> 19, of which waited for: 9 -> 8; matrix products, arithmetic and copies ran while one was open for 0% -> 0% of each run, Pallas kernels for 19% -> 19%
where the time goes in v8:
time: 89.3 us; the launch traced here: 88.4 us
  starting transfers between devices  34.4 us (39%)
  waiting for transfers between devices  32.3 us (36%)
  Pallas kernels  21 us (24%)
    ppermute x6, waiting for transfers between devices, partner(): lax.ppermute(value, axis, [(i, i ^ 1 << apart) for i in range(lax.axis_si...  21.1 us
    ppermute x6, starting transfers between devices, partner(): lax.ppermute(value, axis, [(i, i ^ 1 << apart) for i in range(lax.axis_si...  20.4 us
    pallas_call x2, Pallas kernels, attend(): pl.pallas_call(functools.partial(attend_kernel, first=first, slot=slot, g...  11.4 us
    ppermute x9, waiting for transfers between devices, in_plane(): lax.ppermute(pieces[m], 'seq', [(i, i ^ m) for i in range(peers)])  11.2 us
    ppermute x9, starting transfers between devices, in_plane(): lax.ppermute(pieces[m], 'seq', [(i, i ^ m) for i in range(peers)])  8.03 us
    pallas_call x2, Pallas kernels, pack(): pl.pallas_call(functools.partial(pack_kernel, order=order, count=count, c...  4.49 us
    all_to_all x1, starting transfers between devices, plane_all_to_all(): lax.all_to_all(value, 'seq', 0, 0, axis_index_groups=planes, tiled=True)  3.99 us
    pallas_call x2, Pallas kernels, unpack(): pl.pallas_call(functools.partial(unpack_kernel, groups=[group for group,...  3.65 us
  transfers between devices with their start and end apart: 19, of which 8 were waited for; matrix products, arithmetic and copies ran while one was open for 0% of the time, Pallas kernels for 19%

profile of v8, /device:TPU:1, one launch (start us, length us, event | category | flops | bytes accessed | tf_op | source)
XLA Modules:
  0.0 88.4 jit_solution(3511859606615852664)
XLA Ops:
  0.6 2.3 %shard_map.93 = (bf16[4,2,128,128]{3,2,1,0:T(8,128)(2,1)}, bf16[4,2,128,128]{3,2,1,0:T(8,128)(2,1)}, bf16[4,2,128,128]{3,2,1,0:T(8,128)(2,1)}, bf16[4,2,128,128]{3,2,1,0:T(8,128)(2,1)}) custom-call(s32[1]{0:T(128)} %bitcast.place, s32[4,4]{1,0:T(4,128)} %sections.11, bf16[128,16,128]{2,1,0:T(8,128)(2,1)} %refs_0_.2, bf16[128,16,128]{2,1,0:T(8,128)(2,1)} %refs_1_.2), custom_call_target="tpu_custom_call" | custom-call | bytes 2097152 | tf_op jit(solution)/shard_map/pallas_call | solution.py:124
  3.0 2.7 %collective-permute-start.1 = (bf16[4,2,128,128]{3,2,1,0:T(8,128)(2,1)}, bf16[4,2,128,128]{3,2,1,0:T(8,128)(2,1)S(1)}, u32[]{:S(2)}, u32[]{:S(2)}) collective-permute-start(bf16[4,2,128,128]{3,2,1,0:T(8,128)(2,1)} %get-tuple-element.51), channel_id=1, source_target_pairs={{0,2},{1,3},{2,0},{3,1},{4,6},{5,7},{6,4},{7,5},{8,10},{9,11},{10,... | collective-permute-start | bytes 786440 | tf_op jit(solution)/shard_map/ppermute | solution.py:648
  5.7 2.2 %shard_map.94 = bf16[4,4,2,128,128]{4,3,2,1,0:T(8,128)(2,1)} custom-call(s32[1]{0:T(128)} %bitcast.place, s32[4,4]{1,0:T(4,128)} %sections.11, bf16[128,16,128]{2,1,0:T(8,128)(2,1)} %refs_0_.3, bf16[128,16,128]{2,1,0:T(8,128)(2,1)} %refs_1_.3), custom_call_target="tpu_custom_call" | custom-call | bytes 2097152 | tf_op jit(solution)/shard_map/pallas_call | solution.py:124
  7.9 4.0 %all-to-all-start = ((bf16[4,4,2,128,128]{4,3,2,1,0:T(8,128)(2,1)}), bf16[4,4,2,128,128]{4,3,2,1,0:T(8,128)(2,1)S(1)}, u32[]{:S(2)}, u32[]{:S(2)}) async-start(bf16[4,4,2,128,128]{4,3,2,1,0:T(8,128)(2,1)} %shard_map.94), calls=%async_computation | async-start | bytes 2097152 | tf_op jit(solution)/shard_map/all_to_all | solution.py:675
  11.9 0.5 collective-permute-done.1.refs_2_
  12.5 6.1 %collective-permute-done.2.refs_3_ = bf16[4,2,128,128]{3,2,1,0:T(8,128)(2,1)S(1)} collective-permute-done((bf16[4,2,128,128]{3,2,1,0:T(8,128)(2,1)}, bf16[4,2,128,128]{3,2,1,0:T(8,128)(2,1)S(1)}, u32[]{:S(2)}, u32[]{:S(2)}) %collective-permute-start.2) | collective-permute-done | bytes 262176 | tf_op jit(solution)/shard_map/ppermute | solution.py:648
  18.7 1.8 %collective-permute-start.3 = (bf16[8,2,128,128]{3,2,1,0:T(8,128)(2,1)S(1)}, bf16[8,2,128,128]{3,2,1,0:T(8,128)(2,1)S(1)}, u32[]{:S(2)}, u32[]{:S(2)}) collective-permute-start(bf16[8,2,128,128]{3,2,1,0:T(8,128)(2,1)S(1)} %get-tuple-element.53), channel_id=1, source_target_pairs={{0,4},{1,5},{2,6},{3,7},{4,0},{5,1},{6,2},{7,3},{8,12},{9,13},{10,... | collective-permute-start | bytes 1572872 | tf_op jit(solution)/shard_map/ppermute | solution.py:397
  20.5 0.7 collective-permute-start.4
  21.2 0.8 shard_map.96
  22.0 3.5 %collective-permute-start.5 = (bf16[4,2,128,128]{3,2,1,0:T(8,128)(2,1)}, bf16[4,2,128,128]{3,2,1,0:T(8,128)(2,1)S(1)}, u32[]{:S(2)}, u32[]{:S(2)}) collective-permute-start(bf16[4,2,128,128]{3,2,1,0:T(8,128)(2,1)} %get-tuple-element.55), channel_id=1, source_target_pairs={{0,8},{1,9},{2,10},{3,11},{4,12},{5,13},{6,14},{7,15},{8,0},{9,1},... | collective-permute-start | bytes 786440 | tf_op jit(solution)/shard_map/ppermute | solution.py:397
  25.5 0.4 collective-permute-start.6
  25.9 6.9 %collective-permute-done.3.refs_5_ = bf16[8,2,128,128]{3,2,1,0:T(8,128)(2,1)S(1)} collective-permute-done((bf16[8,2,128,128]{3,2,1,0:T(8,128)(2,1)S(1)}, bf16[8,2,128,128]{3,2,1,0:T(8,128)(2,1)S(1)}, u32[]{:S(2)}, u32[]{:S(2)}) %collective-permute-start.3) | collective-permute-done | bytes 524320 | tf_op jit(solution)/shard_map/ppermute | solution.py:397
  32.8 5.5 %shard_map.97 = (bf16[6,2,128,128]{3,2,1,0:T(8,128)(2,1)S(1)}, bf16[6,2,128,128]{3,2,1,0:T(8,128)(2,1)S(1)}, bf16[6,2,128,128]{3,2,1,0:T(8,128)(2,1)S(1)}, bf16[...) custom-call(s32[1]{0:T(128)} %bitcast.place, ...), custom_call_target="tpu_custom_call" | custom-call | flops 1207959552 | bytes 5242880 | tf_op jit(solution)/shard_map/pallas_call | solution.py:330
  38.4 10.4 %collective-permute-start.13 = (bf16[4,2,128,128]{3,2,1,0:T(8,128)(2,1)S(1)}, bf16[4,2,128,128]{3,2,1,0:T(8,128)(2,1)S(1)}, u32[]{:S(2)}, u32[]{:S(2)}) collective-permute-start(bf16[4,2,128,128]{3,2,1,0:T(8,128)(2,1)S(1)} %get-tuple-element.70), channel_id=1, source_target_pairs={{0,4},{1,5},{2,6},{3,7},{4,0},{5,1},{6,2},{7,3},{8,12},{9,13},{10,... | collective-permute-start | bytes 786440 | tf_op jit(solution)/shard_map/ppermute | solution.py:397
  48.8 0.7 collective-permute-start.14
  49.5 5.9 %shard_map.98 = (bf16[6,2,128,128]{3,2,1,0:T(8,128)(2,1)S(1)}, bf16[6,2,128,128]{3,2,1,0:T(8,128)(2,1)S(1)}, bf16[6,2,128,128]{3,2,1,0:T(8,128)(2,1)S(1)}, bf16[...) custom-call(s32[1]{0:T(128)} %bitcast.place, ...), custom_call_target="tpu_custom_call", output_to_operand_aliasing={{0}: (12, {}), {1}: (13, {}), {2}: (14, {}), {3}: (15, {})} | custom-call | flops 1207959552 | bytes 5242880 | tf_op jit(solution)/shard_map/pallas_call | solution.py:330
  55.6 0.7 collective-permute-start.15
  56.3 3.4 %collective-permute-start.8 = (bf16[8,2,128,128]{3,2,1,0:T(8,128)(2,1)S(1)}, bf16[8,2,128,128]{3,2,1,0:T(8,128)(2,1)S(1)}, u32[]{:S(2)}, u32[]{:S(2)}) collective-permute-start(bf16[8,2,128,128]{3,2,1,0:T(8,128)(2,1)S(1)} %get-tuple-element.63), channel_id=1, source_target_pairs={{0,4},{1,5},{2,6},{3,7},{4,0},{5,1},{6,2},{7,3},{8,12},{9,13},{10,... | collective-permute-start | bytes 1572872 | tf_op jit(solution)/shard_map/ppermute | solution.py:397
  59.7 0.9 collective-permute-start.7
  60.6 0.7 collective-permute-start.9
  61.2 1.4 %collective-permute-start.16 = (bf16[6,2,128,128]{3,2,1,0:T(8,128)(2,1)S(1)}, bf16[6,2,128,128]{3,2,1,0:T(8,128)(2,1)S(1)}, u32[]{:S(2)}, u32[]{:S(2)}) collective-permute-start(bf16[6,2,128,128]{3,2,1,0:T(8,128)(2,1)S(1)} %get-tuple-element.82), channel_id=1, source_target_pairs={{0,2},{1,3},{2,0},{3,1},{4,6},{5,7},{6,4},{7,5},{8,10},{9,11},{10,... | collective-permute-start | bytes 1179656 | tf_op jit(solution)/shard_map/ppermute | solution.py:648
  62.6 0.8 collective-permute-start.17
  63.4 13.3 %collective-permute-done.7.refs_0_ = bf16[4,2,128,128]{3,2,1,0:T(8,128)(2,1)S(1)} collective-permute-done((bf16[4,2,128,128]{3,2,1,0:T(8,128)(2,1)S(1)}, bf16[4,2,128,128]{3,2,1,0:T(8,128)(2,1)S(1)}, u32[]{:S(2)}, u32[]{:S(2)}) %collective-permute-start.7) | collective-permute-done | bytes 262176 | tf_op jit(solution)/shard_map/ppermute | solution.py:397
  76.7 0.9 collective-permute-done.8.refs_1_
  77.8 0.7 collective-permute-start.10
  78.5 1.2 %collective-permute-start.11 = (bf16[2,2,128,128]{3,2,1,0:T(8,128)(2,1)S(1)}, bf16[2,2,128,128]{3,2,1,0:T(8,128)(2,1)S(1)}, u32[]{:S(2)}, u32[]{:S(2)}) collective-permute-start(bf16[2,2,128,128]{3,2,1,0:T(8,128)(2,1)S(1)} %get-tuple-element.67), channel_id=1, source_target_pairs={{0,2},{1,3},{2,0},{3,1},{4,6},{5,7},{6,4},{7,5},{8,10},{9,11},{10,... | collective-permute-start | bytes 393224 | tf_op jit(solution)/shard_map/ppermute | solution.py:648
  79.7 0.5 collective-permute-start.12
  80.2 0.4 collective-permute-done.17.refs_3_.refs_7_
  80.6 1.8 %shard_map.101 = (bf16[128,16,128]{2,1,0:T(8,128)(2,1)}, bf16[128,16,128]{2,1,0:T(8,128)(2,1)}) custom-call(s32[1]{0:T(128)} %bitcast.place, s32[4,4]{1,0:T(4,128)S(1)} %copy-done.1, bf16[6,2,128,128]{3,2,1,0:T(8,128)(2,1)S(1)} %get-tuple-element.80.refs_0_.refs_4_, bf16[6,2,128,128]{3,2,1,0:T(8,128)(2,1)S(1)} %collective-permute-done.15.refs_1_.refs_5_, ...), custom_call_target="tpu_custom_call" | custom-call | bytes 6291456 | tf_op jit(solution)/shard_map/pallas_call | solution.py:158
  82.4 1.2 %collective-permute-done.11.refs_2_ = bf16[2,2,128,128]{3,2,1,0:T(8,128)(2,1)S(1)} collective-permute-done((bf16[2,2,128,128]{3,2,1,0:T(8,128)(2,1)S(1)}, bf16[2,2,128,128]{3,2,1,0:T(8,128)(2,1)S(1)}, u32[]{:S(2)}, u32[]{:S(2)}) %collective-permute-start.11) | collective-permute-done | bytes 131104 | tf_op jit(solution)/shard_map/ppermute | solution.py:648
  83.6 3.0 %collective-permute-done.12.refs_3_ = bf16[2,2,128,128]{3,2,1,0:T(8,128)(2,1)S(1)} collective-permute-done((bf16[2,2,128,128]{3,2,1,0:T(8,128)(2,1)S(1)}, bf16[2,2,128,128]{3,2,1,0:T(8,128)(2,1)S(1)}, u32[]{:S(2)}, u32[]{:S(2)}) %collective-permute-start.12) | collective-permute-done | bytes 131104 | tf_op jit(solution)/shard_map/ppermute | solution.py:648
  86.6 1.8 %shard_map.102 = (bf16[128,16,128]{2,1,0:T(8,128)(2,1)}, bf16[128,16,128]{2,1,0:T(8,128)(2,1)}) custom-call(s32[1]{0:T(128)} %bitcast.place, s32[4,4]{1,0:T(4,128)S(1)} %copy-done.1, bf16[2,2,128,128]{3,2,1,0:T(8,128)(2,1)S(1)} %get-tuple-element.88.refs_0_, bf16[2,2,128,128]{3,2,1,0:T(8,128)(2,1)S(1)} %collective-permute-done.10.refs_1_, ...), custom_call_target="tpu_custom_call" | custom-call | bytes 4194304 | tf_op jit(solution)/shard_map/pallas_call | solution.py:158
  (22 shorter events, 0.7 us)
Async XLA Ops:
  2.9 9.0 %collective-permute-start = (bf16[4,2,128,128]{3,2,1,0:T(8,128)(2,1)}, bf16[4,2,128,128]{3,2,1,0:T(8,128)(2,1)S(1)}, u32[]{:S(2)}, u32[]{:S(2)}) collective-permute-start(bf16[4,2,128,128]{3,2,1,0:T(8,128)(2,1)} %get-tuple-element.50), channel_id=1, source_target_pairs={{0,1},{1,0},{2,3},{3,2},{4,5},{5,4},{6,7},{7,6},{8,9},{9,8},{10,11... | collective-permute-start | bytes 786440 | tf_op jit(solution)/shard_map/ppermute | solution.py:648
  3.0 9.5 %collective-permute-start.1 = (bf16[4,2,128,128]{3,2,1,0:T(8,128)(2,1)}, bf16[4,2,128,128]{3,2,1,0:T(8,128)(2,1)S(1)}, u32[]{:S(2)}, u32[]{:S(2)}) collective-permute-start(bf16[4,2,128,128]{3,2,1,0:T(8,128)(2,1)} %get-tuple-element.51), channel_id=1, source_target_pairs={{0,2},{1,3},{2,0},{3,1},{4,6},{5,7},{6,4},{7,5},{8,10},{9,11},{10,... | collective-permute-start | bytes 786440 | tf_op jit(solution)/shard_map/ppermute | solution.py:648
  5.6 12.9 %collective-permute-start.2 = (bf16[4,2,128,128]{3,2,1,0:T(8,128)(2,1)}, bf16[4,2,128,128]{3,2,1,0:T(8,128)(2,1)S(1)}, u32[]{:S(2)}, u32[]{:S(2)}) collective-permute-start(bf16[4,2,128,128]{3,2,1,0:T(8,128)(2,1)} %get-tuple-element.52), channel_id=1, source_target_pairs={{0,3},{1,2},{2,1},{3,0},{4,7},{5,6},{6,5},{7,4},{8,11},{9,10},{10,... | collective-permute-start | bytes 786440 | tf_op jit(solution)/shard_map/ppermute | solution.py:648
  7.9 10.7 %copy-start = (bf16[4,2,128,128]{3,2,1,0:T(8,128)(2,1)S(1)}, bf16[4,2,128,128]{3,2,1,0:T(8,128)(2,1)}, u32[]{:S(2)}) copy-start(bf16[4,2,128,128]{3,2,1,0:T(8,128)(2,1)} %get-tuple-element.49.refs_0_) | copy-start | bytes 786436
  7.9 24.9 %all-to-all-start = ((bf16[4,4,2,128,128]{4,3,2,1,0:T(8,128)(2,1)}), bf16[4,4,2,128,128]{4,3,2,1,0:T(8,128)(2,1)S(1)}, u32[]{:S(2)}, u32[]{:S(2)}) async-start(bf16[4,4,2,128,128]{4,3,2,1,0:T(8,128)(2,1)} %shard_map.94), calls=%async_computation | async-start | bytes 2097152 | tf_op jit(solution)/shard_map/all_to_all | solution.py:675
  18.7 14.2 %collective-permute-start.3 = (bf16[8,2,128,128]{3,2,1,0:T(8,128)(2,1)S(1)}, bf16[8,2,128,128]{3,2,1,0:T(8,128)(2,1)S(1)}, u32[]{:S(2)}, u32[]{:S(2)}) collective-permute-start(bf16[8,2,128,128]{3,2,1,0:T(8,128)(2,1)S(1)} %get-tuple-element.53), channel_id=1, source_target_pairs={{0,4},{1,5},{2,6},{3,7},{4,0},{5,1},{6,2},{7,3},{8,12},{9,13},{10,... | collective-permute-start | bytes 1572872 | tf_op jit(solution)/shard_map/ppermute | solution.py:397
  20.5 12.3 %collective-permute-start.4 = (bf16[8,2,128,128]{3,2,1,0:T(8,128)(2,1)S(1)}, bf16[8,2,128,128]{3,2,1,0:T(8,128)(2,1)S(1)}, u32[]{:S(2)}, u32[]{:S(2)}) collective-permute-start(bf16[8,2,128,128]{3,2,1,0:T(8,128)(2,1)S(1)} %get-tuple-element.54), channel_id=1, source_target_pairs={{4,8},{5,9},{6,10},{7,11},{8,4},{9,5},{10,6},{11,7},{20,24},{21,25... | collective-permute-start | bytes 1572872 | tf_op jit(solution)/shard_map/ppermute | solution.py:669
  22.0 10.8 %copy-start.1 = (s32[4,4]{1,0:T(4,128)S(1)}, s32[4,4]{1,0:T(4,128)}, u32[]{:S(2)}) copy-start(s32[4,4]{1,0:T(4,128)} %sections.11) | copy-start | bytes 196
  22.0 10.8 %copy-start.2 = (s32[16]{0:T(128)S(1)}, s32[16]{0:T(128)}, u32[]{:S(2)}) copy-start(s32[16]{0:T(128)} %widths.3) | copy-start | bytes 196
  22.0 27.4 %collective-permute-start.5 = (bf16[4,2,128,128]{3,2,1,0:T(8,128)(2,1)}, bf16[4,2,128,128]{3,2,1,0:T(8,128)(2,1)S(1)}, u32[]{:S(2)}, u32[]{:S(2)}) collective-permute-start(bf16[4,2,128,128]{3,2,1,0:T(8,128)(2,1)} %get-tuple-element.55), channel_id=1, source_target_pairs={{0,8},{1,9},{2,10},{3,11},{4,12},{5,13},{6,14},{7,15},{8,0},{9,1},... | collective-permute-start | bytes 786440 | tf_op jit(solution)/shard_map/ppermute | solution.py:397
  25.5 23.9 %collective-permute-start.6 = (bf16[4,2,128,128]{3,2,1,0:T(8,128)(2,1)}, bf16[4,2,128,128]{3,2,1,0:T(8,128)(2,1)}, u32[]{:S(2)}, u32[]{:S(2)}) collective-permute-start(bf16[4,2,128,128]{3,2,1,0:T(8,128)(2,1)} %get-tuple-element.56), channel_id=1, source_target_pairs={{0,4},{1,5},{2,6},{3,7},{4,0},{5,1},{6,2},{7,3},{8,12},{9,13},{10,... | collective-permute-start | bytes 786440 | tf_op jit(solution)/shard_map/ppermute | solution.py:397
  38.4 17.0 %collective-permute-start.13 = (bf16[4,2,128,128]{3,2,1,0:T(8,128)(2,1)S(1)}, bf16[4,2,128,128]{3,2,1,0:T(8,128)(2,1)S(1)}, u32[]{:S(2)}, u32[]{:S(2)}) collective-permute-start(bf16[4,2,128,128]{3,2,1,0:T(8,128)(2,1)S(1)} %get-tuple-element.70), channel_id=1, source_target_pairs={{0,4},{1,5},{2,6},{3,7},{4,0},{5,1},{6,2},{7,3},{8,12},{9,13},{10,... | collective-permute-start | bytes 786440 | tf_op jit(solution)/shard_map/ppermute | solution.py:397
  48.8 6.6 %collective-permute-start.14 = (bf16[4,2,128,128]{3,2,1,0:T(8,128)(2,1)S(1)}, bf16[4,2,128,128]{3,2,1,0:T(8,128)(2,1)S(1)}, u32[]{:S(2)}, u32[]{:S(2)}) collective-permute-start(bf16[4,2,128,128]{3,2,1,0:T(8,128)(2,1)S(1)} %get-tuple-element.71), channel_id=1, source_target_pairs={{4,8},{5,9},{6,10},{7,11},{8,4},{9,5},{10,6},{11,7},{20,24},{21,25... | collective-permute-start | bytes 786440 | tf_op jit(solution)/shard_map/ppermute | solution.py:669
  55.6 5.6 %collective-permute-start.15 = (bf16[6,2,128,128]{3,2,1,0:T(8,128)(2,1)S(1)}, bf16[6,2,128,128]{3,2,1,0:T(8,128)(2,1)S(1)}, u32[]{:S(2)}, u32[]{:S(2)}) collective-permute-start(bf16[6,2,128,128]{3,2,1,0:T(8,128)(2,1)S(1)} %get-tuple-element.77), channel_id=1, source_target_pairs={{0,1},{1,0},{2,3},{3,2},{4,5},{5,4},{6,7},{7,6},{8,9},{9,8},{10,11... | collective-permute-start | bytes 1179656 | tf_op jit(solution)/shard_map/ppermute | solution.py:648
  56.3 21.2 %collective-permute-start.8 = (bf16[8,2,128,128]{3,2,1,0:T(8,128)(2,1)S(1)}, bf16[8,2,128,128]{3,2,1,0:T(8,128)(2,1)S(1)}, u32[]{:S(2)}, u32[]{:S(2)}) collective-permute-start(bf16[8,2,128,128]{3,2,1,0:T(8,128)(2,1)S(1)} %get-tuple-element.63), channel_id=1, source_target_pairs={{0,4},{1,5},{2,6},{3,7},{4,0},{5,1},{6,2},{7,3},{8,12},{9,13},{10,... | collective-permute-start | bytes 1572872 | tf_op jit(solution)/shard_map/ppermute | solution.py:397
  59.7 17.0 %collective-permute-start.7 = (bf16[4,2,128,128]{3,2,1,0:T(8,128)(2,1)S(1)}, bf16[4,2,128,128]{3,2,1,0:T(8,128)(2,1)S(1)}, u32[]{:S(2)}, u32[]{:S(2)}) collective-permute-start(bf16[4,2,128,128]{3,2,1,0:T(8,128)(2,1)S(1)} %get-tuple-element.62), channel_id=1, source_target_pairs={{0,8},{1,9},{2,10},{3,11},{4,12},{5,13},{6,14},{7,15},{8,0},{9,1},... | collective-permute-start | bytes 786440 | tf_op jit(solution)/shard_map/ppermute | solution.py:397
  60.6 16.1 %collective-permute-start.9 = (bf16[4,2,128,128]{3,2,1,0:T(8,128)(2,1)S(1)}, bf16[4,2,128,128]{3,2,1,0:T(8,128)(2,1)S(1)}, u32[]{:S(2)}, u32[]{:S(2)}) collective-permute-start(bf16[4,2,128,128]{3,2,1,0:T(8,128)(2,1)S(1)} %get-tuple-element.64), channel_id=1, source_target_pairs={{4,8},{5,9},{6,10},{7,11},{8,4},{9,5},{10,6},{11,7},{20,24},{21,25... | collective-permute-start | bytes 786440 | tf_op jit(solution)/shard_map/ppermute | solution.py:669
  61.2 19.0 %collective-permute-start.16 = (bf16[6,2,128,128]{3,2,1,0:T(8,128)(2,1)S(1)}, bf16[6,2,128,128]{3,2,1,0:T(8,128)(2,1)S(1)}, u32[]{:S(2)}, u32[]{:S(2)}) collective-permute-start(bf16[6,2,128,128]{3,2,1,0:T(8,128)(2,1)S(1)} %get-tuple-element.82), channel_id=1, source_target_pairs={{0,2},{1,3},{2,0},{3,1},{4,6},{5,7},{6,4},{7,5},{8,10},{9,11},{10,... | collective-permute-start | bytes 1179656 | tf_op jit(solution)/shard_map/ppermute | solution.py:648
  62.6 18.0 %collective-permute-start.17 = (bf16[6,2,128,128]{3,2,1,0:T(8,128)(2,1)S(1)}, bf16[6,2,128,128]{3,2,1,0:T(8,128)(2,1)S(1)}, u32[]{:S(2)}, u32[]{:S(2)}) collective-permute-start(bf16[6,2,128,128]{3,2,1,0:T(8,128)(2,1)S(1)} %get-tuple-element.83), channel_id=1, source_target_pairs={{0,3},{1,2},{2,1},{3,0},{4,7},{5,6},{6,5},{7,4},{8,11},{9,10},{10,... | collective-permute-start | bytes 1179656 | tf_op jit(solution)/shard_map/ppermute | solution.py:648
  77.8 4.6 %collective-permute-start.10 = (bf16[2,2,128,128]{3,2,1,0:T(8,128)(2,1)S(1)}, bf16[2,2,128,128]{3,2,1,0:T(8,128)(2,1)S(1)}, u32[]{:S(2)}, u32[]{:S(2)}) collective-permute-start(bf16[2,2,128,128]{3,2,1,0:T(8,128)(2,1)S(1)} %get-tuple-element.66), channel_id=1, source_target_pairs={{0,1},{1,0},{2,3},{3,2},{4,5},{5,4},{6,7},{7,6},{8,9},{9,8},{10,11... | collective-permute-start | bytes 393224 | tf_op jit(solution)/shard_map/ppermute | solution.py:648
  78.5 5.1 %collective-permute-start.11 = (bf16[2,2,128,128]{3,2,1,0:T(8,128)(2,1)S(1)}, bf16[2,2,128,128]{3,2,1,0:T(8,128)(2,1)S(1)}, u32[]{:S(2)}, u32[]{:S(2)}) collective-permute-start(bf16[2,2,128,128]{3,2,1,0:T(8,128)(2,1)S(1)} %get-tuple-element.67), channel_id=1, source_target_pairs={{0,2},{1,3},{2,0},{3,1},{4,6},{5,7},{6,4},{7,5},{8,10},{9,11},{10,... | collective-permute-start | bytes 393224 | tf_op jit(solution)/shard_map/ppermute | solution.py:648
  79.7 6.8 %collective-permute-start.12 = (bf16[2,2,128,128]{3,2,1,0:T(8,128)(2,1)S(1)}, bf16[2,2,128,128]{3,2,1,0:T(8,128)(2,1)S(1)}, u32[]{:S(2)}, u32[]{:S(2)}) collective-permute-start(bf16[2,2,128,128]{3,2,1,0:T(8,128)(2,1)S(1)} %get-tuple-element.68), channel_id=1, source_target_pairs={{0,3},{1,2},{2,1},{3,0},{4,7},{5,6},{6,5},{7,4},{8,11},{9,10},{10,... | collective-permute-start | bytes 393224 | tf_op jit(solution)/shard_map/ppermute | solution.py:648

commit v9 on v8

--- a/solution.py
+++ b/solution.py
@@ -689,8 +689,9 @@
     pairs = in_plane(sent)
     next_sent, last_sent = halo_parts(place, pairs)
     far_sent = far_parts(pairs, total - local)
-    halos = (with_next_plane(next_sent), with_last_plane(last_sent))
-    far = (with_other_plane(far_sent[1]), with_next_plane(far_sent[0]))
+    halos = [with_next_plane(next_sent), with_last_plane(last_sent)]
+    halos[0], other_sent = lax.optimization_barrier((halos[0], far_sent[1]))
+    far = (with_other_plane(other_sent), with_next_plane(far_sent[0]))
     rows, part_near, owed = attend(
         *tables, pairs, graded, halos, (), local, 0, total - local, blocks
     )

time: 89.3 us -> 87.2 us (0.976)
  starting transfers between devices: 34.4 us -> 29.4 us
  waiting for transfers between devices: 32.3 us -> 35.8 us
    ppermute x6, starting transfers between devices: 20.4 us -> 13.9 us  [partner(): lax.ppermute(value, axis, [(i, i ^ 1 << apart) for i in range(lax.axis_si...]
    ppermute x6, waiting for transfers between devices: 21.1 us -> 23.7 us  [partner(): lax.ppermute(value, axis, [(i, i ^ 1 << apart) for i in range(lax.axis_si...]
    ppermute x9, starting transfers between devices: 8.03 us -> 9.58 us  [in_plane(): lax.ppermute(pieces[m], 'seq', [(i, i ^ m) for i in range(peers)])]
where the time goes in v9:
time: 87.2 us; the launch traced here: 86.9 us
  waiting for transfers between devices  35.8 us (41%)
  starting transfers between devices  29.4 us (34%)
  Pallas kernels  20.9 us (24%)
    ppermute x6, waiting for transfers between devices, partner(): lax.ppermute(value, axis, [(i, i ^ 1 << apart) for i in range(lax.axis_si...  23.7 us
    ppermute x6, starting transfers between devices, partner(): lax.ppermute(value, axis, [(i, i ^ 1 << apart) for i in range(lax.axis_si...  13.9 us
    ppermute x9, waiting for transfers between devices, in_plane(): lax.ppermute(pieces[m], 'seq', [(i, i ^ m) for i in range(peers)])  12 us
    pallas_call x2, Pallas kernels, attend(): pl.pallas_call(functools.partial(attend_kernel, first=first, slot=slot, g...  11.4 us
    ppermute x9, starting transfers between devices, in_plane(): lax.ppermute(pieces[m], 'seq', [(i, i ^ m) for i in range(peers)])  9.58 us
    pallas_call x2, Pallas kernels, pack(): pl.pallas_call(functools.partial(pack_kernel, order=order, count=count, c...  4.49 us
    all_to_all x1, starting transfers between devices, plane_all_to_all(): lax.all_to_all(value, 'seq', 0, 0, axis_index_groups=planes, tiled=True)  3.99 us
    pallas_call x2, Pallas kernels, unpack(): pl.pallas_call(functools.partial(unpack_kernel, groups=[group for group,...  3.64 us
  transfers between devices with their start and end apart: 19, of which 8 were waited for; matrix products, arithmetic and copies ran while one was open for 0% of the time, Pallas kernels for 19%

profile of v9, /device:TPU:1, one launch (start us, length us, event | category | flops | bytes accessed | tf_op | source)
XLA Modules:
  0.0 86.9 jit_solution(5958875704316724997)
XLA Ops:
  0.6 2.3 %shard_map.93 = (bf16[4,2,128,128]{3,2,1,0:T(8,128)(2,1)}, bf16[4,2,128,128]{3,2,1,0:T(8,128)(2,1)}, bf16[4,2,128,128]{3,2,1,0:T(8,128)(2,1)}, bf16[4,2,128,128]{3,2,1,0:T(8,128)(2,1)}) custom-call(s32[1]{0:T(128)} %bitcast.place, s32[4,4]{1,0:T(4,128)} %sections.11, bf16[128,16,128]{2,1,0:T(8,128)(2,1)} %refs_0_.2, bf16[128,16,128]{2,1,0:T(8,128)(2,1)} %refs_1_.2), custom_call_target="tpu_custom_call" | custom-call | bytes 2097152 | tf_op jit(solution)/shard_map/pallas_call | solution.py:124
  3.0 2.7 %collective-permute-start.1 = (bf16[4,2,128,128]{3,2,1,0:T(8,128)(2,1)}, bf16[4,2,128,128]{3,2,1,0:T(8,128)(2,1)S(1)}, u32[]{:S(2)}, u32[]{:S(2)}) collective-permute-start(bf16[4,2,128,128]{3,2,1,0:T(8,128)(2,1)} %get-tuple-element.53), channel_id=1, source_target_pairs={{0,2},{1,3},{2,0},{3,1},{4,6},{5,7},{6,4},{7,5},{8,10},{9,11},{10,... | collective-permute-start | bytes 786440 | tf_op jit(solution)/shard_map/ppermute | solution.py:648
  5.7 2.2 %shard_map.94 = bf16[4,4,2,128,128]{4,3,2,1,0:T(8,128)(2,1)} custom-call(s32[1]{0:T(128)} %bitcast.place, s32[4,4]{1,0:T(4,128)} %sections.11, bf16[128,16,128]{2,1,0:T(8,128)(2,1)} %refs_0_.3, bf16[128,16,128]{2,1,0:T(8,128)(2,1)} %refs_1_.3), custom_call_target="tpu_custom_call" | custom-call | bytes 2097152 | tf_op jit(solution)/shard_map/pallas_call | solution.py:124
  7.9 4.0 %all-to-all-start = ((bf16[4,4,2,128,128]{4,3,2,1,0:T(8,128)(2,1)}), bf16[4,4,2,128,128]{4,3,2,1,0:T(8,128)(2,1)S(1)}, u32[]{:S(2)}, u32[]{:S(2)}) async-start(bf16[4,4,2,128,128]{4,3,2,1,0:T(8,128)(2,1)} %shard_map.94), calls=%async_computation | async-start | bytes 2097152 | tf_op jit(solution)/shard_map/all_to_all | solution.py:675
  11.9 0.5 collective-permute-done.1.refs_2_
  12.5 6.1 %collective-permute-done.2.refs_3_ = bf16[4,2,128,128]{3,2,1,0:T(8,128)(2,1)S(1)} collective-permute-done((bf16[4,2,128,128]{3,2,1,0:T(8,128)(2,1)}, bf16[4,2,128,128]{3,2,1,0:T(8,128)(2,1)S(1)}, u32[]{:S(2)}, u32[]{:S(2)}) %collective-permute-start.2) | collective-permute-done | bytes 262176 | tf_op jit(solution)/shard_map/ppermute | solution.py:648
  18.7 1.8 %collective-permute-start.3 = (bf16[8,2,128,128]{3,2,1,0:T(8,128)(2,1)S(1)}, bf16[8,2,128,128]{3,2,1,0:T(8,128)(2,1)S(1)}, u32[]{:S(2)}, u32[]{:S(2)}) collective-permute-start(bf16[8,2,128,128]{3,2,1,0:T(8,128)(2,1)S(1)} %get-tuple-element.55), channel_id=1, source_target_pairs={{0,4},{1,5},{2,6},{3,7},{4,0},{5,1},{6,2},{7,3},{8,12},{9,13},{10,... | collective-permute-start | bytes 1572872 | tf_op jit(solution)/shard_map/ppermute | solution.py:397
  20.5 0.7 collective-permute-start.4
  21.2 0.8 shard_map.96
  22.0 3.8 %collective-permute-start.6 = (bf16[4,2,128,128]{3,2,1,0:T(8,128)(2,1)}, bf16[4,2,128,128]{3,2,1,0:T(8,128)(2,1)S(1)}, u32[]{:S(2)}, u32[]{:S(2)}) collective-permute-start(bf16[4,2,128,128]{3,2,1,0:T(8,128)(2,1)} %get-tuple-element.60), channel_id=1, source_target_pairs={{0,4},{1,5},{2,6},{3,7},{4,0},{5,1},{6,2},{7,3},{8,12},{9,13},{10,... | collective-permute-start | bytes 786440 | tf_op jit(solution)/shard_map/ppermute | solution.py:397
  25.8 7.0 %collective-permute-done.3.refs_5_ = bf16[8,2,128,128]{3,2,1,0:T(8,128)(2,1)S(1)} collective-permute-done((bf16[8,2,128,128]{3,2,1,0:T(8,128)(2,1)S(1)}, bf16[8,2,128,128]{3,2,1,0:T(8,128)(2,1)S(1)}, u32[]{:S(2)}, u32[]{:S(2)}) %collective-permute-start.3) | collective-permute-done | bytes 524320 | tf_op jit(solution)/shard_map/ppermute | solution.py:397
  32.8 2.6 %collective-permute-start.5 = (bf16[4,2,128,128]{3,2,1,0:T(8,128)(2,1)}, bf16[4,2,128,128]{3,2,1,0:T(8,128)(2,1)}, u32[]{:S(2)}, u32[]{:S(2)}) collective-permute-start(bf16[4,2,128,128]{3,2,1,0:T(8,128)(2,1)} %get-tuple-element.59), channel_id=1, source_target_pairs={{0,8},{1,9},{2,10},{3,11},{4,12},{5,13},{6,14},{7,15},{8,0},{9,1},... | collective-permute-start | bytes 786440 | tf_op jit(solution)/shard_map/ppermute | solution.py:397
  35.4 5.5 %shard_map.97 = (bf16[6,2,128,128]{3,2,1,0:T(8,128)(2,1)S(1)}, bf16[6,2,128,128]{3,2,1,0:T(8,128)(2,1)S(1)}, bf16[6,2,128,128]{3,2,1,0:T(8,128)(2,1)S(1)}, bf16[...) custom-call(s32[1]{0:T(128)} %bitcast.place, ...), custom_call_target="tpu_custom_call" | custom-call | flops 1207959552 | bytes 5242880 | tf_op jit(solution)/shard_map/pallas_call | solution.py:330
  41.0 2.1 %collective-permute-start.13 = (bf16[4,2,128,128]{3,2,1,0:T(8,128)(2,1)S(1)}, bf16[4,2,128,128]{3,2,1,0:T(8,128)(2,1)S(1)}, u32[]{:S(2)}, u32[]{:S(2)}) collective-permute-start(bf16[4,2,128,128]{3,2,1,0:T(8,128)(2,1)S(1)} %get-tuple-element.74), channel_id=1, source_target_pairs={{0,4},{1,5},{2,6},{3,7},{4,0},{5,1},{6,2},{7,3},{8,12},{9,13},{10,... | collective-permute-start | bytes 786440 | tf_op jit(solution)/shard_map/ppermute | solution.py:397
  43.0 0.7 collective-permute-start.14
  43.7 4.2 %collective-permute-done.5.refs_7_ = bf16[4,2,128,128]{3,2,1,0:T(8,128)(2,1)} collective-permute-done((bf16[4,2,128,128]{3,2,1,0:T(8,128)(2,1)}, bf16[4,2,128,128]{3,2,1,0:T(8,128)(2,1)}, u32[]{:S(2)}, u32[]{:S(2)}) %collective-permute-start.5) | collective-permute-done | bytes 262176 | tf_op jit(solution)/shard_map/ppermute | solution.py:397
  47.9 5.9 %shard_map.98 = (bf16[6,2,128,128]{3,2,1,0:T(8,128)(2,1)S(1)}, bf16[6,2,128,128]{3,2,1,0:T(8,128)(2,1)S(1)}, bf16[6,2,128,128]{3,2,1,0:T(8,128)(2,1)S(1)}, bf16[...) custom-call(s32[1]{0:T(128)} %bitcast.place, ...), custom_call_target="tpu_custom_call", output_to_operand_aliasing={{0}: (12, {}), {1}: (13, {}), {2}: (14, {}), {3}: (15, {})} | custom-call | flops 1207959552 | bytes 5242880 | tf_op jit(solution)/shard_map/pallas_call | solution.py:330
  54.1 1.8 %collective-permute-start.15 = (bf16[6,2,128,128]{3,2,1,0:T(8,128)(2,1)S(1)}, bf16[6,2,128,128]{3,2,1,0:T(8,128)(2,1)S(1)}, u32[]{:S(2)}, u32[]{:S(2)}) collective-permute-start(bf16[6,2,128,128]{3,2,1,0:T(8,128)(2,1)S(1)} %get-tuple-element.81), channel_id=1, source_target_pairs={{0,1},{1,0},{2,3},{3,2},{4,5},{5,4},{6,7},{7,6},{8,9},{9,8},{10,11... | collective-permute-start | bytes 1179656 | tf_op jit(solution)/shard_map/ppermute | solution.py:648
  55.9 0.4 collective-permute-start.8
  56.4 3.1 %collective-permute-start.7 = (bf16[4,2,128,128]{3,2,1,0:T(8,128)(2,1)S(1)}, bf16[4,2,128,128]{3,2,1,0:T(8,128)(2,1)S(1)}, u32[]{:S(2)}, u32[]{:S(2)}) collective-permute-start(bf16[4,2,128,128]{3,2,1,0:T(8,128)(2,1)S(1)} %get-tuple-element.66), channel_id=1, source_target_pairs={{0,8},{1,9},{2,10},{3,11},{4,12},{5,13},{6,14},{7,15},{8,0},{9,1},... | collective-permute-start | bytes 786440 | tf_op jit(solution)/shard_map/ppermute | solution.py:397
  59.5 0.7 collective-permute-start.9
  60.1 1.1 %collective-permute-start.16 = (bf16[6,2,128,128]{3,2,1,0:T(8,128)(2,1)S(1)}, bf16[6,2,128,128]{3,2,1,0:T(8,128)(2,1)S(1)}, u32[]{:S(2)}, u32[]{:S(2)}) collective-permute-start(bf16[6,2,128,128]{3,2,1,0:T(8,128)(2,1)S(1)} %get-tuple-element.86), channel_id=1, source_target_pairs={{0,2},{1,3},{2,0},{3,1},{4,6},{5,7},{6,4},{7,5},{8,10},{9,11},{10,... | collective-permute-start | bytes 1179656 | tf_op jit(solution)/shard_map/ppermute | solution.py:648
  61.3 1.2 %collective-permute-start.17 = (bf16[6,2,128,128]{3,2,1,0:T(8,128)(2,1)S(1)}, bf16[6,2,128,128]{3,2,1,0:T(8,128)(2,1)S(1)}, u32[]{:S(2)}, u32[]{:S(2)}) collective-permute-start(bf16[6,2,128,128]{3,2,1,0:T(8,128)(2,1)S(1)} %get-tuple-element.87), channel_id=1, source_target_pairs={{0,3},{1,2},{2,1},{3,0},{4,7},{5,6},{6,5},{7,4},{8,11},{9,10},{10,... | collective-permute-start | bytes 1179656 | tf_op jit(solution)/shard_map/ppermute | solution.py:648
  62.5 10.8 %collective-permute-done.7.refs_0_ = bf16[4,2,128,128]{3,2,1,0:T(8,128)(2,1)S(1)} collective-permute-done((bf16[4,2,128,128]{3,2,1,0:T(8,128)(2,1)S(1)}, bf16[4,2,128,128]{3,2,1,0:T(8,128)(2,1)S(1)}, u32[]{:S(2)}, u32[]{:S(2)}) %collective-permute-start.7) | collective-permute-done | bytes 262176 | tf_op jit(solution)/shard_map/ppermute | solution.py:397
  73.3 1.7 %collective-permute-done.8.refs_1_ = bf16[8,2,128,128]{3,2,1,0:T(8,128)(2,1)S(1)} collective-permute-done((bf16[8,2,128,128]{3,2,1,0:T(8,128)(2,1)S(1)}, bf16[8,2,128,128]{3,2,1,0:T(8,128)(2,1)S(1)}, u32[]{:S(2)}, u32[]{:S(2)}) %collective-permute-start.8) | collective-permute-done | bytes 524320 | tf_op jit(solution)/shard_map/ppermute | solution.py:397
  75.3 0.9 %collective-permute-start.10 = (bf16[2,2,128,128]{3,2,1,0:T(8,128)(2,1)S(1)}, bf16[2,2,128,128]{3,2,1,0:T(8,128)(2,1)S(1)}, u32[]{:S(2)}, u32[]{:S(2)}) collective-permute-start(bf16[2,2,128,128]{3,2,1,0:T(8,128)(2,1)S(1)} %get-tuple-element.70), channel_id=1, source_target_pairs={{0,1},{1,0},{2,3},{3,2},{4,5},{5,4},{6,7},{7,6},{8,9},{9,8},{10,11... | collective-permute-start | bytes 393224 | tf_op jit(solution)/shard_map/ppermute | solution.py:648
  76.2 1.1 %collective-permute-start.11 = (bf16[2,2,128,128]{3,2,1,0:T(8,128)(2,1)S(1)}, bf16[2,2,128,128]{3,2,1,0:T(8,128)(2,1)S(1)}, u32[]{:S(2)}, u32[]{:S(2)}) collective-permute-start(bf16[2,2,128,128]{3,2,1,0:T(8,128)(2,1)S(1)} %get-tuple-element.71), channel_id=1, source_target_pairs={{0,2},{1,3},{2,0},{3,1},{4,6},{5,7},{6,4},{7,5},{8,10},{9,11},{10,... | collective-permute-start | bytes 393224 | tf_op jit(solution)/shard_map/ppermute | solution.py:648
  77.4 0.6 collective-permute-start.12
  77.9 2.3 %collective-permute-done.17.refs_3_.refs_7_ = bf16[6,2,128,128]{3,2,1,0:T(8,128)(2,1)S(1)} collective-permute-done((bf16[6,2,128,128]{3,2,1,0:T(8,128)(2,1)S(1)}, bf16[6,2,128,128]{3,2,1,0:T(8,128)(2,1)S(1)}, u32[]{:S(2)}, u32[]{:S(2)}) %collective-permute-start.17) | collective-permute-done | bytes 393248 | tf_op jit(solution)/shard_map/ppermute | solution.py:648
  80.2 1.8 %shard_map.101 = (bf16[128,16,128]{2,1,0:T(8,128)(2,1)}, bf16[128,16,128]{2,1,0:T(8,128)(2,1)}) custom-call(s32[1]{0:T(128)} %bitcast.place, s32[4,4]{1,0:T(4,128)S(1)} %copy-done.1, bf16[6,2,128,128]{3,2,1,0:T(8,128)(2,1)S(1)} %get-tuple-element.84.refs_0_.refs_4_, bf16[6,2,128,128]{3,2,1,0:T(8,128)(2,1)S(1)} %collective-permute-done.15.refs_1_.refs_5_, ...), custom_call_target="tpu_custom_call" | custom-call | bytes 6291456 | tf_op jit(solution)/shard_map/pallas_call | solution.py:158
  82.1 3.0 %collective-permute-done.12.refs_3_ = bf16[2,2,128,128]{3,2,1,0:T(8,128)(2,1)S(1)} collective-permute-done((bf16[2,2,128,128]{3,2,1,0:T(8,128)(2,1)S(1)}, bf16[2,2,128,128]{3,2,1,0:T(8,128)(2,1)S(1)}, u32[]{:S(2)}, u32[]{:S(2)}) %collective-permute-start.12) | collective-permute-done | bytes 131104 | tf_op jit(solution)/shard_map/ppermute | solution.py:648
  85.1 1.8 %shard_map.102 = (bf16[128,16,128]{2,1,0:T(8,128)(2,1)}, bf16[128,16,128]{2,1,0:T(8,128)(2,1)}) custom-call(s32[1]{0:T(128)} %bitcast.place, s32[4,4]{1,0:T(4,128)S(1)} %copy-done.1, bf16[2,2,128,128]{3,2,1,0:T(8,128)(2,1)S(1)} %get-tuple-element.92.refs_0_, bf16[2,2,128,128]{3,2,1,0:T(8,128)(2,1)S(1)} %collective-permute-done.10.refs_1_, ...), custom_call_target="tpu_custom_call" | custom-call | bytes 4194304 | tf_op jit(solution)/shard_map/pallas_call | solution.py:158
  (22 shorter events, 0.7 us)
Async XLA Ops:
  2.9 9.0 %collective-permute-start = (bf16[4,2,128,128]{3,2,1,0:T(8,128)(2,1)}, bf16[4,2,128,128]{3,2,1,0:T(8,128)(2,1)S(1)}, u32[]{:S(2)}, u32[]{:S(2)}) collective-permute-start(bf16[4,2,128,128]{3,2,1,0:T(8,128)(2,1)} %get-tuple-element.52), channel_id=1, source_target_pairs={{0,1},{1,0},{2,3},{3,2},{4,5},{5,4},{6,7},{7,6},{8,9},{9,8},{10,11... | collective-permute-start | bytes 786440 | tf_op jit(solution)/shard_map/ppermute | solution.py:648
  3.0 9.5 %collective-permute-start.1 = (bf16[4,2,128,128]{3,2,1,0:T(8,128)(2,1)}, bf16[4,2,128,128]{3,2,1,0:T(8,128)(2,1)S(1)}, u32[]{:S(2)}, u32[]{:S(2)}) collective-permute-start(bf16[4,2,128,128]{3,2,1,0:T(8,128)(2,1)} %get-tuple-element.53), channel_id=1, source_target_pairs={{0,2},{1,3},{2,0},{3,1},{4,6},{5,7},{6,4},{7,5},{8,10},{9,11},{10,... | collective-permute-start | bytes 786440 | tf_op jit(solution)/shard_map/ppermute | solution.py:648
  5.6 12.9 %collective-permute-start.2 = (bf16[4,2,128,128]{3,2,1,0:T(8,128)(2,1)}, bf16[4,2,128,128]{3,2,1,0:T(8,128)(2,1)S(1)}, u32[]{:S(2)}, u32[]{:S(2)}) collective-permute-start(bf16[4,2,128,128]{3,2,1,0:T(8,128)(2,1)} %get-tuple-element.54), channel_id=1, source_target_pairs={{0,3},{1,2},{2,1},{3,0},{4,7},{5,6},{6,5},{7,4},{8,11},{9,10},{10,... | collective-permute-start | bytes 786440 | tf_op jit(solution)/shard_map/ppermute | solution.py:648
  7.9 10.7 %copy-start = (bf16[4,2,128,128]{3,2,1,0:T(8,128)(2,1)S(1)}, bf16[4,2,128,128]{3,2,1,0:T(8,128)(2,1)}, u32[]{:S(2)}) copy-start(bf16[4,2,128,128]{3,2,1,0:T(8,128)(2,1)} %get-tuple-element.51.refs_0_) | copy-start | bytes 786436
  7.9 27.5 %all-to-all-start = ((bf16[4,4,2,128,128]{4,3,2,1,0:T(8,128)(2,1)}), bf16[4,4,2,128,128]{4,3,2,1,0:T(8,128)(2,1)S(1)}, u32[]{:S(2)}, u32[]{:S(2)}) async-start(bf16[4,4,2,128,128]{4,3,2,1,0:T(8,128)(2,1)} %shard_map.94), calls=%async_computation | async-start | bytes 2097152 | tf_op jit(solution)/shard_map/all_to_all | solution.py:675
  18.7 14.2 %collective-permute-start.3 = (bf16[8,2,128,128]{3,2,1,0:T(8,128)(2,1)S(1)}, bf16[8,2,128,128]{3,2,1,0:T(8,128)(2,1)S(1)}, u32[]{:S(2)}, u32[]{:S(2)}) collective-permute-start(bf16[8,2,128,128]{3,2,1,0:T(8,128)(2,1)S(1)} %get-tuple-element.55), channel_id=1, source_target_pairs={{0,4},{1,5},{2,6},{3,7},{4,0},{5,1},{6,2},{7,3},{8,12},{9,13},{10,... | collective-permute-start | bytes 1572872 | tf_op jit(solution)/shard_map/ppermute | solution.py:397
  20.5 14.9 %collective-permute-start.4 = (bf16[8,2,128,128]{3,2,1,0:T(8,128)(2,1)S(1)}, bf16[8,2,128,128]{3,2,1,0:T(8,128)(2,1)S(1)}, u32[]{:S(2)}, u32[]{:S(2)}) collective-permute-start(bf16[8,2,128,128]{3,2,1,0:T(8,128)(2,1)S(1)} %get-tuple-element.58), channel_id=1, source_target_pairs={{4,8},{5,9},{6,10},{7,11},{8,4},{9,5},{10,6},{11,7},{20,24},{21,25... | collective-permute-start | bytes 1572872 | tf_op jit(solution)/shard_map/ppermute | solution.py:669
  22.0 13.4 %copy-start.1 = (s32[4,4]{1,0:T(4,128)S(1)}, s32[4,4]{1,0:T(4,128)}, u32[]{:S(2)}) copy-start(s32[4,4]{1,0:T(4,128)} %sections.11) | copy-start | bytes 196
  22.0 13.4 %copy-start.2 = (s32[16]{0:T(128)S(1)}, s32[16]{0:T(128)}, u32[]{:S(2)}) copy-start(s32[16]{0:T(128)} %widths.3) | copy-start | bytes 196
  22.0 21.7 %collective-permute-start.6 = (bf16[4,2,128,128]{3,2,1,0:T(8,128)(2,1)}, bf16[4,2,128,128]{3,2,1,0:T(8,128)(2,1)S(1)}, u32[]{:S(2)}, u32[]{:S(2)}) collective-permute-start(bf16[4,2,128,128]{3,2,1,0:T(8,128)(2,1)} %get-tuple-element.60), channel_id=1, source_target_pairs={{0,4},{1,5},{2,6},{3,7},{4,0},{5,1},{6,2},{7,3},{8,12},{9,13},{10,... | collective-permute-start | bytes 786440 | tf_op jit(solution)/shard_map/ppermute | solution.py:397
  32.8 15.1 %collective-permute-start.5 = (bf16[4,2,128,128]{3,2,1,0:T(8,128)(2,1)}, bf16[4,2,128,128]{3,2,1,0:T(8,128)(2,1)}, u32[]{:S(2)}, u32[]{:S(2)}) collective-permute-start(bf16[4,2,128,128]{3,2,1,0:T(8,128)(2,1)} %get-tuple-element.59), channel_id=1, source_target_pairs={{0,8},{1,9},{2,10},{3,11},{4,12},{5,13},{6,14},{7,15},{8,0},{9,1},... | collective-permute-start | bytes 786440 | tf_op jit(solution)/shard_map/ppermute | solution.py:397
  41.0 12.9 %collective-permute-start.13 = (bf16[4,2,128,128]{3,2,1,0:T(8,128)(2,1)S(1)}, bf16[4,2,128,128]{3,2,1,0:T(8,128)(2,1)S(1)}, u32[]{:S(2)}, u32[]{:S(2)}) collective-permute-start(bf16[4,2,128,128]{3,2,1,0:T(8,128)(2,1)S(1)} %get-tuple-element.74), channel_id=1, source_target_pairs={{0,4},{1,5},{2,6},{3,7},{4,0},{5,1},{6,2},{7,3},{8,12},{9,13},{10,... | collective-permute-start | bytes 786440 | tf_op jit(solution)/shard_map/ppermute | solution.py:397
  43.0 10.8 %collective-permute-start.14 = (bf16[4,2,128,128]{3,2,1,0:T(8,128)(2,1)S(1)}, bf16[4,2,128,128]{3,2,1,0:T(8,128)(2,1)S(1)}, u32[]{:S(2)}, u32[]{:S(2)}) collective-permute-start(bf16[4,2,128,128]{3,2,1,0:T(8,128)(2,1)S(1)} %get-tuple-element.75), channel_id=1, source_target_pairs={{4,8},{5,9},{6,10},{7,11},{8,4},{9,5},{10,6},{11,7},{20,24},{21,25... | collective-permute-start | bytes 786440 | tf_op jit(solution)/shard_map/ppermute | solution.py:669
  54.1 6.1 %collective-permute-start.15 = (bf16[6,2,128,128]{3,2,1,0:T(8,128)(2,1)S(1)}, bf16[6,2,128,128]{3,2,1,0:T(8,128)(2,1)S(1)}, u32[]{:S(2)}, u32[]{:S(2)}) collective-permute-start(bf16[6,2,128,128]{3,2,1,0:T(8,128)(2,1)S(1)} %get-tuple-element.81), channel_id=1, source_target_pairs={{0,1},{1,0},{2,3},{3,2},{4,5},{5,4},{6,7},{7,6},{8,9},{9,8},{10,11... | collective-permute-start | bytes 1179656 | tf_op jit(solution)/shard_map/ppermute | solution.py:648
  55.9 19.1 %collective-permute-start.8 = (bf16[8,2,128,128]{3,2,1,0:T(8,128)(2,1)S(1)}, bf16[8,2,128,128]{3,2,1,0:T(8,128)(2,1)S(1)}, u32[]{:S(2)}, u32[]{:S(2)}) collective-permute-start(bf16[8,2,128,128]{3,2,1,0:T(8,128)(2,1)S(1)} %get-tuple-element.67), channel_id=1, source_target_pairs={{0,4},{1,5},{2,6},{3,7},{4,0},{5,1},{6,2},{7,3},{8,12},{9,13},{10,... | collective-permute-start | bytes 1572872 | tf_op jit(solution)/shard_map/ppermute | solution.py:397
  56.4 17.0 %collective-permute-start.7 = (bf16[4,2,128,128]{3,2,1,0:T(8,128)(2,1)S(1)}, bf16[4,2,128,128]{3,2,1,0:T(8,128)(2,1)S(1)}, u32[]{:S(2)}, u32[]{:S(2)}) collective-permute-start(bf16[4,2,128,128]{3,2,1,0:T(8,128)(2,1)S(1)} %get-tuple-element.66), channel_id=1, source_target_pairs={{0,8},{1,9},{2,10},{3,11},{4,12},{5,13},{6,14},{7,15},{8,0},{9,1},... | collective-permute-start | bytes 786440 | tf_op jit(solution)/shard_map/ppermute | solution.py:397
  59.5 13.9 %collective-permute-start.9 = (bf16[4,2,128,128]{3,2,1,0:T(8,128)(2,1)S(1)}, bf16[4,2,128,128]{3,2,1,0:T(8,128)(2,1)S(1)}, u32[]{:S(2)}, u32[]{:S(2)}) collective-permute-start(bf16[4,2,128,128]{3,2,1,0:T(8,128)(2,1)S(1)} %get-tuple-element.68), channel_id=1, source_target_pairs={{4,8},{5,9},{6,10},{7,11},{8,4},{9,5},{10,6},{11,7},{20,24},{21,25... | collective-permute-start | bytes 786440 | tf_op jit(solution)/shard_map/ppermute | solution.py:669
  60.1 17.8 %collective-permute-start.16 = (bf16[6,2,128,128]{3,2,1,0:T(8,128)(2,1)S(1)}, bf16[6,2,128,128]{3,2,1,0:T(8,128)(2,1)S(1)}, u32[]{:S(2)}, u32[]{:S(2)}) collective-permute-start(bf16[6,2,128,128]{3,2,1,0:T(8,128)(2,1)S(1)} %get-tuple-element.86), channel_id=1, source_target_pairs={{0,2},{1,3},{2,0},{3,1},{4,6},{5,7},{6,4},{7,5},{8,10},{9,11},{10,... | collective-permute-start | bytes 1179656 | tf_op jit(solution)/shard_map/ppermute | solution.py:648
  61.3 19.0 %collective-permute-start.17 = (bf16[6,2,128,128]{3,2,1,0:T(8,128)(2,1)S(1)}, bf16[6,2,128,128]{3,2,1,0:T(8,128)(2,1)S(1)}, u32[]{:S(2)}, u32[]{:S(2)}) collective-permute-start(bf16[6,2,128,128]{3,2,1,0:T(8,128)(2,1)S(1)} %get-tuple-element.87), channel_id=1, source_target_pairs={{0,3},{1,2},{2,1},{3,0},{4,7},{5,6},{6,5},{7,4},{8,11},{9,10},{10,... | collective-permute-start | bytes 1179656 | tf_op jit(solution)/shard_map/ppermute | solution.py:648
  75.3 6.7 %collective-permute-start.10 = (bf16[2,2,128,128]{3,2,1,0:T(8,128)(2,1)S(1)}, bf16[2,2,128,128]{3,2,1,0:T(8,128)(2,1)S(1)}, u32[]{:S(2)}, u32[]{:S(2)}) collective-permute-start(bf16[2,2,128,128]{3,2,1,0:T(8,128)(2,1)S(1)} %get-tuple-element.70), channel_id=1, source_target_pairs={{0,1},{1,0},{2,3},{3,2},{4,5},{5,4},{6,7},{7,6},{8,9},{9,8},{10,11... | collective-permute-start | bytes 393224 | tf_op jit(solution)/shard_map/ppermute | solution.py:648
  76.2 5.8 %collective-permute-start.11 = (bf16[2,2,128,128]{3,2,1,0:T(8,128)(2,1)S(1)}, bf16[2,2,128,128]{3,2,1,0:T(8,128)(2,1)S(1)}, u32[]{:S(2)}, u32[]{:S(2)}) collective-permute-start(bf16[2,2,128,128]{3,2,1,0:T(8,128)(2,1)S(1)} %get-tuple-element.71), channel_id=1, source_target_pairs={{0,2},{1,3},{2,0},{3,1},{4,6},{5,7},{6,4},{7,5},{8,10},{9,11},{10,... | collective-permute-start | bytes 393224 | tf_op jit(solution)/shard_map/ppermute | solution.py:648
  77.4 7.7 %collective-permute-start.12 = (bf16[2,2,128,128]{3,2,1,0:T(8,128)(2,1)S(1)}, bf16[2,2,128,128]{3,2,1,0:T(8,128)(2,1)S(1)}, u32[]{:S(2)}, u32[]{:S(2)}) collective-permute-start(bf16[2,2,128,128]{3,2,1,0:T(8,128)(2,1)S(1)} %get-tuple-element.72), channel_id=1, source_target_pairs={{0,3},{1,2},{2,1},{3,0},{4,7},{5,6},{6,5},{7,4},{8,11},{9,10},{10,... | collective-permute-start | bytes 393224 | tf_op jit(solution)/shard_map/ppermute | solution.py:648

commit v10 on v9

--- a/solution.py
+++ b/solution.py
@@ -228,25 +228,25 @@
     )(place, *pieces)
 
 
-def attend_kernel(place, widths, sections, *refs, first, slot, group, remote, blocks, aliased):
+def attend_kernel(place, widths, sections, *refs, first, slot, group, picked, remote, blocks, aliased):
     pairs, (graded, with_next, with_last) = refs[:PLANE], refs[PLANE : PLANE + 3]
     rest = refs[PLANE + 3 :]
     if remote:
-        far_in, rest = rest[:2], rest[2:]
+        far_in, rest = rest[0], rest[1:]
     rest = rest[aliased:]
     rows, rest = rest[:PLANE], rest[PLANE:]
-    (part, to_next, to_last), rest = rest[:3], rest[3:]
-    if remote:
+    (to_next, to_last, part), rest = rest[:3], rest[3:]
+    lead = PLANE if remote else 0
+    if remote and 1 in picked:
         to_other, rest = rest[0], rest[1:]
     keys, values, far_keys, far_values, attended, dq = rest[:6]
     accs, far_accs = rest[6:8], rest[8:10]
     me = seat(place)
     scales = (1.0 / math.sqrt(keys.shape[-1]), 1.0)
-    lead = PLANE if remote else 0
     slots = with_next.shape[0] // HALO
     next_at = jnp.where(plane(place) % 2 == 0, HALO + PLANE, 0)
     last_at = HALO + PLANE - next_at
-    for k in range(group):
+    for n, k in enumerate(picked):
         width = widths[sections[first + k, me]]
         bit = 1 << first + k
         far_bias = jnp.where(bit >= width, 0.0, blocked_score).astype(jnp.float32)
@@ -262,8 +262,8 @@
             values[rows_of(last_at + b)] = with_last[at, 1]
         if remote:
             for m in range(PLANE):
-                far_keys[rows_of(me ^ m)] = far_in[1 - k][m, 0]
-                far_values[rows_of(me ^ m)] = far_in[1 - k][m, 1]
+                far_keys[rows_of(me ^ m)] = far_in[m, 0]
+                far_values[rows_of(me ^ m)] = far_in[m, 1]
         for acc in accs:
             acc[...] = jnp.zeros_like(acc)
         for b in range(0, PLANE, 2):
@@ -299,12 +299,12 @@
                         acc[:, there[r] * BLK : (there[r] + 1) * BLK] += far[r]
         for i, (acc, far_acc) in enumerate(zip(accs, far_accs)):
             if remote:
-                target = (to_next, to_other)[k]
+                target = to_other if k else to_next
                 for m in range(PLANE):
                     owed = far_acc[:, rows_of(me ^ m)] * scales[i]
                     target[m, i] = owed.astype(jnp.bfloat16)
             for m in range(PLANE):
-                part[k, m, i] = acc[:, rows_of(HALO + (me ^ m))] * scales[i]
+                part[n, m, i] = acc[:, rows_of(HALO + (me ^ m))] * scales[i]
             for m in range(HALO):
                 b = (me % HALO) ^ m
                 at = m * group + k
@@ -317,79 +317,82 @@
             rows[m][slot + k, 1] = dq[rows_of(me ^ m)]
 
 
-def attend(place, widths, sections, pairs, graded, halos, far, group, first, slot, blocks, rows=()):
+def attend(place, widths, sections, pairs, graded, halos, far, group, first, slot, blocks, picked, shared=()):
     count, _, width = pairs[0].shape[1:]
     tile = (BLK, width)
-    remote = len(far)
-    room = pairs[0].shape[0] + group
     bf16 = jnp.bfloat16
-    owed = [(HALO * group + (PLANE if remote else 0), count, *tile), (HALO * group, count, *tile)]
-    if remote:
-        owed.append((PLANE, count, *tile))
-    inputs = (*pairs, graded, *halos, *far, *rows)
+    inputs = (*pairs, graded, *halos, *far, *shared)
+    sizes = [HALO * group + (PLANE if far else 0), HALO * group]
+    outs = [jax.ShapeDtypeStruct((pairs[0].shape[0] + group, count, *tile), bf16)] * PLANE
+    outs += [jax.ShapeDtypeStruct((size, count, *tile), bf16) for size in sizes]
+    outs.append(jax.ShapeDtypeStruct((len(picked), PLANE, count, *tile), jnp.float32))
+    if far and 1 in picked:
+        outs.append(jax.ShapeDtypeStruct((PLANE, count, *tile), bf16))
     outs = pl.pallas_call(
         functools.partial(
             attend_kernel,
             first=first,
             slot=slot,
             group=group,
-            remote=remote,
+            picked=picked,
+            remote=len(far),
             blocks=blocks,
-            aliased=len(rows),
+            aliased=len(shared),
         ),
         in_specs=[SMEM] * 3 + [VMEM] * len(inputs),
-        out_specs=[VMEM] * (PLANE + 1 + len(owed)),
-        out_shape=[jax.ShapeDtypeStruct((room, count, *tile), bf16)] * PLANE
-        + [jax.ShapeDtypeStruct((group, PLANE, count, *tile), jnp.float32)]
-        + [jax.ShapeDtypeStruct(shape, bf16) for shape in owed],
+        out_specs=[VMEM] * len(outs),
+        out_shape=outs,
         scratch_shapes=[pltpu.VMEM((PADDED * BLK, width), bf16)] * 2
         + [pltpu.VMEM((PLANE * BLK, width), bf16)] * 4
         + [pltpu.VMEM((width, PADDED * BLK), jnp.float32)] * 2
         + [pltpu.VMEM((width, PLANE * BLK), jnp.float32)] * 2,
-        input_output_aliases={3 + len(inputs) - len(rows) + m: m for m in range(len(rows))},
+        input_output_aliases={3 + len(inputs) - len(shared) + m: m for m in range(len(shared))},
         compiler_params=LIMIT,
         cost_estimate=pl.CostEstimate(
-            flops=group * PLANE * 12 * BLK * LINKED * width,
-            transcendentals=group * PLANE * BLK * LINKED,
-            bytes_accessed=40 * group * PLANE * BLK * width,
+            flops=len(picked) * PLANE * 12 * BLK * LINKED * width,
+            transcendentals=len(picked) * PLANE * BLK * LINKED,
+            bytes_accessed=40 * len(picked) * PLANE * BLK * width,
         ),
     )(place, widths, sections, *inputs)
-    return outs[:PLANE], outs[PLANE], outs[PLANE + 1 :]
-
-
-def combine_kernel(place, part, *refs, remote, base, aliased):
-    with_other, (with_next, with_last) = refs[0], refs[remote : remote + 2]
-    outs = refs[remote + 2 + aliased :]
-    group = part.shape[0]
+    return outs[:PLANE], outs[PLANE : PLANE + 2], outs[PLANE + 2 :]
+
+
+def combine_kernel(place, *refs, parts, remote, base, aliased):
+    pieces, rest = refs[:parts], refs[parts:]
+    if remote:
+        with_other, rest = rest[0], rest[1:]
+    (with_next, with_last), outs = rest[:2], rest[2 + aliased :]
+    each = pieces[0].shape[0]
+    group = each * parts
     lead = PLANE if remote else 0
     for m in range(PLANE):
         own_chip = m < HALO
         next_side = facing(place) if own_chip else jnp.logical_not(facing(place))
         for k in range(group):
             slot = (m % HALO) * group + k
-            for i in range(part.shape[2]):
+            for i in range(pieces[0].shape[2]):
                 owed = jnp.where(next_side, with_next[lead + slot, i], with_last[slot, i])
-                total = part[k, m, i] + owed.astype(jnp.float32)
+                total = pieces[k // each][k % each, m, i] + owed.astype(jnp.float32)
                 if remote:
                     far = (with_next, with_other)[k]
                     total += far[m, i].astype(jnp.float32)
                 outs[m][base + k, i] = jnp.transpose(total.astype(jnp.bfloat16))
 
 
-def combine(place, part, owed, rows=(), base=0):
-    group, _, *rest = part.shape
-    inputs = (part, *owed, *rows)
-    shape = rows[0].shape if rows else (group, *rest)
+def combine(place, parts, owed, rows=(), base=0):
+    each, _, *rest = parts[0].shape
+    inputs = (*parts, *owed, *rows)
+    shape = rows[0].shape if rows else (each * len(parts), *rest)
     return pl.pallas_call(
         functools.partial(
-            combine_kernel, remote=len(owed) - 2, base=base, aliased=len(rows)
+            combine_kernel, parts=len(parts), remote=len(owed) > 2, base=base, aliased=len(rows)
         ),
         in_specs=[SMEM] + [VMEM] * len(inputs),
         out_specs=[VMEM] * PLANE,
         out_shape=[jax.ShapeDtypeStruct(shape, jnp.bfloat16)] * PLANE,
         input_output_aliases={1 + len(inputs) - len(rows) + m: m for m in range(len(rows))},
         compiler_params=LIMIT,
-        cost_estimate=moved_cost([part, *owed]),
+        cost_estimate=moved_cost([*parts, *owed]),
     )(place, *inputs)
 
 
@@ -692,18 +695,19 @@
     halos = [with_next_plane(next_sent), with_last_plane(last_sent)]
     halos[0], other_sent = lax.optimization_barrier((halos[0], far_sent[1]))
     far = (with_other_plane(other_sent), with_next_plane(far_sent[0]))
-    rows, part_near, owed = attend(
-        *tables, pairs, graded, halos, (), local, 0, total - local, blocks
-    )
+    given = (*tables, pairs, graded, halos)
+    size = total - local
+    rows, owed, (part_near,) = attend(*given, (), local, 0, size, blocks, range(local))
     owed_near = [with_next_plane(owed[0]), with_last_plane(owed[1])]
-    rows, part_far, owed = attend(
-        *tables, pairs, graded, halos, far, total - local, local, 0, blocks, rows
-    )
-    other_back = with_other_plane(owed[2])
+    rows, owed, (part_next,) = attend(*given, (far[1],), size, local, 0, blocks, (0,), rows)
+    rows, owed, (part_other, far_other) = attend(
+        *given, (far[0],), size, local, 0, blocks, (1,), (*rows, *owed)
+    )
+    other_back = with_other_plane(far_other)
     owed_far = [other_back, with_next_plane(owed[0]), with_last_plane(owed[1])]
-    rows = in_plane(combine(place, part_near, owed_near, rows, total), True)
+    rows = in_plane(combine(place, [part_near], owed_near, rows, total), True)
+    columns = in_plane(combine(place, [part_next, part_other], owed_far))
     attended, query_grad = unpack(place, sections, [(groups[0], rows, 0), (groups[1], rows, 1)])
-    columns = in_plane(combine(place, part_far, owed_far))
     columns, attended, query_grad = lax.optimization_barrier((columns, attended, query_grad))
     key_grad, value_grad = unpack(place, sections, [(groups[0], columns, 0), (groups[1], rows, 2)])
     return attended, query_grad, key_grad, value_grad

time: 87.2 us -> 85.7 us (0.983); the launches traced: 86.9 us -> 84.5 us
  waiting for transfers between devices: 35.8 us -> 32.8 us
    ppermute x6, waiting for transfers between devices: 23.7 us -> 20.9 us  [partner(): lax.ppermute(value, axis, [(i, i ^ 1 << apart) for i in range(lax.axis_si...]
    pallas_call x2 -> x3, Pallas kernels: 11.4 us -> 12.2 us  [attend(): pl.pallas_call(functools.partial(attend_kernel, first=first, slot=slot, g...]
  transfers between devices with their start and end apart: 19 -> 19, of which waited for: 8 -> 9; matrix products, arithmetic and copies ran while one was open for 0% -> 0% of each run, Pallas kernels for 19% -> 21%
where the time goes in v10:
time: 85.7 us; the launch traced here: 84.5 us
  waiting for transfers between devices  32.8 us (38%)
  starting transfers between devices  29.2 us (34%)
  Pallas kernels  21.7 us (25%)
    ppermute x6, waiting for transfers between devices, partner(): lax.ppermute(value, axis, [(i, i ^ 1 << apart) for i in range(lax.axis_si...  20.9 us
    ppermute x6, starting transfers between devices, partner(): lax.ppermute(value, axis, [(i, i ^ 1 << apart) for i in range(lax.axis_si...  14.4 us
    pallas_call x3, Pallas kernels, attend(): pl.pallas_call(functools.partial(attend_kernel, first=first, slot=slot, g...  12.2 us
    ppermute x9, waiting for transfers between devices, in_plane(): lax.ppermute(pieces[m], 'seq', [(i, i ^ m) for i in range(peers)])  11.9 us
    ppermute x9, starting transfers between devices, in_plane(): lax.ppermute(pieces[m], 'seq', [(i, i ^ m) for i in range(peers)])  8.76 us
    pallas_call x2, Pallas kernels, pack(): pl.pallas_call(functools.partial(pack_kernel, order=order, count=count, c...  4.5 us
    all_to_all x1, starting transfers between devices, plane_all_to_all(): lax.all_to_all(value, 'seq', 0, 0, axis_index_groups=planes, tiled=True)  3.99 us
    pallas_call x2, Pallas kernels, unpack(): pl.pallas_call(functools.partial(unpack_kernel, groups=[group for group,...  3.64 us
  transfers between devices with their start and end apart: 19, of which 9 were waited for; matrix products, arithmetic and copies ran while one was open for 0% of the time, Pallas kernels for 21%

profile of v10, /device:TPU:1, one launch (start us, length us, event | category | flops | bytes accessed | tf_op | source)
XLA Modules:
  0.0 84.5 jit_solution(15489924449508129160)
XLA Ops:
  0.6 2.3 %shard_map.93 = (bf16[4,2,128,128]{3,2,1,0:T(8,128)(2,1)}, bf16[4,2,128,128]{3,2,1,0:T(8,128)(2,1)}, bf16[4,2,128,128]{3,2,1,0:T(8,128)(2,1)}, bf16[4,2,128,128]{3,2,1,0:T(8,128)(2,1)}) custom-call(s32[1]{0:T(128)} %bitcast.place, s32[4,4]{1,0:T(4,128)} %sections.13, bf16[128,16,128]{2,1,0:T(8,128)(2,1)} %refs_0_.2, bf16[128,16,128]{2,1,0:T(8,128)(2,1)} %refs_1_.2), custom_call_target="tpu_custom_call" | custom-call | bytes 2097152 | tf_op jit(solution)/shard_map/pallas_call | solution.py:124
  3.0 2.7 %collective-permute-start.1 = (bf16[4,2,128,128]{3,2,1,0:T(8,128)(2,1)}, bf16[4,2,128,128]{3,2,1,0:T(8,128)(2,1)S(1)}, u32[]{:S(2)}, u32[]{:S(2)}) collective-permute-start(bf16[4,2,128,128]{3,2,1,0:T(8,128)(2,1)} %get-tuple-element.60), channel_id=1, source_target_pairs={{0,2},{1,3},{2,0},{3,1},{4,6},{5,7},{6,4},{7,5},{8,10},{9,11},{10,... | collective-permute-start | bytes 786440 | tf_op jit(solution)/shard_map/ppermute | solution.py:651
  5.7 2.2 %shard_map.94 = bf16[4,4,2,128,128]{4,3,2,1,0:T(8,128)(2,1)} custom-call(s32[1]{0:T(128)} %bitcast.place, s32[4,4]{1,0:T(4,128)} %sections.13, bf16[128,16,128]{2,1,0:T(8,128)(2,1)} %refs_0_.3, bf16[128,16,128]{2,1,0:T(8,128)(2,1)} %refs_1_.3), custom_call_target="tpu_custom_call" | custom-call | bytes 2097152 | tf_op jit(solution)/shard_map/pallas_call | solution.py:124
  7.9 4.0 %all-to-all-start = ((bf16[4,4,2,128,128]{4,3,2,1,0:T(8,128)(2,1)}), bf16[4,4,2,128,128]{4,3,2,1,0:T(8,128)(2,1)S(1)}, u32[]{:S(2)}, u32[]{:S(2)}) async-start(bf16[4,4,2,128,128]{4,3,2,1,0:T(8,128)(2,1)} %shard_map.94), calls=%async_computation | async-start | bytes 2097152 | tf_op jit(solution)/shard_map/all_to_all | solution.py:678
  11.9 0.5 collective-permute-done.1.refs_2_
  12.5 6.1 %collective-permute-done.2.refs_3_ = bf16[4,2,128,128]{3,2,1,0:T(8,128)(2,1)S(1)} collective-permute-done((bf16[4,2,128,128]{3,2,1,0:T(8,128)(2,1)}, bf16[4,2,128,128]{3,2,1,0:T(8,128)(2,1)S(1)}, u32[]{:S(2)}, u32[]{:S(2)}) %collective-permute-start.2) | collective-permute-done | bytes 262176 | tf_op jit(solution)/shard_map/ppermute | solution.py:651
  18.7 1.8 %collective-permute-start.3 = (bf16[8,2,128,128]{3,2,1,0:T(8,128)(2,1)S(1)}, bf16[8,2,128,128]{3,2,1,0:T(8,128)(2,1)S(1)}, u32[]{:S(2)}, u32[]{:S(2)}) collective-permute-start(bf16[8,2,128,128]{3,2,1,0:T(8,128)(2,1)S(1)} %get-tuple-element.62), channel_id=1, source_target_pairs={{0,4},{1,5},{2,6},{3,7},{4,0},{5,1},{6,2},{7,3},{8,12},{9,13},{10,... | collective-permute-start | bytes 1572872 | tf_op jit(solution)/shard_map/ppermute | solution.py:400
  20.5 0.7 collective-permute-start.4
  21.2 0.8 shard_map.96
  22.0 3.8 %collective-permute-start.5 = (bf16[4,2,128,128]{3,2,1,0:T(8,128)(2,1)}, bf16[4,2,128,128]{3,2,1,0:T(8,128)(2,1)}, u32[]{:S(2)}, u32[]{:S(2)}) collective-permute-start(bf16[4,2,128,128]{3,2,1,0:T(8,128)(2,1)} %get-tuple-element.66), channel_id=1, source_target_pairs={{0,4},{1,5},{2,6},{3,7},{4,0},{5,1},{6,2},{7,3},{8,12},{9,13},{10,... | collective-permute-start | bytes 786440 | tf_op jit(solution)/shard_map/ppermute | solution.py:400
  25.8 7.0 %collective-permute-done.3.refs_5_ = bf16[8,2,128,128]{3,2,1,0:T(8,128)(2,1)S(1)} collective-permute-done((bf16[8,2,128,128]{3,2,1,0:T(8,128)(2,1)S(1)}, bf16[8,2,128,128]{3,2,1,0:T(8,128)(2,1)S(1)}, u32[]{:S(2)}, u32[]{:S(2)}) %collective-permute-start.3) | collective-permute-done | bytes 524320 | tf_op jit(solution)/shard_map/ppermute | solution.py:400
  32.8 2.6 %collective-permute-start.6 = (bf16[4,2,128,128]{3,2,1,0:T(8,128)(2,1)}, bf16[4,2,128,128]{3,2,1,0:T(8,128)(2,1)S(1)}, u32[]{:S(2)}, u32[]{:S(2)}) collective-permute-start(bf16[4,2,128,128]{3,2,1,0:T(8,128)(2,1)} %get-tuple-element.72), channel_id=1, source_target_pairs={{0,8},{1,9},{2,10},{3,11},{4,12},{5,13},{6,14},{7,15},{8,0},{9,1},... | collective-permute-start | bytes 786440 | tf_op jit(solution)/shard_map/ppermute | solution.py:400
  35.4 5.5 %shard_map.97 = (bf16[6,2,128,128]{3,2,1,0:T(8,128)(2,1)S(1)}, bf16[6,2,128,128]{3,2,1,0:T(8,128)(2,1)S(1)}, bf16[6,2,128,128]{3,2,1,0:T(8,128)(2,1)S(1)}, bf16[...) custom-call(s32[1]{0:T(128)} %bitcast.place, ...), custom_call_target="tpu_custom_call" | custom-call | flops 1207959552 | bytes 5242880 | tf_op jit(solution)/shard_map/pallas_call | solution.py:331
  41.0 2.2 %collective-permute-start.13 = (bf16[4,2,128,128]{3,2,1,0:T(8,128)(2,1)S(1)}, bf16[4,2,128,128]{3,2,1,0:T(8,128)(2,1)S(1)}, u32[]{:S(2)}, u32[]{:S(2)}) collective-permute-start(bf16[4,2,128,128]{3,2,1,0:T(8,128)(2,1)S(1)} %get-tuple-element.88), channel_id=1, source_target_pairs={{0,4},{1,5},{2,6},{3,7},{4,0},{5,1},{6,2},{7,3},{8,12},{9,13},{10,... | collective-permute-start | bytes 786440 | tf_op jit(solution)/shard_map/ppermute | solution.py:400
  43.1 0.7 collective-permute-start.14
  43.8 3.6 %shard_map.98 = (bf16[6,2,128,128]{3,2,1,0:T(8,128)(2,1)S(1)}, bf16[6,2,128,128]{3,2,1,0:T(8,128)(2,1)S(1)}, bf16[6,2,128,128]{3,2,1,0:T(8,128)(2,1)S(1)}, bf16[...) custom-call(s32[1]{0:T(128)} %bitcast.place, ...), custom_call_target="tpu_custom_call", output_to_operand_aliasing={{0}: (11, {}), {1}: (12, {}), {2}: (13, {}), {3}: (14, {})} | custom-call | flops 603979776 | bytes 2621440 | tf_op jit(solution)/shard_map/pallas_call | solution.py:331
  47.8 3.1 %shard_map.99 = (bf16[6,2,128,128]{3,2,1,0:T(8,128)(2,1)S(1)}, bf16[6,2,128,128]{3,2,1,0:T(8,128)(2,1)S(1)}, bf16[6,2,128,128]{3,2,1,0:T(8,128)(2,1)S(1)}, bf16[...) custom-call(s32[1]{0:T(128)} %bitcast.place, ...), custom_call_target="tpu_custom_call", output_to_operand_aliasing={{0}: (11, {}), {1}: (12, {}), {2}: (13, {}), {3}: (14, {}),... | custom-call | flops 603979776 | bytes 2621440 | tf_op jit(solution)/shard_map/pallas_call | solution.py:331
  51.0 0.6 collective-permute-done.13.refs_1_
  51.8 1.2 %collective-permute-start.15 = (bf16[6,2,128,128]{3,2,1,0:T(8,128)(2,1)S(1)}, bf16[6,2,128,128]{3,2,1,0:T(8,128)(2,1)S(1)}, u32[]{:S(2)}, u32[]{:S(2)}) collective-permute-start(bf16[6,2,128,128]{3,2,1,0:T(8,128)(2,1)S(1)} %get-tuple-element.95), channel_id=1, source_target_pairs={{0,1},{1,0},{2,3},{3,2},{4,5},{5,4},{6,7},{7,6},{8,9},{9,8},{10,11... | collective-permute-start | bytes 1179656 | tf_op jit(solution)/shard_map/ppermute | solution.py:651
  53.0 2.1 %collective-permute-start.8 = (bf16[8,2,128,128]{3,2,1,0:T(8,128)(2,1)S(1)}, bf16[8,2,128,128]{3,2,1,0:T(8,128)(2,1)S(1)}, u32[]{:S(2)}, u32[]{:S(2)}) collective-permute-start(bf16[8,2,128,128]{3,2,1,0:T(8,128)(2,1)S(1)} %get-tuple-element.81), channel_id=1, source_target_pairs={{0,4},{1,5},{2,6},{3,7},{4,0},{5,1},{6,2},{7,3},{8,12},{9,13},{10,... | collective-permute-start | bytes 1572872 | tf_op jit(solution)/shard_map/ppermute | solution.py:400
  55.1 2.0 %collective-permute-start.7 = (bf16[4,2,128,128]{3,2,1,0:T(8,128)(2,1)S(1)}, bf16[4,2,128,128]{3,2,1,0:T(8,128)(2,1)S(1)}, u32[]{:S(2)}, u32[]{:S(2)}) collective-permute-start(bf16[4,2,128,128]{3,2,1,0:T(8,128)(2,1)S(1)} %get-tuple-element.80), channel_id=1, source_target_pairs={{0,8},{1,9},{2,10},{3,11},{4,12},{5,13},{6,14},{7,15},{8,0},{9,1},... | collective-permute-start | bytes 786440 | tf_op jit(solution)/shard_map/ppermute | solution.py:400
  57.0 0.7 collective-permute-start.9
  57.7 1.5 %collective-permute-start.16 = (bf16[6,2,128,128]{3,2,1,0:T(8,128)(2,1)S(1)}, bf16[6,2,128,128]{3,2,1,0:T(8,128)(2,1)S(1)}, u32[]{:S(2)}, u32[]{:S(2)}) collective-permute-start(bf16[6,2,128,128]{3,2,1,0:T(8,128)(2,1)S(1)} %get-tuple-element.100), channel_id=1, source_target_pairs={{0,2},{1,3},{2,0},{3,1},{4,6},{5,7},{6,4},{7,5},{8,10},{9,11},{10,... | collective-permute-start | bytes 1179656 | tf_op jit(solution)/shard_map/ppermute | solution.py:651
  59.3 0.8 collective-permute-start.17
  60.1 12.0 %collective-permute-done.7.refs_2_ = bf16[4,2,128,128]{3,2,1,0:T(8,128)(2,1)S(1)} collective-permute-done((bf16[4,2,128,128]{3,2,1,0:T(8,128)(2,1)S(1)}, bf16[4,2,128,128]{3,2,1,0:T(8,128)(2,1)S(1)}, u32[]{:S(2)}, u32[]{:S(2)}) %collective-permute-start.7) | collective-permute-done | bytes 262176 | tf_op jit(solution)/shard_map/ppermute | solution.py:400
  72.0 0.9 %collective-permute-done.8.refs_3_ = bf16[8,2,128,128]{3,2,1,0:T(8,128)(2,1)S(1)} collective-permute-done((bf16[8,2,128,128]{3,2,1,0:T(8,128)(2,1)S(1)}, bf16[8,2,128,128]{3,2,1,0:T(8,128)(2,1)S(1)}, u32[]{:S(2)}, u32[]{:S(2)}) %collective-permute-start.8) | collective-permute-done | bytes 524320 | tf_op jit(solution)/shard_map/ppermute | solution.py:400
  73.2 0.7 collective-permute-start.10
  73.9 1.3 %collective-permute-start.11 = (bf16[2,2,128,128]{3,2,1,0:T(8,128)(2,1)S(1)}, bf16[2,2,128,128]{3,2,1,0:T(8,128)(2,1)S(1)}, u32[]{:S(2)}, u32[]{:S(2)}) collective-permute-start(bf16[2,2,128,128]{3,2,1,0:T(8,128)(2,1)S(1)} %get-tuple-element.85), channel_id=1, source_target_pairs={{0,2},{1,3},{2,0},{3,1},{4,6},{5,7},{6,4},{7,5},{8,10},{9,11},{10,... | collective-permute-start | bytes 393224 | tf_op jit(solution)/shard_map/ppermute | solution.py:651
  75.6 2.1 %collective-permute-done.17.refs_3_.refs_7_ = bf16[6,2,128,128]{3,2,1,0:T(8,128)(2,1)S(1)} collective-permute-done((bf16[6,2,128,128]{3,2,1,0:T(8,128)(2,1)S(1)}, bf16[6,2,128,128]{3,2,1,0:T(8,128)(2,1)S(1)}, u32[]{:S(2)}, u32[]{:S(2)}) %collective-permute-start.17) | collective-permute-done | bytes 393248 | tf_op jit(solution)/shard_map/ppermute | solution.py:651
  77.7 1.8 %shard_map.102 = (bf16[128,16,128]{2,1,0:T(8,128)(2,1)}, bf16[128,16,128]{2,1,0:T(8,128)(2,1)}) custom-call(s32[1]{0:T(128)} %bitcast.place, s32[4,4]{1,0:T(4,128)S(1)} %copy-done.1, bf16[6,2,128,128]{3,2,1,0:T(8,128)(2,1)S(1)} %get-tuple-element.98.refs_0_.refs_4_, bf16[6,2,128,128]{3,2,1,0:T(8,128)(2,1)S(1)} %collective-permute-done.15.refs_1_.refs_5_, ...), custom_call_target="tpu_custom_call" | custom-call | bytes 6291456 | tf_op jit(solution)/shard_map/pallas_call | solution.py:158
  79.6 3.1 %collective-permute-done.12.refs_3_ = bf16[2,2,128,128]{3,2,1,0:T(8,128)(2,1)S(1)} collective-permute-done((bf16[2,2,128,128]{3,2,1,0:T(8,128)(2,1)S(1)}, bf16[2,2,128,128]{3,2,1,0:T(8,128)(2,1)S(1)}, u32[]{:S(2)}, u32[]{:S(2)}) %collective-permute-start.12) | collective-permute-done | bytes 131104 | tf_op jit(solution)/shard_map/ppermute | solution.py:651
  82.7 1.8 %shard_map.103 = (bf16[128,16,128]{2,1,0:T(8,128)(2,1)}, bf16[128,16,128]{2,1,0:T(8,128)(2,1)}) custom-call(s32[1]{0:T(128)} %bitcast.place, s32[4,4]{1,0:T(4,128)S(1)} %copy-done.1, bf16[2,2,128,128]{3,2,1,0:T(8,128)(2,1)S(1)} %get-tuple-element.106.refs_0_, bf16[2,2,128,128]{3,2,1,0:T(8,128)(2,1)S(1)} %collective-permute-done.10.refs_1_, ...), custom_call_target="tpu_custom_call" | custom-call | bytes 4194304 | tf_op jit(solution)/shard_map/pallas_call | solution.py:158
  (23 shorter events, 1.5 us)
Async XLA Ops:
  2.9 9.0 %collective-permute-start = (bf16[4,2,128,128]{3,2,1,0:T(8,128)(2,1)}, bf16[4,2,128,128]{3,2,1,0:T(8,128)(2,1)S(1)}, u32[]{:S(2)}, u32[]{:S(2)}) collective-permute-start(bf16[4,2,128,128]{3,2,1,0:T(8,128)(2,1)} %get-tuple-element.59), channel_id=1, source_target_pairs={{0,1},{1,0},{2,3},{3,2},{4,5},{5,4},{6,7},{7,6},{8,9},{9,8},{10,11... | collective-permute-start | bytes 786440 | tf_op jit(solution)/shard_map/ppermute | solution.py:651
  3.0 9.5 %collective-permute-start.1 = (bf16[4,2,128,128]{3,2,1,0:T(8,128)(2,1)}, bf16[4,2,128,128]{3,2,1,0:T(8,128)(2,1)S(1)}, u32[]{:S(2)}, u32[]{:S(2)}) collective-permute-start(bf16[4,2,128,128]{3,2,1,0:T(8,128)(2,1)} %get-tuple-element.60), channel_id=1, source_target_pairs={{0,2},{1,3},{2,0},{3,1},{4,6},{5,7},{6,4},{7,5},{8,10},{9,11},{10,... | collective-permute-start | bytes 786440 | tf_op jit(solution)/shard_map/ppermute | solution.py:651
  5.6 12.9 %collective-permute-start.2 = (bf16[4,2,128,128]{3,2,1,0:T(8,128)(2,1)}, bf16[4,2,128,128]{3,2,1,0:T(8,128)(2,1)S(1)}, u32[]{:S(2)}, u32[]{:S(2)}) collective-permute-start(bf16[4,2,128,128]{3,2,1,0:T(8,128)(2,1)} %get-tuple-element.61), channel_id=1, source_target_pairs={{0,3},{1,2},{2,1},{3,0},{4,7},{5,6},{6,5},{7,4},{8,11},{9,10},{10,... | collective-permute-start | bytes 786440 | tf_op jit(solution)/shard_map/ppermute | solution.py:651
  7.9 10.6 %copy-start = (bf16[4,2,128,128]{3,2,1,0:T(8,128)(2,1)S(1)}, bf16[4,2,128,128]{3,2,1,0:T(8,128)(2,1)}, u32[]{:S(2)}) copy-start(bf16[4,2,128,128]{3,2,1,0:T(8,128)(2,1)} %get-tuple-element.58.refs_0_) | copy-start | bytes 786436
  7.9 27.5 %all-to-all-start = ((bf16[4,4,2,128,128]{4,3,2,1,0:T(8,128)(2,1)}), bf16[4,4,2,128,128]{4,3,2,1,0:T(8,128)(2,1)S(1)}, u32[]{:S(2)}, u32[]{:S(2)}) async-start(bf16[4,4,2,128,128]{4,3,2,1,0:T(8,128)(2,1)} %shard_map.94), calls=%async_computation | async-start | bytes 2097152 | tf_op jit(solution)/shard_map/all_to_all | solution.py:678
  18.7 14.2 %collective-permute-start.3 = (bf16[8,2,128,128]{3,2,1,0:T(8,128)(2,1)S(1)}, bf16[8,2,128,128]{3,2,1,0:T(8,128)(2,1)S(1)}, u32[]{:S(2)}, u32[]{:S(2)}) collective-permute-start(bf16[8,2,128,128]{3,2,1,0:T(8,128)(2,1)S(1)} %get-tuple-element.62), channel_id=1, source_target_pairs={{0,4},{1,5},{2,6},{3,7},{4,0},{5,1},{6,2},{7,3},{8,12},{9,13},{10,... | collective-permute-start | bytes 1572872 | tf_op jit(solution)/shard_map/ppermute | solution.py:400
  20.5 14.9 %collective-permute-start.4 = (bf16[8,2,128,128]{3,2,1,0:T(8,128)(2,1)S(1)}, bf16[8,2,128,128]{3,2,1,0:T(8,128)(2,1)S(1)}, u32[]{:S(2)}, u32[]{:S(2)}) collective-permute-start(bf16[8,2,128,128]{3,2,1,0:T(8,128)(2,1)S(1)} %get-tuple-element.65), channel_id=1, source_target_pairs={{4,8},{5,9},{6,10},{7,11},{8,4},{9,5},{10,6},{11,7},{20,24},{21,25... | collective-permute-start | bytes 1572872 | tf_op jit(solution)/shard_map/ppermute | solution.py:672
  22.0 13.4 %copy-start.1 = (s32[4,4]{1,0:T(4,128)S(1)}, s32[4,4]{1,0:T(4,128)}, u32[]{:S(2)}) copy-start(s32[4,4]{1,0:T(4,128)} %sections.13) | copy-start | bytes 196
  22.0 13.4 %copy-start.2 = (s32[16]{0:T(128)S(1)}, s32[16]{0:T(128)}, u32[]{:S(2)}) copy-start(s32[16]{0:T(128)} %widths.5) | copy-start | bytes 196
  22.0 21.8 %collective-permute-start.5 = (bf16[4,2,128,128]{3,2,1,0:T(8,128)(2,1)}, bf16[4,2,128,128]{3,2,1,0:T(8,128)(2,1)}, u32[]{:S(2)}, u32[]{:S(2)}) collective-permute-start(bf16[4,2,128,128]{3,2,1,0:T(8,128)(2,1)} %get-tuple-element.66), channel_id=1, source_target_pairs={{0,4},{1,5},{2,6},{3,7},{4,0},{5,1},{6,2},{7,3},{8,12},{9,13},{10,... | collective-permute-start | bytes 786440 | tf_op jit(solution)/shard_map/ppermute | solution.py:400
  32.8 15.0 %collective-permute-start.6 = (bf16[4,2,128,128]{3,2,1,0:T(8,128)(2,1)}, bf16[4,2,128,128]{3,2,1,0:T(8,128)(2,1)S(1)}, u32[]{:S(2)}, u32[]{:S(2)}) collective-permute-start(bf16[4,2,128,128]{3,2,1,0:T(8,128)(2,1)} %get-tuple-element.72), channel_id=1, source_target_pairs={{0,8},{1,9},{2,10},{3,11},{4,12},{5,13},{6,14},{7,15},{8,0},{9,1},... | collective-permute-start | bytes 786440 | tf_op jit(solution)/shard_map/ppermute | solution.py:400
  41.0 10.6 %collective-permute-start.13 = (bf16[4,2,128,128]{3,2,1,0:T(8,128)(2,1)S(1)}, bf16[4,2,128,128]{3,2,1,0:T(8,128)(2,1)S(1)}, u32[]{:S(2)}, u32[]{:S(2)}) collective-permute-start(bf16[4,2,128,128]{3,2,1,0:T(8,128)(2,1)S(1)} %get-tuple-element.88), channel_id=1, source_target_pairs={{0,4},{1,5},{2,6},{3,7},{4,0},{5,1},{6,2},{7,3},{8,12},{9,13},{10,... | collective-permute-start | bytes 786440 | tf_op jit(solution)/shard_map/ppermute | solution.py:400
  43.1 8.5 %collective-permute-start.14 = (bf16[4,2,128,128]{3,2,1,0:T(8,128)(2,1)S(1)}, bf16[4,2,128,128]{3,2,1,0:T(8,128)(2,1)S(1)}, u32[]{:S(2)}, u32[]{:S(2)}) collective-permute-start(bf16[4,2,128,128]{3,2,1,0:T(8,128)(2,1)S(1)} %get-tuple-element.89), channel_id=1, source_target_pairs={{4,8},{5,9},{6,10},{7,11},{8,4},{9,5},{10,6},{11,7},{20,24},{21,25... | collective-permute-start | bytes 786440 | tf_op jit(solution)/shard_map/ppermute | solution.py:672
  51.8 5.9 %collective-permute-start.15 = (bf16[6,2,128,128]{3,2,1,0:T(8,128)(2,1)S(1)}, bf16[6,2,128,128]{3,2,1,0:T(8,128)(2,1)S(1)}, u32[]{:S(2)}, u32[]{:S(2)}) collective-permute-start(bf16[6,2,128,128]{3,2,1,0:T(8,128)(2,1)S(1)} %get-tuple-element.95), channel_id=1, source_target_pairs={{0,1},{1,0},{2,3},{3,2},{4,5},{5,4},{6,7},{7,6},{8,9},{9,8},{10,11... | collective-permute-start | bytes 1179656 | tf_op jit(solution)/shard_map/ppermute | solution.py:651
  53.0 19.9 %collective-permute-start.8 = (bf16[8,2,128,128]{3,2,1,0:T(8,128)(2,1)S(1)}, bf16[8,2,128,128]{3,2,1,0:T(8,128)(2,1)S(1)}, u32[]{:S(2)}, u32[]{:S(2)}) collective-permute-start(bf16[8,2,128,128]{3,2,1,0:T(8,128)(2,1)S(1)} %get-tuple-element.81), channel_id=1, source_target_pairs={{0,4},{1,5},{2,6},{3,7},{4,0},{5,1},{6,2},{7,3},{8,12},{9,13},{10,... | collective-permute-start | bytes 1572872 | tf_op jit(solution)/shard_map/ppermute | solution.py:400
  55.1 17.0 %collective-permute-start.7 = (bf16[4,2,128,128]{3,2,1,0:T(8,128)(2,1)S(1)}, bf16[4,2,128,128]{3,2,1,0:T(8,128)(2,1)S(1)}, u32[]{:S(2)}, u32[]{:S(2)}) collective-permute-start(bf16[4,2,128,128]{3,2,1,0:T(8,128)(2,1)S(1)} %get-tuple-element.80), channel_id=1, source_target_pairs={{0,8},{1,9},{2,10},{3,11},{4,12},{5,13},{6,14},{7,15},{8,0},{9,1},... | collective-permute-start | bytes 786440 | tf_op jit(solution)/shard_map/ppermute | solution.py:400
  57.0 15.0 %collective-permute-start.9 = (bf16[4,2,128,128]{3,2,1,0:T(8,128)(2,1)S(1)}, bf16[4,2,128,128]{3,2,1,0:T(8,128)(2,1)S(1)}, u32[]{:S(2)}, u32[]{:S(2)}) collective-permute-start(bf16[4,2,128,128]{3,2,1,0:T(8,128)(2,1)S(1)} %get-tuple-element.82), channel_id=1, source_target_pairs={{4,8},{5,9},{6,10},{7,11},{8,4},{9,5},{10,6},{11,7},{20,24},{21,25... | collective-permute-start | bytes 786440 | tf_op jit(solution)/shard_map/ppermute | solution.py:672
  57.7 17.9 %collective-permute-start.16 = (bf16[6,2,128,128]{3,2,1,0:T(8,128)(2,1)S(1)}, bf16[6,2,128,128]{3,2,1,0:T(8,128)(2,1)S(1)}, u32[]{:S(2)}, u32[]{:S(2)}) collective-permute-start(bf16[6,2,128,128]{3,2,1,0:T(8,128)(2,1)S(1)} %get-tuple-element.100), channel_id=1, source_target_pairs={{0,2},{1,3},{2,0},{3,1},{4,6},{5,7},{6,4},{7,5},{8,10},{9,11},{10,... | collective-permute-start | bytes 1179656 | tf_op jit(solution)/shard_map/ppermute | solution.py:651
  59.3 18.5 %collective-permute-start.17 = (bf16[6,2,128,128]{3,2,1,0:T(8,128)(2,1)S(1)}, bf16[6,2,128,128]{3,2,1,0:T(8,128)(2,1)S(1)}, u32[]{:S(2)}, u32[]{:S(2)}) collective-permute-start(bf16[6,2,128,128]{3,2,1,0:T(8,128)(2,1)S(1)} %get-tuple-element.101), channel_id=1, source_target_pairs={{0,3},{1,2},{2,1},{3,0},{4,7},{5,6},{6,5},{7,4},{8,11},{9,10},{10,... | collective-permute-start | bytes 1179656 | tf_op jit(solution)/shard_map/ppermute | solution.py:651
  73.2 6.4 %collective-permute-start.10 = (bf16[2,2,128,128]{3,2,1,0:T(8,128)(2,1)S(1)}, bf16[2,2,128,128]{3,2,1,0:T(8,128)(2,1)S(1)}, u32[]{:S(2)}, u32[]{:S(2)}) collective-permute-start(bf16[2,2,128,128]{3,2,1,0:T(8,128)(2,1)S(1)} %get-tuple-element.84), channel_id=1, source_target_pairs={{0,1},{1,0},{2,3},{3,2},{4,5},{5,4},{6,7},{7,6},{8,9},{9,8},{10,11... | collective-permute-start | bytes 393224 | tf_op jit(solution)/shard_map/ppermute | solution.py:651
  73.9 5.7 %collective-permute-start.11 = (bf16[2,2,128,128]{3,2,1,0:T(8,128)(2,1)S(1)}, bf16[2,2,128,128]{3,2,1,0:T(8,128)(2,1)S(1)}, u32[]{:S(2)}, u32[]{:S(2)}) collective-permute-start(bf16[2,2,128,128]{3,2,1,0:T(8,128)(2,1)S(1)} %get-tuple-element.85), channel_id=1, source_target_pairs={{0,2},{1,3},{2,0},{3,1},{4,6},{5,7},{6,4},{7,5},{8,10},{9,11},{10,... | collective-permute-start | bytes 393224 | tf_op jit(solution)/shard_map/ppermute | solution.py:651
  75.2 7.4 %collective-permute-start.12 = (bf16[2,2,128,128]{3,2,1,0:T(8,128)(2,1)S(1)}, bf16[2,2,128,128]{3,2,1,0:T(8,128)(2,1)S(1)}, u32[]{:S(2)}, u32[]{:S(2)}) collective-permute-start(bf16[2,2,128,128]{3,2,1,0:T(8,128)(2,1)S(1)} %get-tuple-element.86), channel_id=1, source_target_pairs={{0,3},{1,2},{2,1},{3,0},{4,7},{5,6},{6,5},{7,4},{8,11},{9,10},{10,... | collective-permute-start | bytes 393224 | tf_op jit(solution)/shard_map/ppermute | solution.py:651

commit v11 on v10

--- a/solution.py
+++ b/solution.py
@@ -650,7 +650,7 @@
     for m in range(1, PLANE):
         pieces[m] = lax.ppermute(pieces[m], "seq", [(i, i ^ m) for i in range(peers)])
         if chip_first and m == 1:
-            pieces = lax.optimization_barrier(pieces)
+            pieces[1], pieces[3] = lax.optimization_barrier((pieces[1], pieces[3]))
     return pieces
 
 

time: 85.7 us -> 85.6 us (level)
  no operation moved by 1% of the time
where the time goes in v11:
time: 85.6 us; the launch traced here: 84.5 us
  waiting for transfers between devices  32.8 us (38%)
  starting transfers between devices  29.2 us (34%)
  Pallas kernels  21.7 us (25%)
    ppermute x6, waiting for transfers between devices, partner(): lax.ppermute(value, axis, [(i, i ^ 1 << apart) for i in range(lax.axis_si...  20.9 us
    ppermute x6, starting transfers between devices, partner(): lax.ppermute(value, axis, [(i, i ^ 1 << apart) for i in range(lax.axis_si...  14.4 us
    pallas_call x3, Pallas kernels, attend(): pl.pallas_call(functools.partial(attend_kernel, first=first, slot=slot, g...  12.2 us
    ppermute x9, waiting for transfers between devices, in_plane(): lax.ppermute(pieces[m], 'seq', [(i, i ^ m) for i in range(peers)])  11.9 us
    ppermute x9, starting transfers between devices, in_plane(): lax.ppermute(pieces[m], 'seq', [(i, i ^ m) for i in range(peers)])  8.76 us
    pallas_call x2, Pallas kernels, pack(): pl.pallas_call(functools.partial(pack_kernel, order=order, count=count, c...  4.5 us
    all_to_all x1, starting transfers between devices, plane_all_to_all(): lax.all_to_all(value, 'seq', 0, 0, axis_index_groups=planes, tiled=True)  3.99 us
    pallas_call x2, Pallas kernels, unpack(): pl.pallas_call(functools.partial(unpack_kernel, groups=[group for group,...  3.64 us
  transfers between devices with their start and end apart: 19, of which 9 were waited for; matrix products, arithmetic and copies ran while one was open for 0% of the time, Pallas kernels for 21%

profile of v11, /device:TPU:1, one launch (start us, length us, event | category | flops | bytes accessed | tf_op | source)
XLA Modules:
  0.0 84.5 jit_solution(2178174601920865460)
XLA Ops:
  0.6 2.3 %shard_map.93 = (bf16[4,2,128,128]{3,2,1,0:T(8,128)(2,1)}, bf16[4,2,128,128]{3,2,1,0:T(8,128)(2,1)}, bf16[4,2,128,128]{3,2,1,0:T(8,128)(2,1)}, bf16[4,2,128,128]{3,2,1,0:T(8,128)(2,1)}) custom-call(s32[1]{0:T(128)} %bitcast.place, s32[4,4]{1,0:T(4,128)} %sections.13, bf16[128,16,128]{2,1,0:T(8,128)(2,1)} %refs_0_.2, bf16[128,16,128]{2,1,0:T(8,128)(2,1)} %refs_1_.2), custom_call_target="tpu_custom_call" | custom-call | bytes 2097152 | tf_op jit(solution)/shard_map/pallas_call | solution.py:124
  3.0 2.7 %collective-permute-start.1 = (bf16[4,2,128,128]{3,2,1,0:T(8,128)(2,1)}, bf16[4,2,128,128]{3,2,1,0:T(8,128)(2,1)S(1)}, u32[]{:S(2)}, u32[]{:S(2)}) collective-permute-start(bf16[4,2,128,128]{3,2,1,0:T(8,128)(2,1)} %get-tuple-element.58), channel_id=1, source_target_pairs={{0,2},{1,3},{2,0},{3,1},{4,6},{5,7},{6,4},{7,5},{8,10},{9,11},{10,... | collective-permute-start | bytes 786440 | tf_op jit(solution)/shard_map/ppermute | solution.py:651
  5.7 2.2 %shard_map.94 = bf16[4,4,2,128,128]{4,3,2,1,0:T(8,128)(2,1)} custom-call(s32[1]{0:T(128)} %bitcast.place, s32[4,4]{1,0:T(4,128)} %sections.13, bf16[128,16,128]{2,1,0:T(8,128)(2,1)} %refs_0_.3, bf16[128,16,128]{2,1,0:T(8,128)(2,1)} %refs_1_.3), custom_call_target="tpu_custom_call" | custom-call | bytes 2097152 | tf_op jit(solution)/shard_map/pallas_call | solution.py:124
  7.9 4.0 %all-to-all-start = ((bf16[4,4,2,128,128]{4,3,2,1,0:T(8,128)(2,1)}), bf16[4,4,2,128,128]{4,3,2,1,0:T(8,128)(2,1)S(1)}, u32[]{:S(2)}, u32[]{:S(2)}) async-start(bf16[4,4,2,128,128]{4,3,2,1,0:T(8,128)(2,1)} %shard_map.94), calls=%async_computation | async-start | bytes 2097152 | tf_op jit(solution)/shard_map/all_to_all | solution.py:678
  11.9 0.5 collective-permute-done.1.refs_2_
  12.5 6.1 %collective-permute-done.2.refs_3_ = bf16[4,2,128,128]{3,2,1,0:T(8,128)(2,1)S(1)} collective-permute-done((bf16[4,2,128,128]{3,2,1,0:T(8,128)(2,1)}, bf16[4,2,128,128]{3,2,1,0:T(8,128)(2,1)S(1)}, u32[]{:S(2)}, u32[]{:S(2)}) %collective-permute-start.2) | collective-permute-done | bytes 262176 | tf_op jit(solution)/shard_map/ppermute | solution.py:651
  18.7 1.8 %collective-permute-start.3 = (bf16[8,2,128,128]{3,2,1,0:T(8,128)(2,1)S(1)}, bf16[8,2,128,128]{3,2,1,0:T(8,128)(2,1)S(1)}, u32[]{:S(2)}, u32[]{:S(2)}) collective-permute-start(bf16[8,2,128,128]{3,2,1,0:T(8,128)(2,1)S(1)} %get-tuple-element.60), channel_id=1, source_target_pairs={{0,4},{1,5},{2,6},{3,7},{4,0},{5,1},{6,2},{7,3},{8,12},{9,13},{10,... | collective-permute-start | bytes 1572872 | tf_op jit(solution)/shard_map/ppermute | solution.py:400
  20.5 0.7 collective-permute-start.4
  21.2 0.8 shard_map.96
  22.0 3.8 %collective-permute-start.5 = (bf16[4,2,128,128]{3,2,1,0:T(8,128)(2,1)}, bf16[4,2,128,128]{3,2,1,0:T(8,128)(2,1)}, u32[]{:S(2)}, u32[]{:S(2)}) collective-permute-start(bf16[4,2,128,128]{3,2,1,0:T(8,128)(2,1)} %get-tuple-element.64), channel_id=1, source_target_pairs={{0,4},{1,5},{2,6},{3,7},{4,0},{5,1},{6,2},{7,3},{8,12},{9,13},{10,... | collective-permute-start | bytes 786440 | tf_op jit(solution)/shard_map/ppermute | solution.py:400
  25.8 7.0 %collective-permute-done.3.refs_5_ = bf16[8,2,128,128]{3,2,1,0:T(8,128)(2,1)S(1)} collective-permute-done((bf16[8,2,128,128]{3,2,1,0:T(8,128)(2,1)S(1)}, bf16[8,2,128,128]{3,2,1,0:T(8,128)(2,1)S(1)}, u32[]{:S(2)}, u32[]{:S(2)}) %collective-permute-start.3) | collective-permute-done | bytes 524320 | tf_op jit(solution)/shard_map/ppermute | solution.py:400
  32.8 2.6 %collective-permute-start.6 = (bf16[4,2,128,128]{3,2,1,0:T(8,128)(2,1)}, bf16[4,2,128,128]{3,2,1,0:T(8,128)(2,1)S(1)}, u32[]{:S(2)}, u32[]{:S(2)}) collective-permute-start(bf16[4,2,128,128]{3,2,1,0:T(8,128)(2,1)} %get-tuple-element.70), channel_id=1, source_target_pairs={{0,8},{1,9},{2,10},{3,11},{4,12},{5,13},{6,14},{7,15},{8,0},{9,1},... | collective-permute-start | bytes 786440 | tf_op jit(solution)/shard_map/ppermute | solution.py:400
  35.4 5.5 %shard_map.97 = (bf16[6,2,128,128]{3,2,1,0:T(8,128)(2,1)S(1)}, bf16[6,2,128,128]{3,2,1,0:T(8,128)(2,1)S(1)}, bf16[6,2,128,128]{3,2,1,0:T(8,128)(2,1)S(1)}, bf16[...) custom-call(s32[1]{0:T(128)} %bitcast.place, ...), custom_call_target="tpu_custom_call" | custom-call | flops 1207959552 | bytes 5242880 | tf_op jit(solution)/shard_map/pallas_call | solution.py:331
  41.0 2.2 %collective-permute-start.13 = (bf16[4,2,128,128]{3,2,1,0:T(8,128)(2,1)S(1)}, bf16[4,2,128,128]{3,2,1,0:T(8,128)(2,1)S(1)}, u32[]{:S(2)}, u32[]{:S(2)}) collective-permute-start(bf16[4,2,128,128]{3,2,1,0:T(8,128)(2,1)S(1)} %get-tuple-element.86), channel_id=1, source_target_pairs={{0,4},{1,5},{2,6},{3,7},{4,0},{5,1},{6,2},{7,3},{8,12},{9,13},{10,... | collective-permute-start | bytes 786440 | tf_op jit(solution)/shard_map/ppermute | solution.py:400
  43.1 0.7 collective-permute-start.14
  43.8 3.6 %shard_map.98 = (bf16[6,2,128,128]{3,2,1,0:T(8,128)(2,1)S(1)}, bf16[6,2,128,128]{3,2,1,0:T(8,128)(2,1)S(1)}, bf16[6,2,128,128]{3,2,1,0:T(8,128)(2,1)S(1)}, bf16[...) custom-call(s32[1]{0:T(128)} %bitcast.place, ...), custom_call_target="tpu_custom_call", output_to_operand_aliasing={{0}: (11, {}), {1}: (12, {}), {2}: (13, {}), {3}: (14, {})} | custom-call | flops 603979776 | bytes 2621440 | tf_op jit(solution)/shard_map/pallas_call | solution.py:331
  47.8 3.1 %shard_map.99 = (bf16[6,2,128,128]{3,2,1,0:T(8,128)(2,1)S(1)}, bf16[6,2,128,128]{3,2,1,0:T(8,128)(2,1)S(1)}, bf16[6,2,128,128]{3,2,1,0:T(8,128)(2,1)S(1)}, bf16[...) custom-call(s32[1]{0:T(128)} %bitcast.place, ...), custom_call_target="tpu_custom_call", output_to_operand_aliasing={{0}: (11, {}), {1}: (12, {}), {2}: (13, {}), {3}: (14, {}),... | custom-call | flops 603979776 | bytes 2621440 | tf_op jit(solution)/shard_map/pallas_call | solution.py:331
  51.0 0.6 collective-permute-done.13.refs_1_
  51.8 1.2 %collective-permute-start.15 = (bf16[6,2,128,128]{3,2,1,0:T(8,128)(2,1)S(1)}, bf16[6,2,128,128]{3,2,1,0:T(8,128)(2,1)S(1)}, u32[]{:S(2)}, u32[]{:S(2)}) collective-permute-start(bf16[6,2,128,128]{3,2,1,0:T(8,128)(2,1)S(1)} %get-tuple-element.93), channel_id=1, source_target_pairs={{0,1},{1,0},{2,3},{3,2},{4,5},{5,4},{6,7},{7,6},{8,9},{9,8},{10,11... | collective-permute-start | bytes 1179656 | tf_op jit(solution)/shard_map/ppermute | solution.py:651
  53.0 2.1 %collective-permute-start.8 = (bf16[8,2,128,128]{3,2,1,0:T(8,128)(2,1)S(1)}, bf16[8,2,128,128]{3,2,1,0:T(8,128)(2,1)S(1)}, u32[]{:S(2)}, u32[]{:S(2)}) collective-permute-start(bf16[8,2,128,128]{3,2,1,0:T(8,128)(2,1)S(1)} %get-tuple-element.79), channel_id=1, source_target_pairs={{0,4},{1,5},{2,6},{3,7},{4,0},{5,1},{6,2},{7,3},{8,12},{9,13},{10,... | collective-permute-start | bytes 1572872 | tf_op jit(solution)/shard_map/ppermute | solution.py:400
  55.1 2.0 %collective-permute-start.7 = (bf16[4,2,128,128]{3,2,1,0:T(8,128)(2,1)S(1)}, bf16[4,2,128,128]{3,2,1,0:T(8,128)(2,1)S(1)}, u32[]{:S(2)}, u32[]{:S(2)}) collective-permute-start(bf16[4,2,128,128]{3,2,1,0:T(8,128)(2,1)S(1)} %get-tuple-element.78), channel_id=1, source_target_pairs={{0,8},{1,9},{2,10},{3,11},{4,12},{5,13},{6,14},{7,15},{8,0},{9,1},... | collective-permute-start | bytes 786440 | tf_op jit(solution)/shard_map/ppermute | solution.py:400
  57.0 0.7 collective-permute-start.9
  57.7 1.5 %collective-permute-start.16 = (bf16[6,2,128,128]{3,2,1,0:T(8,128)(2,1)S(1)}, bf16[6,2,128,128]{3,2,1,0:T(8,128)(2,1)S(1)}, u32[]{:S(2)}, u32[]{:S(2)}) collective-permute-start(bf16[6,2,128,128]{3,2,1,0:T(8,128)(2,1)S(1)} %get-tuple-element.96), channel_id=1, source_target_pairs={{0,2},{1,3},{2,0},{3,1},{4,6},{5,7},{6,4},{7,5},{8,10},{9,11},{10,... | collective-permute-start | bytes 1179656 | tf_op jit(solution)/shard_map/ppermute | solution.py:651
  59.3 0.8 collective-permute-start.17
  60.0 12.0 %collective-permute-done.7.refs_2_ = bf16[4,2,128,128]{3,2,1,0:T(8,128)(2,1)S(1)} collective-permute-done((bf16[4,2,128,128]{3,2,1,0:T(8,128)(2,1)S(1)}, bf16[4,2,128,128]{3,2,1,0:T(8,128)(2,1)S(1)}, u32[]{:S(2)}, u32[]{:S(2)}) %collective-permute-start.7) | collective-permute-done | bytes 262176 | tf_op jit(solution)/shard_map/ppermute | solution.py:400
  72.0 0.9 %collective-permute-done.8.refs_3_ = bf16[8,2,128,128]{3,2,1,0:T(8,128)(2,1)S(1)} collective-permute-done((bf16[8,2,128,128]{3,2,1,0:T(8,128)(2,1)S(1)}, bf16[8,2,128,128]{3,2,1,0:T(8,128)(2,1)S(1)}, u32[]{:S(2)}, u32[]{:S(2)}) %collective-permute-start.8) | collective-permute-done | bytes 524320 | tf_op jit(solution)/shard_map/ppermute | solution.py:400
  73.2 0.7 collective-permute-start.10
  73.9 1.3 %collective-permute-start.11 = (bf16[2,2,128,128]{3,2,1,0:T(8,128)(2,1)S(1)}, bf16[2,2,128,128]{3,2,1,0:T(8,128)(2,1)S(1)}, u32[]{:S(2)}, u32[]{:S(2)}) collective-permute-start(bf16[2,2,128,128]{3,2,1,0:T(8,128)(2,1)S(1)} %get-tuple-element.83), channel_id=1, source_target_pairs={{0,2},{1,3},{2,0},{3,1},{4,6},{5,7},{6,4},{7,5},{8,10},{9,11},{10,... | collective-permute-start | bytes 393224 | tf_op jit(solution)/shard_map/ppermute | solution.py:651
  75.6 2.1 %collective-permute-done.17.refs_3_.refs_7_ = bf16[6,2,128,128]{3,2,1,0:T(8,128)(2,1)S(1)} collective-permute-done((bf16[6,2,128,128]{3,2,1,0:T(8,128)(2,1)S(1)}, bf16[6,2,128,128]{3,2,1,0:T(8,128)(2,1)S(1)}, u32[]{:S(2)}, u32[]{:S(2)}) %collective-permute-start.17) | collective-permute-done | bytes 393248 | tf_op jit(solution)/shard_map/ppermute | solution.py:651
  77.7 1.8 %shard_map.102 = (bf16[128,16,128]{2,1,0:T(8,128)(2,1)}, bf16[128,16,128]{2,1,0:T(8,128)(2,1)}) custom-call(s32[1]{0:T(128)} %bitcast.place, s32[4,4]{1,0:T(4,128)S(1)} %copy-done.1, bf16[6,2,128,128]{3,2,1,0:T(8,128)(2,1)S(1)} %get-tuple-element.92.refs_0_.refs_4_, bf16[6,2,128,128]{3,2,1,0:T(8,128)(2,1)S(1)} %collective-permute-done.15.refs_1_.refs_5_, ...), custom_call_target="tpu_custom_call" | custom-call | bytes 6291456 | tf_op jit(solution)/shard_map/pallas_call | solution.py:158
  79.6 3.1 %collective-permute-done.12.refs_3_ = bf16[2,2,128,128]{3,2,1,0:T(8,128)(2,1)S(1)} collective-permute-done((bf16[2,2,128,128]{3,2,1,0:T(8,128)(2,1)S(1)}, bf16[2,2,128,128]{3,2,1,0:T(8,128)(2,1)S(1)}, u32[]{:S(2)}, u32[]{:S(2)}) %collective-permute-start.12) | collective-permute-done | bytes 131104 | tf_op jit(solution)/shard_map/ppermute | solution.py:651
  82.7 1.8 %shard_map.103 = (bf16[128,16,128]{2,1,0:T(8,128)(2,1)}, bf16[128,16,128]{2,1,0:T(8,128)(2,1)}) custom-call(s32[1]{0:T(128)} %bitcast.place, s32[4,4]{1,0:T(4,128)S(1)} %copy-done.1, bf16[2,2,128,128]{3,2,1,0:T(8,128)(2,1)S(1)} %get-tuple-element.102.refs_0_, bf16[2,2,128,128]{3,2,1,0:T(8,128)(2,1)S(1)} %collective-permute-done.10.refs_1_, ...), custom_call_target="tpu_custom_call" | custom-call | bytes 4194304 | tf_op jit(solution)/shard_map/pallas_call | solution.py:158
  (23 shorter events, 1.5 us)
Async XLA Ops:
  2.9 9.0 %collective-permute-start = (bf16[4,2,128,128]{3,2,1,0:T(8,128)(2,1)}, bf16[4,2,128,128]{3,2,1,0:T(8,128)(2,1)S(1)}, u32[]{:S(2)}, u32[]{:S(2)}) collective-permute-start(bf16[4,2,128,128]{3,2,1,0:T(8,128)(2,1)} %get-tuple-element.57), channel_id=1, source_target_pairs={{0,1},{1,0},{2,3},{3,2},{4,5},{5,4},{6,7},{7,6},{8,9},{9,8},{10,11... | collective-permute-start | bytes 786440 | tf_op jit(solution)/shard_map/ppermute | solution.py:651
  3.0 9.5 %collective-permute-start.1 = (bf16[4,2,128,128]{3,2,1,0:T(8,128)(2,1)}, bf16[4,2,128,128]{3,2,1,0:T(8,128)(2,1)S(1)}, u32[]{:S(2)}, u32[]{:S(2)}) collective-permute-start(bf16[4,2,128,128]{3,2,1,0:T(8,128)(2,1)} %get-tuple-element.58), channel_id=1, source_target_pairs={{0,2},{1,3},{2,0},{3,1},{4,6},{5,7},{6,4},{7,5},{8,10},{9,11},{10,... | collective-permute-start | bytes 786440 | tf_op jit(solution)/shard_map/ppermute | solution.py:651
  5.6 12.9 %collective-permute-start.2 = (bf16[4,2,128,128]{3,2,1,0:T(8,128)(2,1)}, bf16[4,2,128,128]{3,2,1,0:T(8,128)(2,1)S(1)}, u32[]{:S(2)}, u32[]{:S(2)}) collective-permute-start(bf16[4,2,128,128]{3,2,1,0:T(8,128)(2,1)} %get-tuple-element.59), channel_id=1, source_target_pairs={{0,3},{1,2},{2,1},{3,0},{4,7},{5,6},{6,5},{7,4},{8,11},{9,10},{10,... | collective-permute-start | bytes 786440 | tf_op jit(solution)/shard_map/ppermute | solution.py:651
  7.9 10.6 %copy-start = (bf16[4,2,128,128]{3,2,1,0:T(8,128)(2,1)S(1)}, bf16[4,2,128,128]{3,2,1,0:T(8,128)(2,1)}, u32[]{:S(2)}) copy-start(bf16[4,2,128,128]{3,2,1,0:T(8,128)(2,1)} %get-tuple-element.56.refs_0_) | copy-start | bytes 786436
  7.9 27.5 %all-to-all-start = ((bf16[4,4,2,128,128]{4,3,2,1,0:T(8,128)(2,1)}), bf16[4,4,2,128,128]{4,3,2,1,0:T(8,128)(2,1)S(1)}, u32[]{:S(2)}, u32[]{:S(2)}) async-start(bf16[4,4,2,128,128]{4,3,2,1,0:T(8,128)(2,1)} %shard_map.94), calls=%async_computation | async-start | bytes 2097152 | tf_op jit(solution)/shard_map/all_to_all | solution.py:678
  18.7 14.2 %collective-permute-start.3 = (bf16[8,2,128,128]{3,2,1,0:T(8,128)(2,1)S(1)}, bf16[8,2,128,128]{3,2,1,0:T(8,128)(2,1)S(1)}, u32[]{:S(2)}, u32[]{:S(2)}) collective-permute-start(bf16[8,2,128,128]{3,2,1,0:T(8,128)(2,1)S(1)} %get-tuple-element.60), channel_id=1, source_target_pairs={{0,4},{1,5},{2,6},{3,7},{4,0},{5,1},{6,2},{7,3},{8,12},{9,13},{10,... | collective-permute-start | bytes 1572872 | tf_op jit(solution)/shard_map/ppermute | solution.py:400
  20.5 14.9 %collective-permute-start.4 = (bf16[8,2,128,128]{3,2,1,0:T(8,128)(2,1)S(1)}, bf16[8,2,128,128]{3,2,1,0:T(8,128)(2,1)S(1)}, u32[]{:S(2)}, u32[]{:S(2)}) collective-permute-start(bf16[8,2,128,128]{3,2,1,0:T(8,128)(2,1)S(1)} %get-tuple-element.63), channel_id=1, source_target_pairs={{4,8},{5,9},{6,10},{7,11},{8,4},{9,5},{10,6},{11,7},{20,24},{21,25... | collective-permute-start | bytes 1572872 | tf_op jit(solution)/shard_map/ppermute | solution.py:672
  22.0 13.4 %copy-start.1 = (s32[4,4]{1,0:T(4,128)S(1)}, s32[4,4]{1,0:T(4,128)}, u32[]{:S(2)}) copy-start(s32[4,4]{1,0:T(4,128)} %sections.13) | copy-start | bytes 196
  22.0 13.4 %copy-start.2 = (s32[16]{0:T(128)S(1)}, s32[16]{0:T(128)}, u32[]{:S(2)}) copy-start(s32[16]{0:T(128)} %widths.5) | copy-start | bytes 196
  22.0 21.8 %collective-permute-start.5 = (bf16[4,2,128,128]{3,2,1,0:T(8,128)(2,1)}, bf16[4,2,128,128]{3,2,1,0:T(8,128)(2,1)}, u32[]{:S(2)}, u32[]{:S(2)}) collective-permute-start(bf16[4,2,128,128]{3,2,1,0:T(8,128)(2,1)} %get-tuple-element.64), channel_id=1, source_target_pairs={{0,4},{1,5},{2,6},{3,7},{4,0},{5,1},{6,2},{7,3},{8,12},{9,13},{10,... | collective-permute-start | bytes 786440 | tf_op jit(solution)/shard_map/ppermute | solution.py:400
  32.8 15.0 %collective-permute-start.6 = (bf16[4,2,128,128]{3,2,1,0:T(8,128)(2,1)}, bf16[4,2,128,128]{3,2,1,0:T(8,128)(2,1)S(1)}, u32[]{:S(2)}, u32[]{:S(2)}) collective-permute-start(bf16[4,2,128,128]{3,2,1,0:T(8,128)(2,1)} %get-tuple-element.70), channel_id=1, source_target_pairs={{0,8},{1,9},{2,10},{3,11},{4,12},{5,13},{6,14},{7,15},{8,0},{9,1},... | collective-permute-start | bytes 786440 | tf_op jit(solution)/shard_map/ppermute | solution.py:400
  41.0 10.6 %collective-permute-start.13 = (bf16[4,2,128,128]{3,2,1,0:T(8,128)(2,1)S(1)}, bf16[4,2,128,128]{3,2,1,0:T(8,128)(2,1)S(1)}, u32[]{:S(2)}, u32[]{:S(2)}) collective-permute-start(bf16[4,2,128,128]{3,2,1,0:T(8,128)(2,1)S(1)} %get-tuple-element.86), channel_id=1, source_target_pairs={{0,4},{1,5},{2,6},{3,7},{4,0},{5,1},{6,2},{7,3},{8,12},{9,13},{10,... | collective-permute-start | bytes 786440 | tf_op jit(solution)/shard_map/ppermute | solution.py:400
  43.1 8.5 %collective-permute-start.14 = (bf16[4,2,128,128]{3,2,1,0:T(8,128)(2,1)S(1)}, bf16[4,2,128,128]{3,2,1,0:T(8,128)(2,1)S(1)}, u32[]{:S(2)}, u32[]{:S(2)}) collective-permute-start(bf16[4,2,128,128]{3,2,1,0:T(8,128)(2,1)S(1)} %get-tuple-element.87), channel_id=1, source_target_pairs={{4,8},{5,9},{6,10},{7,11},{8,4},{9,5},{10,6},{11,7},{20,24},{21,25... | collective-permute-start | bytes 786440 | tf_op jit(solution)/shard_map/ppermute | solution.py:672
  51.8 7.4 %collective-permute-start.15 = (bf16[6,2,128,128]{3,2,1,0:T(8,128)(2,1)S(1)}, bf16[6,2,128,128]{3,2,1,0:T(8,128)(2,1)S(1)}, u32[]{:S(2)}, u32[]{:S(2)}) collective-permute-start(bf16[6,2,128,128]{3,2,1,0:T(8,128)(2,1)S(1)} %get-tuple-element.93), channel_id=1, source_target_pairs={{0,1},{1,0},{2,3},{3,2},{4,5},{5,4},{6,7},{7,6},{8,9},{9,8},{10,11... | collective-permute-start | bytes 1179656 | tf_op jit(solution)/shard_map/ppermute | solution.py:651
  53.0 19.9 %collective-permute-start.8 = (bf16[8,2,128,128]{3,2,1,0:T(8,128)(2,1)S(1)}, bf16[8,2,128,128]{3,2,1,0:T(8,128)(2,1)S(1)}, u32[]{:S(2)}, u32[]{:S(2)}) collective-permute-start(bf16[8,2,128,128]{3,2,1,0:T(8,128)(2,1)S(1)} %get-tuple-element.79), channel_id=1, source_target_pairs={{0,4},{1,5},{2,6},{3,7},{4,0},{5,1},{6,2},{7,3},{8,12},{9,13},{10,... | collective-permute-start | bytes 1572872 | tf_op jit(solution)/shard_map/ppermute | solution.py:400
  55.1 17.0 %collective-permute-start.7 = (bf16[4,2,128,128]{3,2,1,0:T(8,128)(2,1)S(1)}, bf16[4,2,128,128]{3,2,1,0:T(8,128)(2,1)S(1)}, u32[]{:S(2)}, u32[]{:S(2)}) collective-permute-start(bf16[4,2,128,128]{3,2,1,0:T(8,128)(2,1)S(1)} %get-tuple-element.78), channel_id=1, source_target_pairs={{0,8},{1,9},{2,10},{3,11},{4,12},{5,13},{6,14},{7,15},{8,0},{9,1},... | collective-permute-start | bytes 786440 | tf_op jit(solution)/shard_map/ppermute | solution.py:400
  57.0 15.0 %collective-permute-start.9 = (bf16[4,2,128,128]{3,2,1,0:T(8,128)(2,1)S(1)}, bf16[4,2,128,128]{3,2,1,0:T(8,128)(2,1)S(1)}, u32[]{:S(2)}, u32[]{:S(2)}) collective-permute-start(bf16[4,2,128,128]{3,2,1,0:T(8,128)(2,1)S(1)} %get-tuple-element.80), channel_id=1, source_target_pairs={{4,8},{5,9},{6,10},{7,11},{8,4},{9,5},{10,6},{11,7},{20,24},{21,25... | collective-permute-start | bytes 786440 | tf_op jit(solution)/shard_map/ppermute | solution.py:672
  57.7 17.9 %collective-permute-start.16 = (bf16[6,2,128,128]{3,2,1,0:T(8,128)(2,1)S(1)}, bf16[6,2,128,128]{3,2,1,0:T(8,128)(2,1)S(1)}, u32[]{:S(2)}, u32[]{:S(2)}) collective-permute-start(bf16[6,2,128,128]{3,2,1,0:T(8,128)(2,1)S(1)} %get-tuple-element.96), channel_id=1, source_target_pairs={{0,2},{1,3},{2,0},{3,1},{4,6},{5,7},{6,4},{7,5},{8,10},{9,11},{10,... | collective-permute-start | bytes 1179656 | tf_op jit(solution)/shard_map/ppermute | solution.py:651
  59.3 18.5 %collective-permute-start.17 = (bf16[6,2,128,128]{3,2,1,0:T(8,128)(2,1)S(1)}, bf16[6,2,128,128]{3,2,1,0:T(8,128)(2,1)S(1)}, u32[]{:S(2)}, u32[]{:S(2)}) collective-permute-start(bf16[6,2,128,128]{3,2,1,0:T(8,128)(2,1)S(1)} %get-tuple-element.97), channel_id=1, source_target_pairs={{0,3},{1,2},{2,1},{3,0},{4,7},{5,6},{6,5},{7,4},{8,11},{9,10},{10,... | collective-permute-start | bytes 1179656 | tf_op jit(solution)/shard_map/ppermute | solution.py:651
  73.2 6.4 %collective-permute-start.10 = (bf16[2,2,128,128]{3,2,1,0:T(8,128)(2,1)S(1)}, bf16[2,2,128,128]{3,2,1,0:T(8,128)(2,1)S(1)}, u32[]{:S(2)}, u32[]{:S(2)}) collective-permute-start(bf16[2,2,128,128]{3,2,1,0:T(8,128)(2,1)S(1)} %get-tuple-element.82), channel_id=1, source_target_pairs={{0,1},{1,0},{2,3},{3,2},{4,5},{5,4},{6,7},{7,6},{8,9},{9,8},{10,11... | collective-permute-start | bytes 393224 | tf_op jit(solution)/shard_map/ppermute | solution.py:651
  73.9 5.6 %collective-permute-start.11 = (bf16[2,2,128,128]{3,2,1,0:T(8,128)(2,1)S(1)}, bf16[2,2,128,128]{3,2,1,0:T(8,128)(2,1)S(1)}, u32[]{:S(2)}, u32[]{:S(2)}) collective-permute-start(bf16[2,2,128,128]{3,2,1,0:T(8,128)(2,1)S(1)} %get-tuple-element.83), channel_id=1, source_target_pairs={{0,2},{1,3},{2,0},{3,1},{4,6},{5,7},{6,4},{7,5},{8,10},{9,11},{10,... | collective-permute-start | bytes 393224 | tf_op jit(solution)/shard_map/ppermute | solution.py:651
  75.2 7.4 %collective-permute-start.12 = (bf16[2,2,128,128]{3,2,1,0:T(8,128)(2,1)S(1)}, bf16[2,2,128,128]{3,2,1,0:T(8,128)(2,1)S(1)}, u32[]{:S(2)}, u32[]{:S(2)}) collective-permute-start(bf16[2,2,128,128]{3,2,1,0:T(8,128)(2,1)S(1)} %get-tuple-element.84), channel_id=1, source_target_pairs={{0,3},{1,2},{2,1},{3,0},{4,7},{5,6},{6,5},{7,4},{8,11},{9,10},{10,... | collective-permute-start | bytes 393224 | tf_op jit(solution)/shard_map/ppermute | solution.py:651

commit v12 on v10

--- a/solution.py
+++ b/solution.py
@@ -149,7 +149,7 @@
     flat = [piece for _, pieces, _ in parts for piece in pieces]
     count, tokens, width = flat[0].shape[1:]
     heads = sections.size
-    chunk = tokens // 2
+    chunk = tokens // 4
     specs = [
         pl.BlockSpec((len(group), count, chunk, width), lambda i, run=run: (run, 0, i, 0))
         for group, _, run in parts

time: 85.7 us -> 86.2 us (level)
  Pallas kernels: 21.7 us -> 22.8 us
    pallas_call x2, Pallas kernels: 3.64 us -> 4.72 us  [unpack(): pl.pallas_call(functools.partial(unpack_kernel, groups=[group for group,...]
where the time goes in v12:
time: 86.2 us; the launch traced here: 85.1 us
  waiting for transfers between devices  32.3 us (37%)
  starting transfers between devices  29.2 us (34%)
  Pallas kernels  22.8 us (26%)
    ppermute x6, waiting for transfers between devices, partner(): lax.ppermute(value, axis, [(i, i ^ 1 << apart) for i in range(lax.axis_si...  20.9 us
    ppermute x6, starting transfers between devices, partner(): lax.ppermute(value, axis, [(i, i ^ 1 << apart) for i in range(lax.axis_si...  14.4 us
    pallas_call x3, Pallas kernels, attend(): pl.pallas_call(functools.partial(attend_kernel, first=first, slot=slot, g...  12.2 us
    ppermute x9, waiting for transfers between devices, in_plane(): lax.ppermute(pieces[m], 'seq', [(i, i ^ m) for i in range(peers)])  11.4 us
    ppermute x9, starting transfers between devices, in_plane(): lax.ppermute(pieces[m], 'seq', [(i, i ^ m) for i in range(peers)])  8.76 us
    pallas_call x2, Pallas kernels, unpack(): pl.pallas_call(functools.partial(unpack_kernel, groups=[group for group,...  4.72 us
    pallas_call x2, Pallas kernels, pack(): pl.pallas_call(functools.partial(pack_kernel, order=order, count=count, c...  4.5 us
    all_to_all x1, starting transfers between devices, plane_all_to_all(): lax.all_to_all(value, 'seq', 0, 0, axis_index_groups=planes, tiled=True)  3.99 us
  transfers between devices with their start and end apart: 19, of which 9 were waited for; matrix products, arithmetic and copies ran while one was open for 0% of the time, Pallas kernels for 21%

profile of v12, /device:TPU:1, one launch (start us, length us, event | category | flops | bytes accessed | tf_op | source)
XLA Modules:
  0.0 85.1 jit_solution(5836994114603518494)
XLA Ops:
  0.6 2.3 %shard_map.93 = (bf16[4,2,128,128]{3,2,1,0:T(8,128)(2,1)}, bf16[4,2,128,128]{3,2,1,0:T(8,128)(2,1)}, bf16[4,2,128,128]{3,2,1,0:T(8,128)(2,1)}, bf16[4,2,128,128]{3,2,1,0:T(8,128)(2,1)}) custom-call(s32[1]{0:T(128)} %bitcast.place, s32[4,4]{1,0:T(4,128)} %sections.13, bf16[128,16,128]{2,1,0:T(8,128)(2,1)} %refs_0_.2, bf16[128,16,128]{2,1,0:T(8,128)(2,1)} %refs_1_.2), custom_call_target="tpu_custom_call" | custom-call | bytes 2097152 | tf_op jit(solution)/shard_map/pallas_call | solution.py:124
  3.0 2.7 %collective-permute-start.1 = (bf16[4,2,128,128]{3,2,1,0:T(8,128)(2,1)}, bf16[4,2,128,128]{3,2,1,0:T(8,128)(2,1)S(1)}, u32[]{:S(2)}, u32[]{:S(2)}) collective-permute-start(bf16[4,2,128,128]{3,2,1,0:T(8,128)(2,1)} %get-tuple-element.60), channel_id=1, source_target_pairs={{0,2},{1,3},{2,0},{3,1},{4,6},{5,7},{6,4},{7,5},{8,10},{9,11},{10,... | collective-permute-start | bytes 786440 | tf_op jit(solution)/shard_map/ppermute | solution.py:651
  5.7 2.2 %shard_map.94 = bf16[4,4,2,128,128]{4,3,2,1,0:T(8,128)(2,1)} custom-call(s32[1]{0:T(128)} %bitcast.place, s32[4,4]{1,0:T(4,128)} %sections.13, bf16[128,16,128]{2,1,0:T(8,128)(2,1)} %refs_0_.3, bf16[128,16,128]{2,1,0:T(8,128)(2,1)} %refs_1_.3), custom_call_target="tpu_custom_call" | custom-call | bytes 2097152 | tf_op jit(solution)/shard_map/pallas_call | solution.py:124
  7.9 4.0 %all-to-all-start = ((bf16[4,4,2,128,128]{4,3,2,1,0:T(8,128)(2,1)}), bf16[4,4,2,128,128]{4,3,2,1,0:T(8,128)(2,1)S(1)}, u32[]{:S(2)}, u32[]{:S(2)}) async-start(bf16[4,4,2,128,128]{4,3,2,1,0:T(8,128)(2,1)} %shard_map.94), calls=%async_computation | async-start | bytes 2097152 | tf_op jit(solution)/shard_map/all_to_all | solution.py:678
  11.9 0.5 collective-permute-done.1.refs_2_
  12.5 6.1 %collective-permute-done.2.refs_3_ = bf16[4,2,128,128]{3,2,1,0:T(8,128)(2,1)S(1)} collective-permute-done((bf16[4,2,128,128]{3,2,1,0:T(8,128)(2,1)}, bf16[4,2,128,128]{3,2,1,0:T(8,128)(2,1)S(1)}, u32[]{:S(2)}, u32[]{:S(2)}) %collective-permute-start.2) | collective-permute-done | bytes 262176 | tf_op jit(solution)/shard_map/ppermute | solution.py:651
  18.7 1.8 %collective-permute-start.3 = (bf16[8,2,128,128]{3,2,1,0:T(8,128)(2,1)S(1)}, bf16[8,2,128,128]{3,2,1,0:T(8,128)(2,1)S(1)}, u32[]{:S(2)}, u32[]{:S(2)}) collective-permute-start(bf16[8,2,128,128]{3,2,1,0:T(8,128)(2,1)S(1)} %get-tuple-element.62), channel_id=1, source_target_pairs={{0,4},{1,5},{2,6},{3,7},{4,0},{5,1},{6,2},{7,3},{8,12},{9,13},{10,... | collective-permute-start | bytes 1572872 | tf_op jit(solution)/shard_map/ppermute | solution.py:400
  20.5 0.7 collective-permute-start.4
  21.2 0.8 shard_map.96
  22.0 3.8 %collective-permute-start.5 = (bf16[4,2,128,128]{3,2,1,0:T(8,128)(2,1)}, bf16[4,2,128,128]{3,2,1,0:T(8,128)(2,1)}, u32[]{:S(2)}, u32[]{:S(2)}) collective-permute-start(bf16[4,2,128,128]{3,2,1,0:T(8,128)(2,1)} %get-tuple-element.66), channel_id=1, source_target_pairs={{0,4},{1,5},{2,6},{3,7},{4,0},{5,1},{6,2},{7,3},{8,12},{9,13},{10,... | collective-permute-start | bytes 786440 | tf_op jit(solution)/shard_map/ppermute | solution.py:400
  25.8 7.0 %collective-permute-done.3.refs_5_ = bf16[8,2,128,128]{3,2,1,0:T(8,128)(2,1)S(1)} collective-permute-done((bf16[8,2,128,128]{3,2,1,0:T(8,128)(2,1)S(1)}, bf16[8,2,128,128]{3,2,1,0:T(8,128)(2,1)S(1)}, u32[]{:S(2)}, u32[]{:S(2)}) %collective-permute-start.3) | collective-permute-done | bytes 524320 | tf_op jit(solution)/shard_map/ppermute | solution.py:400
  32.8 2.6 %collective-permute-start.6 = (bf16[4,2,128,128]{3,2,1,0:T(8,128)(2,1)}, bf16[4,2,128,128]{3,2,1,0:T(8,128)(2,1)S(1)}, u32[]{:S(2)}, u32[]{:S(2)}) collective-permute-start(bf16[4,2,128,128]{3,2,1,0:T(8,128)(2,1)} %get-tuple-element.72), channel_id=1, source_target_pairs={{0,8},{1,9},{2,10},{3,11},{4,12},{5,13},{6,14},{7,15},{8,0},{9,1},... | collective-permute-start | bytes 786440 | tf_op jit(solution)/shard_map/ppermute | solution.py:400
  35.4 5.5 %shard_map.97 = (bf16[6,2,128,128]{3,2,1,0:T(8,128)(2,1)S(1)}, bf16[6,2,128,128]{3,2,1,0:T(8,128)(2,1)S(1)}, bf16[6,2,128,128]{3,2,1,0:T(8,128)(2,1)S(1)}, bf16[...) custom-call(s32[1]{0:T(128)} %bitcast.place, ...), custom_call_target="tpu_custom_call" | custom-call | flops 1207959552 | bytes 5242880 | tf_op jit(solution)/shard_map/pallas_call | solution.py:331
  41.0 2.2 %collective-permute-start.13 = (bf16[4,2,128,128]{3,2,1,0:T(8,128)(2,1)S(1)}, bf16[4,2,128,128]{3,2,1,0:T(8,128)(2,1)S(1)}, u32[]{:S(2)}, u32[]{:S(2)}) collective-permute-start(bf16[4,2,128,128]{3,2,1,0:T(8,128)(2,1)S(1)} %get-tuple-element.88), channel_id=1, source_target_pairs={{0,4},{1,5},{2,6},{3,7},{4,0},{5,1},{6,2},{7,3},{8,12},{9,13},{10,... | collective-permute-start | bytes 786440 | tf_op jit(solution)/shard_map/ppermute | solution.py:400
  43.1 0.7 collective-permute-start.14
  43.8 3.6 %shard_map.98 = (bf16[6,2,128,128]{3,2,1,0:T(8,128)(2,1)S(1)}, bf16[6,2,128,128]{3,2,1,0:T(8,128)(2,1)S(1)}, bf16[6,2,128,128]{3,2,1,0:T(8,128)(2,1)S(1)}, bf16[...) custom-call(s32[1]{0:T(128)} %bitcast.place, ...), custom_call_target="tpu_custom_call", output_to_operand_aliasing={{0}: (11, {}), {1}: (12, {}), {2}: (13, {}), {3}: (14, {})} | custom-call | flops 603979776 | bytes 2621440 | tf_op jit(solution)/shard_map/pallas_call | solution.py:331
  47.8 3.1 %shard_map.99 = (bf16[6,2,128,128]{3,2,1,0:T(8,128)(2,1)S(1)}, bf16[6,2,128,128]{3,2,1,0:T(8,128)(2,1)S(1)}, bf16[6,2,128,128]{3,2,1,0:T(8,128)(2,1)S(1)}, bf16[...) custom-call(s32[1]{0:T(128)} %bitcast.place, ...), custom_call_target="tpu_custom_call", output_to_operand_aliasing={{0}: (11, {}), {1}: (12, {}), {2}: (13, {}), {3}: (14, {}),... | custom-call | flops 603979776 | bytes 2621440 | tf_op jit(solution)/shard_map/pallas_call | solution.py:331
  51.0 0.6 collective-permute-done.13.refs_1_
  51.8 1.2 %collective-permute-start.15 = (bf16[6,2,128,128]{3,2,1,0:T(8,128)(2,1)S(1)}, bf16[6,2,128,128]{3,2,1,0:T(8,128)(2,1)S(1)}, u32[]{:S(2)}, u32[]{:S(2)}) collective-permute-start(bf16[6,2,128,128]{3,2,1,0:T(8,128)(2,1)S(1)} %get-tuple-element.95), channel_id=1, source_target_pairs={{0,1},{1,0},{2,3},{3,2},{4,5},{5,4},{6,7},{7,6},{8,9},{9,8},{10,11... | collective-permute-start | bytes 1179656 | tf_op jit(solution)/shard_map/ppermute | solution.py:651
  53.0 2.1 %collective-permute-start.8 = (bf16[8,2,128,128]{3,2,1,0:T(8,128)(2,1)S(1)}, bf16[8,2,128,128]{3,2,1,0:T(8,128)(2,1)S(1)}, u32[]{:S(2)}, u32[]{:S(2)}) collective-permute-start(bf16[8,2,128,128]{3,2,1,0:T(8,128)(2,1)S(1)} %get-tuple-element.81), channel_id=1, source_target_pairs={{0,4},{1,5},{2,6},{3,7},{4,0},{5,1},{6,2},{7,3},{8,12},{9,13},{10,... | collective-permute-start | bytes 1572872 | tf_op jit(solution)/shard_map/ppermute | solution.py:400
  55.1 2.0 %collective-permute-start.7 = (bf16[4,2,128,128]{3,2,1,0:T(8,128)(2,1)S(1)}, bf16[4,2,128,128]{3,2,1,0:T(8,128)(2,1)S(1)}, u32[]{:S(2)}, u32[]{:S(2)}) collective-permute-start(bf16[4,2,128,128]{3,2,1,0:T(8,128)(2,1)S(1)} %get-tuple-element.80), channel_id=1, source_target_pairs={{0,8},{1,9},{2,10},{3,11},{4,12},{5,13},{6,14},{7,15},{8,0},{9,1},... | collective-permute-start | bytes 786440 | tf_op jit(solution)/shard_map/ppermute | solution.py:400
  57.0 0.7 collective-permute-start.9
  57.7 1.5 %collective-permute-start.16 = (bf16[6,2,128,128]{3,2,1,0:T(8,128)(2,1)S(1)}, bf16[6,2,128,128]{3,2,1,0:T(8,128)(2,1)S(1)}, u32[]{:S(2)}, u32[]{:S(2)}) collective-permute-start(bf16[6,2,128,128]{3,2,1,0:T(8,128)(2,1)S(1)} %get-tuple-element.100), channel_id=1, source_target_pairs={{0,2},{1,3},{2,0},{3,1},{4,6},{5,7},{6,4},{7,5},{8,10},{9,11},{10,... | collective-permute-start | bytes 1179656 | tf_op jit(solution)/shard_map/ppermute | solution.py:651
  59.3 0.8 collective-permute-start.17
  60.1 12.0 %collective-permute-done.7.refs_2_ = bf16[4,2,128,128]{3,2,1,0:T(8,128)(2,1)S(1)} collective-permute-done((bf16[4,2,128,128]{3,2,1,0:T(8,128)(2,1)S(1)}, bf16[4,2,128,128]{3,2,1,0:T(8,128)(2,1)S(1)}, u32[]{:S(2)}, u32[]{:S(2)}) %collective-permute-start.7) | collective-permute-done | bytes 262176 | tf_op jit(solution)/shard_map/ppermute | solution.py:400
  72.0 0.9 %collective-permute-done.8.refs_3_ = bf16[8,2,128,128]{3,2,1,0:T(8,128)(2,1)S(1)} collective-permute-done((bf16[8,2,128,128]{3,2,1,0:T(8,128)(2,1)S(1)}, bf16[8,2,128,128]{3,2,1,0:T(8,128)(2,1)S(1)}, u32[]{:S(2)}, u32[]{:S(2)}) %collective-permute-start.8) | collective-permute-done | bytes 524320 | tf_op jit(solution)/shard_map/ppermute | solution.py:400
  73.2 0.7 collective-permute-start.10
  73.9 1.3 %collective-permute-start.11 = (bf16[2,2,128,128]{3,2,1,0:T(8,128)(2,1)S(1)}, bf16[2,2,128,128]{3,2,1,0:T(8,128)(2,1)S(1)}, u32[]{:S(2)}, u32[]{:S(2)}) collective-permute-start(bf16[2,2,128,128]{3,2,1,0:T(8,128)(2,1)S(1)} %get-tuple-element.85), channel_id=1, source_target_pairs={{0,2},{1,3},{2,0},{3,1},{4,6},{5,7},{6,4},{7,5},{8,10},{9,11},{10,... | collective-permute-start | bytes 393224 | tf_op jit(solution)/shard_map/ppermute | solution.py:651
  75.6 2.1 %collective-permute-done.17.refs_3_.refs_7_ = bf16[6,2,128,128]{3,2,1,0:T(8,128)(2,1)S(1)} collective-permute-done((bf16[6,2,128,128]{3,2,1,0:T(8,128)(2,1)S(1)}, bf16[6,2,128,128]{3,2,1,0:T(8,128)(2,1)S(1)}, u32[]{:S(2)}, u32[]{:S(2)}) %collective-permute-start.17) | collective-permute-done | bytes 393248 | tf_op jit(solution)/shard_map/ppermute | solution.py:651
  77.7 2.4 %shard_map.102 = (bf16[128,16,128]{2,1,0:T(8,128)(2,1)}, bf16[128,16,128]{2,1,0:T(8,128)(2,1)}) custom-call(s32[1]{0:T(128)} %bitcast.place, s32[4,4]{1,0:T(4,128)S(1)} %copy-done.1, bf16[6,2,128,128]{3,2,1,0:T(8,128)(2,1)S(1)} %get-tuple-element.98.refs_0_.refs_4_, bf16[6,2,128,128]{3,2,1,0:T(8,128)(2,1)S(1)} %collective-permute-done.15.refs_1_.refs_5_, ...), custom_call_target="tpu_custom_call" | custom-call | bytes 6291456 | tf_op jit(solution)/shard_map/pallas_call | solution.py:158
  80.1 2.6 %collective-permute-done.12.refs_3_ = bf16[2,2,128,128]{3,2,1,0:T(8,128)(2,1)S(1)} collective-permute-done((bf16[2,2,128,128]{3,2,1,0:T(8,128)(2,1)S(1)}, bf16[2,2,128,128]{3,2,1,0:T(8,128)(2,1)S(1)}, u32[]{:S(2)}, u32[]{:S(2)}) %collective-permute-start.12) | collective-permute-done | bytes 131104 | tf_op jit(solution)/shard_map/ppermute | solution.py:651
  82.7 2.4 %shard_map.103 = (bf16[128,16,128]{2,1,0:T(8,128)(2,1)}, bf16[128,16,128]{2,1,0:T(8,128)(2,1)}) custom-call(s32[1]{0:T(128)} %bitcast.place, s32[4,4]{1,0:T(4,128)S(1)} %copy-done.1, bf16[2,2,128,128]{3,2,1,0:T(8,128)(2,1)S(1)} %get-tuple-element.106.refs_0_, bf16[2,2,128,128]{3,2,1,0:T(8,128)(2,1)S(1)} %collective-permute-done.10.refs_1_, ...), custom_call_target="tpu_custom_call" | custom-call | bytes 4194304 | tf_op jit(solution)/shard_map/pallas_call | solution.py:158
  (23 shorter events, 1.5 us)
Async XLA Ops:
  2.9 9.0 %collective-permute-start = (bf16[4,2,128,128]{3,2,1,0:T(8,128)(2,1)}, bf16[4,2,128,128]{3,2,1,0:T(8,128)(2,1)S(1)}, u32[]{:S(2)}, u32[]{:S(2)}) collective-permute-start(bf16[4,2,128,128]{3,2,1,0:T(8,128)(2,1)} %get-tuple-element.59), channel_id=1, source_target_pairs={{0,1},{1,0},{2,3},{3,2},{4,5},{5,4},{6,7},{7,6},{8,9},{9,8},{10,11... | collective-permute-start | bytes 786440 | tf_op jit(solution)/shard_map/ppermute | solution.py:651
  3.0 9.5 %collective-permute-start.1 = (bf16[4,2,128,128]{3,2,1,0:T(8,128)(2,1)}, bf16[4,2,128,128]{3,2,1,0:T(8,128)(2,1)S(1)}, u32[]{:S(2)}, u32[]{:S(2)}) collective-permute-start(bf16[4,2,128,128]{3,2,1,0:T(8,128)(2,1)} %get-tuple-element.60), channel_id=1, source_target_pairs={{0,2},{1,3},{2,0},{3,1},{4,6},{5,7},{6,4},{7,5},{8,10},{9,11},{10,... | collective-permute-start | bytes 786440 | tf_op jit(solution)/shard_map/ppermute | solution.py:651
  5.6 12.9 %collective-permute-start.2 = (bf16[4,2,128,128]{3,2,1,0:T(8,128)(2,1)}, bf16[4,2,128,128]{3,2,1,0:T(8,128)(2,1)S(1)}, u32[]{:S(2)}, u32[]{:S(2)}) collective-permute-start(bf16[4,2,128,128]{3,2,1,0:T(8,128)(2,1)} %get-tuple-element.61), channel_id=1, source_target_pairs={{0,3},{1,2},{2,1},{3,0},{4,7},{5,6},{6,5},{7,4},{8,11},{9,10},{10,... | collective-permute-start | bytes 786440 | tf_op jit(solution)/shard_map/ppermute | solution.py:651
  7.9 10.6 %copy-start = (bf16[4,2,128,128]{3,2,1,0:T(8,128)(2,1)S(1)}, bf16[4,2,128,128]{3,2,1,0:T(8,128)(2,1)}, u32[]{:S(2)}) copy-start(bf16[4,2,128,128]{3,2,1,0:T(8,128)(2,1)} %get-tuple-element.58.refs_0_) | copy-start | bytes 786436
  7.9 27.5 %all-to-all-start = ((bf16[4,4,2,128,128]{4,3,2,1,0:T(8,128)(2,1)}), bf16[4,4,2,128,128]{4,3,2,1,0:T(8,128)(2,1)S(1)}, u32[]{:S(2)}, u32[]{:S(2)}) async-start(bf16[4,4,2,128,128]{4,3,2,1,0:T(8,128)(2,1)} %shard_map.94), calls=%async_computation | async-start | bytes 2097152 | tf_op jit(solution)/shard_map/all_to_all | solution.py:678
  18.7 14.2 %collective-permute-start.3 = (bf16[8,2,128,128]{3,2,1,0:T(8,128)(2,1)S(1)}, bf16[8,2,128,128]{3,2,1,0:T(8,128)(2,1)S(1)}, u32[]{:S(2)}, u32[]{:S(2)}) collective-permute-start(bf16[8,2,128,128]{3,2,1,0:T(8,128)(2,1)S(1)} %get-tuple-element.62), channel_id=1, source_target_pairs={{0,4},{1,5},{2,6},{3,7},{4,0},{5,1},{6,2},{7,3},{8,12},{9,13},{10,... | collective-permute-start | bytes 1572872 | tf_op jit(solution)/shard_map/ppermute | solution.py:400
  20.5 14.9 %collective-permute-start.4 = (bf16[8,2,128,128]{3,2,1,0:T(8,128)(2,1)S(1)}, bf16[8,2,128,128]{3,2,1,0:T(8,128)(2,1)S(1)}, u32[]{:S(2)}, u32[]{:S(2)}) collective-permute-start(bf16[8,2,128,128]{3,2,1,0:T(8,128)(2,1)S(1)} %get-tuple-element.65), channel_id=1, source_target_pairs={{4,8},{5,9},{6,10},{7,11},{8,4},{9,5},{10,6},{11,7},{20,24},{21,25... | collective-permute-start | bytes 1572872 | tf_op jit(solution)/shard_map/ppermute | solution.py:672
  22.0 13.4 %copy-start.1 = (s32[4,4]{1,0:T(4,128)S(1)}, s32[4,4]{1,0:T(4,128)}, u32[]{:S(2)}) copy-start(s32[4,4]{1,0:T(4,128)} %sections.13) | copy-start | bytes 196
  22.0 13.4 %copy-start.2 = (s32[16]{0:T(128)S(1)}, s32[16]{0:T(128)}, u32[]{:S(2)}) copy-start(s32[16]{0:T(128)} %widths.5) | copy-start | bytes 196
  22.0 21.8 %collective-permute-start.5 = (bf16[4,2,128,128]{3,2,1,0:T(8,128)(2,1)}, bf16[4,2,128,128]{3,2,1,0:T(8,128)(2,1)}, u32[]{:S(2)}, u32[]{:S(2)}) collective-permute-start(bf16[4,2,128,128]{3,2,1,0:T(8,128)(2,1)} %get-tuple-element.66), channel_id=1, source_target_pairs={{0,4},{1,5},{2,6},{3,7},{4,0},{5,1},{6,2},{7,3},{8,12},{9,13},{10,... | collective-permute-start | bytes 786440 | tf_op jit(solution)/shard_map/ppermute | solution.py:400
  32.8 15.0 %collective-permute-start.6 = (bf16[4,2,128,128]{3,2,1,0:T(8,128)(2,1)}, bf16[4,2,128,128]{3,2,1,0:T(8,128)(2,1)S(1)}, u32[]{:S(2)}, u32[]{:S(2)}) collective-permute-start(bf16[4,2,128,128]{3,2,1,0:T(8,128)(2,1)} %get-tuple-element.72), channel_id=1, source_target_pairs={{0,8},{1,9},{2,10},{3,11},{4,12},{5,13},{6,14},{7,15},{8,0},{9,1},... | collective-permute-start | bytes 786440 | tf_op jit(solution)/shard_map/ppermute | solution.py:400
  41.0 10.6 %collective-permute-start.13 = (bf16[4,2,128,128]{3,2,1,0:T(8,128)(2,1)S(1)}, bf16[4,2,128,128]{3,2,1,0:T(8,128)(2,1)S(1)}, u32[]{:S(2)}, u32[]{:S(2)}) collective-permute-start(bf16[4,2,128,128]{3,2,1,0:T(8,128)(2,1)S(1)} %get-tuple-element.88), channel_id=1, source_target_pairs={{0,4},{1,5},{2,6},{3,7},{4,0},{5,1},{6,2},{7,3},{8,12},{9,13},{10,... | collective-permute-start | bytes 786440 | tf_op jit(solution)/shard_map/ppermute | solution.py:400
  43.1 8.5 %collective-permute-start.14 = (bf16[4,2,128,128]{3,2,1,0:T(8,128)(2,1)S(1)}, bf16[4,2,128,128]{3,2,1,0:T(8,128)(2,1)S(1)}, u32[]{:S(2)}, u32[]{:S(2)}) collective-permute-start(bf16[4,2,128,128]{3,2,1,0:T(8,128)(2,1)S(1)} %get-tuple-element.89), channel_id=1, source_target_pairs={{4,8},{5,9},{6,10},{7,11},{8,4},{9,5},{10,6},{11,7},{20,24},{21,25... | collective-permute-start | bytes 786440 | tf_op jit(solution)/shard_map/ppermute | solution.py:672
  51.8 5.9 %collective-permute-start.15 = (bf16[6,2,128,128]{3,2,1,0:T(8,128)(2,1)S(1)}, bf16[6,2,128,128]{3,2,1,0:T(8,128)(2,1)S(1)}, u32[]{:S(2)}, u32[]{:S(2)}) collective-permute-start(bf16[6,2,128,128]{3,2,1,0:T(8,128)(2,1)S(1)} %get-tuple-element.95), channel_id=1, source_target_pairs={{0,1},{1,0},{2,3},{3,2},{4,5},{5,4},{6,7},{7,6},{8,9},{9,8},{10,11... | collective-permute-start | bytes 1179656 | tf_op jit(solution)/shard_map/ppermute | solution.py:651
  53.0 19.9 %collective-permute-start.8 = (bf16[8,2,128,128]{3,2,1,0:T(8,128)(2,1)S(1)}, bf16[8,2,128,128]{3,2,1,0:T(8,128)(2,1)S(1)}, u32[]{:S(2)}, u32[]{:S(2)}) collective-permute-start(bf16[8,2,128,128]{3,2,1,0:T(8,128)(2,1)S(1)} %get-tuple-element.81), channel_id=1, source_target_pairs={{0,4},{1,5},{2,6},{3,7},{4,0},{5,1},{6,2},{7,3},{8,12},{9,13},{10,... | collective-permute-start | bytes 1572872 | tf_op jit(solution)/shard_map/ppermute | solution.py:400
  55.1 17.0 %collective-permute-start.7 = (bf16[4,2,128,128]{3,2,1,0:T(8,128)(2,1)S(1)}, bf16[4,2,128,128]{3,2,1,0:T(8,128)(2,1)S(1)}, u32[]{:S(2)}, u32[]{:S(2)}) collective-permute-start(bf16[4,2,128,128]{3,2,1,0:T(8,128)(2,1)S(1)} %get-tuple-element.80), channel_id=1, source_target_pairs={{0,8},{1,9},{2,10},{3,11},{4,12},{5,13},{6,14},{7,15},{8,0},{9,1},... | collective-permute-start | bytes 786440 | tf_op jit(solution)/shard_map/ppermute | solution.py:400
  57.0 15.0 %collective-permute-start.9 = (bf16[4,2,128,128]{3,2,1,0:T(8,128)(2,1)S(1)}, bf16[4,2,128,128]{3,2,1,0:T(8,128)(2,1)S(1)}, u32[]{:S(2)}, u32[]{:S(2)}) collective-permute-start(bf16[4,2,128,128]{3,2,1,0:T(8,128)(2,1)S(1)} %get-tuple-element.82), channel_id=1, source_target_pairs={{4,8},{5,9},{6,10},{7,11},{8,4},{9,5},{10,6},{11,7},{20,24},{21,25... | collective-permute-start | bytes 786440 | tf_op jit(solution)/shard_map/ppermute | solution.py:672
  57.7 17.9 %collective-permute-start.16 = (bf16[6,2,128,128]{3,2,1,0:T(8,128)(2,1)S(1)}, bf16[6,2,128,128]{3,2,1,0:T(8,128)(2,1)S(1)}, u32[]{:S(2)}, u32[]{:S(2)}) collective-permute-start(bf16[6,2,128,128]{3,2,1,0:T(8,128)(2,1)S(1)} %get-tuple-element.100), channel_id=1, source_target_pairs={{0,2},{1,3},{2,0},{3,1},{4,6},{5,7},{6,4},{7,5},{8,10},{9,11},{10,... | collective-permute-start | bytes 1179656 | tf_op jit(solution)/shard_map/ppermute | solution.py:651
  59.3 18.5 %collective-permute-start.17 = (bf16[6,2,128,128]{3,2,1,0:T(8,128)(2,1)S(1)}, bf16[6,2,128,128]{3,2,1,0:T(8,128)(2,1)S(1)}, u32[]{:S(2)}, u32[]{:S(2)}) collective-permute-start(bf16[6,2,128,128]{3,2,1,0:T(8,128)(2,1)S(1)} %get-tuple-element.101), channel_id=1, source_target_pairs={{0,3},{1,2},{2,1},{3,0},{4,7},{5,6},{6,5},{7,4},{8,11},{9,10},{10,... | collective-permute-start | bytes 1179656 | tf_op jit(solution)/shard_map/ppermute | solution.py:651
  73.2 6.9 %collective-permute-start.10 = (bf16[2,2,128,128]{3,2,1,0:T(8,128)(2,1)S(1)}, bf16[2,2,128,128]{3,2,1,0:T(8,128)(2,1)S(1)}, u32[]{:S(2)}, u32[]{:S(2)}) collective-permute-start(bf16[2,2,128,128]{3,2,1,0:T(8,128)(2,1)S(1)} %get-tuple-element.84), channel_id=1, source_target_pairs={{0,1},{1,0},{2,3},{3,2},{4,5},{5,4},{6,7},{7,6},{8,9},{9,8},{10,11... | collective-permute-start | bytes 393224 | tf_op jit(solution)/shard_map/ppermute | solution.py:651
  73.9 6.2 %collective-permute-start.11 = (bf16[2,2,128,128]{3,2,1,0:T(8,128)(2,1)S(1)}, bf16[2,2,128,128]{3,2,1,0:T(8,128)(2,1)S(1)}, u32[]{:S(2)}, u32[]{:S(2)}) collective-permute-start(bf16[2,2,128,128]{3,2,1,0:T(8,128)(2,1)S(1)} %get-tuple-element.85), channel_id=1, source_target_pairs={{0,2},{1,3},{2,0},{3,1},{4,6},{5,7},{6,4},{7,5},{8,10},{9,11},{10,... | collective-permute-start | bytes 393224 | tf_op jit(solution)/shard_map/ppermute | solution.py:651
  75.2 7.4 %collective-permute-start.12 = (bf16[2,2,128,128]{3,2,1,0:T(8,128)(2,1)S(1)}, bf16[2,2,128,128]{3,2,1,0:T(8,128)(2,1)S(1)}, u32[]{:S(2)}, u32[]{:S(2)}) collective-permute-start(bf16[2,2,128,128]{3,2,1,0:T(8,128)(2,1)S(1)} %get-tuple-element.86), channel_id=1, source_target_pairs={{0,3},{1,2},{2,1},{3,0},{4,7},{5,6},{6,5},{7,4},{8,11},{9,10},{10,... | collective-permute-start | bytes 393224 | tf_op jit(solution)/shard_map/ppermute | solution.py:651

commit v13 on v12

--- a/solution.py
+++ b/solution.py
@@ -133,14 +133,14 @@
     )(place, sections, *arrays)
 
 
-def unpack_kernel(place, sections, *refs, groups, count):
+def unpack_kernel(place, sections, *refs, groups, bases, count):
     pieces, outs, held = refs[: len(groups) * PLANE], refs[len(groups) * PLANE : -1], refs[-1]
     for number, group in enumerate(groups):
         for m in range(PLANE):
             for k, s in enumerate(group):
                 head = sections[s, seat(place) ^ m]
                 for i in range(count):
-                    held[i, head] = pieces[number * PLANE + m][k, i]
+                    held[i, head] = pieces[number * PLANE + m][bases[number] + k, i]
     for i in range(count):
         outs[i][...] = jnp.transpose(held[i], (1, 0, 2))
 
@@ -149,19 +149,16 @@
     flat = [piece for _, pieces, _ in parts for piece in pieces]
     count, tokens, width = flat[0].shape[1:]
     heads = sections.size
-    chunk = tokens // 4
-    specs = [
-        pl.BlockSpec((len(group), count, chunk, width), lambda i, run=run: (run, 0, i, 0))
-        for group, _, run in parts
-        for _ in range(PLANE)
-    ]
     return pl.pallas_call(
-        functools.partial(unpack_kernel, groups=[group for group, _, _ in parts], count=count),
-        grid=(tokens // chunk,),
-        in_specs=[SMEM, SMEM] + specs,
-        out_specs=[pl.BlockSpec((chunk, heads, width), lambda i: (i, 0, 0))] * count,
+        functools.partial(
+            unpack_kernel,
+            groups=[group for group, _, _ in parts],
+            bases=[run * len(group) for group, _, run in parts],
+            count=count,
+        ),
+        in_specs=[SMEM, SMEM] + [VMEM] * len(flat),
         out_shape=[jax.ShapeDtypeStruct((tokens, heads, width), jnp.bfloat16)] * count,
-        scratch_shapes=[pltpu.VMEM((count, heads, chunk, width), jnp.bfloat16)],
+        scratch_shapes=[pltpu.VMEM((count, heads, tokens, width), jnp.bfloat16)],
         compiler_params=LIMIT,
         cost_estimate=moved_cost(flat),
     )(place, sections, *flat)

time: 86.2 us -> 85.7 us (level)
  Pallas kernels: 22.8 us -> 21.8 us
    pallas_call x2, Pallas kernels: 4.72 us -> 3.65 us  [unpack(): pl.pallas_call(functools.partial(unpack_kernel, groups=[group for group,...]
where the time goes in v13:
time: 85.7 us; the launch traced here: 84.5 us
  waiting for transfers between devices  32.8 us (38%)
  starting transfers between devices  29.2 us (34%)
  Pallas kernels  21.8 us (25%)
    ppermute x6, waiting for transfers between devices, partner(): lax.ppermute(value, axis, [(i, i ^ 1 << apart) for i in range(lax.axis_si...  20.9 us
    ppermute x6, starting transfers between devices, partner(): lax.ppermute(value, axis, [(i, i ^ 1 << apart) for i in range(lax.axis_si...  14.4 us
    pallas_call x3, Pallas kernels, attend(): pl.pallas_call(functools.partial(attend_kernel, first=first, slot=slot, g...  12.2 us
    ppermute x9, waiting for transfers between devices, in_plane(): lax.ppermute(pieces[m], 'seq', [(i, i ^ m) for i in range(peers)])  11.9 us
    ppermute x9, starting transfers between devices, in_plane(): lax.ppermute(pieces[m], 'seq', [(i, i ^ m) for i in range(peers)])  8.76 us
    pallas_call x2, Pallas kernels, pack(): pl.pallas_call(functools.partial(pack_kernel, order=order, count=count, c...  4.5 us
    all_to_all x1, starting transfers between devices, plane_all_to_all(): lax.all_to_all(value, 'seq', 0, 0, axis_index_groups=planes, tiled=True)  3.99 us
    pallas_call x2, Pallas kernels, unpack(): pl.pallas_call(functools.partial(unpack_kernel, groups=[group for group,...  3.65 us
  transfers between devices with their start and end apart: 19, of which 9 were waited for; matrix products, arithmetic and copies ran while one was open for 0% of the time, Pallas kernels for 21%

profile of v13, /device:TPU:1, one launch (start us, length us, event | category | flops | bytes accessed | tf_op | source)
XLA Modules:
  0.0 84.5 jit_solution(8651132834953134798)
XLA Ops:
  0.6 2.3 %shard_map.93 = (bf16[4,2,128,128]{3,2,1,0:T(8,128)(2,1)}, bf16[4,2,128,128]{3,2,1,0:T(8,128)(2,1)}, bf16[4,2,128,128]{3,2,1,0:T(8,128)(2,1)}, bf16[4,2,128,128]{3,2,1,0:T(8,128)(2,1)}) custom-call(s32[1]{0:T(128)} %bitcast.place, s32[4,4]{1,0:T(4,128)} %sections.13, bf16[128,16,128]{2,1,0:T(8,128)(2,1)} %refs_0_.2, bf16[128,16,128]{2,1,0:T(8,128)(2,1)} %refs_1_.2), custom_call_target="tpu_custom_call" | custom-call | bytes 2097152 | tf_op jit(solution)/shard_map/pallas_call | solution.py:124
  3.0 2.7 %collective-permute-start.1 = (bf16[4,2,128,128]{3,2,1,0:T(8,128)(2,1)}, bf16[4,2,128,128]{3,2,1,0:T(8,128)(2,1)S(1)}, u32[]{:S(2)}, u32[]{:S(2)}) collective-permute-start(bf16[4,2,128,128]{3,2,1,0:T(8,128)(2,1)} %get-tuple-element.60), channel_id=1, source_target_pairs={{0,2},{1,3},{2,0},{3,1},{4,6},{5,7},{6,4},{7,5},{8,10},{9,11},{10,... | collective-permute-start | bytes 786440 | tf_op jit(solution)/shard_map/ppermute | solution.py:648
  5.7 2.2 %shard_map.94 = bf16[4,4,2,128,128]{4,3,2,1,0:T(8,128)(2,1)} custom-call(s32[1]{0:T(128)} %bitcast.place, s32[4,4]{1,0:T(4,128)} %sections.13, bf16[128,16,128]{2,1,0:T(8,128)(2,1)} %refs_0_.3, bf16[128,16,128]{2,1,0:T(8,128)(2,1)} %refs_1_.3), custom_call_target="tpu_custom_call" | custom-call | bytes 2097152 | tf_op jit(solution)/shard_map/pallas_call | solution.py:124
  7.9 4.0 %all-to-all-start = ((bf16[4,4,2,128,128]{4,3,2,1,0:T(8,128)(2,1)}), bf16[4,4,2,128,128]{4,3,2,1,0:T(8,128)(2,1)S(1)}, u32[]{:S(2)}, u32[]{:S(2)}) async-start(bf16[4,4,2,128,128]{4,3,2,1,0:T(8,128)(2,1)} %shard_map.94), calls=%async_computation | async-start | bytes 2097152 | tf_op jit(solution)/shard_map/all_to_all | solution.py:675
  11.9 0.5 collective-permute-done.1.refs_2_
  12.5 6.1 %collective-permute-done.2.refs_3_ = bf16[4,2,128,128]{3,2,1,0:T(8,128)(2,1)S(1)} collective-permute-done((bf16[4,2,128,128]{3,2,1,0:T(8,128)(2,1)}, bf16[4,2,128,128]{3,2,1,0:T(8,128)(2,1)S(1)}, u32[]{:S(2)}, u32[]{:S(2)}) %collective-permute-start.2) | collective-permute-done | bytes 262176 | tf_op jit(solution)/shard_map/ppermute | solution.py:648
  18.7 1.8 %collective-permute-start.3 = (bf16[8,2,128,128]{3,2,1,0:T(8,128)(2,1)S(1)}, bf16[8,2,128,128]{3,2,1,0:T(8,128)(2,1)S(1)}, u32[]{:S(2)}, u32[]{:S(2)}) collective-permute-start(bf16[8,2,128,128]{3,2,1,0:T(8,128)(2,1)S(1)} %get-tuple-element.62), channel_id=1, source_target_pairs={{0,4},{1,5},{2,6},{3,7},{4,0},{5,1},{6,2},{7,3},{8,12},{9,13},{10,... | collective-permute-start | bytes 1572872 | tf_op jit(solution)/shard_map/ppermute | solution.py:397
  20.5 0.7 collective-permute-start.4
  21.2 0.8 shard_map.96
  22.0 3.8 %collective-permute-start.5 = (bf16[4,2,128,128]{3,2,1,0:T(8,128)(2,1)}, bf16[4,2,128,128]{3,2,1,0:T(8,128)(2,1)}, u32[]{:S(2)}, u32[]{:S(2)}) collective-permute-start(bf16[4,2,128,128]{3,2,1,0:T(8,128)(2,1)} %get-tuple-element.66), channel_id=1, source_target_pairs={{0,4},{1,5},{2,6},{3,7},{4,0},{5,1},{6,2},{7,3},{8,12},{9,13},{10,... | collective-permute-start | bytes 786440 | tf_op jit(solution)/shard_map/ppermute | solution.py:397
  25.8 7.0 %collective-permute-done.3.refs_5_ = bf16[8,2,128,128]{3,2,1,0:T(8,128)(2,1)S(1)} collective-permute-done((bf16[8,2,128,128]{3,2,1,0:T(8,128)(2,1)S(1)}, bf16[8,2,128,128]{3,2,1,0:T(8,128)(2,1)S(1)}, u32[]{:S(2)}, u32[]{:S(2)}) %collective-permute-start.3) | collective-permute-done | bytes 524320 | tf_op jit(solution)/shard_map/ppermute | solution.py:397
  32.8 2.6 %collective-permute-start.6 = (bf16[4,2,128,128]{3,2,1,0:T(8,128)(2,1)}, bf16[4,2,128,128]{3,2,1,0:T(8,128)(2,1)S(1)}, u32[]{:S(2)}, u32[]{:S(2)}) collective-permute-start(bf16[4,2,128,128]{3,2,1,0:T(8,128)(2,1)} %get-tuple-element.72), channel_id=1, source_target_pairs={{0,8},{1,9},{2,10},{3,11},{4,12},{5,13},{6,14},{7,15},{8,0},{9,1},... | collective-permute-start | bytes 786440 | tf_op jit(solution)/shard_map/ppermute | solution.py:397
  35.4 5.5 %shard_map.97 = (bf16[6,2,128,128]{3,2,1,0:T(8,128)(2,1)S(1)}, bf16[6,2,128,128]{3,2,1,0:T(8,128)(2,1)S(1)}, bf16[6,2,128,128]{3,2,1,0:T(8,128)(2,1)S(1)}, bf16[...) custom-call(s32[1]{0:T(128)} %bitcast.place, ...), custom_call_target="tpu_custom_call" | custom-call | flops 1207959552 | bytes 5242880 | tf_op jit(solution)/shard_map/pallas_call | solution.py:328
  41.0 2.2 %collective-permute-start.13 = (bf16[4,2,128,128]{3,2,1,0:T(8,128)(2,1)S(1)}, bf16[4,2,128,128]{3,2,1,0:T(8,128)(2,1)S(1)}, u32[]{:S(2)}, u32[]{:S(2)}) collective-permute-start(bf16[4,2,128,128]{3,2,1,0:T(8,128)(2,1)S(1)} %get-tuple-element.88), channel_id=1, source_target_pairs={{0,4},{1,5},{2,6},{3,7},{4,0},{5,1},{6,2},{7,3},{8,12},{9,13},{10,... | collective-permute-start | bytes 786440 | tf_op jit(solution)/shard_map/ppermute | solution.py:397
  43.1 0.7 collective-permute-start.14
  43.8 3.6 %shard_map.98 = (bf16[6,2,128,128]{3,2,1,0:T(8,128)(2,1)S(1)}, bf16[6,2,128,128]{3,2,1,0:T(8,128)(2,1)S(1)}, bf16[6,2,128,128]{3,2,1,0:T(8,128)(2,1)S(1)}, bf16[...) custom-call(s32[1]{0:T(128)} %bitcast.place, ...), custom_call_target="tpu_custom_call", output_to_operand_aliasing={{0}: (11, {}), {1}: (12, {}), {2}: (13, {}), {3}: (14, {})} | custom-call | flops 603979776 | bytes 2621440 | tf_op jit(solution)/shard_map/pallas_call | solution.py:328
  47.8 3.1 %shard_map.99 = (bf16[6,2,128,128]{3,2,1,0:T(8,128)(2,1)S(1)}, bf16[6,2,128,128]{3,2,1,0:T(8,128)(2,1)S(1)}, bf16[6,2,128,128]{3,2,1,0:T(8,128)(2,1)S(1)}, bf16[...) custom-call(s32[1]{0:T(128)} %bitcast.place, ...), custom_call_target="tpu_custom_call", output_to_operand_aliasing={{0}: (11, {}), {1}: (12, {}), {2}: (13, {}), {3}: (14, {}),... | custom-call | flops 603979776 | bytes 2621440 | tf_op jit(solution)/shard_map/pallas_call | solution.py:328
  51.0 0.6 collective-permute-done.13.refs_1_
  51.8 1.2 %collective-permute-start.15 = (bf16[6,2,128,128]{3,2,1,0:T(8,128)(2,1)S(1)}, bf16[6,2,128,128]{3,2,1,0:T(8,128)(2,1)S(1)}, u32[]{:S(2)}, u32[]{:S(2)}) collective-permute-start(bf16[6,2,128,128]{3,2,1,0:T(8,128)(2,1)S(1)} %get-tuple-element.95), channel_id=1, source_target_pairs={{0,1},{1,0},{2,3},{3,2},{4,5},{5,4},{6,7},{7,6},{8,9},{9,8},{10,11... | collective-permute-start | bytes 1179656 | tf_op jit(solution)/shard_map/ppermute | solution.py:648
  53.0 2.1 %collective-permute-start.8 = (bf16[8,2,128,128]{3,2,1,0:T(8,128)(2,1)S(1)}, bf16[8,2,128,128]{3,2,1,0:T(8,128)(2,1)S(1)}, u32[]{:S(2)}, u32[]{:S(2)}) collective-permute-start(bf16[8,2,128,128]{3,2,1,0:T(8,128)(2,1)S(1)} %get-tuple-element.81), channel_id=1, source_target_pairs={{0,4},{1,5},{2,6},{3,7},{4,0},{5,1},{6,2},{7,3},{8,12},{9,13},{10,... | collective-permute-start | bytes 1572872 | tf_op jit(solution)/shard_map/ppermute | solution.py:397
  55.1 2.0 %collective-permute-start.7 = (bf16[4,2,128,128]{3,2,1,0:T(8,128)(2,1)S(1)}, bf16[4,2,128,128]{3,2,1,0:T(8,128)(2,1)S(1)}, u32[]{:S(2)}, u32[]{:S(2)}) collective-permute-start(bf16[4,2,128,128]{3,2,1,0:T(8,128)(2,1)S(1)} %get-tuple-element.80), channel_id=1, source_target_pairs={{0,8},{1,9},{2,10},{3,11},{4,12},{5,13},{6,14},{7,15},{8,0},{9,1},... | collective-permute-start | bytes 786440 | tf_op jit(solution)/shard_map/ppermute | solution.py:397
  57.0 0.7 collective-permute-start.9
  57.7 1.5 %collective-permute-start.16 = (bf16[6,2,128,128]{3,2,1,0:T(8,128)(2,1)S(1)}, bf16[6,2,128,128]{3,2,1,0:T(8,128)(2,1)S(1)}, u32[]{:S(2)}, u32[]{:S(2)}) collective-permute-start(bf16[6,2,128,128]{3,2,1,0:T(8,128)(2,1)S(1)} %get-tuple-element.100), channel_id=1, source_target_pairs={{0,2},{1,3},{2,0},{3,1},{4,6},{5,7},{6,4},{7,5},{8,10},{9,11},{10,... | collective-permute-start | bytes 1179656 | tf_op jit(solution)/shard_map/ppermute | solution.py:648
  59.3 0.8 collective-permute-start.17
  60.1 12.0 %collective-permute-done.7.refs_2_ = bf16[4,2,128,128]{3,2,1,0:T(8,128)(2,1)S(1)} collective-permute-done((bf16[4,2,128,128]{3,2,1,0:T(8,128)(2,1)S(1)}, bf16[4,2,128,128]{3,2,1,0:T(8,128)(2,1)S(1)}, u32[]{:S(2)}, u32[]{:S(2)}) %collective-permute-start.7) | collective-permute-done | bytes 262176 | tf_op jit(solution)/shard_map/ppermute | solution.py:397
  72.0 0.9 %collective-permute-done.8.refs_3_ = bf16[8,2,128,128]{3,2,1,0:T(8,128)(2,1)S(1)} collective-permute-done((bf16[8,2,128,128]{3,2,1,0:T(8,128)(2,1)S(1)}, bf16[8,2,128,128]{3,2,1,0:T(8,128)(2,1)S(1)}, u32[]{:S(2)}, u32[]{:S(2)}) %collective-permute-start.8) | collective-permute-done | bytes 524320 | tf_op jit(solution)/shard_map/ppermute | solution.py:397
  73.2 0.7 collective-permute-start.10
  73.9 1.3 %collective-permute-start.11 = (bf16[2,2,128,128]{3,2,1,0:T(8,128)(2,1)S(1)}, bf16[2,2,128,128]{3,2,1,0:T(8,128)(2,1)S(1)}, u32[]{:S(2)}, u32[]{:S(2)}) collective-permute-start(bf16[2,2,128,128]{3,2,1,0:T(8,128)(2,1)S(1)} %get-tuple-element.85), channel_id=1, source_target_pairs={{0,2},{1,3},{2,0},{3,1},{4,6},{5,7},{6,4},{7,5},{8,10},{9,11},{10,... | collective-permute-start | bytes 393224 | tf_op jit(solution)/shard_map/ppermute | solution.py:648
  75.6 2.1 %collective-permute-done.17.refs_3_.refs_7_ = bf16[6,2,128,128]{3,2,1,0:T(8,128)(2,1)S(1)} collective-permute-done((bf16[6,2,128,128]{3,2,1,0:T(8,128)(2,1)S(1)}, bf16[6,2,128,128]{3,2,1,0:T(8,128)(2,1)S(1)}, u32[]{:S(2)}, u32[]{:S(2)}) %collective-permute-start.17) | collective-permute-done | bytes 393248 | tf_op jit(solution)/shard_map/ppermute | solution.py:648
  77.7 1.8 %shard_map.102 = (bf16[128,16,128]{2,1,0:T(8,128)(2,1)}, bf16[128,16,128]{2,1,0:T(8,128)(2,1)}) custom-call(s32[1]{0:T(128)} %bitcast.place, s32[4,4]{1,0:T(4,128)S(1)} %copy-done.1, bf16[6,2,128,128]{3,2,1,0:T(8,128)(2,1)S(1)} %get-tuple-element.98.refs_0_.refs_4_, bf16[6,2,128,128]{3,2,1,0:T(8,128)(2,1)S(1)} %collective-permute-done.15.refs_1_.refs_5_, ...), custom_call_target="tpu_custom_call" | custom-call | bytes 6291456 | tf_op jit(solution)/shard_map/pallas_call | solution.py:152
  79.6 3.1 %collective-permute-done.12.refs_3_ = bf16[2,2,128,128]{3,2,1,0:T(8,128)(2,1)S(1)} collective-permute-done((bf16[2,2,128,128]{3,2,1,0:T(8,128)(2,1)S(1)}, bf16[2,2,128,128]{3,2,1,0:T(8,128)(2,1)S(1)}, u32[]{:S(2)}, u32[]{:S(2)}) %collective-permute-start.12) | collective-permute-done | bytes 131104 | tf_op jit(solution)/shard_map/ppermute | solution.py:648
  82.7 1.8 %shard_map.103 = (bf16[128,16,128]{2,1,0:T(8,128)(2,1)}, bf16[128,16,128]{2,1,0:T(8,128)(2,1)}) custom-call(s32[1]{0:T(128)} %bitcast.place, s32[4,4]{1,0:T(4,128)S(1)} %copy-done.1, bf16[2,2,128,128]{3,2,1,0:T(8,128)(2,1)S(1)} %get-tuple-element.106.refs_0_, bf16[2,2,128,128]{3,2,1,0:T(8,128)(2,1)S(1)} %collective-permute-done.10.refs_1_, ...), custom_call_target="tpu_custom_call" | custom-call | bytes 4194304 | tf_op jit(solution)/shard_map/pallas_call | solution.py:152
  (23 shorter events, 1.5 us)
Async XLA Ops:
  2.9 9.0 %collective-permute-start = (bf16[4,2,128,128]{3,2,1,0:T(8,128)(2,1)}, bf16[4,2,128,128]{3,2,1,0:T(8,128)(2,1)S(1)}, u32[]{:S(2)}, u32[]{:S(2)}) collective-permute-start(bf16[4,2,128,128]{3,2,1,0:T(8,128)(2,1)} %get-tuple-element.59), channel_id=1, source_target_pairs={{0,1},{1,0},{2,3},{3,2},{4,5},{5,4},{6,7},{7,6},{8,9},{9,8},{10,11... | collective-permute-start | bytes 786440 | tf_op jit(solution)/shard_map/ppermute | solution.py:648
  3.0 9.5 %collective-permute-start.1 = (bf16[4,2,128,128]{3,2,1,0:T(8,128)(2,1)}, bf16[4,2,128,128]{3,2,1,0:T(8,128)(2,1)S(1)}, u32[]{:S(2)}, u32[]{:S(2)}) collective-permute-start(bf16[4,2,128,128]{3,2,1,0:T(8,128)(2,1)} %get-tuple-element.60), channel_id=1, source_target_pairs={{0,2},{1,3},{2,0},{3,1},{4,6},{5,7},{6,4},{7,5},{8,10},{9,11},{10,... | collective-permute-start | bytes 786440 | tf_op jit(solution)/shard_map/ppermute | solution.py:648
  5.6 12.9 %collective-permute-start.2 = (bf16[4,2,128,128]{3,2,1,0:T(8,128)(2,1)}, bf16[4,2,128,128]{3,2,1,0:T(8,128)(2,1)S(1)}, u32[]{:S(2)}, u32[]{:S(2)}) collective-permute-start(bf16[4,2,128,128]{3,2,1,0:T(8,128)(2,1)} %get-tuple-element.61), channel_id=1, source_target_pairs={{0,3},{1,2},{2,1},{3,0},{4,7},{5,6},{6,5},{7,4},{8,11},{9,10},{10,... | collective-permute-start | bytes 786440 | tf_op jit(solution)/shard_map/ppermute | solution.py:648
  7.9 10.6 %copy-start = (bf16[4,2,128,128]{3,2,1,0:T(8,128)(2,1)S(1)}, bf16[4,2,128,128]{3,2,1,0:T(8,128)(2,1)}, u32[]{:S(2)}) copy-start(bf16[4,2,128,128]{3,2,1,0:T(8,128)(2,1)} %get-tuple-element.58.refs_0_) | copy-start | bytes 786436
  7.9 27.5 %all-to-all-start = ((bf16[4,4,2,128,128]{4,3,2,1,0:T(8,128)(2,1)}), bf16[4,4,2,128,128]{4,3,2,1,0:T(8,128)(2,1)S(1)}, u32[]{:S(2)}, u32[]{:S(2)}) async-start(bf16[4,4,2,128,128]{4,3,2,1,0:T(8,128)(2,1)} %shard_map.94), calls=%async_computation | async-start | bytes 2097152 | tf_op jit(solution)/shard_map/all_to_all | solution.py:675
  18.7 14.2 %collective-permute-start.3 = (bf16[8,2,128,128]{3,2,1,0:T(8,128)(2,1)S(1)}, bf16[8,2,128,128]{3,2,1,0:T(8,128)(2,1)S(1)}, u32[]{:S(2)}, u32[]{:S(2)}) collective-permute-start(bf16[8,2,128,128]{3,2,1,0:T(8,128)(2,1)S(1)} %get-tuple-element.62), channel_id=1, source_target_pairs={{0,4},{1,5},{2,6},{3,7},{4,0},{5,1},{6,2},{7,3},{8,12},{9,13},{10,... | collective-permute-start | bytes 1572872 | tf_op jit(solution)/shard_map/ppermute | solution.py:397
  20.5 14.9 %collective-permute-start.4 = (bf16[8,2,128,128]{3,2,1,0:T(8,128)(2,1)S(1)}, bf16[8,2,128,128]{3,2,1,0:T(8,128)(2,1)S(1)}, u32[]{:S(2)}, u32[]{:S(2)}) collective-permute-start(bf16[8,2,128,128]{3,2,1,0:T(8,128)(2,1)S(1)} %get-tuple-element.65), channel_id=1, source_target_pairs={{4,8},{5,9},{6,10},{7,11},{8,4},{9,5},{10,6},{11,7},{20,24},{21,25... | collective-permute-start | bytes 1572872 | tf_op jit(solution)/shard_map/ppermute | solution.py:669
  22.0 13.4 %copy-start.1 = (s32[4,4]{1,0:T(4,128)S(1)}, s32[4,4]{1,0:T(4,128)}, u32[]{:S(2)}) copy-start(s32[4,4]{1,0:T(4,128)} %sections.13) | copy-start | bytes 196
  22.0 13.4 %copy-start.2 = (s32[16]{0:T(128)S(1)}, s32[16]{0:T(128)}, u32[]{:S(2)}) copy-start(s32[16]{0:T(128)} %widths.5) | copy-start | bytes 196
  22.0 21.8 %collective-permute-start.5 = (bf16[4,2,128,128]{3,2,1,0:T(8,128)(2,1)}, bf16[4,2,128,128]{3,2,1,0:T(8,128)(2,1)}, u32[]{:S(2)}, u32[]{:S(2)}) collective-permute-start(bf16[4,2,128,128]{3,2,1,0:T(8,128)(2,1)} %get-tuple-element.66), channel_id=1, source_target_pairs={{0,4},{1,5},{2,6},{3,7},{4,0},{5,1},{6,2},{7,3},{8,12},{9,13},{10,... | collective-permute-start | bytes 786440 | tf_op jit(solution)/shard_map/ppermute | solution.py:397
  32.8 15.0 %collective-permute-start.6 = (bf16[4,2,128,128]{3,2,1,0:T(8,128)(2,1)}, bf16[4,2,128,128]{3,2,1,0:T(8,128)(2,1)S(1)}, u32[]{:S(2)}, u32[]{:S(2)}) collective-permute-start(bf16[4,2,128,128]{3,2,1,0:T(8,128)(2,1)} %get-tuple-element.72), channel_id=1, source_target_pairs={{0,8},{1,9},{2,10},{3,11},{4,12},{5,13},{6,14},{7,15},{8,0},{9,1},... | collective-permute-start | bytes 786440 | tf_op jit(solution)/shard_map/ppermute | solution.py:397
  41.0 10.6 %collective-permute-start.13 = (bf16[4,2,128,128]{3,2,1,0:T(8,128)(2,1)S(1)}, bf16[4,2,128,128]{3,2,1,0:T(8,128)(2,1)S(1)}, u32[]{:S(2)}, u32[]{:S(2)}) collective-permute-start(bf16[4,2,128,128]{3,2,1,0:T(8,128)(2,1)S(1)} %get-tuple-element.88), channel_id=1, source_target_pairs={{0,4},{1,5},{2,6},{3,7},{4,0},{5,1},{6,2},{7,3},{8,12},{9,13},{10,... | collective-permute-start | bytes 786440 | tf_op jit(solution)/shard_map/ppermute | solution.py:397
  43.1 8.5 %collective-permute-start.14 = (bf16[4,2,128,128]{3,2,1,0:T(8,128)(2,1)S(1)}, bf16[4,2,128,128]{3,2,1,0:T(8,128)(2,1)S(1)}, u32[]{:S(2)}, u32[]{:S(2)}) collective-permute-start(bf16[4,2,128,128]{3,2,1,0:T(8,128)(2,1)S(1)} %get-tuple-element.89), channel_id=1, source_target_pairs={{4,8},{5,9},{6,10},{7,11},{8,4},{9,5},{10,6},{11,7},{20,24},{21,25... | collective-permute-start | bytes 786440 | tf_op jit(solution)/shard_map/ppermute | solution.py:669
  51.8 5.9 %collective-permute-start.15 = (bf16[6,2,128,128]{3,2,1,0:T(8,128)(2,1)S(1)}, bf16[6,2,128,128]{3,2,1,0:T(8,128)(2,1)S(1)}, u32[]{:S(2)}, u32[]{:S(2)}) collective-permute-start(bf16[6,2,128,128]{3,2,1,0:T(8,128)(2,1)S(1)} %get-tuple-element.95), channel_id=1, source_target_pairs={{0,1},{1,0},{2,3},{3,2},{4,5},{5,4},{6,7},{7,6},{8,9},{9,8},{10,11... | collective-permute-start | bytes 1179656 | tf_op jit(solution)/shard_map/ppermute | solution.py:648
  53.0 19.9 %collective-permute-start.8 = (bf16[8,2,128,128]{3,2,1,0:T(8,128)(2,1)S(1)}, bf16[8,2,128,128]{3,2,1,0:T(8,128)(2,1)S(1)}, u32[]{:S(2)}, u32[]{:S(2)}) collective-permute-start(bf16[8,2,128,128]{3,2,1,0:T(8,128)(2,1)S(1)} %get-tuple-element.81), channel_id=1, source_target_pairs={{0,4},{1,5},{2,6},{3,7},{4,0},{5,1},{6,2},{7,3},{8,12},{9,13},{10,... | collective-permute-start | bytes 1572872 | tf_op jit(solution)/shard_map/ppermute | solution.py:397
  55.1 17.0 %collective-permute-start.7 = (bf16[4,2,128,128]{3,2,1,0:T(8,128)(2,1)S(1)}, bf16[4,2,128,128]{3,2,1,0:T(8,128)(2,1)S(1)}, u32[]{:S(2)}, u32[]{:S(2)}) collective-permute-start(bf16[4,2,128,128]{3,2,1,0:T(8,128)(2,1)S(1)} %get-tuple-element.80), channel_id=1, source_target_pairs={{0,8},{1,9},{2,10},{3,11},{4,12},{5,13},{6,14},{7,15},{8,0},{9,1},... | collective-permute-start | bytes 786440 | tf_op jit(solution)/shard_map/ppermute | solution.py:397
  57.0 15.0 %collective-permute-start.9 = (bf16[4,2,128,128]{3,2,1,0:T(8,128)(2,1)S(1)}, bf16[4,2,128,128]{3,2,1,0:T(8,128)(2,1)S(1)}, u32[]{:S(2)}, u32[]{:S(2)}) collective-permute-start(bf16[4,2,128,128]{3,2,1,0:T(8,128)(2,1)S(1)} %get-tuple-element.82), channel_id=1, source_target_pairs={{4,8},{5,9},{6,10},{7,11},{8,4},{9,5},{10,6},{11,7},{20,24},{21,25... | collective-permute-start | bytes 786440 | tf_op jit(solution)/shard_map/ppermute | solution.py:669
  57.7 17.9 %collective-permute-start.16 = (bf16[6,2,128,128]{3,2,1,0:T(8,128)(2,1)S(1)}, bf16[6,2,128,128]{3,2,1,0:T(8,128)(2,1)S(1)}, u32[]{:S(2)}, u32[]{:S(2)}) collective-permute-start(bf16[6,2,128,128]{3,2,1,0:T(8,128)(2,1)S(1)} %get-tuple-element.100), channel_id=1, source_target_pairs={{0,2},{1,3},{2,0},{3,1},{4,6},{5,7},{6,4},{7,5},{8,10},{9,11},{10,... | collective-permute-start | bytes 1179656 | tf_op jit(solution)/shard_map/ppermute | solution.py:648
  59.3 18.5 %collective-permute-start.17 = (bf16[6,2,128,128]{3,2,1,0:T(8,128)(2,1)S(1)}, bf16[6,2,128,128]{3,2,1,0:T(8,128)(2,1)S(1)}, u32[]{:S(2)}, u32[]{:S(2)}) collective-permute-start(bf16[6,2,128,128]{3,2,1,0:T(8,128)(2,1)S(1)} %get-tuple-element.101), channel_id=1, source_target_pairs={{0,3},{1,2},{2,1},{3,0},{4,7},{5,6},{6,5},{7,4},{8,11},{9,10},{10,... | collective-permute-start | bytes 1179656 | tf_op jit(solution)/shard_map/ppermute | solution.py:648
  73.2 6.4 %collective-permute-start.10 = (bf16[2,2,128,128]{3,2,1,0:T(8,128)(2,1)S(1)}, bf16[2,2,128,128]{3,2,1,0:T(8,128)(2,1)S(1)}, u32[]{:S(2)}, u32[]{:S(2)}) collective-permute-start(bf16[2,2,128,128]{3,2,1,0:T(8,128)(2,1)S(1)} %get-tuple-element.84), channel_id=1, source_target_pairs={{0,1},{1,0},{2,3},{3,2},{4,5},{5,4},{6,7},{7,6},{8,9},{9,8},{10,11... | collective-permute-start | bytes 393224 | tf_op jit(solution)/shard_map/ppermute | solution.py:648
  73.9 5.7 %collective-permute-start.11 = (bf16[2,2,128,128]{3,2,1,0:T(8,128)(2,1)S(1)}, bf16[2,2,128,128]{3,2,1,0:T(8,128)(2,1)S(1)}, u32[]{:S(2)}, u32[]{:S(2)}) collective-permute-start(bf16[2,2,128,128]{3,2,1,0:T(8,128)(2,1)S(1)} %get-tuple-element.85), channel_id=1, source_target_pairs={{0,2},{1,3},{2,0},{3,1},{4,6},{5,7},{6,4},{7,5},{8,10},{9,11},{10,... | collective-permute-start | bytes 393224 | tf_op jit(solution)/shard_map/ppermute | solution.py:648
  75.2 7.4 %collective-permute-start.12 = (bf16[2,2,128,128]{3,2,1,0:T(8,128)(2,1)S(1)}, bf16[2,2,128,128]{3,2,1,0:T(8,128)(2,1)S(1)}, u32[]{:S(2)}, u32[]{:S(2)}) collective-permute-start(bf16[2,2,128,128]{3,2,1,0:T(8,128)(2,1)S(1)} %get-tuple-element.86), channel_id=1, source_target_pairs={{0,3},{1,2},{2,1},{3,0},{4,7},{5,6},{6,5},{7,4},{8,11},{9,10},{10,... | collective-permute-start | bytes 393224 | tf_op jit(solution)/shard_map/ppermute | solution.py:648
